TPU v7x, 128 devices: a whole 4x4x4 slice. The times are simulated.
128 devices in a mesh: segment: 8 (over y, x_hi), tp: 16 (over x_lo, z, core).
Axes of the slice: x: 4 (x_hi: 2, x_lo: 2; x = x_hi * 2 + x_lo), y: 4, z: 4, core: 2. Of those that a mesh axis runs over, the one named last changes fastest.
Arguments:
- memory: bfloat16 [1024, 4096], P('segment', 'tp'), may hold values from -6 to 6
- norm_gain: float32 [4096], replicated, may hold values from 0.1 to 1.9
- queries: bfloat16 [8, 1024, 4096], P('segment', None, 'tp'), may hold values from -200 to 200
- key_weight: bfloat16 [8, 4096, 4096], P('segment', None, 'tp'), may hold values from -0.09375 to 0.09375
- value_weight: bfloat16 [8, 4096, 4096], P('segment', None, 'tp'), may hold values from -0.09375 to 0.09375
- context_grad: bfloat16 [8, 1024, 4096], P('segment', None, 'tp'), may hold values from -6 to 6
Outputs:
- context: bfloat16 [8, 1024, 4096], P('segment', None, 'tp')
- query_grad: bfloat16 [8, 1024, 4096], P('segment', None, 'tp')
- key_weight_grad: float32 [8, 4096, 4096], P('segment', None, 'tp')
- value_weight_grad: float32 [8, 4096, 4096], P('segment', None, 'tp')
- encoder_output_gradient: float32 [1024, 4096], P('segment', 'tp')
All inputs are finite; a program needn't handle non-finite values.
Results may differ from a plain program's by a relative error of at most 0.015.
The roundings to bfloat16 on the way count: a program that leaves them out, or rounds other values in their place, can miss the bound.
Values may be sent and summed in bfloat16 or wider, within the bound.
No kernel may reach another device: no remote copies, remote signals or barrier semaphores. Data moves between devices by JAX's collectives and lax.ppermute only.
A program may use at most 128 MiB of HBM per device.

v0:
```python
import jax
import jax.numpy as jnp
from jax import lax
from jax.sharding import PartitionSpec as P

HD = 256


def joined_along(pieces, dim):
    pieces = jnp.moveaxis(pieces, 0, dim)
    shape = pieces.shape
    return pieces.reshape(*shape[:dim], shape[dim] * shape[dim + 1], *shape[dim + 2 :])


def sent_to_all(value, axis):
    copies = jnp.broadcast_to(value, (lax.axis_size(axis), *value.shape))
    return lax.all_to_all(copies, axis, split_axis=0, concat_axis=0, tiled=True)


def collect(value, axis, dim):
    return joined_along(sent_to_all(value, axis), dim)


def of_everyone(value, axis):
    return sent_to_all(value, axis).sum(axis=0)


def in_blocks(value, dim, size):
    before, after = (value.shape[:dim], value.shape[dim + 1 :])
    return jnp.moveaxis(value.reshape(*before, size, -1, *after), dim, 0)


def summed_on_arrival(value, axis, dim):
    size = lax.axis_size(axis)
    pieces = lax.all_to_all(in_blocks(value, dim, size), axis, 0, 0, tiled=True)
    return jnp.sum(pieces.astype(jnp.float32), axis=0)


def local(memory, norm_gain, queries, key_weight, value_weight, context_grad):
    epsilon_value = 1e-06
    hidden_width = norm_gain.shape[0]
    piece_cols = memory.shape[1]
    rows_own = memory.shape[0]
    tp_index = lax.axis_index("tp")
    segment_index = lax.axis_index("segment")
    own_gain = lax.dynamic_slice_in_dim(norm_gain, tp_index * piece_cols, piece_cols)
    local_row_block = memory.astype(jnp.float32)
    gathered = collect(memory, "segment", 0)
    source_all = gathered.astype(jnp.float32)
    squares = of_everyone(jnp.sum(source_all * source_all, axis=1), "tp")
    scale_all = lax.rsqrt(squares / hidden_width + epsilon_value)
    normed_piece = (source_all * scale_all[:, None] * own_gain).astype(jnp.bfloat16)
    normed = lax.all_gather(normed_piece, "tp", axis=1, tiled=True)
    local_scale = lax.dynamic_slice_in_dim(scale_all, segment_index * rows_own, rows_own)
    key_mat = key_weight[0]
    value_mat = value_weight[0]
    query_rows = queries[0]
    dctx = context_grad[0]
    source_count = normed.shape[0]
    target_count = query_rows.shape[0]
    head_count = key_mat.shape[1] // HD
    scale = HD ** (-0.5)
    key_rows = jnp.dot(normed, key_mat, preferred_element_type=jnp.float32).astype(jnp.bfloat16)
    value_rows = jnp.dot(normed, value_mat, preferred_element_type=jnp.float32).astype(jnp.bfloat16)
    qh = query_rows.reshape(target_count, head_count, HD)
    kh = key_rows.reshape(source_count, head_count, HD)
    vh = value_rows.reshape(source_count, head_count, HD)
    dch = dctx.reshape(target_count, head_count, HD)
    scores = jnp.einsum("qhd,khd->hqk", qh, kh, preferred_element_type=jnp.float32) * scale
    maxima = jnp.max(scores, axis=-1, keepdims=True)
    exponent = jnp.exp(scores - maxima)
    attend = exponent / jnp.sum(exponent, axis=-1, keepdims=True)
    attend_low = attend.astype(jnp.bfloat16)
    context = jnp.einsum("hqk,khd->qhd", attend_low, vh, preferred_element_type=jnp.float32).astype(
        jnp.bfloat16
    )
    grad_attend = jnp.einsum("qhd,khd->hqk", dch, vh, preferred_element_type=jnp.float32)
    row_dots = jnp.sum(grad_attend * attend, axis=-1, keepdims=True)
    grad_scores = (attend * (grad_attend - row_dots) * scale).astype(jnp.bfloat16)
    query_grad = jnp.einsum(
        "hqk,khd->qhd", grad_scores, kh, preferred_element_type=jnp.float32
    ).astype(jnp.bfloat16)
    grad_keys = jnp.einsum(
        "hqk,qhd->khd", grad_scores, qh, preferred_element_type=jnp.float32
    ).astype(jnp.bfloat16)
    grad_values = jnp.einsum(
        "hqk,qhd->khd", attend_low, dch, preferred_element_type=jnp.float32
    ).astype(jnp.bfloat16)
    grad_keys = grad_keys.reshape(source_count, head_count * HD)
    grad_values = grad_values.reshape(source_count, head_count * HD)
    key_grad = jnp.einsum("sd,sc->dc", normed, grad_keys, preferred_element_type=jnp.float32)
    value_grad = jnp.einsum("sd,sc->dc", normed, grad_values, preferred_element_type=jnp.float32)
    total = jnp.einsum("sc,dc->sd", grad_keys, key_mat, preferred_element_type=jnp.float32)
    segment_part = lax.psum_scatter(
        (
            total
            + jnp.einsum("sc,dc->sd", grad_values, value_mat, preferred_element_type=jnp.float32)
        ).astype(jnp.bfloat16),
        "segment",
        scatter_dimension=0,
        tiled=True,
    )
    summed = summed_on_arrival(segment_part, "tp", 1)
    upper_term = summed * own_gain
    centered_normalized = local_row_block * local_scale[:, None]
    inner_product = of_everyone(jnp.sum(upper_term * centered_normalized, axis=1), "tp")
    encoder_output_gradient = local_scale[:, None] * (
        upper_term - centered_normalized * (inner_product / hidden_width)[:, None]
    )
    return (
        context.reshape(1, target_count, head_count * HD),
        query_grad.reshape(1, target_count, head_count * HD),
        key_grad[None],
        value_grad[None],
        encoder_output_gradient,
    )


def solution(mesh):
    placed = (
        P("segment", "tp"),
        P(),
        P("segment", None, "tp"),
        P("segment", None, "tp"),
        P("segment", None, "tp"),
        P("segment", None, "tp"),
    )
    return jax.shard_map(
        local,
        mesh=mesh,
        in_specs=placed,
        out_specs=(
            P("segment", None, "tp"),
            P("segment", None, "tp"),
            P("segment", None, "tp"),
            P("segment", None, "tp"),
            P("segment", "tp"),
        ),
        check_vma=False,
    )
```

profile of v0, /device:TPU:1, one launch (start us, length us, event | category | flops | bytes accessed | tf_op | source)
XLA Modules:
  0.0 292.4 jit_solution(10155391424537069540)
XLA Ops:
  7.2 1.0 broadcast_in_dim.12
  8.2 18.0 %all_to_all.22 = bf16[8,128,256]{2,1,0:T(8,128)(2,1)S(1)} all-to-all(bf16[8,128,256]{2,1,0:T(8,128)(2,1)S(1)} %broadcast_in_dim.12), channel_id=1, replica_groups=mesh['segment'=8,'tp'=16] {'segment'}, dimensions={0} | all-to-all | bytes 1048576 | tf_op jit(solution)/shard_map/all_to_all | solution.py:17
  27.0 7.2 %all-to-all-start.1 = ((f32[16,1,1024]{2,1,0:T(1,128)}), f32[16,1,1024]{2,1,0:T(1,128)S(1)}, u32[]{:S(2)}, u32[]{:S(2)}) async-start(f32[16,1,1024]{2,1,0:T(1,128)} %broadcast_in_dim.28), calls=%async_computation.1 | async-start | bytes 131072 | tf_op jit(solution)/shard_map/all_to_all | solution.py:17
  35.1 5.0 %all-to-all-done.1 = f32[16,1,1024]{2,1,0:T(1,128)S(1)} async-done(((f32[16,1,1024]{2,1,0:T(1,128)}), f32[16,1,1024]{2,1,0:T(1,128)S(1)}, u32[]{:S(2)}, u32[]{:S(2)}) %all-to-all-start.1) | async-done | bytes 65568 | tf_op jit(solution)/shard_map/all_to_all | solution.py:17
  41.2 57.2 %all-gather.2.cloned.1.call-done = bf16[1024,4096]{1,0:T(8,128)(2,1)} async-done(((bf16[1024,256]{1,0:T(8,128)(2,1)}), bf16[1024,4096]{1,0:T(8,128)(2,1)}) %all-gather.2.cloned.1.call-update) | async-done | bytes 8388624 | tf_op jit(solution)/shard_map/all_gather | solution.py:53
  98.4 5.7 %fusion.16 = bf16[1024,256]{1,0:T(8,128)(2,1)S(1)} fusion(bf16[1024,4096]{1,0:T(8,128)(2,1)} %all-gather.2.cloned.1.call-done, bf16[1,4096,256]{2,1,0:T(8,128)(2,1)S(1)} %copy-done), kind=kOutput, calls=%fused_computation.23 | convolution fusion | flops 2147745792 | bytes 11010048 | tf_op jit(solution)/shard_map/dot_general | solution.py:63
  106.7 2.0 slice-done
  109.3 1.2 slice-done.1
  110.5 2.3 fusion.13
  112.9 1.5 fusion
  114.4 1.3 fusion.3
  115.7 1.3 copy-done.3
  117.7 8.1 %fusion.6 = f32[1024,4096]{1,0:T(8,128)} fusion(bf16[1024,256]{1,0:T(8,128)(2,1)S(1)} %convolution_convert_fusion.1, bf16[1,4096,256]{2,1,0:T(8,128)(2,1)S(1)} %copy-done), kind=kOutput, calls=%fused_computation.14 | convolution fusion | flops 2147483648 | bytes 19398656 | tf_op jit(solution)/shard_map/sc,dc->sd/dot_general | solution.py:93
  125.8 11.6 %add_convert_fusion = bf16[1024,4096]{1,0:T(8,128)(2,1)} fusion(f32[1024,4096]{1,0:T(8,128)} %fusion.6, bf16[1024,256]{1,0:T(8,128)(2,1)S(1)} %convolution_convert_fusion, bf16[1,4096,256]{2,1,0:T(8,128)(2,1)S(1)} %copy-done.5), kind=kOutput, calls=%fused_computation | convolution fusion | flops 2155872256 | bytes 27787264 | tf_op jit(solution)/shard_map/sc,dc->sd/dot_general | solution.py:97
  137.5 7.8 %convolution_bitcast_fusion.1 = f32[1,4096,256]{2,1,0:T(8,128)} fusion(bf16[1024,4096]{1,0:T(8,128)(2,1)} %all-gather.2.cloned.1.call-done, bf16[1024,256]{1,0:T(8,128)(2,1)S(1)} %convolution_convert_fusion.1), kind=kOutput, calls=%fused_computation.2 | convolution fusion | flops 2147483648 | bytes 13107200 | tf_op jit(solution)/shard_map/sd,sc->dc/dot_general | solution.py:91
  145.3 104.9 %reduce-scatter.2.cloned.1.call-done = bf16[128,4096]{1,0:T(8,128)(2,1)} async-done(((bf16[1024,4096]{1,0:T(8,128)(2,1)}), bf16[128,4096]{1,0:T(8,128)(2,1)}) %reduce-scatter.2.cloned.1.call-update) | async-done | bytes 1048592 | tf_op jit(solution)/shard_map/reduce_scatter | solution.py:94
  250.2 2.4 copy.31
  252.6 5.7 %all-to-all-start.2 = ((bf16[16,128,256]{2,1,0:T(8,128)(2,1)}), bf16[16,128,256]{2,1,0:T(8,128)(2,1)S(1)}, u32[]{:S(2)}, u32[]{:S(2)}) async-start(bf16[16,128,256]{2,1,0:T(8,128)(2,1)} %bitcast.89), calls=%async_computation.3 | async-start | bytes 2097152 | tf_op jit(solution)/shard_map/all_to_all | solution.py:35
  258.3 4.2 %fusion.19 = bf16[1,1024,256]{1,2,0:T(8,128)(2,1)} fusion(bf16[1024,256]{1,0:T(8,128)(2,1)S(1)} %copy-done.12, f32[1024,1024]{1,0:T(8,128)} %copy-done.2, f32[1024]{0:T(1024)S(1)} %fusion.5, f32[1024]{0:T(1024)S(1)} %get-tuple-element.25), kind=kOutput, calls=%fused_computation.28 | convolution fusion | flops 541327360 | bytes 5251072 | tf_op jit(solution)/shard_map/hqk,khd->qhd/dot_general | solution.py:74
  262.5 8.0 %convolution_bitcast_fusion = f32[1,4096,256]{2,1,0:T(8,128)} fusion(bf16[1024,4096]{1,0:T(8,128)(2,1)} %all-gather.2.cloned.1.call-done, bf16[1024,256]{1,0:T(8,128)(2,1)S(1)} %copy-done.9), kind=kOutput, calls=%fused_computation.1 | convolution fusion | flops 2147483648 | bytes 13107200 | tf_op jit(solution)/shard_map/sd,sc->dc/dot_general | solution.py:92
  270.5 3.6 %all-to-all-done.2 = bf16[16,128,256]{2,1,0:T(8,128)(2,1)S(1)} async-done(((bf16[16,128,256]{2,1,0:T(8,128)(2,1)}), bf16[16,128,256]{2,1,0:T(8,128)(2,1)S(1)}, u32[]{:S(2)}, u32[]{:S(2)}) %all-to-all-start.2) | async-done | bytes 1048608 | tf_op jit(solution)/shard_map/all_to_all | solution.py:35
  275.1 4.1 %all-to-all-start.3 = ((f32[16,1,128]{2,1,0:T(1,128)}), f32[16,1,128]{2,1,0:T(1,128)S(1)}, u32[]{:S(2)}, u32[]{:S(2)}) async-start(f32[16,1,128]{2,1,0:T(1,128)} %broadcast_in_dim.31), calls=%async_computation.4 | async-start | bytes 16384 | tf_op jit(solution)/shard_map/all_to_all | solution.py:17
  279.2 2.5 fusion.20
  281.7 2.0 copy.26
  (51 shorter events, 9.5 us)
Async XLA Ops:
  7.2 91.2 %copy-start = (bf16[1,4096,256]{2,1,0:T(8,128)(2,1)S(1)}, bf16[1,4096,256]{2,1,0:T(8,128)(2,1)}, u32[]{:S(2)}) copy-start(bf16[1,4096,256]{2,1,0:T(8,128)(2,1)} %param.9) | copy-start | bytes 6291460
  27.0 13.0 %all-to-all-start.1 = ((f32[16,1,1024]{2,1,0:T(1,128)}), f32[16,1,1024]{2,1,0:T(1,128)S(1)}, u32[]{:S(2)}, u32[]{:S(2)}) async-start(f32[16,1,1024]{2,1,0:T(1,128)} %broadcast_in_dim.28), calls=%async_computation.1 | async-start | bytes 131072 | tf_op jit(solution)/shard_map/all_to_all | solution.py:17
  34.3 64.1 %all-gather.2.cloned.1.call-start = ((), (), s32[]{:S(2)}) async-start(), calls=%async_computation.5 | async-start | bytes 8912896 | tf_op jit(solution)/shard_map/all_gather | solution.py:53
  41.2 62.9 %copy-start.7 = (bf16[1,1024,256]{2,1,0:T(8,128)(2,1)S(1)}, bf16[1,1024,256]{2,1,0:T(8,128)(2,1)}, u32[]{:S(2)}) copy-start(bf16[1,1024,256]{2,1,0:T(8,128)(2,1)} %param.8) | copy-start | bytes 1572868
  41.2 209.0 %reduce-scatter.2.cloned.1.call-start = ((), (), s32[]{:S(2)}) async-start(), calls=%async_computation.6 | async-start | bytes 9437184 | tf_op jit(solution)/shard_map/reduce_scatter | solution.py:94
  104.1 1.5 copy-start.4
  104.1 1.5 copy-start.10
  104.9 9.5 %copy-start.2 = (f32[1024,1024]{1,0:T(8,128)}, f32[1024,1024]{1,0:T(8,128)S(1)}, u32[]{:S(2)}) copy-start(f32[1024,1024]{1,0:T(8,128)S(1)} %get-tuple-element.26) | copy-start | bytes 12582916
  104.9 3.7 %slice-start = ((s8[8388608]{0:T(1024)(128)(4,1)}), s8[4194304]{0:T(1024)(128)(4,1)S(1)}, s32[]{:S(2)}) async-start(s8[8388608]{0:T(1024)(128)(4,1)} %bitcast.93), calls=%async_computation.7 | async-start | bytes 8388608
  105.7 3.6 %copy-start.5 = (bf16[1,4096,256]{2,1,0:T(8,128)(2,1)S(1)}, bf16[1,4096,256]{2,1,0:T(8,128)(2,1)}, u32[]{:S(2)}) copy-start(bf16[1,4096,256]{2,1,0:T(8,128)(2,1)} %param.10) | copy-start | bytes 6291460
  105.7 4.8 %slice-start.1 = ((s8[8388608]{0:T(1024)(128)(4,1)}), s8[4194304]{0:T(1024)(128)(4,1)S(1)}, s32[]{:S(2)}) async-start(s8[8388608]{0:T(1024)(128)(4,1)} %bitcast.93), calls=%async_computation.8 | async-start | bytes 8388608
  110.5 15.3 %copy-start.8 = (bf16[1024,256]{1,0:T(8,128)(2,1)}, bf16[1024,256]{1,0:T(8,128)(2,1)S(1)}, u32[]{:S(2)}) copy-start(bf16[1024,256]{1,0:T(8,128)(2,1)S(1)} %convolution_convert_fusion) | copy-start | bytes 1572868
  112.8 1.5 copy-start.11
  115.7 1.3 copy-start.3
  145.3 113.0 %copy-start.12 = (bf16[1024,256]{1,0:T(8,128)(2,1)S(1)}, bf16[1024,256]{1,0:T(8,128)(2,1)}, u32[]{:S(2)}) copy-start(bf16[1024,256]{1,0:T(8,128)(2,1)} %copy-done.11) | copy-start | bytes 1572868
  252.6 21.5 %all-to-all-start.2 = ((bf16[16,128,256]{2,1,0:T(8,128)(2,1)}), bf16[16,128,256]{2,1,0:T(8,128)(2,1)S(1)}, u32[]{:S(2)}, u32[]{:S(2)}) async-start(bf16[16,128,256]{2,1,0:T(8,128)(2,1)} %bitcast.89), calls=%async_computation.3 | async-start | bytes 2097152 | tf_op jit(solution)/shard_map/all_to_all | solution.py:35
  258.3 4.2 %copy-start.9 = (bf16[1024,256]{1,0:T(8,128)(2,1)S(1)}, bf16[1024,256]{1,0:T(8,128)(2,1)}, u32[]{:S(2)}) copy-start(bf16[1024,256]{1,0:T(8,128)(2,1)} %copy-done.8) | copy-start | bytes 1572868
  262.5 11.8 %copy-start.6 = (bf16[128,256]{1,0:T(8,128)(2,1)S(1)}, bf16[128,256]{1,0:T(8,128)(2,1)}, u32[]{:S(2)}) copy-start(bf16[128,256]{1,0:T(8,128)(2,1)} %param.6) | copy-start | bytes 196612
  262.5 23.1 %copy-start.1 = (bf16[1,4096,256]{2,1,0:T(8,128)(2,1)S(1)}, bf16[1,4096,256]{2,1,0:T(8,128)(2,1)}, u32[]{:S(2)}) copy-start(bf16[1,4096,256]{2,1,0:T(8,128)(2,1)} %param.9) | copy-start | bytes 6291460
  275.1 9.7 %all-to-all-start.3 = ((f32[16,1,128]{2,1,0:T(1,128)}), f32[16,1,128]{2,1,0:T(1,128)S(1)}, u32[]{:S(2)}, u32[]{:S(2)}) async-start(f32[16,1,128]{2,1,0:T(1,128)} %broadcast_in_dim.31), calls=%async_computation.4 | async-start | bytes 16384 | tf_op jit(solution)/shard_map/all_to_all | solution.py:17
Sparse Core Ops, SparseCore 0:
  41.3 57.0 all-gather.1
  137.5 112.6 reduce-scatter.1
where the time goes:
time: 293 us; the launch traced here: 292 us
  waiting for transfers between devices  171 us (58%)
  matrix products  54.2 us (18%)
  blocking collectives  18 us (6%)
  starting transfers between devices  17.1 us (6%)
  between operations  14.3 us (5%)
  local copies, waits for them, and re-layouts  13.8 us (5%)
  other arithmetic  4.37 us (1%)
    reduce_scatter x1, waiting for transfers between devices, local(): lax.psum_scatter((total + jnp.einsum('sc,dc->sd', grad_values, value_mat,...  105 us
    all_gather x1, waiting for transfers between devices, local(): normed = lax.all_gather(normed_piece, 'tp', axis=1, tiled=True)  57.2 us
    all_to_all x1, blocking collectives, sent_to_all(): return lax.all_to_all(copies, axis, split_axis=0, concat_axis=0, tiled=True)  18 us
    dot_general x1, matrix products, local(): jnp.einsum('sc,dc->sd', grad_values, value_mat, preferred_element_type=jn...  11.6 us
    all_to_all x2, starting transfers between devices, sent_to_all(): return lax.all_to_all(copies, axis, split_axis=0, concat_axis=0, tiled=True)  11.3 us
    unnamed x32, local copies, waits for them, and re-layouts  8.26 us
    dot_general x1, matrix products, local(): jnp.einsum('sc,dc->sd', grad_keys, key_mat, preferred_element_type=jnp.fl...  8.1 us
    dot_general x1, matrix products, local(): jnp.einsum('sd,sc->dc', normed, grad_values, preferred_element_type=jnp.f...  8.01 us
  transfers between devices with their start and end apart: 5, of which 4 were waited for; matrix products, arithmetic and copies ran while one was open for 9% of the time, Pallas kernels for 0%

commit v1 on v0

v1 whole, which is shorter than its diff:
```python
import functools

import jax
import jax.numpy as jnp
from jax import lax
from jax.experimental import pallas as pl
from jax.experimental.pallas import tpu as pltpu
from jax.sharding import Mesh
from jax.sharding import PartitionSpec as P

HD = 256
AXES = ("y", "xh", "xl", "z", "c")
CHIPS = ("y", "xh", "xl", "z")
EPS = 1e-06
F32 = jnp.float32
BF16 = jnp.bfloat16
VMEM_LIMIT = 56 * 2**20


def params():
    return pltpu.CompilerParams(vmem_limit_bytes=VMEM_LIMIT)


def nn(a, b):
    return lax.dot_general(a, b, (((1,), (0,)), ((), ())), preferred_element_type=F32)


def nt(a, b):
    return lax.dot_general(a, b, (((1,), (1,)), ((), ())), preferred_element_type=F32)


def tn(a, b):
    return lax.dot_general(a, b, (((0,), (0,)), ((), ())), preferred_element_type=F32)


def project_body(blocks, x_ref, gain_ref, ko_ref, vo_ref, ks_ref, vs_ref,
                 own_ref, sib_ref, normed_ref, scale_ref, held, acc_own, acc_sib, squares):
    i = pl.program_id(0)
    rows, width = held.shape[1:]

    @pl.when(i == 0)
    def _():
        squares[...] = jnp.zeros_like(squares)
        acc_own[...] = jnp.zeros_like(acc_own)
        acc_sib[...] = jnp.zeros_like(acc_sib)

    @pl.when(i < blocks)
    def _():
        block = x_ref[:, 0].reshape(rows, width)
        held[i] = block
        wide = block.astype(F32)
        squares[...] += jnp.sum(wide * wide, axis=1, keepdims=True)

    @pl.when(i == blocks)
    def _():
        scale_ref[...] = lax.rsqrt(squares[...] / (blocks * width) + EPS)

    @pl.when(i >= blocks)
    def _():
        block = (held[i - blocks].astype(F32) * scale_ref[...] * gain_ref[0]).astype(BF16)
        normed_ref[0] = block
        acc_own[:, :HD] += nn(block, ko_ref[...])
        acc_own[:, HD:] += nn(block, vo_ref[...])
        acc_sib[:, :HD] += nn(block, ks_ref[...])
        acc_sib[:, HD:] += nn(block, vs_ref[...])

    @pl.when(i == 2 * blocks - 1)
    def _():
        own_ref[...] = acc_own[...].astype(BF16)
        sib_ref[...] = acc_sib[...].astype(BF16)


def project(x, gain, key_own, value_own, key_sib, value_sib):
    segs, blocks, part, width = x.shape
    rows = segs * part
    late = lambda i: jnp.maximum(i - blocks, 0)
    weight = pl.BlockSpec((width, HD), lambda i: (late(i), 0))
    whole = pl.BlockSpec((rows, 2 * HD), lambda i: (0, 0))
    return pl.pallas_call(
        functools.partial(project_body, blocks),
        grid=(2 * blocks,),
        in_specs=[
            pl.BlockSpec((segs, 1, part, width), lambda i: (0, jnp.minimum(i, blocks - 1), 0, 0)),
            pl.BlockSpec((1, 1, width), lambda i: (late(i), 0, 0)),
            weight, weight, weight, weight,
        ],
        out_specs=[
            whole, whole,
            pl.BlockSpec((1, rows, width), lambda i: (late(i), 0, 0)),
            pl.BlockSpec((rows, 1), lambda i: (0, 0)),
        ],
        out_shape=[
            jax.ShapeDtypeStruct((rows, 2 * HD), BF16),
            jax.ShapeDtypeStruct((rows, 2 * HD), BF16),
            jax.ShapeDtypeStruct((blocks, rows, width), BF16),
            jax.ShapeDtypeStruct((rows, 1), F32),
        ],
        scratch_shapes=[
            pltpu.VMEM((blocks, rows, width), BF16),
            pltpu.VMEM((rows, 2 * HD), F32),
            pltpu.VMEM((rows, 2 * HD), F32),
            pltpu.VMEM((rows, 1), F32),
        ],
        compiler_params=params(),
        cost_estimate=pl.CostEstimate(flops=2 * rows * blocks * width * 4 * HD, bytes_accessed=16 * 2**20, transcendentals=0),
        name="project",
    )(x, gain.reshape(blocks, 1, width), key_own, value_own, key_sib, value_sib)


def attend_body(q_ref, dc_ref, near_ref, far_ref, ctx_ref, qg_ref, gnear_ref, gfar_ref,
                keys, values, gkeys, gvalues):
    i = pl.program_id(0)
    half = near_ref.shape[0]
    scale = HD ** (-0.5)

    @pl.when(i == 0)
    def _():
        keys[:half] = near_ref[:, :HD]
        keys[half:] = far_ref[:, :HD]
        values[:half] = near_ref[:, HD:]
        values[half:] = far_ref[:, HD:]
        gkeys[...] = jnp.zeros_like(gkeys)
        gvalues[...] = jnp.zeros_like(gvalues)

    q, dc, k, v = q_ref[...], dc_ref[...], keys[...], values[...]
    scores = nt(q, k) * scale
    expo = jnp.exp(scores - jnp.max(scores, axis=-1, keepdims=True))
    attend = expo / jnp.sum(expo, axis=-1, keepdims=True)
    low = attend.astype(BF16)
    ctx_ref[...] = nn(low, v).astype(BF16)
    gattend = nt(dc, v)
    dots = jnp.sum(gattend * attend, axis=-1, keepdims=True)
    gscores = (attend * (gattend - dots) * scale).astype(BF16)
    qg_ref[...] = nn(gscores, k).astype(BF16)
    gkeys[...] += tn(gscores, q)
    gvalues[...] += tn(low, dc)

    @pl.when(i == pl.num_programs(0) - 1)
    def _():
        gnear_ref[:, :HD] = gkeys[:half].astype(BF16)
        gnear_ref[:, HD:] = gvalues[:half].astype(BF16)
        gfar_ref[:, :HD] = gkeys[half:].astype(BF16)
        gfar_ref[:, HD:] = gvalues[half:].astype(BF16)


def attention(q, dc, near, far, tile=256):
    targets, half = q.shape[0], near.shape[0]
    tiled = pl.BlockSpec((tile, HD), lambda i: (i, 0))
    whole = pl.BlockSpec((half, 2 * HD), lambda i: (0, 0))
    return pl.pallas_call(
        attend_body,
        grid=(targets // tile,),
        in_specs=[tiled, tiled, whole, whole],
        out_specs=[tiled, tiled, whole, whole],
        out_shape=[jax.ShapeDtypeStruct((targets, HD), BF16)] * 2
        + [jax.ShapeDtypeStruct((half, 2 * HD), BF16)] * 2,
        scratch_shapes=[pltpu.VMEM((2 * half, HD), BF16)] * 2 + [pltpu.VMEM((2 * half, HD), F32)] * 2,
        compiler_params=params(),
        cost_estimate=pl.CostEstimate(flops=12 * targets * 2 * half * HD, bytes_accessed=8 * 2**20, transcendentals=targets * 2 * half),
        name="attention",
    )(q, dc, near, far)


def back_body(own_ref, sib_ref, ko_ref, vo_ref, ks_ref, vs_ref, out_ref):
    total = nt(own_ref[:, :HD], ko_ref[...])
    total += nt(own_ref[:, HD:], vo_ref[...])
    total += nt(sib_ref[:, :HD], ks_ref[...])
    total += nt(sib_ref[:, HD:], vs_ref[...])
    out_ref[:, 0] = total.astype(BF16).reshape(out_ref.shape[0], *out_ref.shape[2:])


def back(own, sib, key_own, value_own, key_sib, value_sib, segs, blocks):
    rows = own.shape[0]
    width = key_own.shape[0] // blocks
    weight = pl.BlockSpec((width, HD), lambda i: (i, 0))
    whole = pl.BlockSpec((rows, 2 * HD), lambda i: (0, 0))
    return pl.pallas_call(
        back_body,
        grid=(blocks,),
        in_specs=[whole, whole, weight, weight, weight, weight],
        out_specs=pl.BlockSpec((segs, 1, rows // segs, width), lambda i: (0, i, 0, 0)),
        out_shape=jax.ShapeDtypeStruct((segs, blocks, rows // segs, width), BF16),
        compiler_params=params(),
        cost_estimate=pl.CostEstimate(flops=2 * rows * blocks * width * 4 * HD, bytes_accessed=14 * 2**20, transcendentals=0),
        name="back",
    )(own, sib, key_own, value_own, key_sib, value_sib)


def weights_body(near_ref, far_ref, gnear_ref, gfar_ref, gk_ref, gv_ref):
    total = tn(near_ref[0], gnear_ref[...]) + tn(far_ref[0], gfar_ref[...])
    gk_ref[...] = total[:, :HD]
    gv_ref[...] = total[:, HD:]


def weight_grads(near, far, gnear, gfar):
    blocks, rows, width = near.shape
    block = pl.BlockSpec((1, rows, width), lambda i: (i, 0, 0))
    whole = pl.BlockSpec((rows, 2 * HD), lambda i: (0, 0))
    out = pl.BlockSpec((width, HD), lambda i: (i, 0))
    return pl.pallas_call(
        weights_body,
        grid=(blocks,),
        in_specs=[block, block, whole, whole],
        out_specs=[out, out],
        out_shape=[jax.ShapeDtypeStruct((blocks * width, HD), F32)] * 2,
        compiler_params=params(),
        cost_estimate=pl.CostEstimate(flops=8 * rows * blocks * width * HD, bytes_accessed=17 * 2**20, transcendentals=0),
        name="weight_grads",
    )(near, far, gnear, gfar)


def swapped(value):
    return lax.ppermute(value, "c", [(0, 1), (1, 0)])


def local(memory, norm_gain, queries, key_weight, value_weight, context_grad):
    hidden = norm_gain.shape[0]
    rows_own, cols_own = memory.shape
    half, width = rows_own // 2, 2 * cols_own
    core = lax.axis_index("c")
    segment = lax.axis_index(("y", "xh"))
    pair = lax.axis_index(("xl", "z"))
    segs = lax.axis_size(("y", "xh"))
    blocks = lax.axis_size(("xl", "z"))
    key_own, value_own = key_weight[0], value_weight[0]
    halves = memory.reshape(2, half, cols_own)
    mine = lax.dynamic_index_in_dim(halves, core, 0, keepdims=False)
    other = swapped(lax.dynamic_index_in_dim(halves, 1 - core, 0, keepdims=False))
    key_sib, value_sib = swapped(key_own), swapped(value_own)
    block = jnp.where(
        core == 0, jnp.concatenate([mine, other], axis=1), jnp.concatenate([other, mine], axis=1)
    )
    copies = jnp.broadcast_to(block, (segs * blocks, half, width))
    everything = lax.all_to_all(copies, CHIPS, 0, 0, tiled=True).reshape(segs, blocks, half, width)
    own, sib, normed, scale = project(everything, norm_gain, key_own, value_own, key_sib, value_sib)
    far = swapped(sib)
    normed_far = swapped(normed)
    context, query_grad, gnear, gfar = attention(queries[0], context_grad[0], own, far)
    gsib = swapped(gfar)
    parts = back(gnear, gsib, key_own, value_own, key_sib, value_sib, segs, blocks)
    arrived = lax.all_to_all(parts.reshape(segs * blocks, half, width), CHIPS, 0, 0, tiled=True)
    key_grad, value_grad = weight_grads(normed, normed_far, gnear, gfar)
    summed = jnp.sum(arrived.astype(F32), axis=0)
    own_gain = lax.dynamic_slice_in_dim(norm_gain, pair * width, width)
    own_scale = lax.dynamic_slice_in_dim(scale, segment * half, half)
    upper = summed * own_gain
    centered = block.astype(F32) * own_scale
    inner = jnp.sum(upper * centered, axis=1)
    inner = lax.all_to_all(jnp.broadcast_to(inner, (blocks, half)), ("xl", "z"), 0, 0, tiled=True).sum(axis=0)
    result = own_scale * (upper - centered * (inner / hidden)[:, None])
    result = jnp.moveaxis(result.reshape(half, 2, cols_own), 1, 0)
    kept = lax.dynamic_index_in_dim(result, core, 0, keepdims=False)
    came = swapped(lax.dynamic_index_in_dim(result, 1 - core, 0, keepdims=False))
    result = jnp.where(core == 0, jnp.concatenate([kept, came]), jnp.concatenate([came, kept]))
    return context[None], query_grad[None], key_grad[None], value_grad[None], result


def solution(mesh):
    fine = Mesh(mesh.devices.reshape(4, 2, 2, 4, 2), AXES)
    seg, tp = ("y", "xh"), ("xl", "z", "c")
    heads = P(seg, None, tp)
    return jax.shard_map(
        local,
        mesh=fine,
        in_specs=(P(seg, tp), P(), heads, heads, heads, heads),
        out_specs=(heads, heads, heads, heads, P(seg, tp)),
        check_vma=False,
    )
```

time: 293 us -> 204 us (0.70)
  waiting for transfers between devices: 171 us -> 107 us
  matrix products: 54.2 us -> 0 us
  Pallas kernels: 0 us -> 46.4 us
  starting transfers between devices: 17.1 us -> 36.7 us
  blocking collectives: 18 us -> 0 us
  between operations: 14.3 us -> 0.7 us
  local copies, waits for them, and re-layouts: 13.8 us -> 8.51 us
    reduce_scatter x1 -> x0, waiting for transfers between devices: 105 us -> none  [local(): lax.psum_scatter((total + jnp.einsum('sc,dc->sd', grad_values, value_mat,...]
    all_to_all x3, waiting for transfers between devices: 8.64 us -> 96.5 us  [the longest x1 48.6 us: local(): lax.all_to_all(parts.reshape(segs * blocks, half, width), CHIPS, 0, 0, ti...]
    all_gather x1 -> x0, waiting for transfers between devices: 57.2 us -> none  [local(): normed = lax.all_gather(normed_piece, 'tp', axis=1, tiled=True)]
    dot_general x12 -> x0, matrix products: 54.2 us -> none  [the longest x1 11.6 us: local(): jnp.einsum('sc,dc->sd', grad_values, value_mat, preferred_element_type=jn...]
    pallas_call x0 -> x4, Pallas kernels: none -> 46.4 us  [the longest x1 16.2 us: project(): pl.pallas_call(functools.partial(project_body, blocks), grid=(2 * blocks,...]
    all_to_all x1 -> x0, blocking collectives: 18 us -> none  [sent_to_all(): return lax.all_to_all(copies, axis, split_axis=0, concat_axis=0, tiled=True)]
    all_to_all x3, starting transfers between devices: 17 us -> 28.9 us  [the longest x1 11.6 us: local(): lax.all_to_all(copies, CHIPS, 0, 0, tiled=True)]
    ppermute x0 -> x7, waiting for transfers between devices: none -> 10.1 us  [swapped(): return lax.ppermute(value, 'c', [(0, 1), (1, 0)])]
  transfers between devices with their start and end apart: 5 -> 10, of which waited for: 4 -> 7; matrix products, arithmetic and copies ran while one was open for 9% -> 3% of each run, Pallas kernels for 0% -> 6%
where the time goes in v1:
time: 204 us; the launch traced here: 203 us
  waiting for transfers between devices  107 us (52%)
  Pallas kernels  46.4 us (23%)
  starting transfers between devices  36.7 us (18%)
  local copies, waits for them, and re-layouts  8.51 us (4%)
  other arithmetic  3.81 us (2%)
    all_to_all x1, waiting for transfers between devices, local(): lax.all_to_all(parts.reshape(segs * blocks, half, width), CHIPS, 0, 0, ti...  48.6 us
    all_to_all x1, waiting for transfers between devices, local(): lax.all_to_all(copies, CHIPS, 0, 0, tiled=True)  43 us
    pallas_call x1, Pallas kernels, project(): pl.pallas_call(functools.partial(project_body, blocks), grid=(2 * blocks,...  16.2 us
    all_to_all x1, starting transfers between devices, local(): lax.all_to_all(copies, CHIPS, 0, 0, tiled=True)  11.6 us
    pallas_call x1, Pallas kernels, weight_grads(): pl.pallas_call(weights_body, grid=(blocks,), in_specs=[block, block, whol...  11.2 us
    all_to_all x1, starting transfers between devices, local(): lax.all_to_all(parts.reshape(segs * blocks, half, width), CHIPS, 0, 0, ti...  10.6 us
    pallas_call x1, Pallas kernels, back(): pl.pallas_call(back_body, grid=(blocks,), in_specs=[whole, whole, weight,...  10.6 us
    ppermute x7, waiting for transfers between devices, swapped(): return lax.ppermute(value, 'c', [(0, 1), (1, 0)])  10.1 us
  transfers between devices with their start and end apart: 10, of which 7 were waited for; matrix products, arithmetic and copies ran while one was open for 3% of the time, Pallas kernels for 6%

profile of v1, /device:TPU:1, one launch (start us, length us, event | category | flops | bytes accessed | tf_op | source)
XLA Modules:
  0.0 202.8 jit_solution(10252365049044968519)
XLA Ops:
  0.6 0.8 dynamic-slice_bitcast_fusion.3
  1.4 1.5 collective-permute-start
  2.9 0.9 collective-permute-done
  3.8 2.5 %broadcast_in_dim.20 = bf16[64,64,512]{2,1,0:T(8,128)(2,1)} broadcast(bf16[64,512]{1,0:T(8,128)(2,1)S(1)} %maximum_select_fusion.1), dimensions={1,2} | broadcast | bytes 4259840 | tf_op jit(solution)/shard_map/broadcast_in_dim | solution.py:233
  6.3 11.6 %all-to-all-start = ((bf16[64,64,512]{2,1,0:T(8,128)(2,1)}), bf16[64,64,512]{2,1,0:T(8,128)(2,1)}, u32[]{:S(2)}, u32[]{:S(2)}) async-start(bf16[64,64,512]{2,1,0:T(8,128)(2,1)} %broadcast_in_dim.20), calls=%async_computation | async-start | bytes 8388608 | tf_op jit(solution)/shard_map/all_to_all | solution.py:234
  18.7 5.8 %collective-permute-done.1.ks_ref = bf16[4096,256]{1,0:T(8,128)(2,1)S(1)} collective-permute-done((bf16[4096,256]{1,0:T(8,128)(2,1)S(1)}, bf16[4096,256]{1,0:T(8,128)(2,1)S(1)}, u32[]{:S(2)}, u32[]{:S(2)}) %collective-permute-start.1) | collective-permute-done | bytes 2097184 | tf_op jit(solution)/shard_map/ppermute | solution.py:213
  24.5 1.3 copy-done.1
  25.8 43.0 %all-to-all-done = bf16[64,64,512]{2,1,0:T(8,128)(2,1)} async-done(((bf16[64,64,512]{2,1,0:T(8,128)(2,1)}), bf16[64,64,512]{2,1,0:T(8,128)(2,1)}, u32[]{:S(2)}, u32[]{:S(2)}) %all-to-all-start) | async-done | bytes 4194336 | tf_op jit(solution)/shard_map/all_to_all | solution.py:234
  68.8 16.2 %project.1 = (bf16[512,512]{1,0:T(8,128)(2,1)}, bf16[512,512]{1,0:T(8,128)(2,1)}, bf16[8,512,512]{2,1,0:T(8,128)(2,1)}, f32[512,1]{1,0:T(8,128)}) custom-call(bf16[8,8,64,512]{3,2,1,0:T(8,128)(2,1)} %bitcast.5.x_ref, f32[8,1,512]{2,1,0:T(1,128)} %bitcast.36, bf16[4096,256]{1,0:T(8,128)(2,1)} %bitcast.37, bf16[4096,256]{1,0:T(8,128)(2,1)} %bitcast.41, ...), custom_call_target="tpu_custom_call" | custom-call | flops 4294967296 | bytes 16777216 | tf_op jit(solution)/shard_map/project/pallas_call | solution.py:79
  85.0 1.4 collective-permute-start.3
  86.5 1.7 collective-permute-done.3.far_ref
  88.2 0.8 copy-done.2
  89.0 8.5 %attention.1 = (bf16[1024,256]{1,0:T(8,128)(2,1)}, bf16[1024,256]{1,0:T(8,128)(2,1)}, bf16[512,512]{1,0:T(8,128)(2,1)}, bf16[512,512]{1,0:T(8,128)(2,1)}) custom-call(bf16[1024,256]{1,0:T(8,128)(2,1)} %bitcast.43, bf16[1024,256]{1,0:T(8,128)(2,1)} %bitcast.44, bf16[512,512]{1,0:T(8,128)(2,1)} %get-tuple-element.15.near_ref, bf16[512,512]{1,0:T(8,128)(2,1)} %copy-done.2), custom_call_target="tpu_custom_call" | custom-call | flops 3221225472 | bytes 8388608 | tf_op jit(solution)/shard_map/attention/pallas_call | solution.py:150
  98.0 1.7 collective-permute-done.5.sib_ref
  99.7 0.8 copy-done.3
  100.5 10.6 %back.1 = bf16[8,8,64,512]{3,2,1,0:T(8,128)(2,1)} custom-call(bf16[512,512]{1,0:T(8,128)(2,1)} %get-tuple-element.20.gnear_ref.own_ref, bf16[512,512]{1,0:T(8,128)(2,1)} %copy-done.3, bf16[4096,256]{1,0:T(8,128)(2,1)} %bitcast.38, bf16[4096,256]{1,0:T(8,128)(2,1)} %bitcast.42, bf16[4096,256]{1,0:T(8,128)(2,1)} %copy-done.1, ...), custom_call_target="tpu_custom_call" | custom-call | flops 4294967296 | bytes 14680064 | tf_op jit(solution)/shard_map/back/pallas_call | solution.py:177
  111.1 10.6 %all-to-all-start.1 = ((bf16[64,64,512]{2,1,0:T(8,128)(2,1)}), bf16[64,64,512]{2,1,0:T(8,128)(2,1)}, u32[]{:S(2)}, u32[]{:S(2)}) async-start(bf16[64,64,512]{2,1,0:T(8,128)(2,1)} %bitcast.31), calls=%async_computation.1 | async-start | bytes 8388608 | tf_op jit(solution)/shard_map/all_to_all | solution.py:241
  123.2 0.9 dynamic-slice_reduce_fusion
  124.0 48.6 %all-to-all-done.1 = bf16[64,64,512]{2,1,0:T(8,128)(2,1)} async-done(((bf16[64,64,512]{2,1,0:T(8,128)(2,1)}), bf16[64,64,512]{2,1,0:T(8,128)(2,1)}, u32[]{:S(2)}, u32[]{:S(2)}) %all-to-all-start.1) | async-done | bytes 4194336 | tf_op jit(solution)/shard_map/all_to_all | solution.py:241
  172.7 2.8 %convert_reduce_fusion = f32[64,512]{1,0:T(8,128)S(1)} fusion(bf16[64,64,512]{2,1,0:T(8,128)(2,1)} %all-to-all-done.1), kind=kLoop, calls=%fused_computation | loop fusion | flops 4161536 | bytes 4325376 | tf_op jit(solution)/shard_map/reduce_sum | solution.py:243
  176.3 6.7 %all-to-all-start.2 = ((f32[8,1,64]{2,1,0:T(1,128)}), f32[8,1,64]{2,1,0:T(1,128)S(1)}, u32[]{:S(2)}, u32[]{:S(2)}) async-start(f32[8,1,64]{2,1,0:T(1,128)} %broadcast_in_dim.25), calls=%async_computation.2 | async-start | bytes 8192 | tf_op jit(solution)/shard_map/all_to_all | solution.py:249
  183.0 4.9 %all-to-all-done.2 = f32[8,1,64]{2,1,0:T(1,128)S(1)} async-done(((f32[8,1,64]{2,1,0:T(1,128)}), f32[8,1,64]{2,1,0:T(1,128)S(1)}, u32[]{:S(2)}, u32[]{:S(2)}) %all-to-all-start.2) | async-done | bytes 2080 | tf_op jit(solution)/shard_map/all_to_all | solution.py:249
  188.1 2.9 %collective-permute-start.6 = (f32[64,256]{1,0:T(8,128)S(1)}, f32[64,256]{1,0:T(8,128)S(1)}, u32[]{:S(2)}, u32[]{:S(2)}) collective-permute-start(f32[64,256]{1,0:T(8,128)S(1)} %get-tuple-element.26), channel_id=1, source_target_pairs={{0,1},{1,0},{2,3},{3,2},{4,5},{5,4},{6,7},{7,6},{8,9},{9,8},{10,11... | collective-permute-start | bytes 196616 | tf_op jit(solution)/shard_map/ppermute | solution.py:213
  191.0 11.2 %weight_grads.1 = (f32[4096,256]{1,0:T(8,128)}, f32[4096,256]{1,0:T(8,128)}) custom-call(bf16[8,512,512]{2,1,0:T(8,128)(2,1)} %get-tuple-element.19.near_ref, bf16[8,512,512]{2,1,0:T(8,128)(2,1)} %collective-permute-done.4.far_ref, bf16[512,512]{1,0:T(8,128)(2,1)} %get-tuple-element.20.gnear_ref.own_ref, bf16[512,512]{1,0:T(8,128)(2,1)} %get-tuple-element.21.gfar_ref), custom_call_target="tpu_custom_call" | custom-call | flops 4294967296 | bytes 17825792 | tf_op jit(solution)/shard_map/weight_grads/pallas_call | solution.py:200
  (22 shorter events, 4.4 us)
Async XLA Ops:
  1.4 2.3 %collective-permute-start = (bf16[64,256]{1,0:T(8,128)(2,1)S(1)}, bf16[64,256]{1,0:T(8,128)(2,1)S(1)}, u32[]{:S(2)}, u32[]{:S(2)}) collective-permute-start(bf16[64,256]{1,0:T(8,128)(2,1)S(1)} %get-tuple-element.28), channel_id=1, source_target_pairs={{0,1},{1,0},{2,3},{3,2},{4,5},{5,4},{6,7},{7,6},{8,9},{9,8},{10,11... | collective-permute-start | bytes 98312 | tf_op jit(solution)/shard_map/ppermute | solution.py:213
  6.3 11.6 %copy-start = (bf16[1,4096,256]{2,1,0:T(8,128)(2,1)S(1)}, bf16[1,4096,256]{2,1,0:T(8,128)(2,1)}, u32[]{:S(2)}) copy-start(bf16[1,4096,256]{2,1,0:T(8,128)(2,1)} %param.9) | copy-start | bytes 6291460
  6.3 62.5 %all-to-all-start = ((bf16[64,64,512]{2,1,0:T(8,128)(2,1)}), bf16[64,64,512]{2,1,0:T(8,128)(2,1)}, u32[]{:S(2)}, u32[]{:S(2)}) async-start(bf16[64,64,512]{2,1,0:T(8,128)(2,1)} %broadcast_in_dim.20), calls=%async_computation | async-start | bytes 8388608 | tf_op jit(solution)/shard_map/all_to_all | solution.py:234
  17.9 6.6 %collective-permute-start.1 = (bf16[4096,256]{1,0:T(8,128)(2,1)S(1)}, bf16[4096,256]{1,0:T(8,128)(2,1)S(1)}, u32[]{:S(2)}, u32[]{:S(2)}) collective-permute-start(bf16[4096,256]{1,0:T(8,128)(2,1)S(1)} %bitcast.39), channel_id=1, source_target_pairs={{0,1},{1,0},{2,3},{3,2},{4,5},{5,4},{6,7},{7,6},{8,9},{9,8},{10,11... | collective-permute-start | bytes 6291464 | tf_op jit(solution)/shard_map/ppermute | solution.py:213
  18.6 7.2 %collective-permute-start.2 = (bf16[4096,256]{1,0:T(8,128)(2,1)}, bf16[4096,256]{1,0:T(8,128)(2,1)}, u32[]{:S(2)}, u32[]{:S(2)}) collective-permute-start(bf16[4096,256]{1,0:T(8,128)(2,1)} %bitcast.40), channel_id=1, source_target_pairs={{0,1},{1,0},{2,3},{3,2},{4,5},{5,4},{6,7},{7,6},{8,9},{9,8},{10,11... | collective-permute-start | bytes 6291464 | tf_op jit(solution)/shard_map/ppermute | solution.py:213
  24.5 1.3 copy-start.1
  85.0 3.2 %collective-permute-start.3 = (bf16[512,512]{1,0:T(8,128)(2,1)}, bf16[512,512]{1,0:T(8,128)(2,1)S(1)}, u32[]{:S(2)}, u32[]{:S(2)}) collective-permute-start(bf16[512,512]{1,0:T(8,128)(2,1)} %get-tuple-element.16), channel_id=1, source_target_pairs={{0,1},{1,0},{2,3},{3,2},{4,5},{5,4},{6,7},{7,6},{8,9},{9,8},{10,11... | collective-permute-start | bytes 1572872 | tf_op jit(solution)/shard_map/ppermute | solution.py:213
  88.2 0.8 copy-start.2
  97.5 2.2 %collective-permute-start.5 = (bf16[512,512]{1,0:T(8,128)(2,1)}, bf16[512,512]{1,0:T(8,128)(2,1)S(1)}, u32[]{:S(2)}, u32[]{:S(2)}) collective-permute-start(bf16[512,512]{1,0:T(8,128)(2,1)} %get-tuple-element.21.gfar_ref), channel_id=1, source_target_pairs={{0,1},{1,0},{2,3},{3,2},{4,5},{5,4},{6,7},{7,6},{8,9},{9,8},{10,11... | collective-permute-start | bytes 1572872 | tf_op jit(solution)/shard_map/ppermute | solution.py:213
  99.7 0.8 copy-start.3
  111.1 61.6 %all-to-all-start.1 = ((bf16[64,64,512]{2,1,0:T(8,128)(2,1)}), bf16[64,64,512]{2,1,0:T(8,128)(2,1)}, u32[]{:S(2)}, u32[]{:S(2)}) async-start(bf16[64,64,512]{2,1,0:T(8,128)(2,1)} %bitcast.31), calls=%async_computation.1 | async-start | bytes 8388608 | tf_op jit(solution)/shard_map/all_to_all | solution.py:241
  121.7 69.3 %collective-permute-start.4 = (bf16[8,512,512]{2,1,0:T(8,128)(2,1)}, bf16[8,512,512]{2,1,0:T(8,128)(2,1)}, u32[]{:S(2)}, u32[]{:S(2)}) collective-permute-start(bf16[8,512,512]{2,1,0:T(8,128)(2,1)} %get-tuple-element.19.near_ref), channel_id=1, source_target_pairs={{0,1},{1,0},{2,3},{3,2},{4,5},{5,4},{6,7},{7,6},{8,9},{9,8},{10,11... | collective-permute-start | bytes 12582920 | tf_op jit(solution)/shard_map/ppermute | solution.py:213
  176.3 11.7 %all-to-all-start.2 = ((f32[8,1,64]{2,1,0:T(1,128)}), f32[8,1,64]{2,1,0:T(1,128)S(1)}, u32[]{:S(2)}, u32[]{:S(2)}) async-start(f32[8,1,64]{2,1,0:T(1,128)} %broadcast_in_dim.25), calls=%async_computation.2 | async-start | bytes 8192 | tf_op jit(solution)/shard_map/all_to_all | solution.py:249
  188.1 14.1 %collective-permute-start.6 = (f32[64,256]{1,0:T(8,128)S(1)}, f32[64,256]{1,0:T(8,128)S(1)}, u32[]{:S(2)}, u32[]{:S(2)}) collective-permute-start(f32[64,256]{1,0:T(8,128)S(1)} %get-tuple-element.26), channel_id=1, source_target_pairs={{0,1},{1,0},{2,3},{3,2},{4,5},{5,4},{6,7},{7,6},{8,9},{9,8},{10,11... | collective-permute-start | bytes 196616 | tf_op jit(solution)/shard_map/ppermute | solution.py:213

commit v2 on v1

v2 whole, which is shorter than its diff:
```python
import functools

import jax
import jax.numpy as jnp
from jax import lax
from jax.experimental import pallas as pl
from jax.experimental.pallas import tpu as pltpu
from jax.sharding import Mesh
from jax.sharding import PartitionSpec as P

HD = 256
AXES = ("y", "xh", "xl", "z", "c")
PLANE = ("y", "xh", "xl")
RING = 4
EPS = 1e-06
F32 = jnp.float32
BF16 = jnp.bfloat16
MIB = 2**20


def nn(a, b):
    return lax.dot_general(a, b, (((1,), (0,)), ((), ())), preferred_element_type=F32)


def nt(a, b):
    return lax.dot_general(a, b, (((1,), (1,)), ((), ())), preferred_element_type=F32)


def tn(a, b):
    return lax.dot_general(a, b, (((0,), (0,)), ((), ())), preferred_element_type=F32)


def project_body(pieces, z_ref, gain_ref, *refs):
    xs = refs[: len(pieces)]
    w_own, w_sib, own_ref, sib_ref, scale_ref, normed_ref = refs[len(pieces) : len(pieces) + 6]
    held, rows_low, weights, x_sem, w_sem, out_sem = refs[len(pieces) + 6 :]
    blocks, segs, part, width = held.shape
    rows = segs * part
    z = z_ref[0]
    loads = [pltpu.make_async_copy(w, weights.at[i], w_sem.at[i]) for i, w in enumerate((w_own, w_sib))]
    copies = []
    for (distance, first, depth), x in zip(pieces, xs):
        for side in range(2):
            place = side * RING + lax.rem(z + distance, RING)
            source = x.at[:, side] if depth is None else x.at[:, side, depth]
            target = held.at[place, pl.ds(first, source.shape[0])]
            copies.append(pltpu.make_async_copy(source, target, x_sem.at[len(copies)]))
    for copy in copies:
        copy.start()
    for load in loads:
        load.start()
    for copy in copies:
        copy.wait()
    squares = jnp.zeros((rows, 128), F32)
    for p in range(blocks):
        wide = held[p].reshape(rows, width).astype(F32)
        wide = wide * wide
        for i in range(width // 128):
            squares += wide[:, i * 128 : (i + 1) * 128]
    scale = lax.rsqrt(jnp.sum(squares, axis=1, keepdims=True) / (blocks * width) + EPS)
    scale_ref[...] = scale
    for p in range(blocks):
        wide = held[p].reshape(rows, width).astype(F32)
        rows_low[:, p * width : (p + 1) * width] = (wide * scale * gain_ref[p]).astype(BF16)
    out = pltpu.make_async_copy(rows_low, normed_ref, out_sem)
    out.start()
    for load, out_ref, i in zip(loads, (own_ref, sib_ref), range(2)):
        load.wait()
        for j in range(out_ref.shape[1] // HD):
            out_ref[:, j * HD : (j + 1) * HD] = nn(rows_low[...], weights[i, :, j * HD : (j + 1) * HD]).astype(BF16)
    out.wait()


def project(pieces, xs, z, gain, w_own, w_sib, segs, name):
    part, width = xs[0].shape[-2:]
    blocks = gain.shape[0] // width
    rows = segs * part
    anywhere = pl.BlockSpec(memory_space=pl.ANY)
    vmem = pl.BlockSpec(memory_space=pltpu.VMEM)
    return pl.pallas_call(
        functools.partial(project_body, pieces),
        in_specs=[pl.BlockSpec(memory_space=pltpu.SMEM), vmem] + [anywhere] * (len(xs) + 2),
        out_specs=[vmem, vmem, vmem, anywhere],
        out_shape=[
            jax.ShapeDtypeStruct((rows, 2 * HD), BF16),
            jax.ShapeDtypeStruct((rows, 2 * HD), BF16),
            jax.ShapeDtypeStruct((rows, 1), F32),
            jax.ShapeDtypeStruct((rows, blocks * width), BF16),
        ],
        scratch_shapes=[
            pltpu.VMEM((blocks, segs, part, width), BF16),
            pltpu.VMEM((rows, blocks * width), BF16),
            pltpu.VMEM((2, blocks * width, 2 * HD), BF16),
            pltpu.SemaphoreType.DMA((2 * len(xs),)),
            pltpu.SemaphoreType.DMA((2,)),
            pltpu.SemaphoreType.DMA(()),
        ],
        compiler_params=pltpu.CompilerParams(vmem_limit_bytes=24 * MIB),
        cost_estimate=pl.CostEstimate(flops=2 * rows * blocks * width * 4 * HD, bytes_accessed=12 * MIB, transcendentals=0),
        name=name,
    )(z, gain.reshape(blocks, 1, width), *xs, w_own, w_sib)


def attend_body(q_ref, dc_ref, near_a, near_b, far_a, far_b, ctx_ref, qg_ref, gnear_ref, gfar_ref,
                keys, values, gkeys, gvalues):
    i = pl.program_id(0)
    part = near_a.shape[0]
    scale = HD ** (-0.5)

    @pl.when(i == 0)
    def _():
        for j, ref in enumerate((near_a, near_b, far_a, far_b)):
            keys[j * part : (j + 1) * part] = ref[:, :HD]
            values[j * part : (j + 1) * part] = ref[:, HD:]
        gkeys[...] = jnp.zeros_like(gkeys)
        gvalues[...] = jnp.zeros_like(gvalues)

    q, dc, k, v = q_ref[...], dc_ref[...], keys[...], values[...]
    scores = nt(q, k) * scale
    expo = jnp.exp(scores - jnp.max(scores, axis=-1, keepdims=True))
    attend = expo / jnp.sum(expo, axis=-1, keepdims=True)
    low = attend.astype(BF16)
    ctx_ref[...] = nn(low, v).astype(BF16)
    gattend = nt(dc, v)
    dots = jnp.sum(gattend * attend, axis=-1, keepdims=True)
    gscores = (attend * (gattend - dots) * scale).astype(BF16)
    qg_ref[...] = nn(gscores, k).astype(BF16)
    gkeys[...] += tn(gscores, q)
    gvalues[...] += tn(low, dc)

    @pl.when(i == pl.num_programs(0) - 1)
    def _():
        half = 2 * part
        gnear_ref[:, :HD] = gkeys[:half].astype(BF16)
        gnear_ref[:, HD:] = gvalues[:half].astype(BF16)
        gfar_ref[:, :HD] = gkeys[half:].astype(BF16)
        gfar_ref[:, HD:] = gvalues[half:].astype(BF16)


def attention(q, dc, near_a, near_b, far_a, far_b, tile=256):
    targets, half = q.shape[0], 2 * near_a.shape[0]
    tiled = pl.BlockSpec((tile, HD), lambda i: (i, 0))
    quarter = pl.BlockSpec((half // 2, 2 * HD), lambda i: (0, 0))
    whole = pl.BlockSpec((half, 2 * HD), lambda i: (0, 0))
    return pl.pallas_call(
        attend_body,
        grid=(targets // tile,),
        in_specs=[tiled, tiled] + [quarter] * 4,
        out_specs=[tiled, tiled, whole, whole],
        out_shape=[jax.ShapeDtypeStruct((targets, HD), BF16)] * 2
        + [jax.ShapeDtypeStruct((half, 2 * HD), BF16)] * 2,
        scratch_shapes=[pltpu.VMEM((2 * half, HD), BF16)] * 2 + [pltpu.VMEM((2 * half, HD), F32)] * 2,
        compiler_params=pltpu.CompilerParams(vmem_limit_bytes=24 * MIB),
        cost_estimate=pl.CostEstimate(flops=12 * targets * 2 * half * HD, bytes_accessed=8 * MIB, transcendentals=targets * 2 * half),
        name="attention",
    )(q, dc, near_a, near_b, far_a, far_b)


def back_body(order, lands, z_ref, own_ref, sib_ref, o0_ref, o1_ref, s0_ref, s1_ref, *outs):
    del z_ref
    step = pl.program_id(0)
    own, sib = own_ref[...], sib_ref[...]
    sides = []
    for wo, ws in ((o0_ref, s0_ref), (o1_ref, s1_ref)):
        sides.append((nn(own, wo[...]) + nn(sib, ws[...])).astype(BF16))
    parts, segs, part, width = 2, 8, own.shape[0] // 16, o0_ref.shape[1]
    for i, distance in enumerate(order):

        @pl.when(step == i)
        def _():
            for index, first in lands[distance]:
                out = outs[index]
                count = out.shape[0]
                for side in range(2):
                    value = sides[side].reshape(parts, segs, part, width)
                    for k in range(parts):
                        piece = value[k, first : first + count]
                        if len(out.shape) == 4:
                            out[:, side, k * part : (k + 1) * part] = piece
                        else:
                            out[:, side, 0, k * part : (k + 1) * part] = piece


def back(z, own, sib, wt_own, wt_sib, feature_half, order, lands, out_shapes, out_specs, name):
    rows, width = own.shape[0], HD

    def column(side):
        def index(i, z_ref):
            distance = jnp.int32(order[0])
            for j in range(1, len(order)):
                distance = jnp.where(i == j, order[j], distance)
            block = side * RING + lax.rem(z_ref[0] + distance, RING)
            return 0, 2 * block + feature_half
        return pl.BlockSpec((2 * HD, width), index)

    whole = pl.BlockSpec((rows, 2 * HD), lambda i, z_ref: (0, 0))
    return pl.pallas_call(
        functools.partial(back_body, order, lands),
        grid_spec=pltpu.PrefetchScalarGridSpec(
            num_scalar_prefetch=1,
            grid=(RING,),
            in_specs=[whole, whole, column(0), column(1), column(0), column(1)],
            out_specs=out_specs,
        ),
        out_shape=out_shapes,
        compiler_params=pltpu.CompilerParams(vmem_limit_bytes=24 * MIB),
        cost_estimate=pl.CostEstimate(flops=2 * rows * 8 * width * 4 * HD, bytes_accessed=7 * MIB, transcendentals=0),
        name=name,
    )(z, own, sib, wt_own, wt_own, wt_sib, wt_sib)


def weights_body(near_a, near_b, far_a, far_b, gnear_ref, gfar_ref, gk_ref, gv_ref):
    part = near_a.shape[0]
    total = tn(near_a[...], gnear_ref[:part]) + tn(near_b[...], gnear_ref[part:])
    total += tn(far_a[...], gfar_ref[:part]) + tn(far_b[...], gfar_ref[part:])
    gk_ref[...] = total[:, :HD]
    gv_ref[...] = total[:, HD:]


def weight_grads(near_a, near_b, far_a, far_b, gnear, gfar, width=512):
    rows, hidden = near_a.shape
    block = pl.BlockSpec((rows, width), lambda i: (0, i))
    whole = pl.BlockSpec((2 * rows, 2 * HD), lambda i: (0, 0))
    out = pl.BlockSpec((width, HD), lambda i: (i, 0))
    return pl.pallas_call(
        weights_body,
        grid=(hidden // width,),
        in_specs=[block] * 4 + [whole, whole],
        out_specs=[out, out],
        out_shape=[jax.ShapeDtypeStruct((hidden, HD), F32)] * 2,
        compiler_params=pltpu.CompilerParams(vmem_limit_bytes=24 * MIB),
        cost_estimate=pl.CostEstimate(flops=16 * rows * hidden * HD, bytes_accessed=17 * MIB, transcendentals=0),
        name="weight_grads",
    )(near_a, near_b, far_a, far_b, gnear, gfar)


def swapped(value):
    return lax.ppermute(value, "c", [(0, 1), (1, 0)])


def shifted(value, by):
    return lax.ppermute(value, "z", [(i, (i + by) % RING) for i in range(RING)])


def exchanged(value, axis, bit):
    size = lax.axis_size(axis)
    return lax.ppermute(value, axis, [(i, i ^ bit) for i in range(size)])


def over_plane(value):
    return lax.all_to_all(value, PLANE, 0, 0, tiled=True)


def local(memory, norm_gain, queries, key_weight, value_weight, context_grad):
    hidden = norm_gain.shape[0]
    rows_own, cols_own = memory.shape
    half, width = rows_own // 2, 2 * cols_own
    part = half // 2
    core, z = lax.axis_index("c"), lax.axis_index("z")
    segment = lax.axis_index(("y", "xh"))
    pair = lax.axis_index(("xl", "z"))
    segs, plane = lax.axis_size(("y", "xh")), lax.axis_size(PLANE)
    z_array = z.astype(jnp.int32).reshape(1)

    halves = memory.reshape(2, half, cols_own)
    mine = lax.dynamic_index_in_dim(halves, core, 0, keepdims=False)
    other = swapped(lax.dynamic_index_in_dim(halves, 1 - core, 0, keepdims=False))
    block = jnp.where(
        core == 0, jnp.concatenate([mine, other], axis=1), jnp.concatenate([other, mine], axis=1)
    )
    first_a = over_plane(jnp.broadcast_to(block[:part], (plane, part, width)))
    high = block[part:]
    near_z = jnp.stack([high, shifted(high, -1), shifted(high, 2), shifted(high, 1)])
    all_b = over_plane(jnp.broadcast_to(near_z, (plane, RING, part, width)))
    all_b = all_b.reshape(segs, 2, RING, part, width)
    low_0, high_0 = first_a[: plane // 2], first_a[plane // 2 :]
    low_3, high_1 = shifted(low_0, 1), shifted(high_0, -1)
    high_3, low_1 = shifted(high_0, 1), shifted(low_0, -1)
    low_2, high_2 = shifted(low_3, 1), shifted(high_1, -1)
    deep = lambda value: value.reshape(segs // 2, 2, part, width)

    w_own = jnp.concatenate([key_weight[0], value_weight[0]], axis=1)
    w_sib = swapped(w_own)
    wt_own, wt_sib = w_own.T, w_sib.T

    pieces_a = [(0, 0, None), (3, 0, None), (3, 4, None), (1, 0, None), (1, 4, None), (2, 0, None), (2, 4, None)]
    xs_a = [first_a.reshape(segs, 2, part, width)] + [deep(v) for v in (low_3, high_3, low_1, high_1, low_2, high_2)]
    own_a, sib_a, scale_a, normed_a = project(pieces_a, xs_a, z_array, norm_gain, w_own, w_sib, segs, "project_a")
    pieces_b = [(d, 0, d) for d in range(RING)]
    own_b, sib_b, scale_b, normed_b = project(pieces_b, [all_b] * RING, z_array, norm_gain, w_own, w_sib, segs, "project_b")
    far_a, far_b = swapped(sib_a), swapped(sib_b)
    context, query_grad, gnear, gfar = attention(queries[0], context_grad[0], own_a, own_b, far_a, far_b)
    gsib = swapped(gfar)

    half_shape = jax.ShapeDtypeStruct((segs // 2, 2, half, HD), BF16)
    half_spec = pl.BlockSpec((segs // 2, 2, half, HD), lambda i, z_ref: (0, 0, 0, 0))
    full_shape = jax.ShapeDtypeStruct((segs, 2, half, HD), BF16)
    full_spec = pl.BlockSpec((segs, 2, half, HD), lambda i, z_ref: (0, 0, 0, 0))
    parts_b, = back(
        z_array, gnear, gsib, wt_own, wt_sib, 1, (0, 1, 2, 3), {d: [(0, 0)] for d in range(RING)},
        [jax.ShapeDtypeStruct((segs, 2, RING, half, HD), BF16)],
        [pl.BlockSpec((segs, 2, 1, half, HD), lambda i, z_ref: (0, 0, i, 0, 0))],
        "back_b",
    )
    opp_low, opp_high, up_low, up_high, down_low, down_high, kept = back(
        z_array, gnear, gsib, wt_own, wt_sib, 0, (2, 1, 3, 0),
        {2: [(0, 0), (1, 4)], 1: [(2, 0), (3, 4)], 3: [(4, 0), (5, 4)], 0: [(6, 0)]},
        [half_shape] * 6 + [full_shape], [half_spec] * 6 + [full_spec],
        "back_a",
    )
    arrived_b = over_plane(parts_b.reshape(plane, RING, half, HD))
    from_low, from_high = shifted(opp_low, 1), shifted(opp_high, -1)
    got_high, got_low = shifted(up_high, 1), shifted(down_low, -1)
    wide = lambda value: value.astype(F32)
    last_low = shifted((wide(up_low) + wide(from_low)).astype(BF16), 1)
    last_high = shifted((wide(down_high) + wide(from_high)).astype(BF16), -1)
    summed_low = wide(kept[: segs // 2]) + wide(got_low) + wide(last_low)
    summed_high = wide(kept[segs // 2 :]) + wide(got_high) + wide(last_high)
    summed_a = jnp.concatenate([summed_low, summed_high]).astype(BF16).reshape(plane, half, HD)

    normed_far_a, normed_far_b = swapped(normed_a), swapped(normed_b)
    key_grad, value_grad = weight_grads(normed_a, normed_b, normed_far_a, normed_far_b, gnear, gfar)

    row_dot = lambda g, a, b: jnp.sum(wide(g) * jnp.concatenate([wide(a), wide(b)]), axis=1)
    inner = row_dot(gnear, own_a, own_b) + swapped(row_dot(gfar, far_a, far_b))
    for axis, bit in (("xl", 1), ("z", 1), ("z", 2), ("xh", 1), ("y", 1), ("y", 2)):
        inner = inner + exchanged(inner, axis, bit)
    inner = lax.dynamic_index_in_dim(inner.reshape(2, segs, part), segment, 1, keepdims=False).reshape(half)

    arrived_b, key_grad, value_grad, inner, summed_a = lax.optimization_barrier(
        (arrived_b, key_grad, value_grad, inner, summed_a)
    )
    arrived_a = over_plane(summed_a)
    near_b = jnp.sum(wide(arrived_b), axis=0).astype(BF16)
    total_b = wide(near_b[0]) + wide(shifted(near_b[1], 1)) + wide(shifted(near_b[2], 2)) + wide(shifted(near_b[3], -1))
    total_a = jnp.sum(wide(arrived_a), axis=0)

    scale = jnp.concatenate(
        [lax.dynamic_slice_in_dim(s, segment * part, part) for s in (scale_a, scale_b)]
    )
    gain = lax.dynamic_slice_in_dim(norm_gain, pair * width, width)
    mean = (inner / hidden)[:, None]

    def finish(total, lo):
        centered = wide(block[:, lo : lo + HD]) * scale
        return scale * (total * gain[lo : lo + HD] - centered * mean)

    left, right = finish(total_a, 0), finish(total_b, HD)
    kept_own = jnp.where(core == 0, left, right)
    came = swapped(jnp.where(core == 0, right, left))
    result = jnp.where(core == 0, jnp.concatenate([kept_own, came]), jnp.concatenate([came, kept_own]))
    return context[None], query_grad[None], key_grad[None], value_grad[None], result


def solution(mesh):
    fine = Mesh(mesh.devices.reshape(4, 2, 2, 4, 2), AXES)
    seg, tp = ("y", "xh"), ("xl", "z", "c")
    heads = P(seg, None, tp)
    return jax.shard_map(
        local,
        mesh=fine,
        in_specs=(P(seg, tp), P(), heads, heads, heads, heads),
        out_specs=(heads, heads, heads, heads, P(seg, tp)),
        check_vma=False,
    )
```

time: 204 us -> 213 us (1.044)
  waiting for transfers between devices: 107 us -> 51.8 us
  starting transfers between devices: 36.7 us -> 76.4 us
  local copies, waits for them, and re-layouts: 8.51 us -> 33 us
  Pallas kernels: 46.4 us -> 38.6 us
  other arithmetic: 3.81 us -> 10.4 us
    all_to_all x3 -> x4, waiting for transfers between devices: 96.5 us -> 5.02 us  [over_plane(): return lax.all_to_all(value, PLANE, 0, 0, tiled=True)]
    ppermute x0 -> x24, starting transfers between devices: none -> 37.9 us  [the longest x18 28.5 us: shifted(): return lax.ppermute(value, 'z', [(i, (i + by) % RING) for i in range(RING)])]
    ppermute x0 -> x24, waiting for transfers between devices: none -> 36.5 us  [the longest x6 24.7 us: exchanged(): return lax.ppermute(value, axis, [(i, i ^ bit) for i in range(size)])]
    unnamed x8 -> x48, local copies, waits for them, and re-layouts: 2.95 us -> 14.5 us
    ppermute x7 -> x9, starting transfers between devices: 7.8 us -> 18.4 us  [swapped(): return lax.ppermute(value, 'c', [(0, 1), (1, 0)])]
    all_to_all x3 -> x4, starting transfers between devices: 28.9 us -> 20 us  [over_plane(): return lax.all_to_all(value, PLANE, 0, 0, tiled=True)]
    ppermute x0 -> x1, local copies, waits for them, and re-layouts: none -> 6.41 us  [swapped(): return lax.ppermute(value, 'c', [(0, 1), (1, 0)])]
    pallas_call x3 -> x5, Pallas kernels: 37.9 us -> 31.9 us  [the longest x2 11.2 us: back(): pl.pallas_call(functools.partial(back_body, order, lands), grid_spec=pltp...]
  transfers between devices with their start and end apart: 10 -> 37, of which waited for: 7 -> 19; matrix products, arithmetic and copies ran while one was open for 3% -> 11% of each run, Pallas kernels for 6% -> 15%
where the time goes in v2:
time: 213 us; the launch traced here: 211 us
  starting transfers between devices  76.4 us (36%)
  waiting for transfers between devices  51.8 us (24%)
  Pallas kernels  38.6 us (18%)
  local copies, waits for them, and re-layouts  33 us (15%)
  other arithmetic  10.4 us (5%)
    ppermute x18, starting transfers between devices, shifted(): return lax.ppermute(value, 'z', [(i, (i + by) % RING) for i in range(RING)])  28.5 us
    ppermute x6, waiting for transfers between devices, exchanged(): return lax.ppermute(value, axis, [(i, i ^ bit) for i in range(size)])  24.7 us
    all_to_all x4, starting transfers between devices, over_plane(): return lax.all_to_all(value, PLANE, 0, 0, tiled=True)  20 us
    ppermute x9, starting transfers between devices, swapped(): return lax.ppermute(value, 'c', [(0, 1), (1, 0)])  18.4 us
    unnamed x48, local copies, waits for them, and re-layouts  14.5 us
    ppermute x18, waiting for transfers between devices, shifted(): return lax.ppermute(value, 'z', [(i, (i + by) % RING) for i in range(RING)])  11.7 us
    pallas_call x2, Pallas kernels, back(): pl.pallas_call(functools.partial(back_body, order, lands), grid_spec=pltp...  11.2 us
    pallas_call x1, Pallas kernels, weight_grads(): pl.pallas_call(weights_body, grid=(hidden // width,), in_specs=[block] *...  10.8 us
  transfers between devices with their start and end apart: 37, of which 19 were waited for; matrix products, arithmetic and copies ran while one was open for 11% of the time, Pallas kernels for 15%

profile of v2, /device:TPU:1, one launch (start us, length us, event | category | flops | bytes accessed | tf_op | source)
XLA Modules:
  0.0 211.2 jit_solution(13813146512893962168)
XLA Ops:
  3.6 4.1 %copy.24 = bf16[1,4096,256]{1,2,0:T(8,128)(2,1)} copy(bf16[1,4096,256]{2,1,0:T(8,128)(2,1)} %param.10) | data formatting | bytes 4194304 | tf_op args[4]
  7.7 5.1 %fusion.6 = (bf16[512,4096]{1,0:T(8,128)(2,1)}, bf16[4096,512]{0,1:T(8,128)(2,1)}) fusion(bf16[4096,256]{0,1:T(8,128)(2,1)} %bitcast.61, bf16[4096,256]{0,1:T(8,128)(2,1)S(1)} %bitcast.60), kind=kLoop, calls=%fused_computation.34 | loop fusion | flops 8388608 | bytes 12582912 | tf_op jit(solution)/shard_map/transpose | solution.py:284
  14.3 6.6 %collective-permute-done = bf16[64,256]{1,0:T(8,128)(2,1)S(1)} collective-permute-done((bf16[64,256]{1,0:T(8,128)(2,1)S(1)}, bf16[64,256]{1,0:T(8,128)(2,1)S(1)}, u32[]{:S(2)}, u32[]{:S(2)}) %collective-permute-start) | collective-permute-done | bytes 32800 | tf_op jit(solution)/shard_map/ppermute | solution.py:238
  22.4 6.8 %all-to-all-start = ((bf16[16,32,512]{2,1,0:T(8,128)(2,1)}), bf16[16,32,512]{2,1,0:T(8,128)(2,1)S(1)}, u32[]{:S(2)}, u32[]{:S(2)}) async-start(bf16[16,32,512]{2,1,0:T(8,128)(2,1)} %broadcast_in_dim.21), calls=%async_computation | async-start | bytes 1048576 | tf_op jit(solution)/shard_map/all_to_all | solution.py:251
  29.3 3.7 %collective-permute-start.9 = (bf16[32,512]{1,0:T(8,128)(2,1)S(1)}, bf16[32,512]{1,0:T(8,128)(2,1)S(1)}, u32[]{:S(2)}, u32[]{:S(2)}) collective-permute-start(bf16[32,512]{1,0:T(8,128)(2,1)S(1)} %get-tuple-element.69), channel_id=1, source_target_pairs={{0,4},{2,6},{4,0},{6,2},{1,5},{3,7},{5,1},{7,3},{8,12},{10,14},{12... | collective-permute-start | bytes 98312 | tf_op jit(solution)/shard_map/ppermute | solution.py:242
  41.8 3.8 %all-to-all-start.1 = ((bf16[16,4,32,512]{3,2,1,0:T(8,128)(2,1)}), bf16[16,4,32,512]{3,2,1,0:T(8,128)(2,1)S(1)}, u32[]{:S(2)}, u32[]{:S(2)}) async-start(bf16[16,4,32,512]{3,2,1,0:T(8,128)(2,1)} %broadcast_in_dim.22), calls=%async_computation.1 | async-start | bytes 4194304 | tf_op jit(solution)/shard_map/all_to_all | solution.py:251
  46.4 3.7 %collective-permute-start.4 = (bf16[8,32,512]{2,1,0:T(8,128)(2,1)}, bf16[8,32,512]{2,1,0:T(8,128)(2,1)S(1)}, u32[]{:S(2)}, u32[]{:S(2)}) collective-permute-start(bf16[8,32,512]{2,1,0:T(8,128)(2,1)} %get-tuple-element.61), channel_id=1, source_target_pairs={{0,6},{2,0},{4,2},{6,4},{1,7},{3,1},{5,3},{7,5},{8,14},{10,8},{12,... | collective-permute-start | bytes 786440 | tf_op jit(solution)/shard_map/ppermute | solution.py:242
  54.4 3.3 %collective-permute-start.6 = (bf16[8,32,512]{2,1,0:T(8,128)(2,1)S(1)}, bf16[8,32,512]{2,1,0:T(8,128)(2,1)}, u32[]{:S(2)}, u32[]{:S(2)}) collective-permute-start(bf16[8,32,512]{2,1,0:T(8,128)(2,1)S(1)} %collective-permute-done.4), channel_id=1, source_target_pairs={{0,6},{2,0},{4,2},{6,4},{1,7},{3,1},{5,3},{7,5},{8,14},{10,8},{12,... | collective-permute-start | bytes 786440 | tf_op jit(solution)/shard_map/ppermute | solution.py:242
  57.7 6.5 %copy.25.refs_7_.refs_4_ = bf16[4096,512]{1,0:T(8,128)(2,1)} copy(bf16[4096,512]{0,1:T(8,128)(2,1)} %get-tuple-element.58) | data formatting | bytes 8388608 | tf_op jit(solution)/shard_map/concatenate | solution.py:282
  64.3 6.4 %copy.26.refs_8_.refs_5_ = bf16[4096,512]{1,0:T(8,128)(2,1)} copy(bf16[4096,512]{0,1:T(8,128)(2,1)} %collective-permute-done.7) | data formatting | bytes 8388608 | tf_op jit(solution)/shard_map/ppermute | solution.py:238
  75.4 4.5 %project_b.1 = (bf16[256,512]{1,0:T(8,128)(2,1)S(1)}, bf16[256,512]{1,0:T(8,128)(2,1)S(1)}, f32[256,1]{1,0:T(8,128)S(1)}, bf16[256,4096]{1,0:T(8,128)(2,1)}) custom-call(s32[1]{0:T(128)} %bitcast.2.z_ref, f32[8,1,512]{2,1,0:T(1,128)S(1)} %bitcast.56, bf16[8,2,4,32,512]{4,3,2,1,0:T(8,128)(2,1)S(1)} %bitcast.50, bf16[8,2,4,32,512]{4,3,2,1,0:T(8,128)(2,1)S(1)} %bitcast.51, ...), custom_call_target="tpu_custom_call" | custom-call | flops 2147483648 | bytes 12582912 | tf_op jit(solution)/shard_map/project_b/pallas_call | solution.py:80
  79.9 6.0 %collective-permute-start.12 = (bf16[256,512]{1,0:T(8,128)(2,1)S(1)}, bf16[256,512]{1,0:T(8,128)(2,1)S(1)}, u32[]{:S(2)}, u32[]{:S(2)}) collective-permute-start(bf16[256,512]{1,0:T(8,128)(2,1)S(1)} %get-tuple-element.34), channel_id=1, source_target_pairs={{0,1},{1,0},{2,3},{3,2},{4,5},{5,4},{6,7},{7,6},{8,9},{9,8},{10,11... | collective-permute-start | bytes 786440 | tf_op jit(solution)/shard_map/ppermute | solution.py:238
  86.0 5.3 %project_a.1 = (bf16[256,512]{1,0:T(8,128)(2,1)S(1)}, bf16[256,512]{1,0:T(8,128)(2,1)S(1)}, f32[256,1]{1,0:T(8,128)S(1)}, bf16[256,4096]{1,0:T(8,128)(2,1)}) custom-call(s32[1]{0:T(128)} %bitcast.2.z_ref, f32[8,1,512]{2,1,0:T(1,128)S(1)} %bitcast.57, bf16[8,2,32,512]{3,2,1,0:T(8,128)(2,1)S(1)} %bitcast.54, bf16[4,2,32,512]{3,2,1,0:T(8,128)(2,1)} %bitcast.8.refs_1_, ...), custom_call_target="tpu_custom_call" | custom-call | flops 2147483648 | bytes 12582912 | tf_op jit(solution)/shard_map/project_a/pallas_call | solution.py:80
  92.9 6.7 %attention.1 = (bf16[1024,256]{1,0:T(8,128)(2,1)}, bf16[1024,256]{1,0:T(8,128)(2,1)}, bf16[512,512]{1,0:T(8,128)(2,1)S(1)}, bf16[512,512]{1,0:T(8,128)(2,1)S(1)}) custom-call(bf16[1024,256]{1,0:T(8,128)(2,1)S(1)} %bitcast.58, bf16[1024,256]{1,0:T(8,128)(2,1)S(1)} %bitcast.59, bf16[256,512]{1,0:T(8,128)(2,1)S(1)} %get-tuple-element.31.near_a, ...), custom_call_target="tpu_custom_call" | custom-call | flops 3221225472 | bytes 8388608 | tf_op jit(solution)/shard_map/attention/pallas_call | solution.py:145
  101.6 5.7 %back_b.1 = bf16[8,2,4,64,256]{4,3,2,1,0:T(8,128)(2,1)} custom-call(s32[1]{0:T(128)} %bitcast.2.z_ref, bf16[512,512]{1,0:T(8,128)(2,1)S(1)} %get-tuple-element.37.own_ref.gnear_ref, bf16[512,512]{1,0:T(8,128)(2,1)S(1)} %collective-permute-done.13.sib_ref, bf16[512,4096]{1,0:T(8,128)(2,1)S(1)} %copy-done, bf16[512,4096]{1,0:T(8,128)(2,1)S(1)} %copy-done, ...), custom_call_target="tpu_custom_call" | custom-call | flops 2147483648 | bytes 7340032 | tf_op jit(solution)/shard_map/back_b/pallas_call | solution.py:197
  107.3 5.8 %all-to-all-start.2 = ((bf16[16,4,64,256]{3,2,1,0:T(8,128)(2,1)}), bf16[16,4,64,256]{3,2,1,0:T(8,128)(2,1)}, u32[]{:S(2)}, u32[]{:S(2)}) async-start(bf16[16,4,64,256]{3,2,1,0:T(8,128)(2,1)} %bitcast.25), calls=%async_computation.2 | async-start | bytes 4194304 | tf_op jit(solution)/shard_map/all_to_all | solution.py:251
  115.3 5.5 %back_a.1 = (bf16[4,2,64,256]{3,2,1,0:T(8,128)(2,1)}, bf16[4,2,64,256]{3,2,1,0:T(8,128)(2,1)}, bf16[4,2,64,256]{3,2,1,0:T(8,128)(2,1)S(1)}, bf16[4,2,64,256]{3,2...) custom-call(s32[1]{0:T(128)} %bitcast.2.z_ref, ...), custom_call_target="tpu_custom_call" | custom-call | flops 2147483648 | bytes 7340032 | tf_op jit(solution)/shard_map/back_a/pallas_call | solution.py:197
  126.5 16.7 %collective-permute-done.17 = f32[512]{0:T(512)S(1)} collective-permute-done((f32[512]{0:T(512)S(1)}, f32[512]{0:T(512)S(1)}, u32[]{:S(2)}, u32[]{:S(2)}) %collective-permute-start.17) | collective-permute-done | bytes 2080 | tf_op jit(solution)/shard_map/ppermute | solution.py:247
  146.0 3.3 %collective-permute-start.19 = (f32[512]{0:T(512)S(1)}, f32[512]{0:T(512)S(1)}, u32[]{:S(2)}, u32[]{:S(2)}) collective-permute-start(f32[512]{0:T(512)S(1)} %add.77), channel_id=1, source_target_pairs={{0,4},{2,6},{4,0},{6,2},{1,5},{3,7},{5,1},{7,3},{8,12},{10,14},{12... | collective-permute-start | bytes 6152 | tf_op jit(solution)/shard_map/ppermute | solution.py:247
  151.0 3.3 %collective-permute-done.20 = f32[512]{0:T(512)S(1)} collective-permute-done((f32[512]{0:T(512)S(1)}, f32[512]{0:T(512)S(1)}, u32[]{:S(2)}, u32[]{:S(2)}) %collective-permute-start.20) | collective-permute-done | bytes 2080 | tf_op jit(solution)/shard_map/ppermute | solution.py:247
  175.5 10.8 %weight_grads.1 = (f32[4096,256]{1,0:T(8,128)}, f32[4096,256]{1,0:T(8,128)}) custom-call(bf16[256,4096]{1,0:T(8,128)(2,1)} %get-tuple-element.39.near_a, bf16[256,4096]{1,0:T(8,128)(2,1)} %get-tuple-element.40.near_b, bf16[256,4096]{1,0:T(8,128)(2,1)} %collective-permute-done.14.far_a, bf16[256,4096]{1,0:T(8,128)(2,1)} %collective-permute-done.15.far_b, ...), custom_call_target="tpu_custom_call" | custom-call | flops 4294967296 | bytes 17825792 | tf_op jit(solution)/shard_map/weight_grads/pallas_call | solution.py:225
  186.4 3.6 %all-to-all-start.3 = ((bf16[16,64,256]{2,1,0:T(8,128)(2,1)}), bf16[16,64,256]{2,1,0:T(8,128)(2,1)S(1)}, u32[]{:S(2)}, u32[]{:S(2)}) async-start(bf16[16,64,256]{2,1,0:T(8,128)(2,1)} %bitcast.26), calls=%async_computation.3 | async-start | bytes 1048576 | tf_op jit(solution)/shard_map/all_to_all | solution.py:251
  192.2 3.5 %collective-permute-start.31 = (bf16[64,256]{1,0:T(8,128)(2,1)S(1)}, bf16[64,256]{1,0:T(8,128)(2,1)S(1)}, u32[]{:S(2)}, u32[]{:S(2)}) collective-permute-start(bf16[64,256]{1,0:T(8,128)(2,1)S(1)} %get-tuple-element.66), channel_id=1, source_target_pairs={{0,6},{2,0},{4,2},{6,4},{1,7},{3,1},{5,3},{7,5},{8,14},{10,8},{12,... | collective-permute-start | bytes 98312 | tf_op jit(solution)/shard_map/ppermute | solution.py:242
  200.0 9.6 %collective-permute-start.32 = (f32[64,256]{1,0:T(8,128)S(1)}, f32[64,256]{1,0:T(8,128)S(1)}, u32[]{:S(2)}, u32[]{:S(2)}) collective-permute-start(f32[64,256]{1,0:T(8,128)S(1)} %get-tuple-element.64), channel_id=1, source_target_pairs={{0,1},{1,0},{2,3},{3,2},{4,5},{5,4},{6,7},{7,6},{8,9},{9,8},{10,11... | collective-permute-start | bytes 196616 | tf_op jit(solution)/shard_map/ppermute | solution.py:238
  (143 shorter events, 69.8 us)
Async XLA Ops:
  12.8 51.5 %collective-permute-start.7 = (bf16[4096,512]{0,1:T(8,128)(2,1)}, bf16[4096,512]{0,1:T(8,128)(2,1)}, u32[]{:S(2)}, u32[]{:S(2)}) collective-permute-start(bf16[4096,512]{0,1:T(8,128)(2,1)} %get-tuple-element.58), channel_id=1, source_target_pairs={{0,1},{1,0},{2,3},{3,2},{4,5},{5,4},{6,7},{7,6},{8,9},{9,8},{10,11... | collective-permute-start | bytes 12582920 | tf_op jit(solution)/shard_map/ppermute | solution.py:238
  14.2 6.7 %collective-permute-start = (bf16[64,256]{1,0:T(8,128)(2,1)S(1)}, bf16[64,256]{1,0:T(8,128)(2,1)S(1)}, u32[]{:S(2)}, u32[]{:S(2)}) collective-permute-start(bf16[64,256]{1,0:T(8,128)(2,1)S(1)} %get-tuple-element.72), channel_id=1, source_target_pairs={{0,1},{1,0},{2,3},{3,2},{4,5},{5,4},{6,7},{7,6},{8,9},{9,8},{10,11... | collective-permute-start | bytes 98312 | tf_op jit(solution)/shard_map/ppermute | solution.py:238
  22.4 17.8 %all-to-all-start = ((bf16[16,32,512]{2,1,0:T(8,128)(2,1)}), bf16[16,32,512]{2,1,0:T(8,128)(2,1)S(1)}, u32[]{:S(2)}, u32[]{:S(2)}) async-start(bf16[16,32,512]{2,1,0:T(8,128)(2,1)} %broadcast_in_dim.21), calls=%async_computation | async-start | bytes 1048576 | tf_op jit(solution)/shard_map/all_to_all | solution.py:251
  41.8 29.2 %all-to-all-start.1 = ((bf16[16,4,32,512]{3,2,1,0:T(8,128)(2,1)}), bf16[16,4,32,512]{3,2,1,0:T(8,128)(2,1)S(1)}, u32[]{:S(2)}, u32[]{:S(2)}) async-start(bf16[16,4,32,512]{3,2,1,0:T(8,128)(2,1)} %broadcast_in_dim.22), calls=%async_computation.1 | async-start | bytes 4194304 | tf_op jit(solution)/shard_map/all_to_all | solution.py:251
  46.4 8.0 %collective-permute-start.4 = (bf16[8,32,512]{2,1,0:T(8,128)(2,1)}, bf16[8,32,512]{2,1,0:T(8,128)(2,1)S(1)}, u32[]{:S(2)}, u32[]{:S(2)}) collective-permute-start(bf16[8,32,512]{2,1,0:T(8,128)(2,1)} %get-tuple-element.61), channel_id=1, source_target_pairs={{0,6},{2,0},{4,2},{6,4},{1,7},{3,1},{5,3},{7,5},{8,14},{10,8},{12,... | collective-permute-start | bytes 786440 | tf_op jit(solution)/shard_map/ppermute | solution.py:242
  50.1 7.7 %collective-permute-start.1 = (bf16[8,32,512]{2,1,0:T(8,128)(2,1)}, bf16[8,32,512]{2,1,0:T(8,128)(2,1)}, u32[]{:S(2)}, u32[]{:S(2)}) collective-permute-start(bf16[8,32,512]{2,1,0:T(8,128)(2,1)} %get-tuple-element.62), channel_id=1, source_target_pairs={{0,2},{2,4},{4,6},{6,0},{1,3},{3,5},{5,7},{7,1},{8,10},{10,12},{12... | collective-permute-start | bytes 786440 | tf_op jit(solution)/shard_map/ppermute | solution.py:242
  50.1 35.8 %collective-permute-start.2 = (bf16[8,32,512]{2,1,0:T(8,128)(2,1)}, bf16[8,32,512]{2,1,0:T(8,128)(2,1)}, u32[]{:S(2)}, u32[]{:S(2)}) collective-permute-start(bf16[8,32,512]{2,1,0:T(8,128)(2,1)} %get-tuple-element.61), channel_id=1, source_target_pairs={{0,2},{2,4},{4,6},{6,0},{1,3},{3,5},{5,7},{7,1},{8,10},{10,12},{12... | collective-permute-start | bytes 786440 | tf_op jit(solution)/shard_map/ppermute | solution.py:242
  50.1 35.8 %collective-permute-start.3 = (bf16[8,32,512]{2,1,0:T(8,128)(2,1)}, bf16[8,32,512]{2,1,0:T(8,128)(2,1)}, u32[]{:S(2)}, u32[]{:S(2)}) collective-permute-start(bf16[8,32,512]{2,1,0:T(8,128)(2,1)} %get-tuple-element.62), channel_id=1, source_target_pairs={{0,6},{2,0},{4,2},{6,4},{1,7},{3,1},{5,3},{7,5},{8,14},{10,8},{12,... | collective-permute-start | bytes 786440 | tf_op jit(solution)/shard_map/ppermute | solution.py:242
  54.4 31.5 %collective-permute-start.6 = (bf16[8,32,512]{2,1,0:T(8,128)(2,1)S(1)}, bf16[8,32,512]{2,1,0:T(8,128)(2,1)}, u32[]{:S(2)}, u32[]{:S(2)}) collective-permute-start(bf16[8,32,512]{2,1,0:T(8,128)(2,1)S(1)} %collective-permute-done.4), channel_id=1, source_target_pairs={{0,6},{2,0},{4,2},{6,4},{1,7},{3,1},{5,3},{7,5},{8,14},{10,8},{12,... | collective-permute-start | bytes 786440 | tf_op jit(solution)/shard_map/ppermute | solution.py:242
  57.7 28.2 %collective-permute-start.5 = (bf16[8,32,512]{2,1,0:T(8,128)(2,1)}, bf16[8,32,512]{2,1,0:T(8,128)(2,1)}, u32[]{:S(2)}, u32[]{:S(2)}) collective-permute-start(bf16[8,32,512]{2,1,0:T(8,128)(2,1)} %collective-permute-done.1), channel_id=1, source_target_pairs={{0,2},{2,4},{4,6},{6,0},{1,3},{3,5},{5,7},{7,1},{8,10},{10,12},{12... | collective-permute-start | bytes 786440 | tf_op jit(solution)/shard_map/ppermute | solution.py:242
  79.9 11.5 %collective-permute-start.12 = (bf16[256,512]{1,0:T(8,128)(2,1)S(1)}, bf16[256,512]{1,0:T(8,128)(2,1)S(1)}, u32[]{:S(2)}, u32[]{:S(2)}) collective-permute-start(bf16[256,512]{1,0:T(8,128)(2,1)S(1)} %get-tuple-element.34), channel_id=1, source_target_pairs={{0,1},{1,0},{2,3},{3,2},{4,5},{5,4},{6,7},{7,6},{8,9},{9,8},{10,11... | collective-permute-start | bytes 786440 | tf_op jit(solution)/shard_map/ppermute | solution.py:238
  99.8 75.7 %collective-permute-start.15 = (bf16[256,4096]{1,0:T(8,128)(2,1)}, bf16[256,4096]{1,0:T(8,128)(2,1)}, u32[]{:S(2)}, u32[]{:S(2)}) collective-permute-start(bf16[256,4096]{1,0:T(8,128)(2,1)} %get-tuple-element.40.near_b), channel_id=1, source_target_pairs={{0,1},{1,0},{2,3},{3,2},{4,5},{5,4},{6,7},{7,6},{8,9},{9,8},{10,11... | collective-permute-start | bytes 6291464 | tf_op jit(solution)/shard_map/ppermute | solution.py:238
  100.2 75.3 %collective-permute-start.14 = (bf16[256,4096]{1,0:T(8,128)(2,1)}, bf16[256,4096]{1,0:T(8,128)(2,1)}, u32[]{:S(2)}, u32[]{:S(2)}) collective-permute-start(bf16[256,4096]{1,0:T(8,128)(2,1)} %get-tuple-element.39.near_a), channel_id=1, source_target_pairs={{0,1},{1,0},{2,3},{3,2},{4,5},{5,4},{6,7},{7,6},{8,9},{9,8},{10,11... | collective-permute-start | bytes 6291464 | tf_op jit(solution)/shard_map/ppermute | solution.py:238
  107.3 79.1 %all-to-all-start.2 = ((bf16[16,4,64,256]{3,2,1,0:T(8,128)(2,1)}), bf16[16,4,64,256]{3,2,1,0:T(8,128)(2,1)}, u32[]{:S(2)}, u32[]{:S(2)}) async-start(bf16[16,4,64,256]{3,2,1,0:T(8,128)(2,1)} %bitcast.25), calls=%async_computation.2 | async-start | bytes 4194304 | tf_op jit(solution)/shard_map/all_to_all | solution.py:251
  120.9 38.3 %collective-permute-start.24 = (bf16[4,2,64,256]{3,2,1,0:T(8,128)(2,1)}, bf16[4,2,64,256]{3,2,1,0:T(8,128)(2,1)S(1)}, u32[]{:S(2)}, u32[]{:S(2)}) collective-permute-start(bf16[4,2,64,256]{3,2,1,0:T(8,128)(2,1)} %get-tuple-element.46), channel_id=1, source_target_pairs={{0,2},{2,4},{4,6},{6,0},{1,3},{3,5},{5,7},{7,1},{8,10},{10,12},{12... | collective-permute-start | bytes 786440 | tf_op jit(solution)/shard_map/ppermute | solution.py:242
  122.3 39.5 %collective-permute-start.27 = (bf16[4,2,64,256]{3,2,1,0:T(8,128)(2,1)}, bf16[4,2,64,256]{3,2,1,0:T(8,128)(2,1)S(1)}, u32[]{:S(2)}, u32[]{:S(2)}) collective-permute-start(bf16[4,2,64,256]{3,2,1,0:T(8,128)(2,1)} %get-tuple-element.49), channel_id=1, source_target_pairs={{0,6},{2,0},{4,2},{6,4},{1,7},{3,1},{5,3},{7,5},{8,14},{10,8},{12,... | collective-permute-start | bytes 786440 | tf_op jit(solution)/shard_map/ppermute | solution.py:242
  124.9 18.3 %collective-permute-start.17 = (f32[512]{0:T(512)S(1)}, f32[512]{0:T(512)S(1)}, u32[]{:S(2)}, u32[]{:S(2)}) collective-permute-start(f32[512]{0:T(512)S(1)} %add.75), channel_id=1, source_target_pairs={{0,8},{8,0},{1,9},{9,1},{2,10},{10,2},{3,11},{11,3},{4,12},{12,4},... | collective-permute-start | bytes 6152 | tf_op jit(solution)/shard_map/ppermute | solution.py:247
  161.8 9.4 %collective-permute-start.26 = (bf16[4,2,64,256]{3,2,1,0:T(8,128)(2,1)}, bf16[4,2,64,256]{3,2,1,0:T(8,128)(2,1)S(1)}, u32[]{:S(2)}, u32[]{:S(2)}) collective-permute-start(bf16[4,2,64,256]{3,2,1,0:T(8,128)(2,1)} %copy-done.13), channel_id=1, source_target_pairs={{0,2},{2,4},{4,6},{6,0},{1,3},{3,5},{5,7},{7,1},{8,10},{10,12},{12... | collective-permute-start | bytes 786440 | tf_op jit(solution)/shard_map/ppermute | solution.py:242
  162.0 9.3 %collective-permute-start.25 = (bf16[4,2,64,256]{3,2,1,0:T(8,128)(2,1)S(1)}, bf16[4,2,64,256]{3,2,1,0:T(8,128)(2,1)S(1)}, u32[]{:S(2)}, u32[]{:S(2)}) collective-permute-start(bf16[4,2,64,256]{3,2,1,0:T(8,128)(2,1)S(1)} %add_convert_fusion.3), channel_id=1, source_target_pairs={{0,2},{2,4},{4,6},{6,0},{1,3},{3,5},{5,7},{7,1},{8,10},{10,12},{12... | collective-permute-start | bytes 786440 | tf_op jit(solution)/shard_map/ppermute | solution.py:242
  165.4 9.0 %collective-permute-start.28 = (bf16[4,2,64,256]{3,2,1,0:T(8,128)(2,1)S(1)}, bf16[4,2,64,256]{3,2,1,0:T(8,128)(2,1)S(1)}, u32[]{:S(2)}, u32[]{:S(2)}) collective-permute-start(bf16[4,2,64,256]{3,2,1,0:T(8,128)(2,1)S(1)} %add_convert_fusion.1), channel_id=1, source_target_pairs={{0,6},{2,0},{4,2},{6,4},{1,7},{3,1},{5,3},{7,5},{8,14},{10,8},{12,... | collective-permute-start | bytes 786440 | tf_op jit(solution)/shard_map/ppermute | solution.py:242
  186.4 12.5 %all-to-all-start.3 = ((bf16[16,64,256]{2,1,0:T(8,128)(2,1)}), bf16[16,64,256]{2,1,0:T(8,128)(2,1)S(1)}, u32[]{:S(2)}, u32[]{:S(2)}) async-start(bf16[16,64,256]{2,1,0:T(8,128)(2,1)} %bitcast.26), calls=%async_computation.3 | async-start | bytes 1048576 | tf_op jit(solution)/shard_map/all_to_all | solution.py:251
  192.1 6.9 %collective-permute-start.29 = (bf16[64,256]{1,0:T(8,128)(2,1)S(1)}, bf16[64,256]{1,0:T(8,128)(2,1)S(1)}, u32[]{:S(2)}, u32[]{:S(2)}) collective-permute-start(bf16[64,256]{1,0:T(8,128)(2,1)S(1)} %get-tuple-element.65), channel_id=1, source_target_pairs={{0,2},{2,4},{4,6},{6,0},{1,3},{3,5},{5,7},{7,1},{8,10},{10,12},{12... | collective-permute-start | bytes 98312 | tf_op jit(solution)/shard_map/ppermute | solution.py:242
  192.2 6.9 %collective-permute-start.31 = (bf16[64,256]{1,0:T(8,128)(2,1)S(1)}, bf16[64,256]{1,0:T(8,128)(2,1)S(1)}, u32[]{:S(2)}, u32[]{:S(2)}) collective-permute-start(bf16[64,256]{1,0:T(8,128)(2,1)S(1)} %get-tuple-element.66), channel_id=1, source_target_pairs={{0,6},{2,0},{4,2},{6,4},{1,7},{3,1},{5,3},{7,5},{8,14},{10,8},{12,... | collective-permute-start | bytes 98312 | tf_op jit(solution)/shard_map/ppermute | solution.py:242
  200.0 10.5 %collective-permute-start.32 = (f32[64,256]{1,0:T(8,128)S(1)}, f32[64,256]{1,0:T(8,128)S(1)}, u32[]{:S(2)}, u32[]{:S(2)}) collective-permute-start(f32[64,256]{1,0:T(8,128)S(1)} %get-tuple-element.64), channel_id=1, source_target_pairs={{0,1},{1,0},{2,3},{3,2},{4,5},{5,4},{6,7},{7,6},{8,9},{9,8},{10,11... | collective-permute-start | bytes 196616 | tf_op jit(solution)/shard_map/ppermute | solution.py:238
  (36 other events, 213.1 us)

commit v3 on v2

v3 whole, which is shorter than its diff:
```python
import functools

import jax
import jax.numpy as jnp
from jax import lax
from jax.experimental import pallas as pl
from jax.experimental.pallas import tpu as pltpu
from jax.sharding import Mesh
from jax.sharding import PartitionSpec as P

HD = 256
AXES = ("y", "xh", "xl", "z", "c")
PLANE = ("y", "xh", "xl")
RING = 4
EXTRA = 16
EPS = 1e-06
F32 = jnp.float32
BF16 = jnp.bfloat16
MIB = 2**20
VMEM = pl.BlockSpec(memory_space=pltpu.VMEM)
SMEM = pl.BlockSpec(memory_space=pltpu.SMEM)
ANYWHERE = pl.BlockSpec(memory_space=pl.ANY)


def dot(a, b, contract):
    return lax.dot_general(a, b, ((contract[:1], contract[1:]), ((), ())), preferred_element_type=F32)


def nn(a, b):
    return dot(a, b, (1, 0))


def nt(a, b):
    return dot(a, b, (1, 1))


def tn(a, b):
    return dot(a, b, (0, 0))


def beside(*values):
    return jnp.concatenate(values, axis=1)


def above(*values):
    return jnp.concatenate(values, axis=0)


def limits(mib):
    return pltpu.CompilerParams(vmem_limit_bytes=mib * MIB)


def cost(flops, mib, transcendentals=0):
    return pl.CostEstimate(flops=flops, bytes_accessed=int(mib * MIB), transcendentals=transcendentals)


def project_body(pieces, z_ref, gain_ref, *refs):
    xs = refs[: len(pieces)]
    ko, vo, ks, vs, own_ref, sib_ref, scale_ref, normed_ref = refs[len(pieces) : len(pieces) + 8]
    held, rows_low, x_sem, out_sem = refs[len(pieces) + 8 :]
    blocks, segs, part, width = held.shape
    rows = segs * part
    z = z_ref[0]
    copies = []
    for (distance, first, depth), x in zip(pieces, xs):
        for side in range(2):
            place = side * RING + lax.rem(z + distance, RING)
            source = x.at[:, side] if depth is None else x.at[:, side, depth]
            target = held.at[place, pl.ds(first, source.shape[0])]
            copies.append(pltpu.make_async_copy(source, target, x_sem.at[len(copies)]))
    for copy in copies:
        copy.start()
    for copy in copies:
        copy.wait()
    squares = jnp.zeros((rows, 128), F32)
    for p in range(blocks):
        wide = held[p].reshape(rows, width).astype(F32)
        wide = wide * wide
        for i in range(width // 128):
            squares += wide[:, i * 128 : (i + 1) * 128]
    scale = lax.rsqrt(jnp.sum(squares, axis=1, keepdims=True) / (blocks * width) + EPS)
    scale_ref[...] = scale
    for p in range(blocks):
        wide = held[p].reshape(rows, width).astype(F32)
        rows_low[:, p * width : (p + 1) * width] = (wide * scale * gain_ref[p]).astype(BF16)
    out = pltpu.make_async_copy(rows_low, normed_ref, out_sem)
    out.start()
    for j, (w, out_ref) in enumerate(((ko, own_ref), (vo, own_ref), (ks, sib_ref), (vs, sib_ref))):
        at = (j % 2) * HD
        out_ref[:, at : at + HD] = nn(rows_low[...], w[...]).astype(BF16)
    out.wait()


def project(pieces, xs, z, gain, weights, segs, name):
    part, width = xs[0].shape[-2:]
    blocks = gain.shape[0] // width
    rows = segs * part
    return pl.pallas_call(
        functools.partial(project_body, pieces),
        in_specs=[SMEM, VMEM] + [ANYWHERE] * len(xs) + [VMEM] * 4,
        out_specs=[VMEM, VMEM, VMEM, ANYWHERE],
        out_shape=[
            jax.ShapeDtypeStruct((rows, 2 * HD), BF16),
            jax.ShapeDtypeStruct((rows, 2 * HD), BF16),
            jax.ShapeDtypeStruct((rows, 1), F32),
            jax.ShapeDtypeStruct((rows, blocks * width), BF16),
        ],
        scratch_shapes=[
            pltpu.VMEM((blocks, segs, part, width), BF16),
            pltpu.VMEM((rows, blocks * width), BF16),
            pltpu.SemaphoreType.DMA((2 * len(xs),)),
            pltpu.SemaphoreType.DMA(()),
        ],
        compiler_params=limits(20),
        cost_estimate=cost(2 * rows * blocks * width * 4 * HD, 5),
        name=name,
    )(z, gain.reshape(blocks, 1, width), *xs, *weights)


def attend_body(tile, q_ref, dc_ref, near_a, near_b, far_a, far_b, ctx_ref, qg_ref, gnear_ref, gfar_ref, gkeys, gvalues):
    kv = above(near_a[...], near_b[...], far_a[...], far_b[...])
    k, v = kv[:, :HD], kv[:, HD:]
    half = kv.shape[0] // 2
    scale = HD ** (-0.5)
    for i in range(q_ref.shape[0] // tile):
        here = slice(i * tile, (i + 1) * tile)
        q, dc = q_ref[here], dc_ref[here]
        scores = nt(q, k) * scale
        expo = jnp.exp(scores - jnp.max(scores, axis=-1, keepdims=True))
        attend = expo * (1.0 / jnp.sum(expo, axis=-1, keepdims=True))
        low = attend.astype(BF16)
        ctx_ref[here] = nn(low, v).astype(BF16)
        gattend = nt(dc, v)
        dots = jnp.sum(gattend * attend, axis=-1, keepdims=True)
        gscores = (attend * (gattend - dots) * scale).astype(BF16)
        qg_ref[here] = nn(gscores, k).astype(BF16)
        if i == 0:
            gkeys[...] = tn(gscores, q)
            gvalues[...] = tn(low, dc)
        else:
            gkeys[...] += tn(gscores, q)
            gvalues[...] += tn(low, dc)
    gnear_ref[:, :HD] = gkeys[:half].astype(BF16)
    gnear_ref[:, HD:] = gvalues[:half].astype(BF16)
    gfar_ref[:, :HD] = gkeys[half:].astype(BF16)
    gfar_ref[:, HD:] = gvalues[half:].astype(BF16)


def attention(q, dc, near_a, near_b, far_a, far_b, tile=256):
    targets, half = q.shape[0], 2 * near_a.shape[0]
    return pl.pallas_call(
        functools.partial(attend_body, tile),
        in_specs=[VMEM] * 6,
        out_specs=[VMEM] * 4,
        out_shape=[jax.ShapeDtypeStruct((targets, HD), BF16)] * 2
        + [jax.ShapeDtypeStruct((half, 2 * HD), BF16)] * 2,
        scratch_shapes=[pltpu.VMEM((2 * half, HD), F32)] * 2,
        compiler_params=limits(24),
        cost_estimate=cost(12 * targets * 2 * half * HD, 4, targets * 2 * half),
        name="attention",
    )(q, dc, near_a, near_b, far_a, far_b)


def feature_block(z, own, sib, weights, feature_half, distance, side):
    block = side * RING + lax.rem(z + distance, RING)
    at = pl.ds(pl.multiple_of(block * 2 * HD + feature_half * HD, HD), HD)
    return nt(beside(own, sib), beside(*[w[at] for w in weights])).astype(BF16)


def back_b_body(z_ref, own_ref, sib_ref, own_a, own_b, sib_a, sib_b, ko, vo, ks, vs, out_ref):
    own, sib = own_ref[...], sib_ref[...]
    segs = out_ref.shape[0]
    part = own.shape[0] // segs // 2
    wide = lambda value: value.astype(F32)
    products = beside(
        wide(own) * above(wide(own_a[...]), wide(own_b[...])),
        wide(sib) * above(wide(sib_a[...]), wide(sib_b[...])),
    )
    high = products.astype(BF16)
    low = (products - wide(high)).astype(BF16)
    ones = jnp.ones((EXTRA, high.shape[1]), BF16)
    dots = nt(ones, high) + nt(ones, low)
    out_ref[:, :, RING * 2 * part :] = jnp.broadcast_to(pieces_of(dots), (segs, 2, EXTRA, HD))
    for distance in range(RING):
        for side in range(2):
            value = feature_block(z_ref[0], own, sib, (ko, vo, ks, vs), 1, distance, side)
            value = value.reshape(2, segs, part, HD)
            for k in range(2):
                at = distance * 2 * part + k * part
                out_ref[:, side, at : at + part] = value[k]


def pieces_of(dots):
    high = dots.astype(BF16).astype(F32)
    low = dots - high
    row = lax.broadcasted_iota(jnp.int32, (EXTRA, HD), 0)
    zero = jnp.zeros((EXTRA, HD), F32)
    picked = jnp.where(row == 0, high[:, :HD], jnp.where(row == 1, high[:, HD:], zero))
    picked = jnp.where(row == 2, low[:, :HD], jnp.where(row == 3, low[:, HD:], picked))
    return picked.astype(BF16)


def back_b(z, own, sib, kvs, weights, segs):
    rows = own.shape[0]
    return pl.pallas_call(
        back_b_body,
        in_specs=[SMEM] + [VMEM] * 10,
        out_specs=VMEM,
        out_shape=jax.ShapeDtypeStruct((segs, 2, RING * rows // segs + EXTRA, HD), BF16),
        compiler_params=limits(20),
        cost_estimate=cost(2 * rows * 8 * HD * 4 * HD, 4),
        name="back_b",
    )(z, own, sib, *kvs, *weights)


def back_a_body(z_ref, own_ref, sib_ref, ko, vo, ks, vs, *outs):
    own, sib = own_ref[...], sib_ref[...]
    segs = outs[-1].shape[0]
    part = own.shape[0] // segs // 2
    lands = {2: ((0, 0), (1, segs // 2)), 1: ((2, 0), (3, segs // 2)), 3: ((4, 0), (5, segs // 2)), 0: ((6, 0),)}
    for distance in (2, 1, 3, 0):
        for side in range(2):
            value = feature_block(z_ref[0], own, sib, (ko, vo, ks, vs), 0, distance, side)
            value = value.reshape(2, segs, part, HD)
            for index, first in lands[distance]:
                for k in range(2):
                    count = outs[index].shape[0]
                    outs[index][:, side, k * part : (k + 1) * part] = value[k, first : first + count]


def back_a(z, own, sib, weights, segs):
    rows = own.shape[0]
    half = jax.ShapeDtypeStruct((segs // 2, 2, rows // segs, HD), BF16)
    full = jax.ShapeDtypeStruct((segs, 2, rows // segs, HD), BF16)
    return pl.pallas_call(
        back_a_body,
        in_specs=[SMEM] + [VMEM] * 6,
        out_specs=[VMEM] * 7,
        out_shape=[half] * 6 + [full],
        compiler_params=limits(20),
        cost_estimate=cost(2 * rows * 8 * HD * 4 * HD, 4),
        name="back_a",
    )(z, own, sib, *weights)


def weights_body(near_a, near_b, far_a, far_b, gnear_ref, gfar_ref, gk_ref, gv_ref):
    rows = above(near_a[...], near_b[...], far_a[...], far_b[...])
    total = tn(rows, above(gnear_ref[...], gfar_ref[...]))
    gk_ref[...] = total[:, :HD]
    gv_ref[...] = total[:, HD:]


def weight_grads(near_a, near_b, far_a, far_b, gnear, gfar, width=512):
    rows, hidden = near_a.shape
    block = pl.BlockSpec((rows, width), lambda i: (0, i))
    whole = pl.BlockSpec((2 * rows, 2 * HD), lambda i: (0, 0))
    out = pl.BlockSpec((width, HD), lambda i: (i, 0))
    return pl.pallas_call(
        weights_body,
        grid=(hidden // width,),
        in_specs=[block] * 4 + [whole, whole],
        out_specs=[out, out],
        out_shape=[jax.ShapeDtypeStruct((hidden, HD), F32)] * 2,
        compiler_params=limits(20),
        cost_estimate=cost(16 * rows * hidden * HD, 17),
        name="weight_grads",
    )(near_a, near_b, far_a, far_b, gnear, gfar)


def merge_b_body(arrived_ref, kept_ref, dots_ref, *send_refs):
    half = kept_ref.shape[0]
    total = arrived_ref[0].astype(F32)
    for i in range(1, arrived_ref.shape[0]):
        total += arrived_ref[i].astype(F32)
    kept_ref[...] = total[:half]
    extra = total[RING * half :]
    both = beside(extra[0:1] + extra[2:3], extra[1:2] + extra[3:4])
    dots_ref[...] = both
    pieces = pieces_of(jnp.broadcast_to(both, (EXTRA, 2 * HD)))
    for i, ref in enumerate(send_refs):
        ref[:half] = total[(i + 1) * half : (i + 2) * half].astype(BF16)
        ref[half:] = pieces


def merge_b(arrived, half):
    send = jax.ShapeDtypeStruct((half + EXTRA, HD), BF16)
    return pl.pallas_call(
        merge_b_body,
        in_specs=[VMEM],
        out_specs=[VMEM] * 5,
        out_shape=[jax.ShapeDtypeStruct((half, HD), F32), jax.ShapeDtypeStruct((1, 2 * HD), F32)] + [send] * 3,
        compiler_params=limits(16),
        cost_estimate=cost(0, 3),
        name="merge_b",
    )(arrived)


def finish_body(hidden, place_ref, gain_ref, block_ref, scale_a, scale_b, arrived_ref, kept_ref, dots_ref, r1, r2, r3,
                keep_ref, send_ref):
    core, segment, pair = place_ref[0], place_ref[1], place_ref[2]
    half = block_ref.shape[0]
    part = half // 2
    left = arrived_ref[0].astype(F32)
    for i in range(1, arrived_ref.shape[0]):
        left += arrived_ref[i].astype(F32)
    right, dots = kept_ref[...], dots_ref[...]
    for ref in (r1, r2, r3):
        right += ref[:half].astype(F32)
        extra = ref[half:].astype(F32)
        dots += beside(extra[0:1] + extra[2:3], extra[1:2] + extra[3:4])
    lane = lax.broadcasted_iota(jnp.int32, (part, HD), 1)
    row = lax.broadcasted_iota(jnp.int32, (part, HD), 0)
    mine = lane == row + segment * part
    pick = lambda values: jnp.sum(jnp.where(mine, values, 0.0), axis=1, keepdims=True)
    mean = above(pick(dots[:, :HD]), pick(dots[:, HD:])) / hidden
    rows = pl.ds(pl.multiple_of(segment * part, part), part)
    scale = above(scale_a[rows], scale_b[rows])
    gain = gain_ref[pair]
    for side, total in enumerate((left, right)):
        at = slice(side * HD, (side + 1) * HD)
        value = scale * (total * gain[:, at] - block_ref[:, at].astype(F32) * scale * mean)

        @pl.when(core == side)
        def _():
            keep_ref[...] = value

        @pl.when(core != side)
        def _():
            send_ref[...] = value


def finish(place, gain, block, scale_a, scale_b, arrived, kept, dots, received):
    half, width = block.shape
    hidden = gain.shape[0]
    return pl.pallas_call(
        functools.partial(finish_body, hidden),
        in_specs=[SMEM] + [VMEM] * 10,
        out_specs=[VMEM] * 2,
        out_shape=[jax.ShapeDtypeStruct((half, HD), F32)] * 2,
        compiler_params=limits(16),
        cost_estimate=cost(0, 1),
        name="finish",
    )(place, gain.reshape(hidden // width, 1, width), block, scale_a, scale_b, arrived, kept, dots, *received)


def swapped(value):
    return lax.ppermute(value, "c", [(0, 1), (1, 0)])


def shifted(value, by):
    return lax.ppermute(value, "z", [(i, (i + by) % RING) for i in range(RING)])


def over_plane(value):
    return lax.all_to_all(value, PLANE, 0, 0, tiled=True)


def after(values, *earlier):
    return lax.optimization_barrier((*values, *earlier))[: len(values)]


def local(memory, norm_gain, queries, key_weight, value_weight, context_grad):
    rows_own, cols_own = memory.shape
    half, width = rows_own // 2, 2 * cols_own
    part = half // 2
    core, z = lax.axis_index("c"), lax.axis_index("z")
    segment = lax.axis_index(("y", "xh"))
    pair = lax.axis_index(("xl", "z"))
    segs, plane = lax.axis_size(("y", "xh")), lax.axis_size(PLANE)
    z_array = z.astype(jnp.int32).reshape(1)
    place = jnp.stack([core, segment, pair]).astype(jnp.int32)
    wide = lambda value: value.astype(F32)

    halves = memory.reshape(2, half, cols_own)
    mine = lax.dynamic_index_in_dim(halves, core, 0, keepdims=False)
    other = swapped(lax.dynamic_index_in_dim(halves, 1 - core, 0, keepdims=False))
    block = jnp.where(core == 0, beside(mine, other), beside(other, mine))
    first_a = over_plane(jnp.broadcast_to(block[:part], (plane, part, width)))
    high = block[part:]
    near_z = jnp.stack([high, shifted(high, -1), shifted(high, 2), shifted(high, 1)])
    all_b = over_plane(jnp.broadcast_to(near_z, (plane, RING, part, width)))
    all_b = all_b.reshape(segs, 2, RING, part, width)
    low_0, high_0 = first_a[: plane // 2], first_a[plane // 2 :]
    low_3, high_1 = shifted(low_0, 1), shifted(high_0, -1)
    high_3, low_1 = shifted(high_0, 1), shifted(low_0, -1)
    low_2, high_2 = shifted(low_3, 1), shifted(high_1, -1)
    deep = lambda value: value.reshape(segs // 2, 2, part, width)

    key_own, value_own = after((key_weight[0], value_weight[0]), first_a)
    weights = (key_own, value_own, swapped(key_own), swapped(value_own))

    top = segs // 2
    pieces_a = [(0, 0, None), (3, 0, None), (3, top, None), (1, 0, None), (1, top, None), (2, 0, None), (2, top, None)]
    xs_a = [first_a.reshape(segs, 2, part, width)] + [deep(v) for v in (low_3, high_3, low_1, high_1, low_2, high_2)]
    own_a, sib_a, scale_a, normed_a = project(pieces_a, xs_a, z_array, norm_gain, weights, segs, "project_a")
    far_a = swapped(sib_a)
    all_b, = after((all_b,), own_a)
    pieces_b = [(d, 0, d) for d in range(RING)]
    own_b, sib_b, scale_b, normed_b = project(pieces_b, [all_b] * RING, z_array, norm_gain, weights, segs, "project_b")
    far_b = swapped(sib_b)
    context, query_grad, gnear, gfar = attention(queries[0], context_grad[0], own_a, own_b, far_a, far_b)
    gsib = swapped(gfar)

    parts_b = back_b(z_array, gnear, gsib, (own_a, own_b, sib_a, sib_b), weights, segs)
    arrived_b = over_plane(parts_b.reshape(plane, RING * half + EXTRA, HD))
    z_later, = after((z_array,), parts_b)
    opp_low, opp_high, up_low, up_high, down_low, down_high, kept = back_a(z_later, gnear, gsib, weights, segs)
    normed_far = [swapped(v) for v in after((normed_a, normed_b), gsib)]
    from_low, from_high = shifted(opp_low, 1), shifted(opp_high, -1)
    got_high, got_low = shifted(up_high, 1), shifted(down_low, -1)
    key_grad, value_grad = weight_grads(normed_a, normed_b, *normed_far, gnear, gfar)
    from_low, from_high = after((from_low, from_high), key_grad, value_grad)
    last_low = shifted((wide(up_low) + wide(from_low)).astype(BF16), 1)
    last_high = shifted((wide(down_high) + wide(from_high)).astype(BF16), -1)
    summed_low = wide(kept[: segs // 2]) + wide(got_low) + wide(last_low)
    summed_high = wide(kept[segs // 2 :]) + wide(got_high) + wide(last_high)
    summed_a = above(summed_low, summed_high).astype(BF16).reshape(plane, half, HD)

    arrived_b, summed_a = lax.optimization_barrier((arrived_b, summed_a))
    arrived_a = over_plane(summed_a)
    kept_b, dots, to_1, to_2, to_3 = merge_b(arrived_b, half)
    received = (shifted(to_1, 1), shifted(to_2, 2), shifted(to_3, -1))
    keep, send = finish(place, norm_gain, block, scale_a, scale_b, arrived_a, kept_b, dots, received)
    came = swapped(send)
    result = jnp.where(core == 0, above(keep, came), above(came, keep))
    return context[None], query_grad[None], key_grad[None], value_grad[None], result


def solution(mesh):
    fine = Mesh(mesh.devices.reshape(4, 2, 2, 4, 2), AXES)
    seg, tp = ("y", "xh"), ("xl", "z", "c")
    heads = P(seg, None, tp)
    return jax.shard_map(
        local,
        mesh=fine,
        in_specs=(P(seg, tp), P(), heads, heads, heads, heads),
        out_specs=(heads, heads, heads, heads, P(seg, tp)),
        check_vma=False,
    )
```

time: 213 us -> 161 us (0.76)
  starting transfers between devices: 76.4 us -> 42.7 us
  blocking collectives: 0 us -> 17.4 us
  waiting for transfers between devices: 51.8 us -> 36.3 us
  local copies, waits for them, and re-layouts: 33 us -> 18.9 us
  other arithmetic: 10.4 us -> 2.01 us
  Pallas kernels: 38.6 us -> 41.7 us
    ppermute x6 -> x0, waiting for transfers between devices: 24.7 us -> none  [exchanged(): return lax.ppermute(value, axis, [(i, i ^ bit) for i in range(size)])]
    all_to_all x0 -> x1, blocking collectives: none -> 17.4 us  [over_plane(): return lax.all_to_all(value, PLANE, 0, 0, tiled=True)]
    ppermute x18, waiting for transfers between devices: 11.7 us -> 26.7 us  [shifted(): return lax.ppermute(value, 'z', [(i, (i + by) % RING) for i in range(RING)])]
    ppermute x18, starting transfers between devices: 28.5 us -> 17 us  [shifted(): return lax.ppermute(value, 'z', [(i, (i + by) % RING) for i in range(RING)])]
    ppermute x6 -> x0, starting transfers between devices: 9.44 us -> none  [exchanged(): return lax.ppermute(value, axis, [(i, i ^ bit) for i in range(size)])]
    ppermute x9, starting transfers between devices: 18.4 us -> 11.6 us  [swapped(): return lax.ppermute(value, 'c', [(0, 1), (1, 0)])]
    concatenate x1 -> x0, local copies, waits for them, and re-layouts: 6.53 us -> none  [local(): w_own = jnp.concatenate([key_weight[0], value_weight[0]], axis=1)]
    ppermute x1 -> x0, local copies, waits for them, and re-layouts: 6.41 us -> none  [swapped(): return lax.ppermute(value, 'c', [(0, 1), (1, 0)])]
  transfers between devices with their start and end apart: 37 -> 30, of which waited for: 19 -> 17; matrix products, arithmetic and copies ran while one was open for 11% -> 2% of each run, Pallas kernels for 15% -> 22%
where the time goes in v3:
time: 161 us; the launch traced here: 160 us
  starting transfers between devices  42.7 us (27%)
  Pallas kernels  41.7 us (26%)
  waiting for transfers between devices  36.3 us (23%)
  local copies, waits for them, and re-layouts  18.9 us (12%)
  blocking collectives  17.4 us (11%)
  other arithmetic  2.01 us (1%)
    ppermute x18, waiting for transfers between devices, shifted(): return lax.ppermute(value, 'z', [(i, (i + by) % RING) for i in range(RING)])  26.7 us
    all_to_all x1, blocking collectives, over_plane(): return lax.all_to_all(value, PLANE, 0, 0, tiled=True)  17.4 us
    ppermute x18, starting transfers between devices, shifted(): return lax.ppermute(value, 'z', [(i, (i + by) % RING) for i in range(RING)])  17 us
    unnamed x50, local copies, waits for them, and re-layouts  15.8 us
    all_to_all x3, starting transfers between devices, over_plane(): return lax.all_to_all(value, PLANE, 0, 0, tiled=True)  14.1 us
    pallas_call x2, Pallas kernels, project(): pl.pallas_call(functools.partial(project_body, pieces), in_specs=[SMEM, V...  12.4 us
    ppermute x9, starting transfers between devices, swapped(): return lax.ppermute(value, 'c', [(0, 1), (1, 0)])  11.6 us
    pallas_call x1, Pallas kernels, weight_grads(): pl.pallas_call(weights_body, grid=(hidden // width,), in_specs=[block] *...  10.8 us
  transfers between devices with their start and end apart: 30, of which 17 were waited for; matrix products, arithmetic and copies ran while one was open for 2% of the time, Pallas kernels for 22%

profile of v3, /device:TPU:1, one launch (start us, length us, event | category | flops | bytes accessed | tf_op | source)
XLA Modules:
  0.0 160.0 jit_solution(485351974061402565)
XLA Ops:
  3.8 17.4 %all_to_all.20 = bf16[16,32,512]{2,1,0:T(8,128)(2,1)S(1)} all-to-all(bf16[16,32,512]{2,1,0:T(8,128)(2,1)S(1)} %broadcast_in_dim.18), channel_id=1, replica_groups=mesh['y'=4,'xh'=2,'xl'=2,'z'=4,'c'=2] {'y','xh','xl'}, dimensions={0} | all-to-all | bytes 1048576 | tf_op jit(solution)/shard_map/all_to_all | solution.py:355
  22.9 3.6 %collective-permute-start.10 = (bf16[32,512]{1,0:T(8,128)(2,1)S(1)}, bf16[32,512]{1,0:T(8,128)(2,1)S(1)}, u32[]{:S(2)}, u32[]{:S(2)}) collective-permute-start(bf16[32,512]{1,0:T(8,128)(2,1)S(1)} %get-tuple-element.86), channel_id=1, source_target_pairs={{0,4},{2,6},{4,0},{6,2},{1,5},{3,7},{5,1},{7,3},{8,12},{10,14},{12... | collective-permute-start | bytes 98312 | tf_op jit(solution)/shard_map/ppermute | solution.py:351
  32.5 3.9 %all-to-all-start.1 = ((bf16[16,4,32,512]{3,2,1,0:T(8,128)(2,1)}), bf16[16,4,32,512]{3,2,1,0:T(8,128)(2,1)S(1)}, u32[]{:S(2)}, u32[]{:S(2)}) async-start(bf16[16,4,32,512]{3,2,1,0:T(8,128)(2,1)} %broadcast_in_dim.19), calls=%async_computation.1 | async-start | bytes 4194304 | tf_op jit(solution)/shard_map/all_to_all | solution.py:355
  38.6 4.1 %collective-permute-done.4 = bf16[8,32,512]{2,1,0:T(8,128)(2,1)S(1)} collective-permute-done((bf16[8,32,512]{2,1,0:T(8,128)(2,1)S(1)}, bf16[8,32,512]{2,1,0:T(8,128)(2,1)S(1)}, u32[]{:S(2)}, u32[]{:S(2)}) %collective-permute-start.4) | collective-permute-done | bytes 262176 | tf_op jit(solution)/shard_map/ppermute | solution.py:351
  42.7 2.0 %collective-permute-start.3 = (bf16[8,32,512]{2,1,0:T(8,128)(2,1)}, bf16[8,32,512]{2,1,0:T(8,128)(2,1)}, u32[]{:S(2)}, u32[]{:S(2)}) collective-permute-start(bf16[8,32,512]{2,1,0:T(8,128)(2,1)} %get-tuple-element.84), channel_id=1, source_target_pairs={{0,6},{2,0},{4,2},{6,4},{1,7},{3,1},{5,3},{7,5},{8,14},{10,8},{12,... | collective-permute-start | bytes 786440 | tf_op jit(solution)/shard_map/ppermute | solution.py:351
  45.4 4.6 %collective-permute-done.1 = bf16[8,32,512]{2,1,0:T(8,128)(2,1)S(1)} collective-permute-done((bf16[8,32,512]{2,1,0:T(8,128)(2,1)}, bf16[8,32,512]{2,1,0:T(8,128)(2,1)S(1)}, u32[]{:S(2)}, u32[]{:S(2)}) %collective-permute-start.1) | collective-permute-done | bytes 262176 | tf_op jit(solution)/shard_map/ppermute | solution.py:351
  50.8 2.7 %collective-permute-done.6 = bf16[8,32,512]{2,1,0:T(8,128)(2,1)S(1)} collective-permute-done((bf16[8,32,512]{2,1,0:T(8,128)(2,1)S(1)}, bf16[8,32,512]{2,1,0:T(8,128)(2,1)S(1)}, u32[]{:S(2)}, u32[]{:S(2)}) %collective-permute-start.6) | collective-permute-done | bytes 262176 | tf_op jit(solution)/shard_map/ppermute | solution.py:351
  54.1 2.6 %collective-permute-done.5 = bf16[8,32,512]{2,1,0:T(8,128)(2,1)} collective-permute-done((bf16[8,32,512]{2,1,0:T(8,128)(2,1)S(1)}, bf16[8,32,512]{2,1,0:T(8,128)(2,1)}, u32[]{:S(2)}, u32[]{:S(2)}) %collective-permute-start.5) | collective-permute-done | bytes 262176 | tf_op jit(solution)/shard_map/ppermute | solution.py:351
  62.8 6.7 %project_a.1 = (bf16[256,512]{1,0:T(8,128)(2,1)S(1)}, bf16[256,512]{1,0:T(8,128)(2,1)S(1)}, f32[256,1]{1,0:T(8,128)S(1)}, bf16[256,4096]{1,0:T(8,128)(2,1)}) custom-call(s32[1]{0:T(128)} %bitcast.2.z_ref, f32[8,1,512]{2,1,0:T(1,128)S(1)} %bitcast.53, bf16[8,2,32,512]{3,2,1,0:T(8,128)(2,1)S(1)} %bitcast.48, bf16[4,2,32,512]{3,2,1,0:T(8,128)(2,1)S(1)} %bitcast.51, ...), custom_call_target="tpu_custom_call" | custom-call | flops 2147483648 | bytes 5242880 | tf_op jit(solution)/shard_map/project_a/pallas_call | solution.py:98
  70.2 4.0 %collective-permute-start.12 = (bf16[256,512]{1,0:T(8,128)(2,1)S(1)}, bf16[256,512]{1,0:T(8,128)(2,1)S(1)}, u32[]{:S(2)}, u32[]{:S(2)}) collective-permute-start(bf16[256,512]{1,0:T(8,128)(2,1)S(1)} %get-tuple-element.48.sib_a), channel_id=1, source_target_pairs={{0,1},{1,0},{2,3},{3,2},{4,5},{5,4},{6,7},{7,6},{8,9},{9,8},{10,11... | collective-permute-start | bytes 786440 | tf_op jit(solution)/shard_map/ppermute | solution.py:347
  77.3 5.7 %project_b.1 = (bf16[256,512]{1,0:T(8,128)(2,1)S(1)}, bf16[256,512]{1,0:T(8,128)(2,1)S(1)}, f32[256,1]{1,0:T(8,128)S(1)}, bf16[256,4096]{1,0:T(8,128)(2,1)}) custom-call(s32[1]{0:T(128)} %bitcast.2.z_ref, f32[8,1,512]{2,1,0:T(1,128)S(1)} %bitcast.54, bf16[8,2,4,32,512]{4,3,2,1,0:T(8,128)(2,1)S(1)} %bitcast.33, bf16[8,2,4,32,512]{4,3,2,1,0:T(8,128)(2,1)S(1)} %bitcast.34, ...), custom_call_target="tpu_custom_call" | custom-call | flops 2147483648 | bytes 5242880 | tf_op jit(solution)/shard_map/project_b/pallas_call | solution.py:98
  84.9 5.9 %attention.1 = (bf16[1024,256]{1,0:T(8,128)(2,1)}, bf16[1024,256]{1,0:T(8,128)(2,1)}, bf16[512,512]{1,0:T(8,128)(2,1)S(1)}, bf16[512,512]{1,0:T(8,128)(2,1)S(1)}) custom-call(bf16[1024,256]{1,0:T(8,128)(2,1)S(1)} %bitcast.56, bf16[1024,256]{1,0:T(8,128)(2,1)S(1)} %bitcast.57, bf16[256,512]{1,0:T(8,128)(2,1)S(1)} %get-tuple-element.45.near_a.own_a, ...), custom_call_target="tpu_custom_call" | custom-call | flops 3221225472 | bytes 4194304 | tf_op jit(solution)/shard_map/attention/pallas_call | solution.py:151
  93.2 5.3 %back_b.1 = bf16[8,2,272,256]{3,2,1,0:T(8,128)(2,1)S(1)} custom-call(s32[1]{0:T(128)} %bitcast.2.z_ref, bf16[512,512]{1,0:T(8,128)(2,1)S(1)} %get-tuple-element.57.gnear_ref.own_ref, bf16[512,512]{1,0:T(8,128)(2,1)S(1)} %collective-permute-done.14.sib_ref, bf16[256,512]{1,0:T(8,128)(2,1)S(1)} %get-tuple-element.45.near_a.own_a, ...), custom_call_target="tpu_custom_call" | custom-call | flops 2147483648 | bytes 4194304 | tf_op jit(solution)/shard_map/back_b/pallas_call | solution.py:205
  99.9 6.7 %all-to-all-start.2 = ((bf16[16,272,256]{2,1,0:T(8,128)(2,1)}), bf16[16,272,256]{2,1,0:T(8,128)(2,1)}, u32[]{:S(2)}, u32[]{:S(2)}) async-start(bf16[16,272,256]{2,1,0:T(8,128)(2,1)} %bitcast.47), calls=%async_computation.2 | async-start | bytes 4456448 | tf_op jit(solution)/shard_map/all_to_all | solution.py:355
  108.2 4.6 %back_a.1 = (bf16[4,2,64,256]{3,2,1,0:T(8,128)(2,1)S(1)}, bf16[4,2,64,256]{3,2,1,0:T(8,128)(2,1)S(1)}, bf16[4,2,64,256]{3,2,1,0:T(8,128)(2,1)S(1)}, bf16[4,2,64,...) custom-call(s32[1]{0:T(128)} %bitcast.2.z_ref, ...), custom_call_target="tpu_custom_call" | custom-call | flops 2147483648 | bytes 4194304 | tf_op jit(solution)/shard_map/back_a/pallas_call | solution.py:235
  115.8 10.8 %weight_grads.1 = (f32[4096,256]{1,0:T(8,128)}, f32[4096,256]{1,0:T(8,128)}) custom-call(bf16[256,4096]{1,0:T(8,128)(2,1)} %get-tuple-element.55.near_a, bf16[256,4096]{1,0:T(8,128)(2,1)} %get-tuple-element.56.near_b, bf16[256,4096]{1,0:T(8,128)(2,1)} %collective-permute-done.15.far_a, bf16[256,4096]{1,0:T(8,128)(2,1)} %collective-permute-done.16.far_b, ...), custom_call_target="tpu_custom_call" | custom-call | flops 4294967296 | bytes 17825792 | tf_op jit(solution)/shard_map/weight_grads/pallas_call | solution.py:258
  126.7 2.7 %collective-permute-start.22 = (bf16[4,2,64,256]{3,2,1,0:T(8,128)(2,1)S(1)}, bf16[4,2,64,256]{3,2,1,0:T(8,128)(2,1)S(1)}, u32[]{:S(2)}, u32[]{:S(2)}) collective-permute-start(bf16[4,2,64,256]{3,2,1,0:T(8,128)(2,1)S(1)} %add_convert_fusion.1), channel_id=1, source_target_pairs={{0,6},{2,0},{4,2},{6,4},{1,7},{3,1},{5,3},{7,5},{8,14},{10,8},{12,... | collective-permute-start | bytes 786440 | tf_op jit(solution)/shard_map/ppermute | solution.py:351
  129.6 3.9 %collective-permute-done.22 = bf16[4,2,64,256]{3,2,1,0:T(8,128)(2,1)S(1)} collective-permute-done((bf16[4,2,64,256]{3,2,1,0:T(8,128)(2,1)S(1)}, bf16[4,2,64,256]{3,2,1,0:T(8,128)(2,1)S(1)}, u32[]{:S(2)}, u32[]{:S(2)}) %collective-permute-start.22) | collective-permute-done | bytes 262176 | tf_op jit(solution)/shard_map/ppermute | solution.py:351
  133.5 3.3 %collective-permute-done.20 = bf16[4,2,64,256]{3,2,1,0:T(8,128)(2,1)S(1)} collective-permute-done((bf16[4,2,64,256]{3,2,1,0:T(8,128)(2,1)S(1)}, bf16[4,2,64,256]{3,2,1,0:T(8,128)(2,1)S(1)}, u32[]{:S(2)}, u32[]{:S(2)}) %collective-permute-start.20) | collective-permute-done | bytes 262176 | tf_op jit(solution)/shard_map/ppermute | solution.py:351
  137.9 3.5 %all-to-all-done.2.arrived_ref = bf16[16,272,256]{2,1,0:T(8,128)(2,1)} async-done(((bf16[16,272,256]{2,1,0:T(8,128)(2,1)}), bf16[16,272,256]{2,1,0:T(8,128)(2,1)}, u32[]{:S(2)}, u32[]{:S(2)}) %all-to-all-start.2) | async-done | bytes 2228256 | tf_op jit(solution)/shard_map/all_to_all | solution.py:355
  141.4 3.6 %all-to-all-start.3 = ((bf16[16,64,256]{2,1,0:T(8,128)(2,1)}), bf16[16,64,256]{2,1,0:T(8,128)(2,1)S(1)}, u32[]{:S(2)}, u32[]{:S(2)}) async-start(bf16[16,64,256]{2,1,0:T(8,128)(2,1)} %bitcast.29), calls=%async_computation.3 | async-start | bytes 1048576 | tf_op jit(solution)/shard_map/all_to_all | solution.py:355
  145.0 1.9 %merge_b.1 = (f32[64,256]{1,0:T(8,128)S(1)}, f32[1,512]{1,0:T(1,128)S(1)}, bf16[80,256]{1,0:T(8,128)(2,1)S(1)}, bf16[80,256]{1,0:T(8,128)(2,1)S(1)}, bf16[80,256]{1,0:T(8,128)(2,1)S(1)}) custom-call(bf16[16,272,256]{2,1,0:T(8,128)(2,1)} %all-to-all-done.2.arrived_ref), custom_call_target="tpu_custom_call" | custom-call | bytes 3145728 | tf_op jit(solution)/shard_map/merge_b/pallas_call | solution.py:287
  152.3 1.8 %all-to-all-done.3.arrived_ref = bf16[16,64,256]{2,1,0:T(8,128)(2,1)S(1)} async-done(((bf16[16,64,256]{2,1,0:T(8,128)(2,1)}), bf16[16,64,256]{2,1,0:T(8,128)(2,1)S(1)}, u32[]{:S(2)}, u32[]{:S(2)}) %all-to-all-start.3) | async-done | bytes 524320 | tf_op jit(solution)/shard_map/all_to_all | solution.py:355
  154.9 3.5 %collective-permute-start.26 = (f32[64,256]{1,0:T(8,128)S(1)}, f32[64,256]{1,0:T(8,128)S(1)}, u32[]{:S(2)}, u32[]{:S(2)}) collective-permute-start(f32[64,256]{1,0:T(8,128)S(1)} %get-tuple-element.80), channel_id=1, source_target_pairs={{0,1},{1,0},{2,3},{3,2},{4,5},{5,4},{6,7},{7,6},{8,9},{9,8},{10,11... | collective-permute-start | bytes 196616 | tf_op jit(solution)/shard_map/ppermute | solution.py:347
  (108 shorter events, 44.4 us)
Async XLA Ops:
  21.2 35.6 %collective-permute-start.7 = (bf16[4096,256]{1,0:T(8,128)(2,1)}, bf16[4096,256]{1,0:T(8,128)(2,1)}, u32[]{:S(2)}, u32[]{:S(2)}) collective-permute-start(bf16[4096,256]{1,0:T(8,128)(2,1)} %bitcast.37), channel_id=1, source_target_pairs={{0,1},{1,0},{2,3},{3,2},{4,5},{5,4},{6,7},{7,6},{8,9},{9,8},{10,11... | collective-permute-start | bytes 6291464 | tf_op jit(solution)/shard_map/ppermute | solution.py:347
  22.9 33.9 %collective-permute-start.8 = (bf16[4096,256]{1,0:T(8,128)(2,1)}, bf16[4096,256]{1,0:T(8,128)(2,1)}, u32[]{:S(2)}, u32[]{:S(2)}) collective-permute-start(bf16[4096,256]{1,0:T(8,128)(2,1)} %bitcast.42), channel_id=1, source_target_pairs={{0,1},{1,0},{2,3},{3,2},{4,5},{5,4},{6,7},{7,6},{8,9},{9,8},{10,11... | collective-permute-start | bytes 6291464 | tf_op jit(solution)/shard_map/ppermute | solution.py:347
  22.9 5.1 %collective-permute-start.10 = (bf16[32,512]{1,0:T(8,128)(2,1)S(1)}, bf16[32,512]{1,0:T(8,128)(2,1)S(1)}, u32[]{:S(2)}, u32[]{:S(2)}) collective-permute-start(bf16[32,512]{1,0:T(8,128)(2,1)S(1)} %get-tuple-element.86), channel_id=1, source_target_pairs={{0,4},{2,6},{4,0},{6,2},{1,5},{3,7},{5,1},{7,3},{8,12},{10,14},{12... | collective-permute-start | bytes 98312 | tf_op jit(solution)/shard_map/ppermute | solution.py:351
  32.5 37.7 %all-to-all-start.1 = ((bf16[16,4,32,512]{3,2,1,0:T(8,128)(2,1)}), bf16[16,4,32,512]{3,2,1,0:T(8,128)(2,1)S(1)}, u32[]{:S(2)}, u32[]{:S(2)}) async-start(bf16[16,4,32,512]{3,2,1,0:T(8,128)(2,1)} %broadcast_in_dim.19), calls=%async_computation.1 | async-start | bytes 4194304 | tf_op jit(solution)/shard_map/all_to_all | solution.py:355
  37.1 5.6 %collective-permute-start.4 = (bf16[8,32,512]{2,1,0:T(8,128)(2,1)S(1)}, bf16[8,32,512]{2,1,0:T(8,128)(2,1)S(1)}, u32[]{:S(2)}, u32[]{:S(2)}) collective-permute-start(bf16[8,32,512]{2,1,0:T(8,128)(2,1)S(1)} %get-tuple-element.83), channel_id=1, source_target_pairs={{0,6},{2,0},{4,2},{6,4},{1,7},{3,1},{5,3},{7,5},{8,14},{10,8},{12,... | collective-permute-start | bytes 786440 | tf_op jit(solution)/shard_map/ppermute | solution.py:351
  37.5 7.2 %collective-permute-start.2 = (bf16[8,32,512]{2,1,0:T(8,128)(2,1)S(1)}, bf16[8,32,512]{2,1,0:T(8,128)(2,1)S(1)}, u32[]{:S(2)}, u32[]{:S(2)}) collective-permute-start(bf16[8,32,512]{2,1,0:T(8,128)(2,1)S(1)} %get-tuple-element.83), channel_id=1, source_target_pairs={{0,2},{2,4},{4,6},{6,0},{1,3},{3,5},{5,7},{7,1},{8,10},{10,12},{12... | collective-permute-start | bytes 786440 | tf_op jit(solution)/shard_map/ppermute | solution.py:351
  38.6 11.4 %collective-permute-start.1 = (bf16[8,32,512]{2,1,0:T(8,128)(2,1)}, bf16[8,32,512]{2,1,0:T(8,128)(2,1)S(1)}, u32[]{:S(2)}, u32[]{:S(2)}) collective-permute-start(bf16[8,32,512]{2,1,0:T(8,128)(2,1)} %get-tuple-element.84), channel_id=1, source_target_pairs={{0,2},{2,4},{4,6},{6,0},{1,3},{3,5},{5,7},{7,1},{8,10},{10,12},{12... | collective-permute-start | bytes 786440 | tf_op jit(solution)/shard_map/ppermute | solution.py:351
  42.7 8.0 %collective-permute-start.3 = (bf16[8,32,512]{2,1,0:T(8,128)(2,1)}, bf16[8,32,512]{2,1,0:T(8,128)(2,1)}, u32[]{:S(2)}, u32[]{:S(2)}) collective-permute-start(bf16[8,32,512]{2,1,0:T(8,128)(2,1)} %get-tuple-element.84), channel_id=1, source_target_pairs={{0,6},{2,0},{4,2},{6,4},{1,7},{3,1},{5,3},{7,5},{8,14},{10,8},{12,... | collective-permute-start | bytes 786440 | tf_op jit(solution)/shard_map/ppermute | solution.py:351
  45.4 8.0 %collective-permute-start.6 = (bf16[8,32,512]{2,1,0:T(8,128)(2,1)S(1)}, bf16[8,32,512]{2,1,0:T(8,128)(2,1)S(1)}, u32[]{:S(2)}, u32[]{:S(2)}) collective-permute-start(bf16[8,32,512]{2,1,0:T(8,128)(2,1)S(1)} %collective-permute-done.4), channel_id=1, source_target_pairs={{0,6},{2,0},{4,2},{6,4},{1,7},{3,1},{5,3},{7,5},{8,14},{10,8},{12,... | collective-permute-start | bytes 786440 | tf_op jit(solution)/shard_map/ppermute | solution.py:351
  50.0 6.7 %collective-permute-start.5 = (bf16[8,32,512]{2,1,0:T(8,128)(2,1)S(1)}, bf16[8,32,512]{2,1,0:T(8,128)(2,1)}, u32[]{:S(2)}, u32[]{:S(2)}) collective-permute-start(bf16[8,32,512]{2,1,0:T(8,128)(2,1)S(1)} %collective-permute-done.1), channel_id=1, source_target_pairs={{0,2},{2,4},{4,6},{6,0},{1,3},{3,5},{5,7},{7,1},{8,10},{10,12},{12... | collective-permute-start | bytes 786440 | tf_op jit(solution)/shard_map/ppermute | solution.py:351
  70.2 13.2 %collective-permute-start.12 = (bf16[256,512]{1,0:T(8,128)(2,1)S(1)}, bf16[256,512]{1,0:T(8,128)(2,1)S(1)}, u32[]{:S(2)}, u32[]{:S(2)}) collective-permute-start(bf16[256,512]{1,0:T(8,128)(2,1)S(1)} %get-tuple-element.48.sib_a), channel_id=1, source_target_pairs={{0,1},{1,0},{2,3},{3,2},{4,5},{5,4},{6,7},{7,6},{8,9},{9,8},{10,11... | collective-permute-start | bytes 786440 | tf_op jit(solution)/shard_map/ppermute | solution.py:347
  92.7 23.1 %collective-permute-start.15 = (bf16[256,4096]{1,0:T(8,128)(2,1)}, bf16[256,4096]{1,0:T(8,128)(2,1)}, u32[]{:S(2)}, u32[]{:S(2)}) collective-permute-start(bf16[256,4096]{1,0:T(8,128)(2,1)} %get-tuple-element.55.near_a), channel_id=1, source_target_pairs={{0,1},{1,0},{2,3},{3,2},{4,5},{5,4},{6,7},{7,6},{8,9},{9,8},{10,11... | collective-permute-start | bytes 6291464 | tf_op jit(solution)/shard_map/ppermute | solution.py:347
  92.8 23.0 %collective-permute-start.16 = (bf16[256,4096]{1,0:T(8,128)(2,1)}, bf16[256,4096]{1,0:T(8,128)(2,1)}, u32[]{:S(2)}, u32[]{:S(2)}) collective-permute-start(bf16[256,4096]{1,0:T(8,128)(2,1)} %get-tuple-element.56.near_b), channel_id=1, source_target_pairs={{0,1},{1,0},{2,3},{3,2},{4,5},{5,4},{6,7},{7,6},{8,9},{9,8},{10,11... | collective-permute-start | bytes 6291464 | tf_op jit(solution)/shard_map/ppermute | solution.py:347
  99.9 41.5 %all-to-all-start.2 = ((bf16[16,272,256]{2,1,0:T(8,128)(2,1)}), bf16[16,272,256]{2,1,0:T(8,128)(2,1)}, u32[]{:S(2)}, u32[]{:S(2)}) async-start(bf16[16,272,256]{2,1,0:T(8,128)(2,1)} %bitcast.47), calls=%async_computation.2 | async-start | bytes 4456448 | tf_op jit(solution)/shard_map/all_to_all | solution.py:355
  112.8 16.7 %collective-permute-start.17 = (bf16[4,2,64,256]{3,2,1,0:T(8,128)(2,1)S(1)}, bf16[4,2,64,256]{3,2,1,0:T(8,128)(2,1)S(1)}, u32[]{:S(2)}, u32[]{:S(2)}) collective-permute-start(bf16[4,2,64,256]{3,2,1,0:T(8,128)(2,1)S(1)} %get-tuple-element.64), channel_id=1, source_target_pairs={{0,6},{2,0},{4,2},{6,4},{1,7},{3,1},{5,3},{7,5},{8,14},{10,8},{12,... | collective-permute-start | bytes 786440 | tf_op jit(solution)/shard_map/ppermute | solution.py:351
  113.0 13.6 %collective-permute-start.18 = (bf16[4,2,64,256]{3,2,1,0:T(8,128)(2,1)S(1)}, bf16[4,2,64,256]{3,2,1,0:T(8,128)(2,1)S(1)}, u32[]{:S(2)}, u32[]{:S(2)}) collective-permute-start(bf16[4,2,64,256]{3,2,1,0:T(8,128)(2,1)S(1)} %get-tuple-element.66), channel_id=1, source_target_pairs={{0,2},{2,4},{4,6},{6,0},{1,3},{3,5},{5,7},{7,1},{8,10},{10,12},{12... | collective-permute-start | bytes 786440 | tf_op jit(solution)/shard_map/ppermute | solution.py:351
  114.3 12.3 %collective-permute-start.19 = (bf16[4,2,64,256]{3,2,1,0:T(8,128)(2,1)S(1)}, bf16[4,2,64,256]{3,2,1,0:T(8,128)(2,1)S(1)}, u32[]{:S(2)}, u32[]{:S(2)}) collective-permute-start(bf16[4,2,64,256]{3,2,1,0:T(8,128)(2,1)S(1)} %get-tuple-element.67), channel_id=1, source_target_pairs={{0,6},{2,0},{4,2},{6,4},{1,7},{3,1},{5,3},{7,5},{8,14},{10,8},{12,... | collective-permute-start | bytes 786440 | tf_op jit(solution)/shard_map/ppermute | solution.py:351
  115.7 13.8 %collective-permute-start.21 = (bf16[4,2,64,256]{3,2,1,0:T(8,128)(2,1)S(1)}, bf16[4,2,64,256]{3,2,1,0:T(8,128)(2,1)S(1)}, u32[]{:S(2)}, u32[]{:S(2)}) collective-permute-start(bf16[4,2,64,256]{3,2,1,0:T(8,128)(2,1)S(1)} %get-tuple-element.69), channel_id=1, source_target_pairs={{0,2},{2,4},{4,6},{6,0},{1,3},{3,5},{5,7},{7,1},{8,10},{10,12},{12... | collective-permute-start | bytes 786440 | tf_op jit(solution)/shard_map/ppermute | solution.py:351
  126.7 6.7 %collective-permute-start.22 = (bf16[4,2,64,256]{3,2,1,0:T(8,128)(2,1)S(1)}, bf16[4,2,64,256]{3,2,1,0:T(8,128)(2,1)S(1)}, u32[]{:S(2)}, u32[]{:S(2)}) collective-permute-start(bf16[4,2,64,256]{3,2,1,0:T(8,128)(2,1)S(1)} %add_convert_fusion.1), channel_id=1, source_target_pairs={{0,6},{2,0},{4,2},{6,4},{1,7},{3,1},{5,3},{7,5},{8,14},{10,8},{12,... | collective-permute-start | bytes 786440 | tf_op jit(solution)/shard_map/ppermute | solution.py:351
  129.5 7.3 %collective-permute-start.20 = (bf16[4,2,64,256]{3,2,1,0:T(8,128)(2,1)S(1)}, bf16[4,2,64,256]{3,2,1,0:T(8,128)(2,1)S(1)}, u32[]{:S(2)}, u32[]{:S(2)}) collective-permute-start(bf16[4,2,64,256]{3,2,1,0:T(8,128)(2,1)S(1)} %add_convert_fusion.3), channel_id=1, source_target_pairs={{0,2},{2,4},{4,6},{6,0},{1,3},{3,5},{5,7},{7,1},{8,10},{10,12},{12... | collective-permute-start | bytes 786440 | tf_op jit(solution)/shard_map/ppermute | solution.py:351
  141.4 12.8 %all-to-all-start.3 = ((bf16[16,64,256]{2,1,0:T(8,128)(2,1)}), bf16[16,64,256]{2,1,0:T(8,128)(2,1)S(1)}, u32[]{:S(2)}, u32[]{:S(2)}) async-start(bf16[16,64,256]{2,1,0:T(8,128)(2,1)} %bitcast.29), calls=%async_computation.3 | async-start | bytes 1048576 | tf_op jit(solution)/shard_map/all_to_all | solution.py:355
  146.9 4.1 %collective-permute-start.23 = (bf16[80,256]{1,0:T(8,128)(2,1)S(1)}, bf16[80,256]{1,0:T(8,128)(2,1)S(1)}, u32[]{:S(2)}, u32[]{:S(2)}) collective-permute-start(bf16[80,256]{1,0:T(8,128)(2,1)S(1)} %get-tuple-element.76), channel_id=1, source_target_pairs={{0,2},{2,4},{4,6},{6,0},{1,3},{3,5},{5,7},{7,1},{8,10},{10,12},{12... | collective-permute-start | bytes 122888 | tf_op jit(solution)/shard_map/ppermute | solution.py:351
  147.0 4.5 %collective-permute-start.24 = (bf16[80,256]{1,0:T(8,128)(2,1)S(1)}, bf16[80,256]{1,0:T(8,128)(2,1)S(1)}, u32[]{:S(2)}, u32[]{:S(2)}) collective-permute-start(bf16[80,256]{1,0:T(8,128)(2,1)S(1)} %get-tuple-element.77), channel_id=1, source_target_pairs={{0,4},{2,6},{4,0},{6,2},{1,5},{3,7},{5,1},{7,3},{8,12},{10,14},{12... | collective-permute-start | bytes 122888 | tf_op jit(solution)/shard_map/ppermute | solution.py:351
  154.9 4.4 %collective-permute-start.26 = (f32[64,256]{1,0:T(8,128)S(1)}, f32[64,256]{1,0:T(8,128)S(1)}, u32[]{:S(2)}, u32[]{:S(2)}) collective-permute-start(f32[64,256]{1,0:T(8,128)S(1)} %get-tuple-element.80), channel_id=1, source_target_pairs={{0,1},{1,0},{2,3},{3,2},{4,5},{5,4},{6,7},{7,6},{8,9},{9,8},{10,11... | collective-permute-start | bytes 196616 | tf_op jit(solution)/shard_map/ppermute | solution.py:347
  (31 other events, 159.5 us)

commit v4 on v3

--- a/solution.py
+++ b/solution.py
@@ -56,8 +56,8 @@
 
 def project_body(pieces, z_ref, gain_ref, *refs):
     xs = refs[: len(pieces)]
-    ko, vo, ks, vs, own_ref, sib_ref, scale_ref, normed_ref = refs[len(pieces) : len(pieces) + 8]
-    held, rows_low, x_sem, out_sem = refs[len(pieces) + 8 :]
+    ws, (own_ref, sib_ref, scale_ref, normed_ref) = refs[len(pieces) : len(pieces) + 4], refs[len(pieces) + 4 : len(pieces) + 8]
+    held, rows_low, weights, x_sem, w_sem, out_sem = refs[len(pieces) + 8 :]
     blocks, segs, part, width = held.shape
     rows = segs * part
     z = z_ref[0]
@@ -68,7 +68,8 @@
             source = x.at[:, side] if depth is None else x.at[:, side, depth]
             target = held.at[place, pl.ds(first, source.shape[0])]
             copies.append(pltpu.make_async_copy(source, target, x_sem.at[len(copies)]))
-    for copy in copies:
+    loads = [pltpu.make_async_copy(w, weights.at[i], w_sem.at[i]) for i, w in enumerate(ws)]
+    for copy in copies + loads:
         copy.start()
     for copy in copies:
         copy.wait()
@@ -85,9 +86,10 @@
         rows_low[:, p * width : (p + 1) * width] = (wide * scale * gain_ref[p]).astype(BF16)
     out = pltpu.make_async_copy(rows_low, normed_ref, out_sem)
     out.start()
-    for j, (w, out_ref) in enumerate(((ko, own_ref), (vo, own_ref), (ks, sib_ref), (vs, sib_ref))):
-        at = (j % 2) * HD
-        out_ref[:, at : at + HD] = nn(rows_low[...], w[...]).astype(BF16)
+    for i, load in enumerate(loads):
+        load.wait()
+        out_ref, at = (own_ref, sib_ref)[i // 2], (i % 2) * HD
+        out_ref[:, at : at + HD] = nn(rows_low[...], weights[i]).astype(BF16)
     out.wait()
 
 
@@ -97,7 +99,7 @@
     rows = segs * part
     return pl.pallas_call(
         functools.partial(project_body, pieces),
-        in_specs=[SMEM, VMEM] + [ANYWHERE] * len(xs) + [VMEM] * 4,
+        in_specs=[SMEM, VMEM] + [ANYWHERE] * (len(xs) + 4),
         out_specs=[VMEM, VMEM, VMEM, ANYWHERE],
         out_shape=[
             jax.ShapeDtypeStruct((rows, 2 * HD), BF16),
@@ -108,7 +110,9 @@
         scratch_shapes=[
             pltpu.VMEM((blocks, segs, part, width), BF16),
             pltpu.VMEM((rows, blocks * width), BF16),
+            pltpu.VMEM((4, blocks * width, HD), BF16),
             pltpu.SemaphoreType.DMA((2 * len(xs),)),
+            pltpu.SemaphoreType.DMA((4,)),
             pltpu.SemaphoreType.DMA(()),
         ],
         compiler_params=limits(20),
@@ -161,13 +165,30 @@
     )(q, dc, near_a, near_b, far_a, far_b)
 
 
-def feature_block(z, own, sib, weights, feature_half, distance, side):
-    block = side * RING + lax.rem(z + distance, RING)
-    at = pl.ds(pl.multiple_of(block * 2 * HD + feature_half * HD, HD), HD)
-    return nt(beside(own, sib), beside(*[w[at] for w in weights])).astype(BF16)
-
-
-def back_b_body(z_ref, own_ref, sib_ref, own_a, own_b, sib_a, sib_b, ko, vo, ks, vs, out_ref):
+def weight_loads(z, ws, held, sem, feature_half, order):
+    loads = []
+    for distance in order:
+        for side in range(2):
+            block = side * RING + lax.rem(z + distance, RING)
+            at = pl.ds(pl.multiple_of(block * 2 * HD + feature_half * HD, HD), HD)
+            i = len(loads)
+            loads.append([
+                pltpu.make_async_copy(w.at[at], held.at[i, :, pl.ds(j * HD, HD)], sem.at[i, j]) for j, w in enumerate(ws)
+            ])
+    for group in loads:
+        for load in group:
+            load.start()
+    return loads
+
+
+def feature_block(rows, loads, held, i):
+    for load in loads[i]:
+        load.wait()
+    return nt(rows, held[i]).astype(BF16)
+
+
+def back_b_body(z_ref, own_ref, sib_ref, own_a, own_b, sib_a, sib_b, ko, vo, ks, vs, out_ref, held, stage, w_sem, out_sem):
+    loads = weight_loads(z_ref[0], (ko, vo, ks, vs), held, w_sem, 1, range(RING))
     own, sib = own_ref[...], sib_ref[...]
     segs = out_ref.shape[0]
     part = own.shape[0] // segs // 2
@@ -180,14 +201,21 @@
     low = (products - wide(high)).astype(BF16)
     ones = jnp.ones((EXTRA, high.shape[1]), BF16)
     dots = nt(ones, high) + nt(ones, low)
-    out_ref[:, :, RING * 2 * part :] = jnp.broadcast_to(pieces_of(dots), (segs, 2, EXTRA, HD))
+    tail = RING * 2 * part
+    stage[:, :, tail:] = jnp.broadcast_to(pieces_of(dots), (segs, 2, EXTRA, HD))
+    rows = beside(own, sib)
+    outs = []
     for distance in range(RING):
+        at = distance * 2 * part
         for side in range(2):
-            value = feature_block(z_ref[0], own, sib, (ko, vo, ks, vs), 1, distance, side)
-            value = value.reshape(2, segs, part, HD)
+            value = feature_block(rows, loads, held, distance * 2 + side).reshape(2, segs, part, HD)
             for k in range(2):
-                at = distance * 2 * part + k * part
-                out_ref[:, side, at : at + part] = value[k]
+                stage[:, side, at + k * part : at + (k + 1) * part] = value[k]
+        size = 2 * part if distance < RING - 1 else 2 * part + EXTRA
+        outs.append(pltpu.make_async_copy(stage.at[:, :, pl.ds(at, size)], out_ref.at[:, :, pl.ds(at, size)], out_sem.at[distance]))
+        outs[-1].start()
+    for out in outs:
+        out.wait()
 
 
 def pieces_of(dots):
@@ -204,24 +232,32 @@
     rows = own.shape[0]
     return pl.pallas_call(
         back_b_body,
-        in_specs=[SMEM] + [VMEM] * 10,
-        out_specs=VMEM,
-        out_shape=jax.ShapeDtypeStruct((segs, 2, RING * rows // segs + EXTRA, HD), BF16),
+        in_specs=[SMEM] + [VMEM] * 6 + [ANYWHERE] * 4,
+        out_specs=ANYWHERE,
+        out_shape=pltpu.HBM((segs, 2, RING * rows // segs + EXTRA, HD), BF16),
+        scratch_shapes=[
+            pltpu.VMEM((2 * RING, HD, 4 * HD), BF16),
+            pltpu.VMEM((segs, 2, RING * rows // segs + EXTRA, HD), BF16),
+            pltpu.SemaphoreType.DMA((2 * RING, 4)),
+            pltpu.SemaphoreType.DMA((RING,)),
+        ],
         compiler_params=limits(20),
         cost_estimate=cost(2 * rows * 8 * HD * 4 * HD, 4),
         name="back_b",
     )(z, own, sib, *kvs, *weights)
 
 
-def back_a_body(z_ref, own_ref, sib_ref, ko, vo, ks, vs, *outs):
-    own, sib = own_ref[...], sib_ref[...]
+def back_a_body(z_ref, own_ref, sib_ref, ko, vo, ks, vs, *refs):
+    outs, (held, w_sem) = refs[:7], refs[7:]
+    order = (2, 1, 3, 0)
+    loads = weight_loads(z_ref[0], (ko, vo, ks, vs), held, w_sem, 0, order)
+    rows = beside(own_ref[...], sib_ref[...])
     segs = outs[-1].shape[0]
-    part = own.shape[0] // segs // 2
+    part = rows.shape[0] // segs // 2
     lands = {2: ((0, 0), (1, segs // 2)), 1: ((2, 0), (3, segs // 2)), 3: ((4, 0), (5, segs // 2)), 0: ((6, 0),)}
-    for distance in (2, 1, 3, 0):
+    for i, distance in enumerate(order):
         for side in range(2):
-            value = feature_block(z_ref[0], own, sib, (ko, vo, ks, vs), 0, distance, side)
-            value = value.reshape(2, segs, part, HD)
+            value = feature_block(rows, loads, held, 2 * i + side).reshape(2, segs, part, HD)
             for index, first in lands[distance]:
                 for k in range(2):
                     count = outs[index].shape[0]
@@ -234,9 +270,10 @@
     full = jax.ShapeDtypeStruct((segs, 2, rows // segs, HD), BF16)
     return pl.pallas_call(
         back_a_body,
-        in_specs=[SMEM] + [VMEM] * 6,
+        in_specs=[SMEM] + [VMEM] * 2 + [ANYWHERE] * 4,
         out_specs=[VMEM] * 7,
         out_shape=[half] * 6 + [full],
+        scratch_shapes=[pltpu.VMEM((2 * RING, HD, 4 * HD), BF16), pltpu.SemaphoreType.DMA((2 * RING, 4))],
         compiler_params=limits(20),
         cost_estimate=cost(2 * rows * 8 * HD * 4 * HD, 4),
         name="back_a",
@@ -343,6 +380,10 @@
     )(place, gain.reshape(hidden // width, 1, width), block, scale_a, scale_b, arrived, kept, dots, *received)
 
 
+def in_hbm(value):
+    return pltpu.with_memory_space_constraint(value, pltpu.HBM)
+
+
 def swapped(value):
     return lax.ppermute(value, "c", [(0, 1), (1, 0)])
 
@@ -386,12 +427,13 @@
     low_2, high_2 = shifted(low_3, 1), shifted(high_1, -1)
     deep = lambda value: value.reshape(segs // 2, 2, part, width)
 
-    key_own, value_own = after((key_weight[0], value_weight[0]), first_a)
-    weights = (key_own, value_own, swapped(key_own), swapped(value_own))
+    key_own, value_own = after((key_weight[0], value_weight[0]), near_z)
+    weights = [in_hbm(w) for w in (key_own, value_own, swapped(key_own), swapped(value_own))]
 
     top = segs // 2
     pieces_a = [(0, 0, None), (3, 0, None), (3, top, None), (1, 0, None), (1, top, None), (2, 0, None), (2, top, None)]
     xs_a = [first_a.reshape(segs, 2, part, width)] + [deep(v) for v in (low_3, high_3, low_1, high_1, low_2, high_2)]
+    xs_a = [in_hbm(x) for x in xs_a]
     own_a, sib_a, scale_a, normed_a = project(pieces_a, xs_a, z_array, norm_gain, weights, segs, "project_a")
     far_a = swapped(sib_a)
     all_b, = after((all_b,), own_a)

time: 161 us -> 153 us (0.950)
  blocking collectives: 17.4 us -> 0 us
  local copies, waits for them, and re-layouts: 18.9 us -> 4.26 us
  starting transfers between devices: 42.7 us -> 52.1 us
  Pallas kernels: 41.7 us -> 49.8 us
  waiting for transfers between devices: 36.3 us -> 42.8 us
    all_to_all x1 -> x0, blocking collectives: 17.4 us -> none  [over_plane(): return lax.all_to_all(value, PLANE, 0, 0, tiled=True)]
    unnamed x50 -> x30, local copies, waits for them, and re-layouts: 15.8 us -> 1.01 us
    all_to_all x3 -> x4, starting transfers between devices: 14.1 us -> 24.4 us  [over_plane(): return lax.all_to_all(value, PLANE, 0, 0, tiled=True)]
    pallas_call x2, Pallas kernels: 9.95 us -> 15.8 us  [the longest x1 8.54 us: back_b(): pl.pallas_call(back_b_body, in_specs=[SMEM] + [VMEM] * 6 + [ANYWHERE] * 4...]
    pallas_call x2, Pallas kernels: 12.4 us -> 16.4 us  [project(): pl.pallas_call(functools.partial(project_body, pieces), in_specs=[SMEM, V...]
    ppermute x18, waiting for transfers between devices: 26.7 us -> 30 us  [shifted(): return lax.ppermute(value, 'z', [(i, (i + by) % RING) for i in range(RING)])]
    all_to_all x3 -> x4, waiting for transfers between devices: 5.36 us -> 7.84 us  [over_plane(): return lax.all_to_all(value, PLANE, 0, 0, tiled=True)]
    pallas_call x1, Pallas kernels: 1.92 us -> 0.29 us  [merge_b(): pl.pallas_call(merge_b_body, in_specs=[VMEM], out_specs=[VMEM] * 5, out_s...]
  transfers between devices with their start and end apart: 30 -> 31, of which waited for: 17 -> 19; matrix products, arithmetic and copies ran while one was open for 2% -> 2% of each run, Pallas kernels for 22% -> 29%
where the time goes in v4:
time: 153 us; the launch traced here: 152 us
  starting transfers between devices  52.1 us (34%)
  Pallas kernels  49.8 us (33%)
  waiting for transfers between devices  42.8 us (28%)
  local copies, waits for them, and re-layouts  4.26 us (3%)
  other arithmetic  1.98 us (1%)
    ppermute x18, waiting for transfers between devices, shifted(): return lax.ppermute(value, 'z', [(i, (i + by) % RING) for i in range(RING)])  30 us
    all_to_all x4, starting transfers between devices, over_plane(): return lax.all_to_all(value, PLANE, 0, 0, tiled=True)  24.4 us
    ppermute x18, starting transfers between devices, shifted(): return lax.ppermute(value, 'z', [(i, (i + by) % RING) for i in range(RING)])  16.7 us
    pallas_call x2, Pallas kernels, project(): pl.pallas_call(functools.partial(project_body, pieces), in_specs=[SMEM, V...  16.4 us
    ppermute x9, starting transfers between devices, swapped(): return lax.ppermute(value, 'c', [(0, 1), (1, 0)])  11 us
    pallas_call x1, Pallas kernels, weight_grads(): pl.pallas_call(weights_body, grid=(hidden // width,), in_specs=[block] *...  10.8 us
    pallas_call x1, Pallas kernels, back_b(): pl.pallas_call(back_b_body, in_specs=[SMEM] + [VMEM] * 6 + [ANYWHERE] * 4...  8.54 us
    all_to_all x4, waiting for transfers between devices, over_plane(): return lax.all_to_all(value, PLANE, 0, 0, tiled=True)  7.84 us
  transfers between devices with their start and end apart: 31, of which 19 were waited for; matrix products, arithmetic and copies ran while one was open for 2% of the time, Pallas kernels for 29%

profile of v4, /device:TPU:1, one launch (start us, length us, event | category | flops | bytes accessed | tf_op | source)
XLA Modules:
  0.0 151.9 jit_solution(5278237216645979293)
XLA Ops:
  4.6 6.8 %all-to-all-start = ((bf16[16,32,512]{2,1,0:T(8,128)(2,1)}), bf16[16,32,512]{2,1,0:T(8,128)(2,1)S(1)}, u32[]{:S(2)}, u32[]{:S(2)}) async-start(bf16[16,32,512]{2,1,0:T(8,128)(2,1)} %broadcast_in_dim.18), calls=%async_computation | async-start | bytes 1048576 | tf_op jit(solution)/shard_map/all_to_all | solution.py:396
  11.4 3.7 %collective-permute-start.8 = (bf16[32,512]{1,0:T(8,128)(2,1)S(1)}, bf16[32,512]{1,0:T(8,128)(2,1)S(1)}, u32[]{:S(2)}, u32[]{:S(2)}) collective-permute-start(bf16[32,512]{1,0:T(8,128)(2,1)S(1)} %get-tuple-element.86), channel_id=1, source_target_pairs={{0,4},{2,6},{4,0},{6,2},{1,5},{3,7},{5,1},{7,3},{8,12},{10,14},{12... | collective-permute-start | bytes 98312 | tf_op jit(solution)/shard_map/ppermute | solution.py:392
  19.8 2.1 %collective-permute-start.10 = (bf16[4096,256]{1,0:T(8,128)(2,1)}, bf16[4096,256]{1,0:T(8,128)(2,1)}, u32[]{:S(2)}, u32[]{:S(2)}) collective-permute-start(bf16[4096,256]{1,0:T(8,128)(2,1)} %bitcast.14.refs_7_.refs_4_.ko), channel_id=1, source_target_pairs={{0,1},{1,0},{2,3},{3,2},{4,5},{5,4},{6,7},{7,6},{8,9},{9,8},{10,11... | collective-permute-start | bytes 6291464 | tf_op jit(solution)/shard_map/ppermute | solution.py:388
  23.7 6.9 %all-to-all-start.1 = ((bf16[16,4,32,512]{3,2,1,0:T(8,128)(2,1)}), bf16[16,4,32,512]{3,2,1,0:T(8,128)(2,1)S(1)}, u32[]{:S(2)}, u32[]{:S(2)}) async-start(bf16[16,4,32,512]{3,2,1,0:T(8,128)(2,1)} %broadcast_in_dim.19), calls=%async_computation.1 | async-start | bytes 4194304 | tf_op jit(solution)/shard_map/all_to_all | solution.py:396
  32.3 5.6 %collective-permute-done.4 = bf16[8,32,512]{2,1,0:T(8,128)(2,1)S(1)} collective-permute-done((bf16[8,32,512]{2,1,0:T(8,128)(2,1)S(1)}, bf16[8,32,512]{2,1,0:T(8,128)(2,1)S(1)}, u32[]{:S(2)}, u32[]{:S(2)}) %collective-permute-start.4) | collective-permute-done | bytes 262176 | tf_op jit(solution)/shard_map/ppermute | solution.py:392
  38.8 5.2 %collective-permute-done.1 = bf16[8,32,512]{2,1,0:T(8,128)(2,1)S(1)} collective-permute-done((bf16[8,32,512]{2,1,0:T(8,128)(2,1)S(1)}, bf16[8,32,512]{2,1,0:T(8,128)(2,1)S(1)}, u32[]{:S(2)}, u32[]{:S(2)}) %collective-permute-start.1) | collective-permute-done | bytes 262176 | tf_op jit(solution)/shard_map/ppermute | solution.py:392
  44.7 5.1 %collective-permute-done.6 = bf16[8,32,512]{2,1,0:T(8,128)(2,1)} collective-permute-done((bf16[8,32,512]{2,1,0:T(8,128)(2,1)S(1)}, bf16[8,32,512]{2,1,0:T(8,128)(2,1)}, u32[]{:S(2)}, u32[]{:S(2)}) %collective-permute-start.6) | collective-permute-done | bytes 262176 | tf_op jit(solution)/shard_map/ppermute | solution.py:392
  50.9 9.6 %project_a.1 = (bf16[256,512]{1,0:T(8,128)(2,1)S(1)}, bf16[256,512]{1,0:T(8,128)(2,1)S(1)}, f32[256,1]{1,0:T(8,128)S(1)}, bf16[256,4096]{1,0:T(8,128)(2,1)}) custom-call(s32[1]{0:T(128)} %bitcast.2.z_ref, f32[8,1,512]{2,1,0:T(1,128)S(1)} %bitcast.37, bf16[8,2,32,512]{3,2,1,0:T(8,128)(2,1)} %bitcast.43, bf16[4,2,32,512]{3,2,1,0:T(8,128)(2,1)} %bitcast.47, ...), custom_call_target="tpu_custom_call" | custom-call | flops 2147483648 | bytes 5242880 | tf_op jit(solution)/shard_map/project_a/pallas_call | solution.py:100
  60.5 1.9 %all-to-all-done.1 = bf16[16,4,32,512]{3,2,1,0:T(8,128)(2,1)S(1)} async-done(((bf16[16,4,32,512]{3,2,1,0:T(8,128)(2,1)}), bf16[16,4,32,512]{3,2,1,0:T(8,128)(2,1)S(1)}, u32[]{:S(2)}, u32[]{:S(2)}) %all-to-all-start.1) | async-done | bytes 2097184 | tf_op jit(solution)/shard_map/all_to_all | solution.py:396
  62.4 2.3 %collective-permute-start.12 = (bf16[256,512]{1,0:T(8,128)(2,1)S(1)}, bf16[256,512]{1,0:T(8,128)(2,1)S(1)}, u32[]{:S(2)}, u32[]{:S(2)}) collective-permute-start(bf16[256,512]{1,0:T(8,128)(2,1)S(1)} %get-tuple-element.48.sib_a), channel_id=1, source_target_pairs={{0,1},{1,0},{2,3},{3,2},{4,5},{5,4},{6,7},{7,6},{8,9},{9,8},{10,11... | collective-permute-start | bytes 786440 | tf_op jit(solution)/shard_map/ppermute | solution.py:388
  64.7 6.8 %project_b.1 = (bf16[256,512]{1,0:T(8,128)(2,1)S(1)}, bf16[256,512]{1,0:T(8,128)(2,1)S(1)}, f32[256,1]{1,0:T(8,128)S(1)}, bf16[256,4096]{1,0:T(8,128)(2,1)}) custom-call(s32[1]{0:T(128)} %bitcast.2.z_ref, f32[8,1,512]{2,1,0:T(1,128)S(1)} %bitcast.38, bf16[8,2,4,32,512]{4,3,2,1,0:T(8,128)(2,1)S(1)} %bitcast.33, bf16[8,2,4,32,512]{4,3,2,1,0:T(8,128)(2,1)S(1)} %bitcast.34, ...), custom_call_target="tpu_custom_call" | custom-call | flops 2147483648 | bytes 5242880 | tf_op jit(solution)/shard_map/project_b/pallas_call | solution.py:100
  73.2 5.7 %attention.1 = (bf16[1024,256]{1,0:T(8,128)(2,1)}, bf16[1024,256]{1,0:T(8,128)(2,1)}, bf16[512,512]{1,0:T(8,128)(2,1)S(1)}, bf16[512,512]{1,0:T(8,128)(2,1)S(1)}) custom-call(bf16[1024,256]{1,0:T(8,128)(2,1)S(1)} %bitcast.40, bf16[1024,256]{1,0:T(8,128)(2,1)S(1)} %bitcast.41, bf16[256,512]{1,0:T(8,128)(2,1)S(1)} %get-tuple-element.45.near_a.own_a, ...), custom_call_target="tpu_custom_call" | custom-call | flops 3221225472 | bytes 4194304 | tf_op jit(solution)/shard_map/attention/pallas_call | solution.py:155
  79.0 1.8 %collective-permute-done.14.sib_ref = bf16[512,512]{1,0:T(8,128)(2,1)S(1)} collective-permute-done((bf16[512,512]{1,0:T(8,128)(2,1)S(1)}, bf16[512,512]{1,0:T(8,128)(2,1)S(1)}, u32[]{:S(2)}, u32[]{:S(2)}) %collective-permute-start.14) | collective-permute-done | bytes 524320 | tf_op jit(solution)/shard_map/ppermute | solution.py:388
  82.3 8.5 %back_b.1 = bf16[8,2,272,256]{3,2,1,0:T(8,128)(2,1)} custom-call(s32[1]{0:T(128)} %bitcast.2.z_ref, bf16[512,512]{1,0:T(8,128)(2,1)S(1)} %get-tuple-element.57.gnear_ref.own_ref, bf16[512,512]{1,0:T(8,128)(2,1)S(1)} %collective-permute-done.14.sib_ref, bf16[256,512]{1,0:T(8,128)(2,1)S(1)} %copy-done.1, bf16[256,512]{1,0:T(8,128)(2,1)S(1)} %get-tuple-element.47.near_b.own_b, ...), custom_call_target="tpu_custom_call" | custom-call | flops 2147483648 | bytes 4194304 | tf_op jit(solution)/shard_map/back_b/pallas_call | solution.py:233
  90.8 6.6 %all-to-all-start.2 = ((bf16[16,272,256]{2,1,0:T(8,128)(2,1)}), bf16[16,272,256]{2,1,0:T(8,128)(2,1)S(1)}, u32[]{:S(2)}, u32[]{:S(2)}) async-start(bf16[16,272,256]{2,1,0:T(8,128)(2,1)} %bitcast.42), calls=%async_computation.2 | async-start | bytes 4456448 | tf_op jit(solution)/shard_map/all_to_all | solution.py:396
  97.5 7.3 %back_a.1 = (bf16[4,2,64,256]{3,2,1,0:T(8,128)(2,1)S(1)}, bf16[4,2,64,256]{3,2,1,0:T(8,128)(2,1)S(1)}, bf16[4,2,64,256]{3,2,1,0:T(8,128)(2,1)S(1)}, bf16[4,2,64,...) custom-call(s32[1]{0:T(128)} %bitcast.2.z_ref, ...), custom_call_target="tpu_custom_call" | custom-call | flops 2147483648 | bytes 4194304 | tf_op jit(solution)/shard_map/back_a/pallas_call | solution.py:271
  107.8 10.8 %weight_grads.1 = (f32[4096,256]{1,0:T(8,128)}, f32[4096,256]{1,0:T(8,128)}) custom-call(bf16[256,4096]{1,0:T(8,128)(2,1)} %get-tuple-element.55.near_a, bf16[256,4096]{1,0:T(8,128)(2,1)} %get-tuple-element.56.near_b, bf16[256,4096]{1,0:T(8,128)(2,1)} %collective-permute-done.15.far_a, bf16[256,4096]{1,0:T(8,128)(2,1)} %collective-permute-done.16.far_b, ...), custom_call_target="tpu_custom_call" | custom-call | flops 4294967296 | bytes 17825792 | tf_op jit(solution)/shard_map/weight_grads/pallas_call | solution.py:295
  118.7 2.6 %collective-permute-start.22 = (bf16[4,2,64,256]{3,2,1,0:T(8,128)(2,1)S(1)}, bf16[4,2,64,256]{3,2,1,0:T(8,128)(2,1)S(1)}, u32[]{:S(2)}, u32[]{:S(2)}) collective-permute-start(bf16[4,2,64,256]{3,2,1,0:T(8,128)(2,1)S(1)} %add_convert_fusion.1), channel_id=1, source_target_pairs={{0,6},{2,0},{4,2},{6,4},{1,7},{3,1},{5,3},{7,5},{8,14},{10,8},{12,... | collective-permute-start | bytes 786440 | tf_op jit(solution)/shard_map/ppermute | solution.py:392
  121.4 4.1 %collective-permute-done.22 = bf16[4,2,64,256]{3,2,1,0:T(8,128)(2,1)S(1)} collective-permute-done((bf16[4,2,64,256]{3,2,1,0:T(8,128)(2,1)S(1)}, bf16[4,2,64,256]{3,2,1,0:T(8,128)(2,1)S(1)}, u32[]{:S(2)}, u32[]{:S(2)}) %collective-permute-start.22) | collective-permute-done | bytes 262176 | tf_op jit(solution)/shard_map/ppermute | solution.py:392
  125.6 3.3 %collective-permute-done.20 = bf16[4,2,64,256]{3,2,1,0:T(8,128)(2,1)S(1)} collective-permute-done((bf16[4,2,64,256]{3,2,1,0:T(8,128)(2,1)S(1)}, bf16[4,2,64,256]{3,2,1,0:T(8,128)(2,1)S(1)}, u32[]{:S(2)}, u32[]{:S(2)}) %collective-permute-start.20) | collective-permute-done | bytes 262176 | tf_op jit(solution)/shard_map/ppermute | solution.py:392
  129.9 2.3 %all-to-all-done.2.arrived_ref = bf16[16,272,256]{2,1,0:T(8,128)(2,1)S(1)} async-done(((bf16[16,272,256]{2,1,0:T(8,128)(2,1)}), bf16[16,272,256]{2,1,0:T(8,128)(2,1)S(1)}, u32[]{:S(2)}, u32[]{:S(2)}) %all-to-all-start.2) | async-done | bytes 2228256 | tf_op jit(solution)/shard_map/all_to_all | solution.py:396
  132.2 4.1 %all-to-all-start.3 = ((bf16[16,64,256]{2,1,0:T(8,128)(2,1)}), bf16[16,64,256]{2,1,0:T(8,128)(2,1)S(1)}, u32[]{:S(2)}, u32[]{:S(2)}) async-start(bf16[16,64,256]{2,1,0:T(8,128)(2,1)} %bitcast.44), calls=%async_computation.3 | async-start | bytes 1048576 | tf_op jit(solution)/shard_map/all_to_all | solution.py:396
  141.8 3.5 %all-to-all-done.3.arrived_ref = bf16[16,64,256]{2,1,0:T(8,128)(2,1)S(1)} async-done(((bf16[16,64,256]{2,1,0:T(8,128)(2,1)}), bf16[16,64,256]{2,1,0:T(8,128)(2,1)S(1)}, u32[]{:S(2)}, u32[]{:S(2)}) %all-to-all-start.3) | async-done | bytes 524320 | tf_op jit(solution)/shard_map/all_to_all | solution.py:396
  146.1 4.3 %collective-permute-start.26 = (f32[64,256]{1,0:T(8,128)S(1)}, f32[64,256]{1,0:T(8,128)S(1)}, u32[]{:S(2)}, u32[]{:S(2)}) collective-permute-start(f32[64,256]{1,0:T(8,128)S(1)} %get-tuple-element.80), channel_id=1, source_target_pairs={{0,1},{1,0},{2,3},{3,2},{4,5},{5,4},{6,7},{7,6},{8,9},{9,8},{10,11... | collective-permute-start | bytes 196616 | tf_op jit(solution)/shard_map/ppermute | solution.py:388
  (89 shorter events, 29.9 us)
Async XLA Ops:
  4.6 17.6 %all-to-all-start = ((bf16[16,32,512]{2,1,0:T(8,128)(2,1)}), bf16[16,32,512]{2,1,0:T(8,128)(2,1)S(1)}, u32[]{:S(2)}, u32[]{:S(2)}) async-start(bf16[16,32,512]{2,1,0:T(8,128)(2,1)} %broadcast_in_dim.18), calls=%async_computation | async-start | bytes 1048576 | tf_op jit(solution)/shard_map/all_to_all | solution.py:396
  11.4 5.1 %collective-permute-start.8 = (bf16[32,512]{1,0:T(8,128)(2,1)S(1)}, bf16[32,512]{1,0:T(8,128)(2,1)S(1)}, u32[]{:S(2)}, u32[]{:S(2)}) collective-permute-start(bf16[32,512]{1,0:T(8,128)(2,1)S(1)} %get-tuple-element.86), channel_id=1, source_target_pairs={{0,4},{2,6},{4,0},{6,2},{1,5},{3,7},{5,1},{7,3},{8,12},{10,14},{12... | collective-permute-start | bytes 98312 | tf_op jit(solution)/shard_map/ppermute | solution.py:392
  19.8 31.0 %collective-permute-start.10 = (bf16[4096,256]{1,0:T(8,128)(2,1)}, bf16[4096,256]{1,0:T(8,128)(2,1)}, u32[]{:S(2)}, u32[]{:S(2)}) collective-permute-start(bf16[4096,256]{1,0:T(8,128)(2,1)} %bitcast.14.refs_7_.refs_4_.ko), channel_id=1, source_target_pairs={{0,1},{1,0},{2,3},{3,2},{4,5},{5,4},{6,7},{7,6},{8,9},{9,8},{10,11... | collective-permute-start | bytes 6291464 | tf_op jit(solution)/shard_map/ppermute | solution.py:388
  22.0 28.9 %collective-permute-start.11 = (bf16[4096,256]{1,0:T(8,128)(2,1)}, bf16[4096,256]{1,0:T(8,128)(2,1)}, u32[]{:S(2)}, u32[]{:S(2)}) collective-permute-start(bf16[4096,256]{1,0:T(8,128)(2,1)} %bitcast.15.refs_8_.refs_5_.vo), channel_id=1, source_target_pairs={{0,1},{1,0},{2,3},{3,2},{4,5},{5,4},{6,7},{7,6},{8,9},{9,8},{10,11... | collective-permute-start | bytes 6291464 | tf_op jit(solution)/shard_map/ppermute | solution.py:388
  23.7 38.7 %all-to-all-start.1 = ((bf16[16,4,32,512]{3,2,1,0:T(8,128)(2,1)}), bf16[16,4,32,512]{3,2,1,0:T(8,128)(2,1)S(1)}, u32[]{:S(2)}, u32[]{:S(2)}) async-start(bf16[16,4,32,512]{3,2,1,0:T(8,128)(2,1)} %broadcast_in_dim.19), calls=%async_computation.1 | async-start | bytes 4194304 | tf_op jit(solution)/shard_map/all_to_all | solution.py:396
  30.7 7.2 %collective-permute-start.4 = (bf16[8,32,512]{2,1,0:T(8,128)(2,1)S(1)}, bf16[8,32,512]{2,1,0:T(8,128)(2,1)S(1)}, u32[]{:S(2)}, u32[]{:S(2)}) collective-permute-start(bf16[8,32,512]{2,1,0:T(8,128)(2,1)S(1)} %get-tuple-element.83), channel_id=1, source_target_pairs={{0,6},{2,0},{4,2},{6,4},{1,7},{3,1},{5,3},{7,5},{8,14},{10,8},{12,... | collective-permute-start | bytes 786440 | tf_op jit(solution)/shard_map/ppermute | solution.py:392
  31.5 7.3 %collective-permute-start.2 = (bf16[8,32,512]{2,1,0:T(8,128)(2,1)S(1)}, bf16[8,32,512]{2,1,0:T(8,128)(2,1)S(1)}, u32[]{:S(2)}, u32[]{:S(2)}) collective-permute-start(bf16[8,32,512]{2,1,0:T(8,128)(2,1)S(1)} %get-tuple-element.83), channel_id=1, source_target_pairs={{0,2},{2,4},{4,6},{6,0},{1,3},{3,5},{5,7},{7,1},{8,10},{10,12},{12... | collective-permute-start | bytes 786440 | tf_op jit(solution)/shard_map/ppermute | solution.py:392
  32.2 11.9 %collective-permute-start.1 = (bf16[8,32,512]{2,1,0:T(8,128)(2,1)S(1)}, bf16[8,32,512]{2,1,0:T(8,128)(2,1)S(1)}, u32[]{:S(2)}, u32[]{:S(2)}) collective-permute-start(bf16[8,32,512]{2,1,0:T(8,128)(2,1)S(1)} %get-tuple-element.84), channel_id=1, source_target_pairs={{0,2},{2,4},{4,6},{6,0},{1,3},{3,5},{5,7},{7,1},{8,10},{10,12},{12... | collective-permute-start | bytes 786440 | tf_op jit(solution)/shard_map/ppermute | solution.py:392
  37.9 6.8 %collective-permute-start.3 = (bf16[8,32,512]{2,1,0:T(8,128)(2,1)S(1)}, bf16[8,32,512]{2,1,0:T(8,128)(2,1)}, u32[]{:S(2)}, u32[]{:S(2)}) collective-permute-start(bf16[8,32,512]{2,1,0:T(8,128)(2,1)S(1)} %get-tuple-element.84), channel_id=1, source_target_pairs={{0,6},{2,0},{4,2},{6,4},{1,7},{3,1},{5,3},{7,5},{8,14},{10,8},{12,... | collective-permute-start | bytes 786440 | tf_op jit(solution)/shard_map/ppermute | solution.py:392
  38.8 11.1 %collective-permute-start.6 = (bf16[8,32,512]{2,1,0:T(8,128)(2,1)S(1)}, bf16[8,32,512]{2,1,0:T(8,128)(2,1)}, u32[]{:S(2)}, u32[]{:S(2)}) collective-permute-start(bf16[8,32,512]{2,1,0:T(8,128)(2,1)S(1)} %collective-permute-done.4), channel_id=1, source_target_pairs={{0,6},{2,0},{4,2},{6,4},{1,7},{3,1},{5,3},{7,5},{8,14},{10,8},{12,... | collective-permute-start | bytes 786440 | tf_op jit(solution)/shard_map/ppermute | solution.py:392
  44.1 6.7 %collective-permute-start.5 = (bf16[8,32,512]{2,1,0:T(8,128)(2,1)S(1)}, bf16[8,32,512]{2,1,0:T(8,128)(2,1)}, u32[]{:S(2)}, u32[]{:S(2)}) collective-permute-start(bf16[8,32,512]{2,1,0:T(8,128)(2,1)S(1)} %collective-permute-done.1), channel_id=1, source_target_pairs={{0,2},{2,4},{4,6},{6,0},{1,3},{3,5},{5,7},{7,1},{8,10},{10,12},{12... | collective-permute-start | bytes 786440 | tf_op jit(solution)/shard_map/ppermute | solution.py:392
  62.4 9.2 %collective-permute-start.12 = (bf16[256,512]{1,0:T(8,128)(2,1)S(1)}, bf16[256,512]{1,0:T(8,128)(2,1)S(1)}, u32[]{:S(2)}, u32[]{:S(2)}) collective-permute-start(bf16[256,512]{1,0:T(8,128)(2,1)S(1)} %get-tuple-element.48.sib_a), channel_id=1, source_target_pairs={{0,1},{1,0},{2,3},{3,2},{4,5},{5,4},{6,7},{7,6},{8,9},{9,8},{10,11... | collective-permute-start | bytes 786440 | tf_op jit(solution)/shard_map/ppermute | solution.py:388
  80.8 26.8 %collective-permute-start.15 = (bf16[256,4096]{1,0:T(8,128)(2,1)}, bf16[256,4096]{1,0:T(8,128)(2,1)}, u32[]{:S(2)}, u32[]{:S(2)}) collective-permute-start(bf16[256,4096]{1,0:T(8,128)(2,1)} %get-tuple-element.55.near_a), channel_id=1, source_target_pairs={{0,1},{1,0},{2,3},{3,2},{4,5},{5,4},{6,7},{7,6},{8,9},{9,8},{10,11... | collective-permute-start | bytes 6291464 | tf_op jit(solution)/shard_map/ppermute | solution.py:388
  80.9 26.8 %collective-permute-start.16 = (bf16[256,4096]{1,0:T(8,128)(2,1)}, bf16[256,4096]{1,0:T(8,128)(2,1)}, u32[]{:S(2)}, u32[]{:S(2)}) collective-permute-start(bf16[256,4096]{1,0:T(8,128)(2,1)} %get-tuple-element.56.near_b), channel_id=1, source_target_pairs={{0,1},{1,0},{2,3},{3,2},{4,5},{5,4},{6,7},{7,6},{8,9},{9,8},{10,11... | collective-permute-start | bytes 6291464 | tf_op jit(solution)/shard_map/ppermute | solution.py:388
  90.8 41.4 %all-to-all-start.2 = ((bf16[16,272,256]{2,1,0:T(8,128)(2,1)}), bf16[16,272,256]{2,1,0:T(8,128)(2,1)S(1)}, u32[]{:S(2)}, u32[]{:S(2)}) async-start(bf16[16,272,256]{2,1,0:T(8,128)(2,1)} %bitcast.42), calls=%async_computation.2 | async-start | bytes 4456448 | tf_op jit(solution)/shard_map/all_to_all | solution.py:396
  104.7 16.6 %collective-permute-start.17 = (bf16[4,2,64,256]{3,2,1,0:T(8,128)(2,1)S(1)}, bf16[4,2,64,256]{3,2,1,0:T(8,128)(2,1)S(1)}, u32[]{:S(2)}, u32[]{:S(2)}) collective-permute-start(bf16[4,2,64,256]{3,2,1,0:T(8,128)(2,1)S(1)} %get-tuple-element.64), channel_id=1, source_target_pairs={{0,6},{2,0},{4,2},{6,4},{1,7},{3,1},{5,3},{7,5},{8,14},{10,8},{12,... | collective-permute-start | bytes 786440 | tf_op jit(solution)/shard_map/ppermute | solution.py:392
  104.8 13.8 %collective-permute-start.18 = (bf16[4,2,64,256]{3,2,1,0:T(8,128)(2,1)S(1)}, bf16[4,2,64,256]{3,2,1,0:T(8,128)(2,1)S(1)}, u32[]{:S(2)}, u32[]{:S(2)}) collective-permute-start(bf16[4,2,64,256]{3,2,1,0:T(8,128)(2,1)S(1)} %get-tuple-element.66), channel_id=1, source_target_pairs={{0,2},{2,4},{4,6},{6,0},{1,3},{3,5},{5,7},{7,1},{8,10},{10,12},{12... | collective-permute-start | bytes 786440 | tf_op jit(solution)/shard_map/ppermute | solution.py:392
  106.3 12.3 %collective-permute-start.19 = (bf16[4,2,64,256]{3,2,1,0:T(8,128)(2,1)S(1)}, bf16[4,2,64,256]{3,2,1,0:T(8,128)(2,1)S(1)}, u32[]{:S(2)}, u32[]{:S(2)}) collective-permute-start(bf16[4,2,64,256]{3,2,1,0:T(8,128)(2,1)S(1)} %get-tuple-element.67), channel_id=1, source_target_pairs={{0,6},{2,0},{4,2},{6,4},{1,7},{3,1},{5,3},{7,5},{8,14},{10,8},{12,... | collective-permute-start | bytes 786440 | tf_op jit(solution)/shard_map/ppermute | solution.py:392
  107.6 13.8 %collective-permute-start.21 = (bf16[4,2,64,256]{3,2,1,0:T(8,128)(2,1)S(1)}, bf16[4,2,64,256]{3,2,1,0:T(8,128)(2,1)S(1)}, u32[]{:S(2)}, u32[]{:S(2)}) collective-permute-start(bf16[4,2,64,256]{3,2,1,0:T(8,128)(2,1)S(1)} %get-tuple-element.69), channel_id=1, source_target_pairs={{0,2},{2,4},{4,6},{6,0},{1,3},{3,5},{5,7},{7,1},{8,10},{10,12},{12... | collective-permute-start | bytes 786440 | tf_op jit(solution)/shard_map/ppermute | solution.py:392
  118.7 6.9 %collective-permute-start.22 = (bf16[4,2,64,256]{3,2,1,0:T(8,128)(2,1)S(1)}, bf16[4,2,64,256]{3,2,1,0:T(8,128)(2,1)S(1)}, u32[]{:S(2)}, u32[]{:S(2)}) collective-permute-start(bf16[4,2,64,256]{3,2,1,0:T(8,128)(2,1)S(1)} %add_convert_fusion.1), channel_id=1, source_target_pairs={{0,6},{2,0},{4,2},{6,4},{1,7},{3,1},{5,3},{7,5},{8,14},{10,8},{12,... | collective-permute-start | bytes 786440 | tf_op jit(solution)/shard_map/ppermute | solution.py:392
  121.3 7.5 %collective-permute-start.20 = (bf16[4,2,64,256]{3,2,1,0:T(8,128)(2,1)S(1)}, bf16[4,2,64,256]{3,2,1,0:T(8,128)(2,1)S(1)}, u32[]{:S(2)}, u32[]{:S(2)}) collective-permute-start(bf16[4,2,64,256]{3,2,1,0:T(8,128)(2,1)S(1)} %add_convert_fusion.3), channel_id=1, source_target_pairs={{0,2},{2,4},{4,6},{6,0},{1,3},{3,5},{5,7},{7,1},{8,10},{10,12},{12... | collective-permute-start | bytes 786440 | tf_op jit(solution)/shard_map/ppermute | solution.py:392
  132.2 13.1 %all-to-all-start.3 = ((bf16[16,64,256]{2,1,0:T(8,128)(2,1)}), bf16[16,64,256]{2,1,0:T(8,128)(2,1)S(1)}, u32[]{:S(2)}, u32[]{:S(2)}) async-start(bf16[16,64,256]{2,1,0:T(8,128)(2,1)} %bitcast.44), calls=%async_computation.3 | async-start | bytes 1048576 | tf_op jit(solution)/shard_map/all_to_all | solution.py:396
  136.7 4.5 %collective-permute-start.24 = (bf16[80,256]{1,0:T(8,128)(2,1)S(1)}, bf16[80,256]{1,0:T(8,128)(2,1)S(1)}, u32[]{:S(2)}, u32[]{:S(2)}) collective-permute-start(bf16[80,256]{1,0:T(8,128)(2,1)S(1)} %get-tuple-element.77), channel_id=1, source_target_pairs={{0,4},{2,6},{4,0},{6,2},{1,5},{3,7},{5,1},{7,3},{8,12},{10,14},{12... | collective-permute-start | bytes 122888 | tf_op jit(solution)/shard_map/ppermute | solution.py:392
  146.1 5.2 %collective-permute-start.26 = (f32[64,256]{1,0:T(8,128)S(1)}, f32[64,256]{1,0:T(8,128)S(1)}, u32[]{:S(2)}, u32[]{:S(2)}) collective-permute-start(f32[64,256]{1,0:T(8,128)S(1)} %get-tuple-element.80), channel_id=1, source_target_pairs={{0,1},{1,0},{2,3},{3,2},{4,5},{5,4},{6,7},{7,6},{8,9},{9,8},{10,11... | collective-permute-start | bytes 196616 | tf_op jit(solution)/shard_map/ppermute | solution.py:388
  (22 other events, 188.4 us)

commit v5 on v4

--- a/solution.py
+++ b/solution.py
@@ -54,10 +54,35 @@
     return pl.CostEstimate(flops=flops, bytes_accessed=int(mib * MIB), transcendentals=transcendentals)
 
 
+def stage_body(*refs):
+    sources, out_ref, sem = refs[:-2], refs[-2], refs[-1]
+    copies = [
+        pltpu.make_async_copy(source, out_ref.at[:, pl.ds(i * HD, HD)], sem.at[i]) for i, source in enumerate(sources)
+    ]
+    for copy in copies:
+        copy.start()
+    for copy in copies:
+        copy.wait()
+
+
+def staged(weights):
+    count, hidden = len(weights), weights[0].shape[0]
+    out = pl.pallas_call(
+        stage_body,
+        in_specs=[ANYWHERE] * count,
+        out_specs=ANYWHERE,
+        out_shape=pltpu.HBM((hidden, count * HD), BF16),
+        scratch_shapes=[pltpu.SemaphoreType.DMA((count,))],
+        compiler_params=limits(4),
+        cost_estimate=cost(0, 8),
+        name="stage",
+    )(*[in_hbm(w) for w in weights])
+    return in_hbm(out)
+
+
 def project_body(pieces, z_ref, gain_ref, *refs):
     xs = refs[: len(pieces)]
-    ws, (own_ref, sib_ref, scale_ref, normed_ref) = refs[len(pieces) : len(pieces) + 4], refs[len(pieces) + 4 : len(pieces) + 8]
-    held, rows_low, weights, x_sem, w_sem, out_sem = refs[len(pieces) + 8 :]
+    w_ref, own_ref, sib_ref, scale_ref, normed_ref, held, rows_low, weights, x_sem, w_sem, out_sem = refs[len(pieces) :]
     blocks, segs, part, width = held.shape
     rows = segs * part
     z = z_ref[0]
@@ -68,8 +93,8 @@
             source = x.at[:, side] if depth is None else x.at[:, side, depth]
             target = held.at[place, pl.ds(first, source.shape[0])]
             copies.append(pltpu.make_async_copy(source, target, x_sem.at[len(copies)]))
-    loads = [pltpu.make_async_copy(w, weights.at[i], w_sem.at[i]) for i, w in enumerate(ws)]
-    for copy in copies + loads:
+    load = pltpu.make_async_copy(w_ref, weights, w_sem)
+    for copy in copies + [load]:
         copy.start()
     for copy in copies:
         copy.wait()
@@ -86,10 +111,10 @@
         rows_low[:, p * width : (p + 1) * width] = (wide * scale * gain_ref[p]).astype(BF16)
     out = pltpu.make_async_copy(rows_low, normed_ref, out_sem)
     out.start()
-    for i, load in enumerate(loads):
-        load.wait()
-        out_ref, at = (own_ref, sib_ref)[i // 2], (i % 2) * HD
-        out_ref[:, at : at + HD] = nn(rows_low[...], weights[i]).astype(BF16)
+    load.wait()
+    for i, out_ref in enumerate((own_ref, sib_ref)):
+        at = 2 * HD * i
+        out_ref[...] = nn(rows_low[...], weights[:, at : at + 2 * HD]).astype(BF16)
     out.wait()
 
 
@@ -99,7 +124,7 @@
     rows = segs * part
     return pl.pallas_call(
         functools.partial(project_body, pieces),
-        in_specs=[SMEM, VMEM] + [ANYWHERE] * (len(xs) + 4),
+        in_specs=[SMEM, VMEM] + [ANYWHERE] * (len(xs) + 1),
         out_specs=[VMEM, VMEM, VMEM, ANYWHERE],
         out_shape=[
             jax.ShapeDtypeStruct((rows, 2 * HD), BF16),
@@ -110,22 +135,39 @@
         scratch_shapes=[
             pltpu.VMEM((blocks, segs, part, width), BF16),
             pltpu.VMEM((rows, blocks * width), BF16),
-            pltpu.VMEM((4, blocks * width, HD), BF16),
+            pltpu.VMEM((blocks * width, 4 * HD), BF16),
             pltpu.SemaphoreType.DMA((2 * len(xs),)),
-            pltpu.SemaphoreType.DMA((4,)),
+            pltpu.SemaphoreType.DMA(()),
             pltpu.SemaphoreType.DMA(()),
         ],
-        compiler_params=limits(20),
-        cost_estimate=cost(2 * rows * blocks * width * 4 * HD, 5),
+        compiler_params=limits(24),
+        cost_estimate=cost(2 * rows * blocks * width * 4 * HD, 12),
         name=name,
-    )(z, gain.reshape(blocks, 1, width), *xs, *weights)
-
-
-def attend_body(tile, q_ref, dc_ref, near_a, near_b, far_a, far_b, ctx_ref, qg_ref, gnear_ref, gfar_ref, gkeys, gvalues):
+    )(z, gain.reshape(blocks, 1, width), *xs, weights)
+
+
+def pieces_of(dots):
+    high = dots.astype(BF16).astype(F32)
+    shape = (EXTRA, dots.shape[1])
+    row = lax.broadcasted_iota(jnp.int32, shape, 0)
+    low = jnp.broadcast_to(dots - high, shape)
+    return jnp.where(row == 0, jnp.broadcast_to(high, shape), jnp.where(row == 1, low, 0.0)).astype(BF16)
+
+
+def in_two_rows(pieces):
+    return above(pieces[:, :HD], pieces[:, HD:])
+
+
+def dots_of(rows):
+    return beside(rows[0:1] + rows[1:2], rows[EXTRA : EXTRA + 1] + rows[EXTRA + 1 : EXTRA + 2])
+
+
+def attend_body(tile, q_ref, dc_ref, near_a, near_b, far_a, far_b, ctx_ref, qg_ref, gnear_ref, gfar_ref, near_dots, gkeys, gvalues):
     kv = above(near_a[...], near_b[...], far_a[...], far_b[...])
     k, v = kv[:, :HD], kv[:, HD:]
     half = kv.shape[0] // 2
     scale = HD ** (-0.5)
+    row_products = jnp.zeros((8, kv.shape[0]), F32)
     for i in range(q_ref.shape[0] // tile):
         here = slice(i * tile, (i + 1) * tile)
         q, dc = q_ref[here], dc_ref[here]
@@ -136,7 +178,10 @@
         ctx_ref[here] = nn(low, v).astype(BF16)
         gattend = nt(dc, v)
         dots = jnp.sum(gattend * attend, axis=-1, keepdims=True)
-        gscores = (attend * (gattend - dots) * scale).astype(BF16)
+        gscores = attend * (gattend - dots)
+        both = gscores * scores + attend * gattend
+        row_products += jnp.sum(both.reshape(tile // 8, 8, kv.shape[0]), axis=0)
+        gscores = (gscores * scale).astype(BF16)
         qg_ref[here] = nn(gscores, k).astype(BF16)
         if i == 0:
             gkeys[...] = tn(gscores, q)
@@ -146,8 +191,11 @@
             gvalues[...] += tn(low, dc)
     gnear_ref[:, :HD] = gkeys[:half].astype(BF16)
     gnear_ref[:, HD:] = gvalues[:half].astype(BF16)
-    gfar_ref[:, :HD] = gkeys[half:].astype(BF16)
-    gfar_ref[:, HD:] = gvalues[half:].astype(BF16)
+    gfar_ref[:half, :HD] = gkeys[half:].astype(BF16)
+    gfar_ref[:half, HD:] = gvalues[half:].astype(BF16)
+    row_products = jnp.sum(row_products, axis=0, keepdims=True)
+    near_dots[...] = row_products[:, :half]
+    gfar_ref[half:] = pieces_of(row_products[:, half:])
 
 
 def attention(q, dc, near_a, near_b, far_a, far_b, tile=256):
@@ -155,55 +203,44 @@
     return pl.pallas_call(
         functools.partial(attend_body, tile),
         in_specs=[VMEM] * 6,
-        out_specs=[VMEM] * 4,
+        out_specs=[VMEM] * 5,
         out_shape=[jax.ShapeDtypeStruct((targets, HD), BF16)] * 2
-        + [jax.ShapeDtypeStruct((half, 2 * HD), BF16)] * 2,
+        + [
+            jax.ShapeDtypeStruct((half, 2 * HD), BF16),
+            jax.ShapeDtypeStruct((half + EXTRA, 2 * HD), BF16),
+            jax.ShapeDtypeStruct((1, half), F32),
+        ],
         scratch_shapes=[pltpu.VMEM((2 * half, HD), F32)] * 2,
-        compiler_params=limits(24),
+        compiler_params=limits(20),
         cost_estimate=cost(12 * targets * 2 * half * HD, 4, targets * 2 * half),
         name="attention",
     )(q, dc, near_a, near_b, far_a, far_b)
 
 
-def weight_loads(z, ws, held, sem, feature_half, order):
+def weight_loads(z, w_ref, held, sem, feature_half, order):
     loads = []
     for distance in order:
         for side in range(2):
             block = side * RING + lax.rem(z + distance, RING)
             at = pl.ds(pl.multiple_of(block * 2 * HD + feature_half * HD, HD), HD)
             i = len(loads)
-            loads.append([
-                pltpu.make_async_copy(w.at[at], held.at[i, :, pl.ds(j * HD, HD)], sem.at[i, j]) for j, w in enumerate(ws)
-            ])
-    for group in loads:
-        for load in group:
-            load.start()
+            loads.append(pltpu.make_async_copy(w_ref.at[at], held.at[i], sem.at[i]))
+    for load in loads:
+        load.start()
     return loads
 
 
 def feature_block(rows, loads, held, i):
-    for load in loads[i]:
-        load.wait()
+    loads[i].wait()
     return nt(rows, held[i]).astype(BF16)
 
 
-def back_b_body(z_ref, own_ref, sib_ref, own_a, own_b, sib_a, sib_b, ko, vo, ks, vs, out_ref, held, stage, w_sem, out_sem):
-    loads = weight_loads(z_ref[0], (ko, vo, ks, vs), held, w_sem, 1, range(RING))
-    own, sib = own_ref[...], sib_ref[...]
+def back_b_body(z_ref, own_ref, sib_ref, dots_ref, w_ref, out_ref, stage, held, w_sem, out_sem):
+    loads = weight_loads(z_ref[0], w_ref, held, w_sem, 1, range(RING))
+    half = own_ref.shape[0]
     segs = out_ref.shape[0]
-    part = own.shape[0] // segs // 2
-    wide = lambda value: value.astype(F32)
-    products = beside(
-        wide(own) * above(wide(own_a[...]), wide(own_b[...])),
-        wide(sib) * above(wide(sib_a[...]), wide(sib_b[...])),
-    )
-    high = products.astype(BF16)
-    low = (products - wide(high)).astype(BF16)
-    ones = jnp.ones((EXTRA, high.shape[1]), BF16)
-    dots = nt(ones, high) + nt(ones, low)
-    tail = RING * 2 * part
-    stage[:, :, tail:] = jnp.broadcast_to(pieces_of(dots), (segs, 2, EXTRA, HD))
-    rows = beside(own, sib)
+    part = half // segs // 2
+    rows = beside(own_ref[...], sib_ref[:half])
     outs = []
     for distance in range(RING):
         at = distance * 2 * part
@@ -211,47 +248,43 @@
             value = feature_block(rows, loads, held, distance * 2 + side).reshape(2, segs, part, HD)
             for k in range(2):
                 stage[:, side, at + k * part : at + (k + 1) * part] = value[k]
-        size = 2 * part if distance < RING - 1 else 2 * part + EXTRA
+        size = 2 * part
+        if distance == RING - 1:
+            extra = sib_ref[half:].astype(F32)
+            pieces = in_two_rows(pieces_of(dots_ref[...] + extra[0:1] + extra[1:2]))
+            stage[:, :, at + size :] = jnp.broadcast_to(pieces, (segs, 2, 2 * EXTRA, HD))
+            size += 2 * EXTRA
         outs.append(pltpu.make_async_copy(stage.at[:, :, pl.ds(at, size)], out_ref.at[:, :, pl.ds(at, size)], out_sem.at[distance]))
         outs[-1].start()
     for out in outs:
         out.wait()
 
 
-def pieces_of(dots):
-    high = dots.astype(BF16).astype(F32)
-    low = dots - high
-    row = lax.broadcasted_iota(jnp.int32, (EXTRA, HD), 0)
-    zero = jnp.zeros((EXTRA, HD), F32)
-    picked = jnp.where(row == 0, high[:, :HD], jnp.where(row == 1, high[:, HD:], zero))
-    picked = jnp.where(row == 2, low[:, :HD], jnp.where(row == 3, low[:, HD:], picked))
-    return picked.astype(BF16)
-
-
-def back_b(z, own, sib, kvs, weights, segs):
+def back_b(z, own, sib, dots, weights, segs):
     rows = own.shape[0]
+    shape = (segs, 2, RING * rows // segs + 2 * EXTRA, HD)
     return pl.pallas_call(
         back_b_body,
-        in_specs=[SMEM] + [VMEM] * 6 + [ANYWHERE] * 4,
+        in_specs=[SMEM] + [VMEM] * 3 + [ANYWHERE],
         out_specs=ANYWHERE,
-        out_shape=pltpu.HBM((segs, 2, RING * rows // segs + EXTRA, HD), BF16),
+        out_shape=pltpu.HBM(shape, BF16),
         scratch_shapes=[
+            pltpu.VMEM(shape, BF16),
             pltpu.VMEM((2 * RING, HD, 4 * HD), BF16),
-            pltpu.VMEM((segs, 2, RING * rows // segs + EXTRA, HD), BF16),
-            pltpu.SemaphoreType.DMA((2 * RING, 4)),
+            pltpu.SemaphoreType.DMA((2 * RING,)),
             pltpu.SemaphoreType.DMA((RING,)),
         ],
-        compiler_params=limits(20),
+        compiler_params=limits(16),
         cost_estimate=cost(2 * rows * 8 * HD * 4 * HD, 4),
         name="back_b",
-    )(z, own, sib, *kvs, *weights)
-
-
-def back_a_body(z_ref, own_ref, sib_ref, ko, vo, ks, vs, *refs):
+    )(z, own, sib, dots, weights)
+
+
+def back_a_body(z_ref, own_ref, sib_ref, w_ref, *refs):
     outs, (held, w_sem) = refs[:7], refs[7:]
     order = (2, 1, 3, 0)
-    loads = weight_loads(z_ref[0], (ko, vo, ks, vs), held, w_sem, 0, order)
-    rows = beside(own_ref[...], sib_ref[...])
+    loads = weight_loads(z_ref[0], w_ref, held, w_sem, 0, order)
+    rows = beside(own_ref[...], sib_ref[: own_ref.shape[0]])
     segs = outs[-1].shape[0]
     part = rows.shape[0] // segs // 2
     lands = {2: ((0, 0), (1, segs // 2)), 1: ((2, 0), (3, segs // 2)), 3: ((4, 0), (5, segs // 2)), 0: ((6, 0),)}
@@ -270,19 +303,19 @@
     full = jax.ShapeDtypeStruct((segs, 2, rows // segs, HD), BF16)
     return pl.pallas_call(
         back_a_body,
-        in_specs=[SMEM] + [VMEM] * 2 + [ANYWHERE] * 4,
+        in_specs=[SMEM] + [VMEM] * 2 + [ANYWHERE],
         out_specs=[VMEM] * 7,
         out_shape=[half] * 6 + [full],
-        scratch_shapes=[pltpu.VMEM((2 * RING, HD, 4 * HD), BF16), pltpu.SemaphoreType.DMA((2 * RING, 4))],
-        compiler_params=limits(20),
+        scratch_shapes=[pltpu.VMEM((2 * RING, HD, 4 * HD), BF16), pltpu.SemaphoreType.DMA((2 * RING,))],
+        compiler_params=limits(16),
         cost_estimate=cost(2 * rows * 8 * HD * 4 * HD, 4),
         name="back_a",
-    )(z, own, sib, *weights)
+    )(z, own, sib, weights)
 
 
 def weights_body(near_a, near_b, far_a, far_b, gnear_ref, gfar_ref, gk_ref, gv_ref):
     rows = above(near_a[...], near_b[...], far_a[...], far_b[...])
-    total = tn(rows, above(gnear_ref[...], gfar_ref[...]))
+    total = tn(rows, above(gnear_ref[...], gfar_ref[: gnear_ref.shape[0]]))
     gk_ref[...] = total[:, :HD]
     gv_ref[...] = total[:, HD:]
 
@@ -290,15 +323,16 @@
 def weight_grads(near_a, near_b, far_a, far_b, gnear, gfar, width=512):
     rows, hidden = near_a.shape
     block = pl.BlockSpec((rows, width), lambda i: (0, i))
-    whole = pl.BlockSpec((2 * rows, 2 * HD), lambda i: (0, 0))
+    near = pl.BlockSpec(gnear.shape, lambda i: (0, 0))
+    far = pl.BlockSpec(gfar.shape, lambda i: (0, 0))
     out = pl.BlockSpec((width, HD), lambda i: (i, 0))
     return pl.pallas_call(
         weights_body,
         grid=(hidden // width,),
-        in_specs=[block] * 4 + [whole, whole],
+        in_specs=[block] * 4 + [near, far],
         out_specs=[out, out],
         out_shape=[jax.ShapeDtypeStruct((hidden, HD), F32)] * 2,
-        compiler_params=limits(20),
+        compiler_params=limits(16),
         cost_estimate=cost(16 * rows * hidden * HD, 17),
         name="weight_grads",
     )(near_a, near_b, far_a, far_b, gnear, gfar)
@@ -310,17 +344,16 @@
     for i in range(1, arrived_ref.shape[0]):
         total += arrived_ref[i].astype(F32)
     kept_ref[...] = total[:half]
-    extra = total[RING * half :]
-    both = beside(extra[0:1] + extra[2:3], extra[1:2] + extra[3:4])
+    both = dots_of(total[RING * half :])
     dots_ref[...] = both
-    pieces = pieces_of(jnp.broadcast_to(both, (EXTRA, 2 * HD)))
+    pieces = in_two_rows(pieces_of(both))
     for i, ref in enumerate(send_refs):
         ref[:half] = total[(i + 1) * half : (i + 2) * half].astype(BF16)
         ref[half:] = pieces
 
 
 def merge_b(arrived, half):
-    send = jax.ShapeDtypeStruct((half + EXTRA, HD), BF16)
+    send = jax.ShapeDtypeStruct((half + 2 * EXTRA, HD), BF16)
     return pl.pallas_call(
         merge_b_body,
         in_specs=[VMEM],
@@ -343,8 +376,7 @@
     right, dots = kept_ref[...], dots_ref[...]
     for ref in (r1, r2, r3):
         right += ref[:half].astype(F32)
-        extra = ref[half:].astype(F32)
-        dots += beside(extra[0:1] + extra[2:3], extra[1:2] + extra[3:4])
+        dots += dots_of(ref[half:].astype(F32))
     lane = lax.broadcasted_iota(jnp.int32, (part, HD), 1)
     row = lax.broadcasted_iota(jnp.int32, (part, HD), 0)
     mine = lane == row + segment * part
@@ -427,8 +459,8 @@
     low_2, high_2 = shifted(low_3, 1), shifted(high_1, -1)
     deep = lambda value: value.reshape(segs // 2, 2, part, width)
 
-    key_own, value_own = after((key_weight[0], value_weight[0]), near_z)
-    weights = [in_hbm(w) for w in (key_own, value_own, swapped(key_own), swapped(value_own))]
+    key_own, value_own = after((key_weight[0], value_weight[0]), near_z, first_a)
+    weights = staged((key_own, value_own, swapped(key_own), swapped(value_own)))
 
     top = segs // 2
     pieces_a = [(0, 0, None), (3, 0, None), (3, top, None), (1, 0, None), (1, top, None), (2, 0, None), (2, top, None)]
@@ -440,11 +472,11 @@
     pieces_b = [(d, 0, d) for d in range(RING)]
     own_b, sib_b, scale_b, normed_b = project(pieces_b, [all_b] * RING, z_array, norm_gain, weights, segs, "project_b")
     far_b = swapped(sib_b)
-    context, query_grad, gnear, gfar = attention(queries[0], context_grad[0], own_a, own_b, far_a, far_b)
+    context, query_grad, gnear, gfar, near_dots = attention(queries[0], context_grad[0], own_a, own_b, far_a, far_b)
     gsib = swapped(gfar)
 
-    parts_b = back_b(z_array, gnear, gsib, (own_a, own_b, sib_a, sib_b), weights, segs)
-    arrived_b = over_plane(parts_b.reshape(plane, RING * half + EXTRA, HD))
+    parts_b = back_b(z_array, gnear, gsib, near_dots, weights, segs)
+    arrived_b = over_plane(parts_b.reshape(plane, RING * half + 2 * EXTRA, HD))
     z_later, = after((z_array,), parts_b)
     opp_low, opp_high, up_low, up_high, down_low, down_high, kept = back_a(z_later, gnear, gsib, weights, segs)
     normed_far = [swapped(v) for v in after((normed_a, normed_b), gsib)]

time: 153 us -> 396 us (2.59)
  Pallas kernels: 49.8 us -> 302 us
  waiting for transfers between devices: 42.8 us -> 31.2 us
    pallas_call x2 -> x3, Pallas kernels: 15.8 us -> 270 us  [the longest x1 255 us: staged(): pl.pallas_call(stage_body, in_specs=[ANYWHERE] * count, out_specs=ANYWHER...]
    ppermute x18, waiting for transfers between devices: 30 us -> 17.3 us  [shifted(): return lax.ppermute(value, 'z', [(i, (i + by) % RING) for i in range(RING)])]
    ppermute x18, starting transfers between devices: 16.7 us -> 21 us  [shifted(): return lax.ppermute(value, 'z', [(i, (i + by) % RING) for i in range(RING)])]
  transfers between devices with their start and end apart: 31 -> 31, of which waited for: 19 -> 16; matrix products, arithmetic and copies ran while one was open for 2% -> 1% of each run, Pallas kernels for 29% -> 73%
where the time goes in v5:
time: 396 us; the launch traced here: 395 us
  Pallas kernels  302 us (76%)
  starting transfers between devices  54.2 us (14%)
  waiting for transfers between devices  31.2 us (8%)
  local copies, waits for them, and re-layouts  4.62 us (1%)
    pallas_call x1, Pallas kernels, staged(): pl.pallas_call(stage_body, in_specs=[ANYWHERE] * count, out_specs=ANYWHER...  255 us
    all_to_all x4, starting transfers between devices, over_plane(): return lax.all_to_all(value, PLANE, 0, 0, tiled=True)  22.2 us
    ppermute x18, starting transfers between devices, shifted(): return lax.ppermute(value, 'z', [(i, (i + by) % RING) for i in range(RING)])  21 us
    ppermute x18, waiting for transfers between devices, shifted(): return lax.ppermute(value, 'z', [(i, (i + by) % RING) for i in range(RING)])  17.3 us
    pallas_call x2, Pallas kernels, project(): pl.pallas_call(functools.partial(project_body, pieces), in_specs=[SMEM, V...  14 us
    ppermute x9, starting transfers between devices, swapped(): return lax.ppermute(value, 'c', [(0, 1), (1, 0)])  11 us
    pallas_call x1, Pallas kernels, weight_grads(): pl.pallas_call(weights_body, grid=(hidden // width,), in_specs=[block] *...  10.8 us
    all_to_all x4, waiting for transfers between devices, over_plane(): return lax.all_to_all(value, PLANE, 0, 0, tiled=True)  9.36 us
  transfers between devices with their start and end apart: 31, of which 16 were waited for; matrix products, arithmetic and copies ran while one was open for 1% of the time, Pallas kernels for 73%

profile of v5, /device:TPU:1, one launch (start us, length us, event | category | flops | bytes accessed | tf_op | source)
XLA Modules:
  0.0 395.4 jit_solution(282159064731595355)
XLA Ops:
  4.6 6.8 %all-to-all-start = ((bf16[16,32,512]{2,1,0:T(8,128)(2,1)}), bf16[16,32,512]{2,1,0:T(8,128)(2,1)S(1)}, u32[]{:S(2)}, u32[]{:S(2)}) async-start(bf16[16,32,512]{2,1,0:T(8,128)(2,1)} %broadcast_in_dim.18), calls=%async_computation | async-start | bytes 1048576 | tf_op jit(solution)/shard_map/all_to_all | solution.py:428
  11.4 3.8 collective-permute-start.7
  16.3 3.5 collective-permute-done.8
  19.8 2.3 all-to-all-done
  25.5 4.8 %all-to-all-start.1 = ((bf16[16,4,32,512]{3,2,1,0:T(8,128)(2,1)}), bf16[16,4,32,512]{3,2,1,0:T(8,128)(2,1)S(1)}, u32[]{:S(2)}, u32[]{:S(2)}) async-start(bf16[16,4,32,512]{3,2,1,0:T(8,128)(2,1)} %broadcast_in_dim.19), calls=%async_computation.1 | async-start | bytes 4194304 | tf_op jit(solution)/shard_map/all_to_all | solution.py:428
  31.0 2.2 collective-permute-start.4
  34.6 4.2 %collective-permute-done.1 = bf16[8,32,512]{2,1,0:T(8,128)(2,1)S(1)} collective-permute-done((bf16[8,32,512]{2,1,0:T(8,128)(2,1)S(1)}, bf16[8,32,512]{2,1,0:T(8,128)(2,1)S(1)}, u32[]{:S(2)}, u32[]{:S(2)}) %collective-permute-start.1) | collective-permute-done | bytes 262176 | tf_op jit(solution)/shard_map/ppermute | solution.py:424
  41.6 255.2 %stage.1.refs_7_.refs_4_.w_ref = bf16[4096,1024]{1,0:T(8,128)(2,1)} custom-call(bf16[4096,256]{1,0:T(8,128)(2,1)} %bitcast.14.refs_0_, bf16[4096,256]{1,0:T(8,128)(2,1)} %bitcast.15.refs_1_, bf16[4096,256]{1,0:T(8,128)(2,1)} %collective-permute-done.10.refs_2_, bf16[4096,256]{1,0:T(8,128)(2,1)} %collective-permute-done.11.refs_3_), custom_call_target="tpu_custom_call" | custom-call | bytes 8388608 | tf_op jit(solution)/shard_map/stage/pallas_call | solution.py:70
  297.6 7.3 %project_a.1 = (bf16[256,512]{1,0:T(8,128)(2,1)S(1)}, bf16[256,512]{1,0:T(8,128)(2,1)S(1)}, f32[256,1]{1,0:T(8,128)S(1)}, bf16[256,4096]{1,0:T(8,128)(2,1)}) custom-call(s32[1]{0:T(128)} %bitcast.2.z_ref, f32[8,1,512]{2,1,0:T(1,128)S(1)} %bitcast.37, bf16[8,2,32,512]{3,2,1,0:T(8,128)(2,1)} %bitcast.43, bf16[4,2,32,512]{3,2,1,0:T(8,128)(2,1)} %bitcast.45, ...), custom_call_target="tpu_custom_call" | custom-call | flops 2147483648 | bytes 12582912 | tf_op jit(solution)/shard_map/project_a/pallas_call | solution.py:125
  305.5 6.8 %project_b.1 = (bf16[256,512]{1,0:T(8,128)(2,1)S(1)}, bf16[256,512]{1,0:T(8,128)(2,1)S(1)}, f32[256,1]{1,0:T(8,128)S(1)}, bf16[256,4096]{1,0:T(8,128)(2,1)}) custom-call(s32[1]{0:T(128)} %bitcast.2.z_ref, f32[8,1,512]{2,1,0:T(1,128)S(1)} %bitcast.38, bf16[8,2,4,32,512]{4,3,2,1,0:T(8,128)(2,1)S(1)} %bitcast.33, bf16[8,2,4,32,512]{4,3,2,1,0:T(8,128)(2,1)S(1)} %bitcast.34, ...), custom_call_target="tpu_custom_call" | custom-call | flops 2147483648 | bytes 12582912 | tf_op jit(solution)/shard_map/project_b/pallas_call | solution.py:125
  312.3 3.4 collective-permute-start.13
  317.3 6.3 %attention.1 = (bf16[1024,256]{1,0:T(8,128)(2,1)}, bf16[1024,256]{1,0:T(8,128)(2,1)}, bf16[512,512]{1,0:T(8,128)(2,1)S(1)}, bf16[528,512]{1,0:T(8,128)(2,1)S(1)}, f32[1,512]{1,0:T(1,128)S(1)}) custom-call(bf16[1024,256]{1,0:T(8,128)(2,1)S(1)} %bitcast.40, bf16[1024,256]{1,0:T(8,128)(2,1)S(1)} %bitcast.41, bf16[256,512]{1,0:T(8,128)(2,1)S(1)} %get-tuple-element.46.near_a, ...), custom_call_target="tpu_custom_call" | custom-call | flops 3221225472 | bytes 4194304 | tf_op jit(solution)/shard_map/attention/pallas_call | solution.py:203
  326.0 7.9 %back_b.1 = bf16[8,2,288,256]{3,2,1,0:T(8,128)(2,1)} custom-call(s32[1]{0:T(128)} %bitcast.2.z_ref, bf16[512,512]{1,0:T(8,128)(2,1)S(1)} %get-tuple-element.58.gnear_ref.own_ref, bf16[528,512]{1,0:T(8,128)(2,1)S(1)} %collective-permute-done.14.sib_ref, f32[1,512]{1,0:T(1,128)S(1)} %get-tuple-element.63.dots_ref, bf16[4096,1024]{1,0:T(8,128)(2,1)} %stage.1.refs_7_.refs_4_.w_ref), custom_call_target="tpu_custom_call" | custom-call | flops 2147483648 | bytes 4194304 | tf_op jit(solution)/shard_map/back_b/pallas_call | solution.py:266
  333.9 7.0 %all-to-all-start.2 = ((bf16[16,288,256]{2,1,0:T(8,128)(2,1)}), bf16[16,288,256]{2,1,0:T(8,128)(2,1)S(1)}, u32[]{:S(2)}, u32[]{:S(2)}) async-start(bf16[16,288,256]{2,1,0:T(8,128)(2,1)} %bitcast.42), calls=%async_computation.2 | async-start | bytes 4718592 | tf_op jit(solution)/shard_map/all_to_all | solution.py:428
  340.9 7.0 %back_a.1 = (bf16[4,2,64,256]{3,2,1,0:T(8,128)(2,1)S(1)}, bf16[4,2,64,256]{3,2,1,0:T(8,128)(2,1)S(1)}, bf16[4,2,64,256]{3,2,1,0:T(8,128)(2,1)S(1)}, bf16[4,2,64,...) custom-call(s32[1]{0:T(128)} %bitcast.2.z_ref, ...), custom_call_target="tpu_custom_call" | custom-call | flops 2147483648 | bytes 4194304 | tf_op jit(solution)/shard_map/back_a/pallas_call | solution.py:304
  348.0 2.7 collective-permute-start.19
  352.1 10.8 %weight_grads.1 = (f32[4096,256]{1,0:T(8,128)}, f32[4096,256]{1,0:T(8,128)}) custom-call(bf16[256,4096]{1,0:T(8,128)(2,1)} %get-tuple-element.56.near_a, bf16[256,4096]{1,0:T(8,128)(2,1)} %get-tuple-element.57.near_b, bf16[256,4096]{1,0:T(8,128)(2,1)} %collective-permute-done.15.far_a, bf16[256,4096]{1,0:T(8,128)(2,1)} %collective-permute-done.16.far_b, ...), custom_call_target="tpu_custom_call" | custom-call | flops 4294967296 | bytes 17825792 | tf_op jit(solution)/shard_map/weight_grads/pallas_call | solution.py:329
  364.9 4.2 %collective-permute-done.22 = bf16[4,2,64,256]{3,2,1,0:T(8,128)(2,1)S(1)} collective-permute-done((bf16[4,2,64,256]{3,2,1,0:T(8,128)(2,1)S(1)}, bf16[4,2,64,256]{3,2,1,0:T(8,128)(2,1)S(1)}, u32[]{:S(2)}, u32[]{:S(2)}) %collective-permute-start.22) | collective-permute-done | bytes 262176 | tf_op jit(solution)/shard_map/ppermute | solution.py:424
  369.1 2.7 collective-permute-done.20
  373.0 3.9 all-to-all-done.2.arrived_ref
  376.9 3.6 all-to-all-start.3
  380.9 2.8 collective-permute-start.24
  386.7 3.1 all-to-all-done.3.arrived_ref
  390.5 3.3 collective-permute-start.26
  (86 shorter events, 28.7 us)
Async XLA Ops:
  4.6 17.6 %all-to-all-start = ((bf16[16,32,512]{2,1,0:T(8,128)(2,1)}), bf16[16,32,512]{2,1,0:T(8,128)(2,1)S(1)}, u32[]{:S(2)}, u32[]{:S(2)}) async-start(bf16[16,32,512]{2,1,0:T(8,128)(2,1)} %broadcast_in_dim.18), calls=%async_computation | async-start | bytes 1048576 | tf_op jit(solution)/shard_map/all_to_all | solution.py:428
  11.4 4.9 %collective-permute-start.7 = (bf16[32,512]{1,0:T(8,128)(2,1)S(1)}, bf16[32,512]{1,0:T(8,128)(2,1)S(1)}, u32[]{:S(2)}, u32[]{:S(2)}) collective-permute-start(bf16[32,512]{1,0:T(8,128)(2,1)S(1)} %get-tuple-element.88), channel_id=1, source_target_pairs={{0,6},{2,0},{4,2},{6,4},{1,7},{3,1},{5,3},{7,5},{8,14},{10,8},{12,... | collective-permute-start | bytes 98312 | tf_op jit(solution)/shard_map/ppermute | solution.py:424
  15.3 4.6 %collective-permute-start.8 = (bf16[32,512]{1,0:T(8,128)(2,1)S(1)}, bf16[32,512]{1,0:T(8,128)(2,1)S(1)}, u32[]{:S(2)}, u32[]{:S(2)}) collective-permute-start(bf16[32,512]{1,0:T(8,128)(2,1)S(1)} %get-tuple-element.88), channel_id=1, source_target_pairs={{0,4},{2,6},{4,0},{6,2},{1,5},{3,7},{5,1},{7,3},{8,12},{10,14},{12... | collective-permute-start | bytes 98312 | tf_op jit(solution)/shard_map/ppermute | solution.py:424
  22.2 17.8 %collective-permute-start.10 = (bf16[4096,256]{1,0:T(8,128)(2,1)}, bf16[4096,256]{1,0:T(8,128)(2,1)}, u32[]{:S(2)}, u32[]{:S(2)}) collective-permute-start(bf16[4096,256]{1,0:T(8,128)(2,1)} %bitcast.14.refs_0_), channel_id=1, source_target_pairs={{0,1},{1,0},{2,3},{3,2},{4,5},{5,4},{6,7},{7,6},{8,9},{9,8},{10,11... | collective-permute-start | bytes 6291464 | tf_op jit(solution)/shard_map/ppermute | solution.py:420
  23.9 17.7 %collective-permute-start.11 = (bf16[4096,256]{1,0:T(8,128)(2,1)}, bf16[4096,256]{1,0:T(8,128)(2,1)}, u32[]{:S(2)}, u32[]{:S(2)}) collective-permute-start(bf16[4096,256]{1,0:T(8,128)(2,1)} %bitcast.15.refs_1_), channel_id=1, source_target_pairs={{0,1},{1,0},{2,3},{3,2},{4,5},{5,4},{6,7},{7,6},{8,9},{9,8},{10,11... | collective-permute-start | bytes 6291464 | tf_op jit(solution)/shard_map/ppermute | solution.py:420
  25.5 280.0 %all-to-all-start.1 = ((bf16[16,4,32,512]{3,2,1,0:T(8,128)(2,1)}), bf16[16,4,32,512]{3,2,1,0:T(8,128)(2,1)S(1)}, u32[]{:S(2)}, u32[]{:S(2)}) async-start(bf16[16,4,32,512]{3,2,1,0:T(8,128)(2,1)} %broadcast_in_dim.19), calls=%async_computation.1 | async-start | bytes 4194304 | tf_op jit(solution)/shard_map/all_to_all | solution.py:428
  30.4 8.4 %collective-permute-start.1 = (bf16[8,32,512]{2,1,0:T(8,128)(2,1)S(1)}, bf16[8,32,512]{2,1,0:T(8,128)(2,1)S(1)}, u32[]{:S(2)}, u32[]{:S(2)}) collective-permute-start(bf16[8,32,512]{2,1,0:T(8,128)(2,1)S(1)} %get-tuple-element.86), channel_id=1, source_target_pairs={{0,2},{2,4},{4,6},{6,0},{1,3},{3,5},{5,7},{7,1},{8,10},{10,12},{12... | collective-permute-start | bytes 786440 | tf_op jit(solution)/shard_map/ppermute | solution.py:424
  31.0 7.8 %collective-permute-start.4 = (bf16[8,32,512]{2,1,0:T(8,128)(2,1)S(1)}, bf16[8,32,512]{2,1,0:T(8,128)(2,1)S(1)}, u32[]{:S(2)}, u32[]{:S(2)}) collective-permute-start(bf16[8,32,512]{2,1,0:T(8,128)(2,1)S(1)} %get-tuple-element.85), channel_id=1, source_target_pairs={{0,6},{2,0},{4,2},{6,4},{1,7},{3,1},{5,3},{7,5},{8,14},{10,8},{12,... | collective-permute-start | bytes 786440 | tf_op jit(solution)/shard_map/ppermute | solution.py:424
  33.2 263.7 %collective-permute-start.3 = (bf16[8,32,512]{2,1,0:T(8,128)(2,1)S(1)}, bf16[8,32,512]{2,1,0:T(8,128)(2,1)S(1)}, u32[]{:S(2)}, u32[]{:S(2)}) collective-permute-start(bf16[8,32,512]{2,1,0:T(8,128)(2,1)S(1)} %get-tuple-element.86), channel_id=1, source_target_pairs={{0,6},{2,0},{4,2},{6,4},{1,7},{3,1},{5,3},{7,5},{8,14},{10,8},{12,... | collective-permute-start | bytes 786440 | tf_op jit(solution)/shard_map/ppermute | solution.py:424
  38.8 258.1 %collective-permute-start.2 = (bf16[8,32,512]{2,1,0:T(8,128)(2,1)S(1)}, bf16[8,32,512]{2,1,0:T(8,128)(2,1)}, u32[]{:S(2)}, u32[]{:S(2)}) collective-permute-start(bf16[8,32,512]{2,1,0:T(8,128)(2,1)S(1)} %get-tuple-element.85), channel_id=1, source_target_pairs={{0,2},{2,4},{4,6},{6,0},{1,3},{3,5},{5,7},{7,1},{8,10},{10,12},{12... | collective-permute-start | bytes 786440 | tf_op jit(solution)/shard_map/ppermute | solution.py:424
  38.8 258.1 %collective-permute-start.5 = (bf16[8,32,512]{2,1,0:T(8,128)(2,1)S(1)}, bf16[8,32,512]{2,1,0:T(8,128)(2,1)}, u32[]{:S(2)}, u32[]{:S(2)}) collective-permute-start(bf16[8,32,512]{2,1,0:T(8,128)(2,1)S(1)} %collective-permute-done.1), channel_id=1, source_target_pairs={{0,2},{2,4},{4,6},{6,0},{1,3},{3,5},{5,7},{7,1},{8,10},{10,12},{12... | collective-permute-start | bytes 786440 | tf_op jit(solution)/shard_map/ppermute | solution.py:424
  40.0 256.9 %collective-permute-start.6 = (bf16[8,32,512]{2,1,0:T(8,128)(2,1)S(1)}, bf16[8,32,512]{2,1,0:T(8,128)(2,1)}, u32[]{:S(2)}, u32[]{:S(2)}) collective-permute-start(bf16[8,32,512]{2,1,0:T(8,128)(2,1)S(1)} %collective-permute-done.4), channel_id=1, source_target_pairs={{0,6},{2,0},{4,2},{6,4},{1,7},{3,1},{5,3},{7,5},{8,14},{10,8},{12,... | collective-permute-start | bytes 786440 | tf_op jit(solution)/shard_map/ppermute | solution.py:424
  312.3 4.6 %collective-permute-start.13 = (bf16[256,512]{1,0:T(8,128)(2,1)S(1)}, bf16[256,512]{1,0:T(8,128)(2,1)S(1)}, u32[]{:S(2)}, u32[]{:S(2)}) collective-permute-start(bf16[256,512]{1,0:T(8,128)(2,1)S(1)} %get-tuple-element.50), channel_id=1, source_target_pairs={{0,1},{1,0},{2,3},{3,2},{4,5},{5,4},{6,7},{7,6},{8,9},{9,8},{10,11... | collective-permute-start | bytes 786440 | tf_op jit(solution)/shard_map/ppermute | solution.py:420
  325.5 25.6 %collective-permute-start.15 = (bf16[256,4096]{1,0:T(8,128)(2,1)}, bf16[256,4096]{1,0:T(8,128)(2,1)}, u32[]{:S(2)}, u32[]{:S(2)}) collective-permute-start(bf16[256,4096]{1,0:T(8,128)(2,1)} %get-tuple-element.56.near_a), channel_id=1, source_target_pairs={{0,1},{1,0},{2,3},{3,2},{4,5},{5,4},{6,7},{7,6},{8,9},{9,8},{10,11... | collective-permute-start | bytes 6291464 | tf_op jit(solution)/shard_map/ppermute | solution.py:420
  325.9 26.2 %collective-permute-start.16 = (bf16[256,4096]{1,0:T(8,128)(2,1)}, bf16[256,4096]{1,0:T(8,128)(2,1)}, u32[]{:S(2)}, u32[]{:S(2)}) collective-permute-start(bf16[256,4096]{1,0:T(8,128)(2,1)} %get-tuple-element.57.near_b), channel_id=1, source_target_pairs={{0,1},{1,0},{2,3},{3,2},{4,5},{5,4},{6,7},{7,6},{8,9},{9,8},{10,11... | collective-permute-start | bytes 6291464 | tf_op jit(solution)/shard_map/ppermute | solution.py:420
  333.9 43.0 %all-to-all-start.2 = ((bf16[16,288,256]{2,1,0:T(8,128)(2,1)}), bf16[16,288,256]{2,1,0:T(8,128)(2,1)S(1)}, u32[]{:S(2)}, u32[]{:S(2)}) async-start(bf16[16,288,256]{2,1,0:T(8,128)(2,1)} %bitcast.42), calls=%async_computation.2 | async-start | bytes 4718592 | tf_op jit(solution)/shard_map/all_to_all | solution.py:428
  347.9 15.1 %collective-permute-start.18 = (bf16[4,2,64,256]{3,2,1,0:T(8,128)(2,1)S(1)}, bf16[4,2,64,256]{3,2,1,0:T(8,128)(2,1)S(1)}, u32[]{:S(2)}, u32[]{:S(2)}) collective-permute-start(bf16[4,2,64,256]{3,2,1,0:T(8,128)(2,1)S(1)} %get-tuple-element.68), channel_id=1, source_target_pairs={{0,2},{2,4},{4,6},{6,0},{1,3},{3,5},{5,7},{7,1},{8,10},{10,12},{12... | collective-permute-start | bytes 786440 | tf_op jit(solution)/shard_map/ppermute | solution.py:424
  348.0 15.0 %collective-permute-start.19 = (bf16[4,2,64,256]{3,2,1,0:T(8,128)(2,1)S(1)}, bf16[4,2,64,256]{3,2,1,0:T(8,128)(2,1)S(1)}, u32[]{:S(2)}, u32[]{:S(2)}) collective-permute-start(bf16[4,2,64,256]{3,2,1,0:T(8,128)(2,1)S(1)} %get-tuple-element.69), channel_id=1, source_target_pairs={{0,6},{2,0},{4,2},{6,4},{1,7},{3,1},{5,3},{7,5},{8,14},{10,8},{12,... | collective-permute-start | bytes 786440 | tf_op jit(solution)/shard_map/ppermute | solution.py:424
  350.6 14.3 %collective-permute-start.17 = (bf16[4,2,64,256]{3,2,1,0:T(8,128)(2,1)S(1)}, bf16[4,2,64,256]{3,2,1,0:T(8,128)(2,1)S(1)}, u32[]{:S(2)}, u32[]{:S(2)}) collective-permute-start(bf16[4,2,64,256]{3,2,1,0:T(8,128)(2,1)S(1)} %get-tuple-element.66), channel_id=1, source_target_pairs={{0,6},{2,0},{4,2},{6,4},{1,7},{3,1},{5,3},{7,5},{8,14},{10,8},{12,... | collective-permute-start | bytes 786440 | tf_op jit(solution)/shard_map/ppermute | solution.py:424
  351.1 13.8 %collective-permute-start.21 = (bf16[4,2,64,256]{3,2,1,0:T(8,128)(2,1)S(1)}, bf16[4,2,64,256]{3,2,1,0:T(8,128)(2,1)S(1)}, u32[]{:S(2)}, u32[]{:S(2)}) collective-permute-start(bf16[4,2,64,256]{3,2,1,0:T(8,128)(2,1)S(1)} %get-tuple-element.71), channel_id=1, source_target_pairs={{0,2},{2,4},{4,6},{6,0},{1,3},{3,5},{5,7},{7,1},{8,10},{10,12},{12... | collective-permute-start | bytes 786440 | tf_op jit(solution)/shard_map/ppermute | solution.py:424
  363.0 6.1 %collective-permute-start.22 = (bf16[4,2,64,256]{3,2,1,0:T(8,128)(2,1)S(1)}, bf16[4,2,64,256]{3,2,1,0:T(8,128)(2,1)S(1)}, u32[]{:S(2)}, u32[]{:S(2)}) collective-permute-start(bf16[4,2,64,256]{3,2,1,0:T(8,128)(2,1)S(1)} %add_convert_fusion.1), channel_id=1, source_target_pairs={{0,6},{2,0},{4,2},{6,4},{1,7},{3,1},{5,3},{7,5},{8,14},{10,8},{12,... | collective-permute-start | bytes 786440 | tf_op jit(solution)/shard_map/ppermute | solution.py:424
  364.8 7.0 %collective-permute-start.20 = (bf16[4,2,64,256]{3,2,1,0:T(8,128)(2,1)S(1)}, bf16[4,2,64,256]{3,2,1,0:T(8,128)(2,1)S(1)}, u32[]{:S(2)}, u32[]{:S(2)}) collective-permute-start(bf16[4,2,64,256]{3,2,1,0:T(8,128)(2,1)S(1)} %add_convert_fusion.3), channel_id=1, source_target_pairs={{0,2},{2,4},{4,6},{6,0},{1,3},{3,5},{5,7},{7,1},{8,10},{10,12},{12... | collective-permute-start | bytes 786440 | tf_op jit(solution)/shard_map/ppermute | solution.py:424
  376.9 12.9 %all-to-all-start.3 = ((bf16[16,64,256]{2,1,0:T(8,128)(2,1)}), bf16[16,64,256]{2,1,0:T(8,128)(2,1)S(1)}, u32[]{:S(2)}, u32[]{:S(2)}) async-start(bf16[16,64,256]{2,1,0:T(8,128)(2,1)} %bitcast.44), calls=%async_computation.3 | async-start | bytes 1048576 | tf_op jit(solution)/shard_map/all_to_all | solution.py:428
  380.9 4.8 %collective-permute-start.24 = (bf16[96,256]{1,0:T(8,128)(2,1)S(1)}, bf16[96,256]{1,0:T(8,128)(2,1)S(1)}, u32[]{:S(2)}, u32[]{:S(2)}) collective-permute-start(bf16[96,256]{1,0:T(8,128)(2,1)S(1)} %get-tuple-element.79), channel_id=1, source_target_pairs={{0,4},{2,6},{4,0},{6,2},{1,5},{3,7},{5,1},{7,3},{8,12},{10,14},{12... | collective-permute-start | bytes 147464 | tf_op jit(solution)/shard_map/ppermute | solution.py:424
  (20 other events, 894.9 us)

commit v6 on v5

--- a/solution.py
+++ b/solution.py
@@ -55,34 +55,32 @@
 
 
 def stage_body(*refs):
-    sources, out_ref, sem = refs[:-2], refs[-2], refs[-1]
-    copies = [
-        pltpu.make_async_copy(source, out_ref.at[:, pl.ds(i * HD, HD)], sem.at[i]) for i, source in enumerate(sources)
-    ]
-    for copy in copies:
-        copy.start()
-    for copy in copies:
-        copy.wait()
+    sources, (first_ref, second_ref) = refs[:-2], refs[-2:]
+    for i, source in enumerate(sources):
+        first_ref[0, :, i * HD : (i + 1) * HD] = source[:HD]
+        second_ref[0, :, i * HD : (i + 1) * HD] = source[HD:]
 
 
 def staged(weights):
-    count, hidden = len(weights), weights[0].shape[0]
-    out = pl.pallas_call(
+    count, blocks = len(weights), weights[0].shape[0] // (2 * HD)
+    block = pl.BlockSpec((1, HD, count * HD), lambda i: (i, 0, 0))
+    out = pltpu.HBM((blocks, HD, count * HD), BF16)
+    return pl.pallas_call(
         stage_body,
-        in_specs=[ANYWHERE] * count,
-        out_specs=ANYWHERE,
-        out_shape=pltpu.HBM((hidden, count * HD), BF16),
-        scratch_shapes=[pltpu.SemaphoreType.DMA((count,))],
-        compiler_params=limits(4),
-        cost_estimate=cost(0, 8),
+        grid=(blocks,),
+        in_specs=[pl.BlockSpec((2 * HD, HD), lambda i: (i, 0))] * count,
+        out_specs=[block] * 2,
+        out_shape=[out] * 2,
+        compiler_params=limits(8),
+        cost_estimate=cost(0, 16),
         name="stage",
     )(*[in_hbm(w) for w in weights])
-    return in_hbm(out)
 
 
 def project_body(pieces, z_ref, gain_ref, *refs):
     xs = refs[: len(pieces)]
-    w_ref, own_ref, sib_ref, scale_ref, normed_ref, held, rows_low, weights, x_sem, w_sem, out_sem = refs[len(pieces) :]
+    w_refs, refs = refs[len(pieces) : len(pieces) + 2], refs[len(pieces) + 2 :]
+    own_ref, sib_ref, scale_ref, normed_ref, held, rows_low, weights, x_sem, w_sem, out_sem = refs
     blocks, segs, part, width = held.shape
     rows = segs * part
     z = z_ref[0]
@@ -93,8 +91,12 @@
             source = x.at[:, side] if depth is None else x.at[:, side, depth]
             target = held.at[place, pl.ds(first, source.shape[0])]
             copies.append(pltpu.make_async_copy(source, target, x_sem.at[len(copies)]))
-    load = pltpu.make_async_copy(w_ref, weights, w_sem)
-    for copy in copies + [load]:
+    loads = [
+        pltpu.make_async_copy(w.at[p], weights.at[pl.ds((2 * p + i) * HD, HD)], w_sem.at[2 * p + i])
+        for p in range(blocks)
+        for i, w in enumerate(w_refs)
+    ]
+    for copy in copies + loads:
         copy.start()
     for copy in copies:
         copy.wait()
@@ -111,7 +113,8 @@
         rows_low[:, p * width : (p + 1) * width] = (wide * scale * gain_ref[p]).astype(BF16)
     out = pltpu.make_async_copy(rows_low, normed_ref, out_sem)
     out.start()
-    load.wait()
+    for load in loads:
+        load.wait()
     for i, out_ref in enumerate((own_ref, sib_ref)):
         at = 2 * HD * i
         out_ref[...] = nn(rows_low[...], weights[:, at : at + 2 * HD]).astype(BF16)
@@ -124,7 +127,7 @@
     rows = segs * part
     return pl.pallas_call(
         functools.partial(project_body, pieces),
-        in_specs=[SMEM, VMEM] + [ANYWHERE] * (len(xs) + 1),
+        in_specs=[SMEM, VMEM] + [ANYWHERE] * (len(xs) + 2),
         out_specs=[VMEM, VMEM, VMEM, ANYWHERE],
         out_shape=[
             jax.ShapeDtypeStruct((rows, 2 * HD), BF16),
@@ -137,13 +140,13 @@
             pltpu.VMEM((rows, blocks * width), BF16),
             pltpu.VMEM((blocks * width, 4 * HD), BF16),
             pltpu.SemaphoreType.DMA((2 * len(xs),)),
-            pltpu.SemaphoreType.DMA(()),
+            pltpu.SemaphoreType.DMA((2 * blocks,)),
             pltpu.SemaphoreType.DMA(()),
         ],
         compiler_params=limits(24),
         cost_estimate=cost(2 * rows * blocks * width * 4 * HD, 12),
         name=name,
-    )(z, gain.reshape(blocks, 1, width), *xs, weights)
+    )(z, gain.reshape(blocks, 1, width), *xs, *[in_hbm(w) for w in weights])
 
 
 def pieces_of(dots):
@@ -217,26 +220,11 @@
     )(q, dc, near_a, near_b, far_a, far_b)
 
 
-def weight_loads(z, w_ref, held, sem, feature_half, order):
-    loads = []
-    for distance in order:
-        for side in range(2):
-            block = side * RING + lax.rem(z + distance, RING)
-            at = pl.ds(pl.multiple_of(block * 2 * HD + feature_half * HD, HD), HD)
-            i = len(loads)
-            loads.append(pltpu.make_async_copy(w_ref.at[at], held.at[i], sem.at[i]))
-    for load in loads:
-        load.start()
-    return loads
-
-
-def feature_block(rows, loads, held, i):
-    loads[i].wait()
-    return nt(rows, held[i]).astype(BF16)
-
-
-def back_b_body(z_ref, own_ref, sib_ref, dots_ref, w_ref, out_ref, stage, held, w_sem, out_sem):
-    loads = weight_loads(z_ref[0], w_ref, held, w_sem, 1, range(RING))
+def feature_block(z, rows, w_ref, distance, side):
+    return nt(rows, w_ref[side * RING + lax.rem(z + distance, RING)]).astype(BF16)
+
+
+def back_b_body(z_ref, own_ref, sib_ref, dots_ref, w_ref, out_ref, stage, out_sem):
     half = own_ref.shape[0]
     segs = out_ref.shape[0]
     part = half // segs // 2
@@ -245,7 +233,7 @@
     for distance in range(RING):
         at = distance * 2 * part
         for side in range(2):
-            value = feature_block(rows, loads, held, distance * 2 + side).reshape(2, segs, part, HD)
+            value = feature_block(z_ref[0], rows, w_ref, distance, side).reshape(2, segs, part, HD)
             for k in range(2):
                 stage[:, side, at + k * part : at + (k + 1) * part] = value[k]
         size = 2 * part
@@ -265,32 +253,27 @@
     shape = (segs, 2, RING * rows // segs + 2 * EXTRA, HD)
     return pl.pallas_call(
         back_b_body,
-        in_specs=[SMEM] + [VMEM] * 3 + [ANYWHERE],
+        in_specs=[SMEM] + [VMEM] * 4,
         out_specs=ANYWHERE,
         out_shape=pltpu.HBM(shape, BF16),
         scratch_shapes=[
             pltpu.VMEM(shape, BF16),
-            pltpu.VMEM((2 * RING, HD, 4 * HD), BF16),
-            pltpu.SemaphoreType.DMA((2 * RING,)),
             pltpu.SemaphoreType.DMA((RING,)),
         ],
         compiler_params=limits(16),
         cost_estimate=cost(2 * rows * 8 * HD * 4 * HD, 4),
         name="back_b",
-    )(z, own, sib, dots, weights)
-
-
-def back_a_body(z_ref, own_ref, sib_ref, w_ref, *refs):
-    outs, (held, w_sem) = refs[:7], refs[7:]
-    order = (2, 1, 3, 0)
-    loads = weight_loads(z_ref[0], w_ref, held, w_sem, 0, order)
+    )(z, own, sib, dots, in_vmem(weights))
+
+
+def back_a_body(z_ref, own_ref, sib_ref, w_ref, *outs):
     rows = beside(own_ref[...], sib_ref[: own_ref.shape[0]])
     segs = outs[-1].shape[0]
     part = rows.shape[0] // segs // 2
     lands = {2: ((0, 0), (1, segs // 2)), 1: ((2, 0), (3, segs // 2)), 3: ((4, 0), (5, segs // 2)), 0: ((6, 0),)}
-    for i, distance in enumerate(order):
+    for distance in (2, 1, 3, 0):
         for side in range(2):
-            value = feature_block(rows, loads, held, 2 * i + side).reshape(2, segs, part, HD)
+            value = feature_block(z_ref[0], rows, w_ref, distance, side).reshape(2, segs, part, HD)
             for index, first in lands[distance]:
                 for k in range(2):
                     count = outs[index].shape[0]
@@ -303,14 +286,13 @@
     full = jax.ShapeDtypeStruct((segs, 2, rows // segs, HD), BF16)
     return pl.pallas_call(
         back_a_body,
-        in_specs=[SMEM] + [VMEM] * 2 + [ANYWHERE],
+        in_specs=[SMEM] + [VMEM] * 3,
         out_specs=[VMEM] * 7,
         out_shape=[half] * 6 + [full],
-        scratch_shapes=[pltpu.VMEM((2 * RING, HD, 4 * HD), BF16), pltpu.SemaphoreType.DMA((2 * RING,))],
         compiler_params=limits(16),
         cost_estimate=cost(2 * rows * 8 * HD * 4 * HD, 4),
         name="back_a",
-    )(z, own, sib, weights)
+    )(z, own, sib, in_vmem(weights))
 
 
 def weights_body(near_a, near_b, far_a, far_b, gnear_ref, gfar_ref, gk_ref, gv_ref):
@@ -412,6 +394,10 @@
     )(place, gain.reshape(hidden // width, 1, width), block, scale_a, scale_b, arrived, kept, dots, *received)
 
 
+def in_vmem(value):
+    return pltpu.with_memory_space_constraint(value, pltpu.VMEM)
+
+
 def in_hbm(value):
     return pltpu.with_memory_space_constraint(value, pltpu.HBM)
 
@@ -475,11 +461,11 @@
     context, query_grad, gnear, gfar, near_dots = attention(queries[0], context_grad[0], own_a, own_b, far_a, far_b)
     gsib = swapped(gfar)
 
-    parts_b = back_b(z_array, gnear, gsib, near_dots, weights, segs)
+    parts_b = back_b(z_array, gnear, gsib, near_dots, weights[1], segs)
     arrived_b = over_plane(parts_b.reshape(plane, RING * half + 2 * EXTRA, HD))
     z_later, = after((z_array,), parts_b)
-    opp_low, opp_high, up_low, up_high, down_low, down_high, kept = back_a(z_later, gnear, gsib, weights, segs)
-    normed_far = [swapped(v) for v in after((normed_a, normed_b), gsib)]
+    opp_low, opp_high, up_low, up_high, down_low, down_high, kept = back_a(z_later, gnear, gsib, weights[0], segs)
+    normed_far = [swapped(v) for v in after((normed_a, normed_b), parts_b)]
     from_low, from_high = shifted(opp_low, 1), shifted(opp_high, -1)
     got_high, got_low = shifted(up_high, 1), shifted(down_low, -1)
     key_grad, value_grad = weight_grads(normed_a, normed_b, *normed_far, gnear, gfar)

time: 396 us -> 147 us (0.37)
  Pallas kernels: 302 us -> 47.2 us
    pallas_call x3, Pallas kernels: 270 us -> 14.7 us  [the longest x1 9.05 us: staged(): pl.pallas_call(stage_body, grid=(blocks,), in_specs=[pl.BlockSpec((2 * HD...]
  transfers between devices with their start and end apart: 31 -> 31, of which waited for: 16 -> 16; matrix products, arithmetic and copies ran while one was open for 1% -> 2% of each run, Pallas kernels for 73% -> 25%
where the time goes in v6:
time: 147 us; the launch traced here: 146 us
  starting transfers between devices  53.2 us (36%)
  Pallas kernels  47.2 us (32%)
  waiting for transfers between devices  35.1 us (24%)
  local copies, waits for them, and re-layouts  7.6 us (5%)
  other arithmetic  2 us (1%)
    ppermute x18, starting transfers between devices, shifted(): return lax.ppermute(value, 'z', [(i, (i + by) % RING) for i in range(RING)])  22.5 us
    all_to_all x4, starting transfers between devices, over_plane(): return lax.all_to_all(value, PLANE, 0, 0, tiled=True)  21.8 us
    ppermute x18, waiting for transfers between devices, shifted(): return lax.ppermute(value, 'z', [(i, (i + by) % RING) for i in range(RING)])  18.2 us
    pallas_call x2, Pallas kernels, project(): pl.pallas_call(functools.partial(project_body, pieces), in_specs=[SMEM, V...  14.4 us
    all_to_all x4, waiting for transfers between devices, over_plane(): return lax.all_to_all(value, PLANE, 0, 0, tiled=True)  11.9 us
    pallas_call x1, Pallas kernels, weight_grads(): pl.pallas_call(weights_body, grid=(hidden // width,), in_specs=[block] *...  10.8 us
    pallas_call x1, Pallas kernels, staged(): pl.pallas_call(stage_body, grid=(blocks,), in_specs=[pl.BlockSpec((2 * HD...  9.05 us
    ppermute x9, starting transfers between devices, swapped(): return lax.ppermute(value, 'c', [(0, 1), (1, 0)])  8.92 us
  transfers between devices with their start and end apart: 31, of which 16 were waited for; matrix products, arithmetic and copies ran while one was open for 2% of the time, Pallas kernels for 25%

profile of v6, /device:TPU:1, one launch (start us, length us, event | category | flops | bytes accessed | tf_op | source)
XLA Modules:
  0.0 146.1 jit_solution(18356278162845852596)
XLA Ops:
  4.6 6.8 %all-to-all-start = ((bf16[16,32,512]{2,1,0:T(8,128)(2,1)}), bf16[16,32,512]{2,1,0:T(8,128)(2,1)S(1)}, u32[]{:S(2)}, u32[]{:S(2)}) async-start(bf16[16,32,512]{2,1,0:T(8,128)(2,1)} %broadcast_in_dim.18), calls=%async_computation | async-start | bytes 1048576 | tf_op jit(solution)/shard_map/all_to_all | solution.py:414
  11.4 3.7 %collective-permute-start.8 = (bf16[32,512]{1,0:T(8,128)(2,1)S(1)}, bf16[32,512]{1,0:T(8,128)(2,1)S(1)}, u32[]{:S(2)}, u32[]{:S(2)}) collective-permute-start(bf16[32,512]{1,0:T(8,128)(2,1)S(1)} %get-tuple-element.92), channel_id=1, source_target_pairs={{0,4},{2,6},{4,0},{6,2},{1,5},{3,7},{5,1},{7,3},{8,12},{10,14},{12... | collective-permute-start | bytes 98312 | tf_op jit(solution)/shard_map/ppermute | solution.py:410
  19.8 2.3 %all-to-all-done = bf16[16,32,512]{2,1,0:T(8,128)(2,1)S(1)} async-done(((bf16[16,32,512]{2,1,0:T(8,128)(2,1)}), bf16[16,32,512]{2,1,0:T(8,128)(2,1)S(1)}, u32[]{:S(2)}, u32[]{:S(2)}) %all-to-all-start) | async-done | bytes 524320 | tf_op jit(solution)/shard_map/all_to_all | solution.py:414
  25.5 5.0 %all-to-all-start.1 = ((bf16[16,4,32,512]{3,2,1,0:T(8,128)(2,1)}), bf16[16,4,32,512]{3,2,1,0:T(8,128)(2,1)S(1)}, u32[]{:S(2)}, u32[]{:S(2)}) async-start(bf16[16,4,32,512]{3,2,1,0:T(8,128)(2,1)} %broadcast_in_dim.19), calls=%async_computation.1 | async-start | bytes 4194304 | tf_op jit(solution)/shard_map/all_to_all | solution.py:414
  30.6 2.5 %collective-permute-start.4 = (bf16[8,32,512]{2,1,0:T(8,128)(2,1)S(1)}, bf16[8,32,512]{2,1,0:T(8,128)(2,1)S(1)}, u32[]{:S(2)}, u32[]{:S(2)}) collective-permute-start(bf16[8,32,512]{2,1,0:T(8,128)(2,1)S(1)} %get-tuple-element.89), channel_id=1, source_target_pairs={{0,6},{2,0},{4,2},{6,4},{1,7},{3,1},{5,3},{7,5},{8,14},{10,8},{12,... | collective-permute-start | bytes 786440 | tf_op jit(solution)/shard_map/ppermute | solution.py:410
  33.1 5.2 %collective-permute-done.4 = bf16[8,32,512]{2,1,0:T(8,128)(2,1)S(1)} collective-permute-done((bf16[8,32,512]{2,1,0:T(8,128)(2,1)S(1)}, bf16[8,32,512]{2,1,0:T(8,128)(2,1)S(1)}, u32[]{:S(2)}, u32[]{:S(2)}) %collective-permute-start.4) | collective-permute-done | bytes 262176 | tf_op jit(solution)/shard_map/ppermute | solution.py:410
  38.3 3.4 %collective-permute-start.3 = (bf16[8,32,512]{2,1,0:T(8,128)(2,1)S(1)}, bf16[8,32,512]{2,1,0:T(8,128)(2,1)}, u32[]{:S(2)}, u32[]{:S(2)}) collective-permute-start(bf16[8,32,512]{2,1,0:T(8,128)(2,1)S(1)} %get-tuple-element.90), channel_id=1, source_target_pairs={{0,6},{2,0},{4,2},{6,4},{1,7},{3,1},{5,3},{7,5},{8,14},{10,8},{12,... | collective-permute-start | bytes 786440 | tf_op jit(solution)/shard_map/ppermute | solution.py:410
  43.2 9.1 %stage.1 = (bf16[8,256,1024]{2,1,0:T(8,128)(2,1)}, bf16[8,256,1024]{2,1,0:T(8,128)(2,1)}) custom-call(bf16[4096,256]{1,0:T(8,128)(2,1)} %bitcast.14.refs_0_, bf16[4096,256]{1,0:T(8,128)(2,1)} %bitcast.15.refs_1_, bf16[4096,256]{1,0:T(8,128)(2,1)} %collective-permute-done.10.refs_2_, bf16[4096,256]{1,0:T(8,128)(2,1)} %collective-permute-done.11.refs_3_), custom_call_target="tpu_custom_call" | custom-call | bytes 16777216 | tf_op jit(solution)/shard_map/stage/pallas_call | solution.py:68
  52.7 7.6 %project_a.1 = (bf16[256,512]{1,0:T(8,128)(2,1)S(1)}, bf16[256,512]{1,0:T(8,128)(2,1)S(1)}, f32[256,1]{1,0:T(8,128)S(1)}, bf16[256,4096]{1,0:T(8,128)(2,1)}) custom-call(s32[1]{0:T(128)} %bitcast.2.z_ref, f32[8,1,512]{2,1,0:T(1,128)S(1)} %bitcast.37, bf16[8,2,32,512]{3,2,1,0:T(8,128)(2,1)} %bitcast.42, bf16[4,2,32,512]{3,2,1,0:T(8,128)(2,1)} %bitcast.46, ...), custom_call_target="tpu_custom_call" | custom-call | flops 2147483648 | bytes 12582912 | tf_op jit(solution)/shard_map/project_a/pallas_call | solution.py:128
  63.9 6.8 %project_b.1 = (bf16[256,512]{1,0:T(8,128)(2,1)S(1)}, bf16[256,512]{1,0:T(8,128)(2,1)S(1)}, f32[256,1]{1,0:T(8,128)S(1)}, bf16[256,4096]{1,0:T(8,128)(2,1)}) custom-call(s32[1]{0:T(128)} %bitcast.2.z_ref, f32[8,1,512]{2,1,0:T(1,128)S(1)} %bitcast.38, bf16[8,2,4,32,512]{4,3,2,1,0:T(8,128)(2,1)S(1)} %bitcast.33, bf16[8,2,4,32,512]{4,3,2,1,0:T(8,128)(2,1)S(1)} %bitcast.34, ...), custom_call_target="tpu_custom_call" | custom-call | flops 2147483648 | bytes 12582912 | tf_op jit(solution)/shard_map/project_b/pallas_call | solution.py:128
  72.5 6.2 %attention.1 = (bf16[1024,256]{1,0:T(8,128)(2,1)}, bf16[1024,256]{1,0:T(8,128)(2,1)}, bf16[512,512]{1,0:T(8,128)(2,1)S(1)}, bf16[528,512]{1,0:T(8,128)(2,1)S(1)}, f32[1,512]{1,0:T(1,128)S(1)}) custom-call(bf16[1024,256]{1,0:T(8,128)(2,1)S(1)} %bitcast.40, bf16[1024,256]{1,0:T(8,128)(2,1)S(1)} %bitcast.41, bf16[256,512]{1,0:T(8,128)(2,1)S(1)} %get-tuple-element.50.near_a, ...), custom_call_target="tpu_custom_call" | custom-call | flops 3221225472 | bytes 4194304 | tf_op jit(solution)/shard_map/attention/pallas_call | solution.py:206
  80.6 3.3 %back_b.1 = bf16[8,2,288,256]{3,2,1,0:T(8,128)(2,1)} custom-call(s32[1]{0:T(128)} %bitcast.2.z_ref, bf16[512,512]{1,0:T(8,128)(2,1)S(1)} %get-tuple-element.59.own_ref.gnear_ref, bf16[528,512]{1,0:T(8,128)(2,1)S(1)} %collective-permute-done.14.sib_ref, f32[1,512]{1,0:T(1,128)S(1)} %get-tuple-element.61.dots_ref, bf16[8,256,1024]{2,1,0:T(8,128)(2,1)S(1)} %copy-done.1), custom_call_target="tpu_custom_call" | custom-call | flops 2147483648 | bytes 4194304 | tf_op jit(solution)/shard_map/back_b/pallas_call | solution.py:254
  84.6 6.3 %all-to-all-start.2 = ((bf16[16,288,256]{2,1,0:T(8,128)(2,1)}), bf16[16,288,256]{2,1,0:T(8,128)(2,1)S(1)}, u32[]{:S(2)}, u32[]{:S(2)}) async-start(bf16[16,288,256]{2,1,0:T(8,128)(2,1)} %bitcast.43), calls=%async_computation.2 | async-start | bytes 4718592 | tf_op jit(solution)/shard_map/all_to_all | solution.py:414
  95.2 2.4 %back_a.1 = (bf16[4,2,64,256]{3,2,1,0:T(8,128)(2,1)S(1)}, bf16[4,2,64,256]{3,2,1,0:T(8,128)(2,1)S(1)}, bf16[4,2,64,256]{3,2,1,0:T(8,128)(2,1)S(1)}, bf16[4,2,64,...) custom-call(s32[1]{0:T(128)} %bitcast.2.z_ref, ...), custom_call_target="tpu_custom_call" | custom-call | flops 2147483648 | bytes 4194304 | tf_op jit(solution)/shard_map/back_a/pallas_call | solution.py:287
  99.1 2.4 %collective-permute-start.19 = (bf16[4,2,64,256]{3,2,1,0:T(8,128)(2,1)S(1)}, bf16[4,2,64,256]{3,2,1,0:T(8,128)(2,1)S(1)}, u32[]{:S(2)}, u32[]{:S(2)}) collective-permute-start(bf16[4,2,64,256]{3,2,1,0:T(8,128)(2,1)S(1)} %get-tuple-element.73), channel_id=1, source_target_pairs={{0,6},{2,0},{4,2},{6,4},{1,7},{3,1},{5,3},{7,5},{8,14},{10,8},{12,... | collective-permute-start | bytes 786440 | tf_op jit(solution)/shard_map/ppermute | solution.py:410
  101.5 10.8 %weight_grads.1 = (f32[4096,256]{1,0:T(8,128)}, f32[4096,256]{1,0:T(8,128)}) custom-call(bf16[256,4096]{1,0:T(8,128)(2,1)} %get-tuple-element.62.near_a, bf16[256,4096]{1,0:T(8,128)(2,1)} %get-tuple-element.63.near_b, bf16[256,4096]{1,0:T(8,128)(2,1)} %collective-permute-done.15.far_a, bf16[256,4096]{1,0:T(8,128)(2,1)} %collective-permute-done.16.far_b, ...), custom_call_target="tpu_custom_call" | custom-call | flops 4294967296 | bytes 17825792 | tf_op jit(solution)/shard_map/weight_grads/pallas_call | solution.py:311
  112.5 2.7 %collective-permute-start.22 = (bf16[4,2,64,256]{3,2,1,0:T(8,128)(2,1)S(1)}, bf16[4,2,64,256]{3,2,1,0:T(8,128)(2,1)S(1)}, u32[]{:S(2)}, u32[]{:S(2)}) collective-permute-start(bf16[4,2,64,256]{3,2,1,0:T(8,128)(2,1)S(1)} %add_convert_fusion.1), channel_id=1, source_target_pairs={{0,6},{2,0},{4,2},{6,4},{1,7},{3,1},{5,3},{7,5},{8,14},{10,8},{12,... | collective-permute-start | bytes 786440 | tf_op jit(solution)/shard_map/ppermute | solution.py:410
  115.3 3.9 %collective-permute-done.22 = bf16[4,2,64,256]{3,2,1,0:T(8,128)(2,1)S(1)} collective-permute-done((bf16[4,2,64,256]{3,2,1,0:T(8,128)(2,1)S(1)}, bf16[4,2,64,256]{3,2,1,0:T(8,128)(2,1)S(1)}, u32[]{:S(2)}, u32[]{:S(2)}) %collective-permute-start.22) | collective-permute-done | bytes 262176 | tf_op jit(solution)/shard_map/ppermute | solution.py:410
  119.2 3.3 %collective-permute-done.20 = bf16[4,2,64,256]{3,2,1,0:T(8,128)(2,1)S(1)} collective-permute-done((bf16[4,2,64,256]{3,2,1,0:T(8,128)(2,1)S(1)}, bf16[4,2,64,256]{3,2,1,0:T(8,128)(2,1)S(1)}, u32[]{:S(2)}, u32[]{:S(2)}) %collective-permute-start.20) | collective-permute-done | bytes 262176 | tf_op jit(solution)/shard_map/ppermute | solution.py:410
  123.6 3.9 %all-to-all-done.2.arrived_ref = bf16[16,288,256]{2,1,0:T(8,128)(2,1)S(1)} async-done(((bf16[16,288,256]{2,1,0:T(8,128)(2,1)}), bf16[16,288,256]{2,1,0:T(8,128)(2,1)S(1)}, u32[]{:S(2)}, u32[]{:S(2)}) %all-to-all-start.2) | async-done | bytes 2359328 | tf_op jit(solution)/shard_map/all_to_all | solution.py:414
  127.5 3.7 %all-to-all-start.3 = ((bf16[16,64,256]{2,1,0:T(8,128)(2,1)}), bf16[16,64,256]{2,1,0:T(8,128)(2,1)S(1)}, u32[]{:S(2)}, u32[]{:S(2)}) async-start(bf16[16,64,256]{2,1,0:T(8,128)(2,1)} %bitcast.44), calls=%async_computation.3 | async-start | bytes 1048576 | tf_op jit(solution)/shard_map/all_to_all | solution.py:414
  131.5 2.4 %collective-permute-start.24 = (bf16[96,256]{1,0:T(8,128)(2,1)S(1)}, bf16[96,256]{1,0:T(8,128)(2,1)S(1)}, u32[]{:S(2)}, u32[]{:S(2)}) collective-permute-start(bf16[96,256]{1,0:T(8,128)(2,1)S(1)} %get-tuple-element.83), channel_id=1, source_target_pairs={{0,4},{2,6},{4,0},{6,2},{1,5},{3,7},{5,1},{7,3},{8,12},{10,14},{12... | collective-permute-start | bytes 147464 | tf_op jit(solution)/shard_map/ppermute | solution.py:410
  136.9 3.7 %all-to-all-done.3.arrived_ref = bf16[16,64,256]{2,1,0:T(8,128)(2,1)S(1)} async-done(((bf16[16,64,256]{2,1,0:T(8,128)(2,1)}), bf16[16,64,256]{2,1,0:T(8,128)(2,1)S(1)}, u32[]{:S(2)}, u32[]{:S(2)}) %all-to-all-start.3) | async-done | bytes 524320 | tf_op jit(solution)/shard_map/all_to_all | solution.py:414
  141.4 3.1 %collective-permute-start.26 = (f32[64,256]{1,0:T(8,128)S(1)}, f32[64,256]{1,0:T(8,128)S(1)}, u32[]{:S(2)}, u32[]{:S(2)}) collective-permute-start(f32[64,256]{1,0:T(8,128)S(1)} %get-tuple-element.86), channel_id=1, source_target_pairs={{0,1},{1,0},{2,3},{3,2},{4,5},{5,4},{6,7},{7,6},{8,9},{9,8},{10,11... | collective-permute-start | bytes 196616 | tf_op jit(solution)/shard_map/ppermute | solution.py:406
  (88 shorter events, 34.6 us)
Async XLA Ops:
  4.6 17.6 %all-to-all-start = ((bf16[16,32,512]{2,1,0:T(8,128)(2,1)}), bf16[16,32,512]{2,1,0:T(8,128)(2,1)S(1)}, u32[]{:S(2)}, u32[]{:S(2)}) async-start(bf16[16,32,512]{2,1,0:T(8,128)(2,1)} %broadcast_in_dim.18), calls=%async_computation | async-start | bytes 1048576 | tf_op jit(solution)/shard_map/all_to_all | solution.py:414
  11.4 5.1 %collective-permute-start.8 = (bf16[32,512]{1,0:T(8,128)(2,1)S(1)}, bf16[32,512]{1,0:T(8,128)(2,1)S(1)}, u32[]{:S(2)}, u32[]{:S(2)}) collective-permute-start(bf16[32,512]{1,0:T(8,128)(2,1)S(1)} %get-tuple-element.92), channel_id=1, source_target_pairs={{0,4},{2,6},{4,0},{6,2},{1,5},{3,7},{5,1},{7,3},{8,12},{10,14},{12... | collective-permute-start | bytes 98312 | tf_op jit(solution)/shard_map/ppermute | solution.py:410
  22.2 19.6 %collective-permute-start.10 = (bf16[4096,256]{1,0:T(8,128)(2,1)}, bf16[4096,256]{1,0:T(8,128)(2,1)}, u32[]{:S(2)}, u32[]{:S(2)}) collective-permute-start(bf16[4096,256]{1,0:T(8,128)(2,1)} %bitcast.14.refs_0_), channel_id=1, source_target_pairs={{0,1},{1,0},{2,3},{3,2},{4,5},{5,4},{6,7},{7,6},{8,9},{9,8},{10,11... | collective-permute-start | bytes 6291464 | tf_op jit(solution)/shard_map/ppermute | solution.py:406
  23.9 19.3 %collective-permute-start.11 = (bf16[4096,256]{1,0:T(8,128)(2,1)}, bf16[4096,256]{1,0:T(8,128)(2,1)}, u32[]{:S(2)}, u32[]{:S(2)}) collective-permute-start(bf16[4096,256]{1,0:T(8,128)(2,1)} %bitcast.15.refs_1_), channel_id=1, source_target_pairs={{0,1},{1,0},{2,3},{3,2},{4,5},{5,4},{6,7},{7,6},{8,9},{9,8},{10,11... | collective-permute-start | bytes 6291464 | tf_op jit(solution)/shard_map/ppermute | solution.py:406
  25.5 36.8 %all-to-all-start.1 = ((bf16[16,4,32,512]{3,2,1,0:T(8,128)(2,1)}), bf16[16,4,32,512]{3,2,1,0:T(8,128)(2,1)S(1)}, u32[]{:S(2)}, u32[]{:S(2)}) async-start(bf16[16,4,32,512]{3,2,1,0:T(8,128)(2,1)} %broadcast_in_dim.19), calls=%async_computation.1 | async-start | bytes 4194304 | tf_op jit(solution)/shard_map/all_to_all | solution.py:414
  30.6 7.7 %collective-permute-start.4 = (bf16[8,32,512]{2,1,0:T(8,128)(2,1)S(1)}, bf16[8,32,512]{2,1,0:T(8,128)(2,1)S(1)}, u32[]{:S(2)}, u32[]{:S(2)}) collective-permute-start(bf16[8,32,512]{2,1,0:T(8,128)(2,1)S(1)} %get-tuple-element.89), channel_id=1, source_target_pairs={{0,6},{2,0},{4,2},{6,4},{1,7},{3,1},{5,3},{7,5},{8,14},{10,8},{12,... | collective-permute-start | bytes 786440 | tf_op jit(solution)/shard_map/ppermute | solution.py:410
  33.1 8.6 %collective-permute-start.1 = (bf16[8,32,512]{2,1,0:T(8,128)(2,1)S(1)}, bf16[8,32,512]{2,1,0:T(8,128)(2,1)S(1)}, u32[]{:S(2)}, u32[]{:S(2)}) collective-permute-start(bf16[8,32,512]{2,1,0:T(8,128)(2,1)S(1)} %get-tuple-element.90), channel_id=1, source_target_pairs={{0,2},{2,4},{4,6},{6,0},{1,3},{3,5},{5,7},{7,1},{8,10},{10,12},{12... | collective-permute-start | bytes 786440 | tf_op jit(solution)/shard_map/ppermute | solution.py:410
  33.1 19.1 %collective-permute-start.2 = (bf16[8,32,512]{2,1,0:T(8,128)(2,1)S(1)}, bf16[8,32,512]{2,1,0:T(8,128)(2,1)}, u32[]{:S(2)}, u32[]{:S(2)}) collective-permute-start(bf16[8,32,512]{2,1,0:T(8,128)(2,1)S(1)} %get-tuple-element.89), channel_id=1, source_target_pairs={{0,2},{2,4},{4,6},{6,0},{1,3},{3,5},{5,7},{7,1},{8,10},{10,12},{12... | collective-permute-start | bytes 786440 | tf_op jit(solution)/shard_map/ppermute | solution.py:410
  38.3 14.0 %collective-permute-start.3 = (bf16[8,32,512]{2,1,0:T(8,128)(2,1)S(1)}, bf16[8,32,512]{2,1,0:T(8,128)(2,1)}, u32[]{:S(2)}, u32[]{:S(2)}) collective-permute-start(bf16[8,32,512]{2,1,0:T(8,128)(2,1)S(1)} %get-tuple-element.90), channel_id=1, source_target_pairs={{0,6},{2,0},{4,2},{6,4},{1,7},{3,1},{5,3},{7,5},{8,14},{10,8},{12,... | collective-permute-start | bytes 786440 | tf_op jit(solution)/shard_map/ppermute | solution.py:410
  41.7 10.6 %collective-permute-start.6 = (bf16[8,32,512]{2,1,0:T(8,128)(2,1)S(1)}, bf16[8,32,512]{2,1,0:T(8,128)(2,1)}, u32[]{:S(2)}, u32[]{:S(2)}) collective-permute-start(bf16[8,32,512]{2,1,0:T(8,128)(2,1)S(1)} %collective-permute-done.4), channel_id=1, source_target_pairs={{0,6},{2,0},{4,2},{6,4},{1,7},{3,1},{5,3},{7,5},{8,14},{10,8},{12,... | collective-permute-start | bytes 786440 | tf_op jit(solution)/shard_map/ppermute | solution.py:410
  41.8 10.9 %collective-permute-start.5 = (bf16[8,32,512]{2,1,0:T(8,128)(2,1)S(1)}, bf16[8,32,512]{2,1,0:T(8,128)(2,1)}, u32[]{:S(2)}, u32[]{:S(2)}) collective-permute-start(bf16[8,32,512]{2,1,0:T(8,128)(2,1)S(1)} %collective-permute-done.1), channel_id=1, source_target_pairs={{0,2},{2,4},{4,6},{6,0},{1,3},{3,5},{5,7},{7,1},{8,10},{10,12},{12... | collective-permute-start | bytes 786440 | tf_op jit(solution)/shard_map/ppermute | solution.py:410
  62.3 8.7 %collective-permute-start.12 = (bf16[256,512]{1,0:T(8,128)(2,1)S(1)}, bf16[256,512]{1,0:T(8,128)(2,1)S(1)}, u32[]{:S(2)}, u32[]{:S(2)}) collective-permute-start(bf16[256,512]{1,0:T(8,128)(2,1)S(1)} %get-tuple-element.53), channel_id=1, source_target_pairs={{0,1},{1,0},{2,3},{3,2},{4,5},{5,4},{6,7},{7,6},{8,9},{9,8},{10,11... | collective-permute-start | bytes 786440 | tf_op jit(solution)/shard_map/ppermute | solution.py:406
  84.0 17.5 %collective-permute-start.15 = (bf16[256,4096]{1,0:T(8,128)(2,1)}, bf16[256,4096]{1,0:T(8,128)(2,1)}, u32[]{:S(2)}, u32[]{:S(2)}) collective-permute-start(bf16[256,4096]{1,0:T(8,128)(2,1)} %get-tuple-element.62.near_a), channel_id=1, source_target_pairs={{0,1},{1,0},{2,3},{3,2},{4,5},{5,4},{6,7},{7,6},{8,9},{9,8},{10,11... | collective-permute-start | bytes 6291464 | tf_op jit(solution)/shard_map/ppermute | solution.py:406
  84.2 17.3 %collective-permute-start.16 = (bf16[256,4096]{1,0:T(8,128)(2,1)}, bf16[256,4096]{1,0:T(8,128)(2,1)}, u32[]{:S(2)}, u32[]{:S(2)}) collective-permute-start(bf16[256,4096]{1,0:T(8,128)(2,1)} %get-tuple-element.63.near_b), channel_id=1, source_target_pairs={{0,1},{1,0},{2,3},{3,2},{4,5},{5,4},{6,7},{7,6},{8,9},{9,8},{10,11... | collective-permute-start | bytes 6291464 | tf_op jit(solution)/shard_map/ppermute | solution.py:406
  84.6 42.9 %all-to-all-start.2 = ((bf16[16,288,256]{2,1,0:T(8,128)(2,1)}), bf16[16,288,256]{2,1,0:T(8,128)(2,1)S(1)}, u32[]{:S(2)}, u32[]{:S(2)}) async-start(bf16[16,288,256]{2,1,0:T(8,128)(2,1)} %bitcast.43), calls=%async_computation.2 | async-start | bytes 4718592 | tf_op jit(solution)/shard_map/all_to_all | solution.py:414
  97.5 17.8 %collective-permute-start.17 = (bf16[4,2,64,256]{3,2,1,0:T(8,128)(2,1)S(1)}, bf16[4,2,64,256]{3,2,1,0:T(8,128)(2,1)S(1)}, u32[]{:S(2)}, u32[]{:S(2)}) collective-permute-start(bf16[4,2,64,256]{3,2,1,0:T(8,128)(2,1)S(1)} %get-tuple-element.70), channel_id=1, source_target_pairs={{0,6},{2,0},{4,2},{6,4},{1,7},{3,1},{5,3},{7,5},{8,14},{10,8},{12,... | collective-permute-start | bytes 786440 | tf_op jit(solution)/shard_map/ppermute | solution.py:410
  98.8 13.5 %collective-permute-start.18 = (bf16[4,2,64,256]{3,2,1,0:T(8,128)(2,1)S(1)}, bf16[4,2,64,256]{3,2,1,0:T(8,128)(2,1)S(1)}, u32[]{:S(2)}, u32[]{:S(2)}) collective-permute-start(bf16[4,2,64,256]{3,2,1,0:T(8,128)(2,1)S(1)} %get-tuple-element.72), channel_id=1, source_target_pairs={{0,2},{2,4},{4,6},{6,0},{1,3},{3,5},{5,7},{7,1},{8,10},{10,12},{12... | collective-permute-start | bytes 786440 | tf_op jit(solution)/shard_map/ppermute | solution.py:410
  99.1 13.3 %collective-permute-start.19 = (bf16[4,2,64,256]{3,2,1,0:T(8,128)(2,1)S(1)}, bf16[4,2,64,256]{3,2,1,0:T(8,128)(2,1)S(1)}, u32[]{:S(2)}, u32[]{:S(2)}) collective-permute-start(bf16[4,2,64,256]{3,2,1,0:T(8,128)(2,1)S(1)} %get-tuple-element.73), channel_id=1, source_target_pairs={{0,6},{2,0},{4,2},{6,4},{1,7},{3,1},{5,3},{7,5},{8,14},{10,8},{12,... | collective-permute-start | bytes 786440 | tf_op jit(solution)/shard_map/ppermute | solution.py:410
  101.5 13.8 %collective-permute-start.21 = (bf16[4,2,64,256]{3,2,1,0:T(8,128)(2,1)S(1)}, bf16[4,2,64,256]{3,2,1,0:T(8,128)(2,1)S(1)}, u32[]{:S(2)}, u32[]{:S(2)}) collective-permute-start(bf16[4,2,64,256]{3,2,1,0:T(8,128)(2,1)S(1)} %get-tuple-element.75), channel_id=1, source_target_pairs={{0,2},{2,4},{4,6},{6,0},{1,3},{3,5},{5,7},{7,1},{8,10},{10,12},{12... | collective-permute-start | bytes 786440 | tf_op jit(solution)/shard_map/ppermute | solution.py:410
  112.5 6.8 %collective-permute-start.22 = (bf16[4,2,64,256]{3,2,1,0:T(8,128)(2,1)S(1)}, bf16[4,2,64,256]{3,2,1,0:T(8,128)(2,1)S(1)}, u32[]{:S(2)}, u32[]{:S(2)}) collective-permute-start(bf16[4,2,64,256]{3,2,1,0:T(8,128)(2,1)S(1)} %add_convert_fusion.1), channel_id=1, source_target_pairs={{0,6},{2,0},{4,2},{6,4},{1,7},{3,1},{5,3},{7,5},{8,14},{10,8},{12,... | collective-permute-start | bytes 786440 | tf_op jit(solution)/shard_map/ppermute | solution.py:410
  115.2 7.2 %collective-permute-start.20 = (bf16[4,2,64,256]{3,2,1,0:T(8,128)(2,1)S(1)}, bf16[4,2,64,256]{3,2,1,0:T(8,128)(2,1)S(1)}, u32[]{:S(2)}, u32[]{:S(2)}) collective-permute-start(bf16[4,2,64,256]{3,2,1,0:T(8,128)(2,1)S(1)} %add_convert_fusion.3), channel_id=1, source_target_pairs={{0,2},{2,4},{4,6},{6,0},{1,3},{3,5},{5,7},{7,1},{8,10},{10,12},{12... | collective-permute-start | bytes 786440 | tf_op jit(solution)/shard_map/ppermute | solution.py:410
  127.5 13.1 %all-to-all-start.3 = ((bf16[16,64,256]{2,1,0:T(8,128)(2,1)}), bf16[16,64,256]{2,1,0:T(8,128)(2,1)S(1)}, u32[]{:S(2)}, u32[]{:S(2)}) async-start(bf16[16,64,256]{2,1,0:T(8,128)(2,1)} %bitcast.44), calls=%async_computation.3 | async-start | bytes 1048576 | tf_op jit(solution)/shard_map/all_to_all | solution.py:414
  131.5 4.7 %collective-permute-start.23 = (bf16[96,256]{1,0:T(8,128)(2,1)S(1)}, bf16[96,256]{1,0:T(8,128)(2,1)S(1)}, u32[]{:S(2)}, u32[]{:S(2)}) collective-permute-start(bf16[96,256]{1,0:T(8,128)(2,1)S(1)} %get-tuple-element.82), channel_id=1, source_target_pairs={{0,2},{2,4},{4,6},{6,0},{1,3},{3,5},{5,7},{7,1},{8,10},{10,12},{12... | collective-permute-start | bytes 147464 | tf_op jit(solution)/shard_map/ppermute | solution.py:410
  131.5 4.7 %collective-permute-start.24 = (bf16[96,256]{1,0:T(8,128)(2,1)S(1)}, bf16[96,256]{1,0:T(8,128)(2,1)S(1)}, u32[]{:S(2)}, u32[]{:S(2)}) collective-permute-start(bf16[96,256]{1,0:T(8,128)(2,1)S(1)} %get-tuple-element.83), channel_id=1, source_target_pairs={{0,4},{2,6},{4,0},{6,2},{1,5},{3,7},{5,1},{7,3},{8,12},{10,14},{12... | collective-permute-start | bytes 147464 | tf_op jit(solution)/shard_map/ppermute | solution.py:410
  (21 other events, 115.8 us)

commit v7 on v6

--- a/solution.py
+++ b/solution.py
@@ -91,11 +91,7 @@
             source = x.at[:, side] if depth is None else x.at[:, side, depth]
             target = held.at[place, pl.ds(first, source.shape[0])]
             copies.append(pltpu.make_async_copy(source, target, x_sem.at[len(copies)]))
-    loads = [
-        pltpu.make_async_copy(w.at[p], weights.at[pl.ds((2 * p + i) * HD, HD)], w_sem.at[2 * p + i])
-        for p in range(blocks)
-        for i, w in enumerate(w_refs)
-    ]
+    loads = [pltpu.make_async_copy(w, weights.at[i], w_sem.at[i]) for i, w in enumerate(w_refs)]
     for copy in copies + loads:
         copy.start()
     for copy in copies:
@@ -113,11 +109,13 @@
         rows_low[:, p * width : (p + 1) * width] = (wide * scale * gain_ref[p]).astype(BF16)
     out = pltpu.make_async_copy(rows_low, normed_ref, out_sem)
     out.start()
-    for load in loads:
+    total = 0.0
+    for i, load in enumerate(loads):
         load.wait()
-    for i, out_ref in enumerate((own_ref, sib_ref)):
-        at = 2 * HD * i
-        out_ref[...] = nn(rows_low[...], weights[:, at : at + 2 * HD]).astype(BF16)
+        columns = beside(*[rows_low[:, (2 * p + i) * HD : (2 * p + i + 1) * HD] for p in range(blocks)])
+        total += nn(columns, weights[i].reshape(blocks * HD, 4 * HD))
+    own_ref[...] = total[:, : 2 * HD].astype(BF16)
+    sib_ref[...] = total[:, 2 * HD :].astype(BF16)
     out.wait()
 
 
@@ -138,9 +136,9 @@
         scratch_shapes=[
             pltpu.VMEM((blocks, segs, part, width), BF16),
             pltpu.VMEM((rows, blocks * width), BF16),
-            pltpu.VMEM((blocks * width, 4 * HD), BF16),
+            pltpu.VMEM((2, blocks, HD, 4 * HD), BF16),
             pltpu.SemaphoreType.DMA((2 * len(xs),)),
-            pltpu.SemaphoreType.DMA((2 * blocks,)),
+            pltpu.SemaphoreType.DMA((2,)),
             pltpu.SemaphoreType.DMA(()),
         ],
         compiler_params=limits(24),
@@ -157,12 +155,15 @@
     return jnp.where(row == 0, jnp.broadcast_to(high, shape), jnp.where(row == 1, low, 0.0)).astype(BF16)
 
 
-def in_two_rows(pieces):
-    return above(pieces[:, :HD], pieces[:, HD:])
+def in_four_rows(dots):
+    left, right = pieces_of(dots[:, :HD]).astype(F32), pieces_of(dots[:, HD:]).astype(F32)
+    row = lax.broadcasted_iota(jnp.int32, left.shape, 0)
+    later = jnp.where(row == 2, right[0:1], jnp.where(row == 3, right[1:2], 0.0))
+    return jnp.where(row < 2, left, later).astype(BF16)
 
 
 def dots_of(rows):
-    return beside(rows[0:1] + rows[1:2], rows[EXTRA : EXTRA + 1] + rows[EXTRA + 1 : EXTRA + 2])
+    return beside(rows[0:1] + rows[1:2], rows[2:3] + rows[3:4])
 
 
 def attend_body(tile, q_ref, dc_ref, near_a, near_b, far_a, far_b, ctx_ref, qg_ref, gnear_ref, gfar_ref, near_dots, gkeys, gvalues):
@@ -239,9 +240,9 @@
         size = 2 * part
         if distance == RING - 1:
             extra = sib_ref[half:].astype(F32)
-            pieces = in_two_rows(pieces_of(dots_ref[...] + extra[0:1] + extra[1:2]))
-            stage[:, :, at + size :] = jnp.broadcast_to(pieces, (segs, 2, 2 * EXTRA, HD))
-            size += 2 * EXTRA
+            pieces = in_four_rows(dots_ref[...] + extra[0:1] + extra[1:2])
+            stage[:, :, at + size :] = jnp.broadcast_to(pieces, (segs, 2, EXTRA, HD))
+            size += EXTRA
         outs.append(pltpu.make_async_copy(stage.at[:, :, pl.ds(at, size)], out_ref.at[:, :, pl.ds(at, size)], out_sem.at[distance]))
         outs[-1].start()
     for out in outs:
@@ -250,7 +251,7 @@
 
 def back_b(z, own, sib, dots, weights, segs):
     rows = own.shape[0]
-    shape = (segs, 2, RING * rows // segs + 2 * EXTRA, HD)
+    shape = (segs, 2, RING * rows // segs + EXTRA, HD)
     return pl.pallas_call(
         back_b_body,
         in_specs=[SMEM] + [VMEM] * 4,
@@ -328,14 +329,14 @@
     kept_ref[...] = total[:half]
     both = dots_of(total[RING * half :])
     dots_ref[...] = both
-    pieces = in_two_rows(pieces_of(both))
+    pieces = in_four_rows(both)
     for i, ref in enumerate(send_refs):
         ref[:half] = total[(i + 1) * half : (i + 2) * half].astype(BF16)
         ref[half:] = pieces
 
 
 def merge_b(arrived, half):
-    send = jax.ShapeDtypeStruct((half + 2 * EXTRA, HD), BF16)
+    send = jax.ShapeDtypeStruct((half + EXTRA, HD), BF16)
     return pl.pallas_call(
         merge_b_body,
         in_specs=[VMEM],
@@ -462,7 +463,7 @@
     gsib = swapped(gfar)
 
     parts_b = back_b(z_array, gnear, gsib, near_dots, weights[1], segs)
-    arrived_b = over_plane(parts_b.reshape(plane, RING * half + 2 * EXTRA, HD))
+    arrived_b = over_plane(parts_b.reshape(plane, RING * half + EXTRA, HD))
     z_later, = after((z_array,), parts_b)
     opp_low, opp_high, up_low, up_high, down_low, down_high, kept = back_a(z_later, gnear, gsib, weights[0], segs)
     normed_far = [swapped(v) for v in after((normed_a, normed_b), parts_b)]

time: 147 us -> 145 us (0.986)
    unnamed x28 -> x24, local copies, waits for them, and re-layouts: 4.31 us -> 3.27 us
where the time goes in v7:
time: 145 us; the launch traced here: 144 us
  starting transfers between devices  54.6 us (38%)
  Pallas kernels  46.3 us (32%)
  waiting for transfers between devices  33.7 us (23%)
  local copies, waits for them, and re-layouts  6.54 us (5%)
  other arithmetic  1.98 us (1%)
    ppermute x18, starting transfers between devices, shifted(): return lax.ppermute(value, 'z', [(i, (i + by) % RING) for i in range(RING)])  23.6 us
    all_to_all x4, starting transfers between devices, over_plane(): return lax.all_to_all(value, PLANE, 0, 0, tiled=True)  21.1 us
    ppermute x18, waiting for transfers between devices, shifted(): return lax.ppermute(value, 'z', [(i, (i + by) % RING) for i in range(RING)])  18.1 us
    pallas_call x2, Pallas kernels, project(): pl.pallas_call(functools.partial(project_body, pieces), in_specs=[SMEM, V...  13.5 us
    pallas_call x1, Pallas kernels, weight_grads(): pl.pallas_call(weights_body, grid=(hidden // width,), in_specs=[block] *...  10.8 us
    all_to_all x4, waiting for transfers between devices, over_plane(): return lax.all_to_all(value, PLANE, 0, 0, tiled=True)  10.5 us
    ppermute x9, starting transfers between devices, swapped(): return lax.ppermute(value, 'c', [(0, 1), (1, 0)])  9.99 us
    pallas_call x1, Pallas kernels, staged(): pl.pallas_call(stage_body, grid=(blocks,), in_specs=[pl.BlockSpec((2 * HD...  9.05 us
  transfers between devices with their start and end apart: 31, of which 16 were waited for; matrix products, arithmetic and copies ran while one was open for 2% of the time, Pallas kernels for 25%

profile of v7, /device:TPU:1, one launch (start us, length us, event | category | flops | bytes accessed | tf_op | source)
XLA Modules:
  0.0 144.0 jit_solution(5709251514792953790)
XLA Ops:
  4.6 6.8 %all-to-all-start = ((bf16[16,32,512]{2,1,0:T(8,128)(2,1)}), bf16[16,32,512]{2,1,0:T(8,128)(2,1)S(1)}, u32[]{:S(2)}, u32[]{:S(2)}) async-start(bf16[16,32,512]{2,1,0:T(8,128)(2,1)} %broadcast_in_dim.18), calls=%async_computation | async-start | bytes 1048576 | tf_op jit(solution)/shard_map/all_to_all | solution.py:415
  11.4 3.7 %collective-permute-start.8 = (bf16[32,512]{1,0:T(8,128)(2,1)S(1)}, bf16[32,512]{1,0:T(8,128)(2,1)S(1)}, u32[]{:S(2)}, u32[]{:S(2)}) collective-permute-start(bf16[32,512]{1,0:T(8,128)(2,1)S(1)} %get-tuple-element.92), channel_id=1, source_target_pairs={{0,4},{2,6},{4,0},{6,2},{1,5},{3,7},{5,1},{7,3},{8,12},{10,14},{12... | collective-permute-start | bytes 98312 | tf_op jit(solution)/shard_map/ppermute | solution.py:411
  25.5 5.0 %all-to-all-start.1 = ((bf16[16,4,32,512]{3,2,1,0:T(8,128)(2,1)}), bf16[16,4,32,512]{3,2,1,0:T(8,128)(2,1)S(1)}, u32[]{:S(2)}, u32[]{:S(2)}) async-start(bf16[16,4,32,512]{3,2,1,0:T(8,128)(2,1)} %broadcast_in_dim.19), calls=%async_computation.1 | async-start | bytes 4194304 | tf_op jit(solution)/shard_map/all_to_all | solution.py:415
  30.6 2.5 %collective-permute-start.4 = (bf16[8,32,512]{2,1,0:T(8,128)(2,1)S(1)}, bf16[8,32,512]{2,1,0:T(8,128)(2,1)S(1)}, u32[]{:S(2)}, u32[]{:S(2)}) collective-permute-start(bf16[8,32,512]{2,1,0:T(8,128)(2,1)S(1)} %get-tuple-element.89), channel_id=1, source_target_pairs={{0,6},{2,0},{4,2},{6,4},{1,7},{3,1},{5,3},{7,5},{8,14},{10,8},{12,... | collective-permute-start | bytes 786440 | tf_op jit(solution)/shard_map/ppermute | solution.py:411
  33.1 5.2 %collective-permute-done.4 = bf16[8,32,512]{2,1,0:T(8,128)(2,1)S(1)} collective-permute-done((bf16[8,32,512]{2,1,0:T(8,128)(2,1)S(1)}, bf16[8,32,512]{2,1,0:T(8,128)(2,1)S(1)}, u32[]{:S(2)}, u32[]{:S(2)}) %collective-permute-start.4) | collective-permute-done | bytes 262176 | tf_op jit(solution)/shard_map/ppermute | solution.py:411
  38.3 3.4 %collective-permute-start.3 = (bf16[8,32,512]{2,1,0:T(8,128)(2,1)S(1)}, bf16[8,32,512]{2,1,0:T(8,128)(2,1)}, u32[]{:S(2)}, u32[]{:S(2)}) collective-permute-start(bf16[8,32,512]{2,1,0:T(8,128)(2,1)S(1)} %get-tuple-element.90), channel_id=1, source_target_pairs={{0,6},{2,0},{4,2},{6,4},{1,7},{3,1},{5,3},{7,5},{8,14},{10,8},{12,... | collective-permute-start | bytes 786440 | tf_op jit(solution)/shard_map/ppermute | solution.py:411
  43.2 9.1 %stage.1 = (bf16[8,256,1024]{2,1,0:T(8,128)(2,1)}, bf16[8,256,1024]{2,1,0:T(8,128)(2,1)}) custom-call(bf16[4096,256]{1,0:T(8,128)(2,1)} %bitcast.14.refs_0_, bf16[4096,256]{1,0:T(8,128)(2,1)} %bitcast.15.refs_1_, bf16[4096,256]{1,0:T(8,128)(2,1)} %collective-permute-done.10.refs_2_, bf16[4096,256]{1,0:T(8,128)(2,1)} %collective-permute-done.11.refs_3_), custom_call_target="tpu_custom_call" | custom-call | bytes 16777216 | tf_op jit(solution)/shard_map/stage/pallas_call | solution.py:68
  52.7 6.7 %project_a.1 = (bf16[256,512]{1,0:T(8,128)(2,1)S(1)}, bf16[256,512]{1,0:T(8,128)(2,1)S(1)}, f32[256,1]{1,0:T(8,128)S(1)}, bf16[256,4096]{1,0:T(8,128)(2,1)}) custom-call(s32[1]{0:T(128)} %bitcast.2.z_ref, f32[8,1,512]{2,1,0:T(1,128)S(1)} %bitcast.37, bf16[8,2,32,512]{3,2,1,0:T(8,128)(2,1)} %bitcast.42, bf16[4,2,32,512]{3,2,1,0:T(8,128)(2,1)} %bitcast.46, ...), custom_call_target="tpu_custom_call" | custom-call | flops 2147483648 | bytes 12582912 | tf_op jit(solution)/shard_map/project_a/pallas_call | solution.py:126
  59.5 2.9 %all-to-all-done.1 = bf16[16,4,32,512]{3,2,1,0:T(8,128)(2,1)S(1)} async-done(((bf16[16,4,32,512]{3,2,1,0:T(8,128)(2,1)}), bf16[16,4,32,512]{3,2,1,0:T(8,128)(2,1)S(1)}, u32[]{:S(2)}, u32[]{:S(2)}) %all-to-all-start.1) | async-done | bytes 2097184 | tf_op jit(solution)/shard_map/all_to_all | solution.py:415
  63.9 6.8 %project_b.1 = (bf16[256,512]{1,0:T(8,128)(2,1)S(1)}, bf16[256,512]{1,0:T(8,128)(2,1)S(1)}, f32[256,1]{1,0:T(8,128)S(1)}, bf16[256,4096]{1,0:T(8,128)(2,1)}) custom-call(s32[1]{0:T(128)} %bitcast.2.z_ref, f32[8,1,512]{2,1,0:T(1,128)S(1)} %bitcast.38, bf16[8,2,4,32,512]{4,3,2,1,0:T(8,128)(2,1)S(1)} %bitcast.33, bf16[8,2,4,32,512]{4,3,2,1,0:T(8,128)(2,1)S(1)} %bitcast.34, ...), custom_call_target="tpu_custom_call" | custom-call | flops 2147483648 | bytes 12582912 | tf_op jit(solution)/shard_map/project_b/pallas_call | solution.py:126
  72.3 6.2 %attention.1 = (bf16[1024,256]{1,0:T(8,128)(2,1)}, bf16[1024,256]{1,0:T(8,128)(2,1)}, bf16[512,512]{1,0:T(8,128)(2,1)S(1)}, bf16[528,512]{1,0:T(8,128)(2,1)S(1)}, f32[1,512]{1,0:T(1,128)S(1)}) custom-call(bf16[1024,256]{1,0:T(8,128)(2,1)S(1)} %bitcast.40, bf16[1024,256]{1,0:T(8,128)(2,1)S(1)} %bitcast.41, bf16[256,512]{1,0:T(8,128)(2,1)S(1)} %get-tuple-element.50.near_a, ...), custom_call_target="tpu_custom_call" | custom-call | flops 3221225472 | bytes 4194304 | tf_op jit(solution)/shard_map/attention/pallas_call | solution.py:207
  80.4 3.3 %back_b.1 = bf16[8,2,272,256]{3,2,1,0:T(8,128)(2,1)} custom-call(s32[1]{0:T(128)} %bitcast.2.z_ref, bf16[512,512]{1,0:T(8,128)(2,1)S(1)} %get-tuple-element.59.own_ref.gnear_ref, bf16[528,512]{1,0:T(8,128)(2,1)S(1)} %collective-permute-done.14.sib_ref, f32[1,512]{1,0:T(1,128)S(1)} %get-tuple-element.61.dots_ref, bf16[8,256,1024]{2,1,0:T(8,128)(2,1)S(1)} %copy-done.1), custom_call_target="tpu_custom_call" | custom-call | flops 2147483648 | bytes 4194304 | tf_op jit(solution)/shard_map/back_b/pallas_call | solution.py:255
  84.3 5.6 %all-to-all-start.2 = ((bf16[16,272,256]{2,1,0:T(8,128)(2,1)}), bf16[16,272,256]{2,1,0:T(8,128)(2,1)S(1)}, u32[]{:S(2)}, u32[]{:S(2)}) async-start(bf16[16,272,256]{2,1,0:T(8,128)(2,1)} %bitcast.43), calls=%async_computation.2 | async-start | bytes 4456448 | tf_op jit(solution)/shard_map/all_to_all | solution.py:415
  93.2 2.4 %back_a.1 = (bf16[4,2,64,256]{3,2,1,0:T(8,128)(2,1)S(1)}, bf16[4,2,64,256]{3,2,1,0:T(8,128)(2,1)S(1)}, bf16[4,2,64,256]{3,2,1,0:T(8,128)(2,1)S(1)}, bf16[4,2,64,...) custom-call(s32[1]{0:T(128)} %bitcast.2.z_ref, ...), custom_call_target="tpu_custom_call" | custom-call | flops 2147483648 | bytes 4194304 | tf_op jit(solution)/shard_map/back_a/pallas_call | solution.py:288
  97.1 2.7 %collective-permute-start.19 = (bf16[4,2,64,256]{3,2,1,0:T(8,128)(2,1)S(1)}, bf16[4,2,64,256]{3,2,1,0:T(8,128)(2,1)S(1)}, u32[]{:S(2)}, u32[]{:S(2)}) collective-permute-start(bf16[4,2,64,256]{3,2,1,0:T(8,128)(2,1)S(1)} %get-tuple-element.73), channel_id=1, source_target_pairs={{0,6},{2,0},{4,2},{6,4},{1,7},{3,1},{5,3},{7,5},{8,14},{10,8},{12,... | collective-permute-start | bytes 786440 | tf_op jit(solution)/shard_map/ppermute | solution.py:411
  99.8 10.8 %weight_grads.1 = (f32[4096,256]{1,0:T(8,128)}, f32[4096,256]{1,0:T(8,128)}) custom-call(bf16[256,4096]{1,0:T(8,128)(2,1)} %get-tuple-element.62.near_a, bf16[256,4096]{1,0:T(8,128)(2,1)} %get-tuple-element.63.near_b, bf16[256,4096]{1,0:T(8,128)(2,1)} %collective-permute-done.15.far_a, bf16[256,4096]{1,0:T(8,128)(2,1)} %collective-permute-done.16.far_b, ...), custom_call_target="tpu_custom_call" | custom-call | flops 4294967296 | bytes 17825792 | tf_op jit(solution)/shard_map/weight_grads/pallas_call | solution.py:312
  110.7 2.7 %collective-permute-start.22 = (bf16[4,2,64,256]{3,2,1,0:T(8,128)(2,1)S(1)}, bf16[4,2,64,256]{3,2,1,0:T(8,128)(2,1)S(1)}, u32[]{:S(2)}, u32[]{:S(2)}) collective-permute-start(bf16[4,2,64,256]{3,2,1,0:T(8,128)(2,1)S(1)} %add_convert_fusion.1), channel_id=1, source_target_pairs={{0,6},{2,0},{4,2},{6,4},{1,7},{3,1},{5,3},{7,5},{8,14},{10,8},{12,... | collective-permute-start | bytes 786440 | tf_op jit(solution)/shard_map/ppermute | solution.py:411
  113.6 4.1 %collective-permute-done.22 = bf16[4,2,64,256]{3,2,1,0:T(8,128)(2,1)S(1)} collective-permute-done((bf16[4,2,64,256]{3,2,1,0:T(8,128)(2,1)S(1)}, bf16[4,2,64,256]{3,2,1,0:T(8,128)(2,1)S(1)}, u32[]{:S(2)}, u32[]{:S(2)}) %collective-permute-start.22) | collective-permute-done | bytes 262176 | tf_op jit(solution)/shard_map/ppermute | solution.py:411
  117.7 3.3 %collective-permute-done.20 = bf16[4,2,64,256]{3,2,1,0:T(8,128)(2,1)S(1)} collective-permute-done((bf16[4,2,64,256]{3,2,1,0:T(8,128)(2,1)S(1)}, bf16[4,2,64,256]{3,2,1,0:T(8,128)(2,1)S(1)}, u32[]{:S(2)}, u32[]{:S(2)}) %collective-permute-start.20) | collective-permute-done | bytes 262176 | tf_op jit(solution)/shard_map/ppermute | solution.py:411
  122.0 2.6 %all-to-all-done.2.arrived_ref = bf16[16,272,256]{2,1,0:T(8,128)(2,1)S(1)} async-done(((bf16[16,272,256]{2,1,0:T(8,128)(2,1)}), bf16[16,272,256]{2,1,0:T(8,128)(2,1)S(1)}, u32[]{:S(2)}, u32[]{:S(2)}) %all-to-all-start.2) | async-done | bytes 2228256 | tf_op jit(solution)/shard_map/all_to_all | solution.py:415
  124.7 3.6 %all-to-all-start.3 = ((bf16[16,64,256]{2,1,0:T(8,128)(2,1)}), bf16[16,64,256]{2,1,0:T(8,128)(2,1)S(1)}, u32[]{:S(2)}, u32[]{:S(2)}) async-start(bf16[16,64,256]{2,1,0:T(8,128)(2,1)} %bitcast.44), calls=%async_computation.3 | async-start | bytes 1048576 | tf_op jit(solution)/shard_map/all_to_all | solution.py:415
  128.7 3.1 %collective-permute-start.24 = (bf16[80,256]{1,0:T(8,128)(2,1)S(1)}, bf16[80,256]{1,0:T(8,128)(2,1)S(1)}, u32[]{:S(2)}, u32[]{:S(2)}) collective-permute-start(bf16[80,256]{1,0:T(8,128)(2,1)S(1)} %get-tuple-element.83), channel_id=1, source_target_pairs={{0,4},{2,6},{4,0},{6,2},{1,5},{3,7},{5,1},{7,3},{8,12},{10,14},{12... | collective-permute-start | bytes 122888 | tf_op jit(solution)/shard_map/ppermute | solution.py:411
  134.6 2.7 %all-to-all-done.3.arrived_ref = bf16[16,64,256]{2,1,0:T(8,128)(2,1)S(1)} async-done(((bf16[16,64,256]{2,1,0:T(8,128)(2,1)}), bf16[16,64,256]{2,1,0:T(8,128)(2,1)S(1)}, u32[]{:S(2)}, u32[]{:S(2)}) %all-to-all-start.3) | async-done | bytes 524320 | tf_op jit(solution)/shard_map/all_to_all | solution.py:415
  138.0 4.4 %collective-permute-start.26 = (f32[64,256]{1,0:T(8,128)S(1)}, f32[64,256]{1,0:T(8,128)S(1)}, u32[]{:S(2)}, u32[]{:S(2)}) collective-permute-start(f32[64,256]{1,0:T(8,128)S(1)} %get-tuple-element.86), channel_id=1, source_target_pairs={{0,1},{1,0},{2,3},{3,2},{4,5},{5,4},{6,7},{7,6},{8,9},{9,8},{10,11... | collective-permute-start | bytes 196616 | tf_op jit(solution)/shard_map/ppermute | solution.py:407
  (84 shorter events, 33.6 us)
Async XLA Ops:
  4.6 17.6 %all-to-all-start = ((bf16[16,32,512]{2,1,0:T(8,128)(2,1)}), bf16[16,32,512]{2,1,0:T(8,128)(2,1)S(1)}, u32[]{:S(2)}, u32[]{:S(2)}) async-start(bf16[16,32,512]{2,1,0:T(8,128)(2,1)} %broadcast_in_dim.18), calls=%async_computation | async-start | bytes 1048576 | tf_op jit(solution)/shard_map/all_to_all | solution.py:415
  11.4 5.1 %collective-permute-start.8 = (bf16[32,512]{1,0:T(8,128)(2,1)S(1)}, bf16[32,512]{1,0:T(8,128)(2,1)S(1)}, u32[]{:S(2)}, u32[]{:S(2)}) collective-permute-start(bf16[32,512]{1,0:T(8,128)(2,1)S(1)} %get-tuple-element.92), channel_id=1, source_target_pairs={{0,4},{2,6},{4,0},{6,2},{1,5},{3,7},{5,1},{7,3},{8,12},{10,14},{12... | collective-permute-start | bytes 98312 | tf_op jit(solution)/shard_map/ppermute | solution.py:411
  22.2 19.6 %collective-permute-start.10 = (bf16[4096,256]{1,0:T(8,128)(2,1)}, bf16[4096,256]{1,0:T(8,128)(2,1)}, u32[]{:S(2)}, u32[]{:S(2)}) collective-permute-start(bf16[4096,256]{1,0:T(8,128)(2,1)} %bitcast.14.refs_0_), channel_id=1, source_target_pairs={{0,1},{1,0},{2,3},{3,2},{4,5},{5,4},{6,7},{7,6},{8,9},{9,8},{10,11... | collective-permute-start | bytes 6291464 | tf_op jit(solution)/shard_map/ppermute | solution.py:407
  23.9 19.3 %collective-permute-start.11 = (bf16[4096,256]{1,0:T(8,128)(2,1)}, bf16[4096,256]{1,0:T(8,128)(2,1)}, u32[]{:S(2)}, u32[]{:S(2)}) collective-permute-start(bf16[4096,256]{1,0:T(8,128)(2,1)} %bitcast.15.refs_1_), channel_id=1, source_target_pairs={{0,1},{1,0},{2,3},{3,2},{4,5},{5,4},{6,7},{7,6},{8,9},{9,8},{10,11... | collective-permute-start | bytes 6291464 | tf_op jit(solution)/shard_map/ppermute | solution.py:407
  25.5 36.8 %all-to-all-start.1 = ((bf16[16,4,32,512]{3,2,1,0:T(8,128)(2,1)}), bf16[16,4,32,512]{3,2,1,0:T(8,128)(2,1)S(1)}, u32[]{:S(2)}, u32[]{:S(2)}) async-start(bf16[16,4,32,512]{3,2,1,0:T(8,128)(2,1)} %broadcast_in_dim.19), calls=%async_computation.1 | async-start | bytes 4194304 | tf_op jit(solution)/shard_map/all_to_all | solution.py:415
  30.6 7.7 %collective-permute-start.4 = (bf16[8,32,512]{2,1,0:T(8,128)(2,1)S(1)}, bf16[8,32,512]{2,1,0:T(8,128)(2,1)S(1)}, u32[]{:S(2)}, u32[]{:S(2)}) collective-permute-start(bf16[8,32,512]{2,1,0:T(8,128)(2,1)S(1)} %get-tuple-element.89), channel_id=1, source_target_pairs={{0,6},{2,0},{4,2},{6,4},{1,7},{3,1},{5,3},{7,5},{8,14},{10,8},{12,... | collective-permute-start | bytes 786440 | tf_op jit(solution)/shard_map/ppermute | solution.py:411
  33.1 8.6 %collective-permute-start.1 = (bf16[8,32,512]{2,1,0:T(8,128)(2,1)S(1)}, bf16[8,32,512]{2,1,0:T(8,128)(2,1)S(1)}, u32[]{:S(2)}, u32[]{:S(2)}) collective-permute-start(bf16[8,32,512]{2,1,0:T(8,128)(2,1)S(1)} %get-tuple-element.90), channel_id=1, source_target_pairs={{0,2},{2,4},{4,6},{6,0},{1,3},{3,5},{5,7},{7,1},{8,10},{10,12},{12... | collective-permute-start | bytes 786440 | tf_op jit(solution)/shard_map/ppermute | solution.py:411
  33.1 19.1 %collective-permute-start.2 = (bf16[8,32,512]{2,1,0:T(8,128)(2,1)S(1)}, bf16[8,32,512]{2,1,0:T(8,128)(2,1)}, u32[]{:S(2)}, u32[]{:S(2)}) collective-permute-start(bf16[8,32,512]{2,1,0:T(8,128)(2,1)S(1)} %get-tuple-element.89), channel_id=1, source_target_pairs={{0,2},{2,4},{4,6},{6,0},{1,3},{3,5},{5,7},{7,1},{8,10},{10,12},{12... | collective-permute-start | bytes 786440 | tf_op jit(solution)/shard_map/ppermute | solution.py:411
  38.3 14.0 %collective-permute-start.3 = (bf16[8,32,512]{2,1,0:T(8,128)(2,1)S(1)}, bf16[8,32,512]{2,1,0:T(8,128)(2,1)}, u32[]{:S(2)}, u32[]{:S(2)}) collective-permute-start(bf16[8,32,512]{2,1,0:T(8,128)(2,1)S(1)} %get-tuple-element.90), channel_id=1, source_target_pairs={{0,6},{2,0},{4,2},{6,4},{1,7},{3,1},{5,3},{7,5},{8,14},{10,8},{12,... | collective-permute-start | bytes 786440 | tf_op jit(solution)/shard_map/ppermute | solution.py:411
  41.7 10.6 %collective-permute-start.6 = (bf16[8,32,512]{2,1,0:T(8,128)(2,1)S(1)}, bf16[8,32,512]{2,1,0:T(8,128)(2,1)}, u32[]{:S(2)}, u32[]{:S(2)}) collective-permute-start(bf16[8,32,512]{2,1,0:T(8,128)(2,1)S(1)} %collective-permute-done.4), channel_id=1, source_target_pairs={{0,6},{2,0},{4,2},{6,4},{1,7},{3,1},{5,3},{7,5},{8,14},{10,8},{12,... | collective-permute-start | bytes 786440 | tf_op jit(solution)/shard_map/ppermute | solution.py:411
  41.8 10.9 %collective-permute-start.5 = (bf16[8,32,512]{2,1,0:T(8,128)(2,1)S(1)}, bf16[8,32,512]{2,1,0:T(8,128)(2,1)}, u32[]{:S(2)}, u32[]{:S(2)}) collective-permute-start(bf16[8,32,512]{2,1,0:T(8,128)(2,1)S(1)} %collective-permute-done.1), channel_id=1, source_target_pairs={{0,2},{2,4},{4,6},{6,0},{1,3},{3,5},{5,7},{7,1},{8,10},{10,12},{12... | collective-permute-start | bytes 786440 | tf_op jit(solution)/shard_map/ppermute | solution.py:411
  62.3 8.5 %collective-permute-start.12 = (bf16[256,512]{1,0:T(8,128)(2,1)S(1)}, bf16[256,512]{1,0:T(8,128)(2,1)S(1)}, u32[]{:S(2)}, u32[]{:S(2)}) collective-permute-start(bf16[256,512]{1,0:T(8,128)(2,1)S(1)} %get-tuple-element.53), channel_id=1, source_target_pairs={{0,1},{1,0},{2,3},{3,2},{4,5},{5,4},{6,7},{7,6},{8,9},{9,8},{10,11... | collective-permute-start | bytes 786440 | tf_op jit(solution)/shard_map/ppermute | solution.py:407
  83.8 16.0 %collective-permute-start.15 = (bf16[256,4096]{1,0:T(8,128)(2,1)}, bf16[256,4096]{1,0:T(8,128)(2,1)}, u32[]{:S(2)}, u32[]{:S(2)}) collective-permute-start(bf16[256,4096]{1,0:T(8,128)(2,1)} %get-tuple-element.62.near_a), channel_id=1, source_target_pairs={{0,1},{1,0},{2,3},{3,2},{4,5},{5,4},{6,7},{7,6},{8,9},{9,8},{10,11... | collective-permute-start | bytes 6291464 | tf_op jit(solution)/shard_map/ppermute | solution.py:407
  84.0 15.8 %collective-permute-start.16 = (bf16[256,4096]{1,0:T(8,128)(2,1)}, bf16[256,4096]{1,0:T(8,128)(2,1)}, u32[]{:S(2)}, u32[]{:S(2)}) collective-permute-start(bf16[256,4096]{1,0:T(8,128)(2,1)} %get-tuple-element.63.near_b), channel_id=1, source_target_pairs={{0,1},{1,0},{2,3},{3,2},{4,5},{5,4},{6,7},{7,6},{8,9},{9,8},{10,11... | collective-permute-start | bytes 6291464 | tf_op jit(solution)/shard_map/ppermute | solution.py:407
  84.3 40.3 %all-to-all-start.2 = ((bf16[16,272,256]{2,1,0:T(8,128)(2,1)}), bf16[16,272,256]{2,1,0:T(8,128)(2,1)S(1)}, u32[]{:S(2)}, u32[]{:S(2)}) async-start(bf16[16,272,256]{2,1,0:T(8,128)(2,1)} %bitcast.43), calls=%async_computation.2 | async-start | bytes 4456448 | tf_op jit(solution)/shard_map/all_to_all | solution.py:415
  95.6 18.0 %collective-permute-start.17 = (bf16[4,2,64,256]{3,2,1,0:T(8,128)(2,1)S(1)}, bf16[4,2,64,256]{3,2,1,0:T(8,128)(2,1)S(1)}, u32[]{:S(2)}, u32[]{:S(2)}) collective-permute-start(bf16[4,2,64,256]{3,2,1,0:T(8,128)(2,1)S(1)} %get-tuple-element.70), channel_id=1, source_target_pairs={{0,6},{2,0},{4,2},{6,4},{1,7},{3,1},{5,3},{7,5},{8,14},{10,8},{12,... | collective-permute-start | bytes 786440 | tf_op jit(solution)/shard_map/ppermute | solution.py:411
  97.1 13.5 %collective-permute-start.18 = (bf16[4,2,64,256]{3,2,1,0:T(8,128)(2,1)S(1)}, bf16[4,2,64,256]{3,2,1,0:T(8,128)(2,1)S(1)}, u32[]{:S(2)}, u32[]{:S(2)}) collective-permute-start(bf16[4,2,64,256]{3,2,1,0:T(8,128)(2,1)S(1)} %get-tuple-element.72), channel_id=1, source_target_pairs={{0,2},{2,4},{4,6},{6,0},{1,3},{3,5},{5,7},{7,1},{8,10},{10,12},{12... | collective-permute-start | bytes 786440 | tf_op jit(solution)/shard_map/ppermute | solution.py:411
  97.1 13.5 %collective-permute-start.19 = (bf16[4,2,64,256]{3,2,1,0:T(8,128)(2,1)S(1)}, bf16[4,2,64,256]{3,2,1,0:T(8,128)(2,1)S(1)}, u32[]{:S(2)}, u32[]{:S(2)}) collective-permute-start(bf16[4,2,64,256]{3,2,1,0:T(8,128)(2,1)S(1)} %get-tuple-element.73), channel_id=1, source_target_pairs={{0,6},{2,0},{4,2},{6,4},{1,7},{3,1},{5,3},{7,5},{8,14},{10,8},{12,... | collective-permute-start | bytes 786440 | tf_op jit(solution)/shard_map/ppermute | solution.py:411
  99.8 13.8 %collective-permute-start.21 = (bf16[4,2,64,256]{3,2,1,0:T(8,128)(2,1)S(1)}, bf16[4,2,64,256]{3,2,1,0:T(8,128)(2,1)S(1)}, u32[]{:S(2)}, u32[]{:S(2)}) collective-permute-start(bf16[4,2,64,256]{3,2,1,0:T(8,128)(2,1)S(1)} %get-tuple-element.75), channel_id=1, source_target_pairs={{0,2},{2,4},{4,6},{6,0},{1,3},{3,5},{5,7},{7,1},{8,10},{10,12},{12... | collective-permute-start | bytes 786440 | tf_op jit(solution)/shard_map/ppermute | solution.py:411
  110.7 7.0 %collective-permute-start.22 = (bf16[4,2,64,256]{3,2,1,0:T(8,128)(2,1)S(1)}, bf16[4,2,64,256]{3,2,1,0:T(8,128)(2,1)S(1)}, u32[]{:S(2)}, u32[]{:S(2)}) collective-permute-start(bf16[4,2,64,256]{3,2,1,0:T(8,128)(2,1)S(1)} %add_convert_fusion.1), channel_id=1, source_target_pairs={{0,6},{2,0},{4,2},{6,4},{1,7},{3,1},{5,3},{7,5},{8,14},{10,8},{12,... | collective-permute-start | bytes 786440 | tf_op jit(solution)/shard_map/ppermute | solution.py:411
  113.5 7.5 %collective-permute-start.20 = (bf16[4,2,64,256]{3,2,1,0:T(8,128)(2,1)S(1)}, bf16[4,2,64,256]{3,2,1,0:T(8,128)(2,1)S(1)}, u32[]{:S(2)}, u32[]{:S(2)}) collective-permute-start(bf16[4,2,64,256]{3,2,1,0:T(8,128)(2,1)S(1)} %add_convert_fusion.3), channel_id=1, source_target_pairs={{0,2},{2,4},{4,6},{6,0},{1,3},{3,5},{5,7},{7,1},{8,10},{10,12},{12... | collective-permute-start | bytes 786440 | tf_op jit(solution)/shard_map/ppermute | solution.py:411
  124.7 12.6 %all-to-all-start.3 = ((bf16[16,64,256]{2,1,0:T(8,128)(2,1)}), bf16[16,64,256]{2,1,0:T(8,128)(2,1)S(1)}, u32[]{:S(2)}, u32[]{:S(2)}) async-start(bf16[16,64,256]{2,1,0:T(8,128)(2,1)} %bitcast.44), calls=%async_computation.3 | async-start | bytes 1048576 | tf_op jit(solution)/shard_map/all_to_all | solution.py:415
  128.7 4.9 %collective-permute-start.24 = (bf16[80,256]{1,0:T(8,128)(2,1)S(1)}, bf16[80,256]{1,0:T(8,128)(2,1)S(1)}, u32[]{:S(2)}, u32[]{:S(2)}) collective-permute-start(bf16[80,256]{1,0:T(8,128)(2,1)S(1)} %get-tuple-element.83), channel_id=1, source_target_pairs={{0,4},{2,6},{4,0},{6,2},{1,5},{3,7},{5,1},{7,3},{8,12},{10,14},{12... | collective-permute-start | bytes 122888 | tf_op jit(solution)/shard_map/ppermute | solution.py:411
  138.0 5.3 %collective-permute-start.26 = (f32[64,256]{1,0:T(8,128)S(1)}, f32[64,256]{1,0:T(8,128)S(1)}, u32[]{:S(2)}, u32[]{:S(2)}) collective-permute-start(f32[64,256]{1,0:T(8,128)S(1)} %get-tuple-element.86), channel_id=1, source_target_pairs={{0,1},{1,0},{2,3},{3,2},{4,5},{5,4},{6,7},{7,6},{8,9},{9,8},{10,11... | collective-permute-start | bytes 196616 | tf_op jit(solution)/shard_map/ppermute | solution.py:407
  (19 other events, 109.0 us)

commit v8 on v7

--- a/solution.py
+++ b/solution.py
@@ -296,29 +296,25 @@
     )(z, own, sib, in_vmem(weights))
 
 
-def weights_body(near_a, near_b, far_a, far_b, gnear_ref, gfar_ref, gk_ref, gv_ref):
+def weights_body(near_a, near_b, far_a, far_b, gnear_ref, gfar_ref, out_ref):
     rows = above(near_a[...], near_b[...], far_a[...], far_b[...])
-    total = tn(rows, above(gnear_ref[...], gfar_ref[: gnear_ref.shape[0]]))
-    gk_ref[...] = total[:, :HD]
-    gv_ref[...] = total[:, HD:]
-
-
-def weight_grads(near_a, near_b, far_a, far_b, gnear, gfar, width=512):
-    rows, hidden = near_a.shape
+    out_ref[...] = tn(rows, above(gnear_ref[...], gfar_ref[...]))
+
+
+def weight_grad(normed, gnear, gfar, which, width=1024):
+    rows, hidden = normed[0].shape
     block = pl.BlockSpec((rows, width), lambda i: (0, i))
-    near = pl.BlockSpec(gnear.shape, lambda i: (0, 0))
-    far = pl.BlockSpec(gfar.shape, lambda i: (0, 0))
-    out = pl.BlockSpec((width, HD), lambda i: (i, 0))
+    columns = pl.BlockSpec((2 * rows, HD), lambda i: (0, which))
     return pl.pallas_call(
         weights_body,
         grid=(hidden // width,),
-        in_specs=[block] * 4 + [near, far],
-        out_specs=[out, out],
-        out_shape=[jax.ShapeDtypeStruct((hidden, HD), F32)] * 2,
-        compiler_params=limits(16),
-        cost_estimate=cost(16 * rows * hidden * HD, 17),
-        name="weight_grads",
-    )(near_a, near_b, far_a, far_b, gnear, gfar)
+        in_specs=[block] * 4 + [columns, columns],
+        out_specs=pl.BlockSpec((width, HD), lambda i: (i, 0)),
+        out_shape=jax.ShapeDtypeStruct((hidden, HD), F32),
+        compiler_params=limits(24),
+        cost_estimate=cost(8 * rows * hidden * HD, 13),
+        name=("key_grad", "value_grad")[which],
+    )(*normed, gnear, gfar)
 
 
 def merge_b_body(arrived_ref, kept_ref, dots_ref, *send_refs):
@@ -446,7 +442,7 @@
     low_2, high_2 = shifted(low_3, 1), shifted(high_1, -1)
     deep = lambda value: value.reshape(segs // 2, 2, part, width)
 
-    key_own, value_own = after((key_weight[0], value_weight[0]), near_z, first_a)
+    key_own, value_own = after((key_weight[0], value_weight[0]), block)
     weights = staged((key_own, value_own, swapped(key_own), swapped(value_own)))
 
     top = segs // 2
@@ -456,9 +452,11 @@
     own_a, sib_a, scale_a, normed_a = project(pieces_a, xs_a, z_array, norm_gain, weights, segs, "project_a")
     far_a = swapped(sib_a)
     all_b, = after((all_b,), own_a)
+    normed_far_a = swapped(after((normed_a,), all_b, far_a)[0])
     pieces_b = [(d, 0, d) for d in range(RING)]
     own_b, sib_b, scale_b, normed_b = project(pieces_b, [all_b] * RING, z_array, norm_gain, weights, segs, "project_b")
     far_b = swapped(sib_b)
+    normed_far_b = swapped(after((normed_b,), far_b)[0])
     context, query_grad, gnear, gfar, near_dots = attention(queries[0], context_grad[0], own_a, own_b, far_a, far_b)
     gsib = swapped(gfar)
 
@@ -466,13 +464,15 @@
     arrived_b = over_plane(parts_b.reshape(plane, RING * half + EXTRA, HD))
     z_later, = after((z_array,), parts_b)
     opp_low, opp_high, up_low, up_high, down_low, down_high, kept = back_a(z_later, gnear, gsib, weights[0], segs)
-    normed_far = [swapped(v) for v in after((normed_a, normed_b), parts_b)]
     from_low, from_high = shifted(opp_low, 1), shifted(opp_high, -1)
     got_high, got_low = shifted(up_high, 1), shifted(down_low, -1)
-    key_grad, value_grad = weight_grads(normed_a, normed_b, *normed_far, gnear, gfar)
-    from_low, from_high = after((from_low, from_high), key_grad, value_grad)
+    all_normed = (normed_a, normed_b, normed_far_a, normed_far_b)
+    key_grad = weight_grad(all_normed, gnear, gfar, 0)
+    from_low, from_high = after((from_low, from_high), key_grad)
     last_low = shifted((wide(up_low) + wide(from_low)).astype(BF16), 1)
     last_high = shifted((wide(down_high) + wide(from_high)).astype(BF16), -1)
+    value_grad = weight_grad(all_normed, gnear, gfar, 1)
+    got_low, got_high = after((got_low, got_high), value_grad)
     summed_low = wide(kept[: segs // 2]) + wide(got_low) + wide(last_low)
     summed_high = wide(kept[segs // 2 :]) + wide(got_high) + wide(last_high)
     summed_a = above(summed_low, summed_high).astype(BF16).reshape(plane, half, HD)

time: 145 us -> 143 us (0.986)
  waiting for transfers between devices: 33.7 us -> 28 us
  Pallas kernels: 46.3 us -> 50 us
    ppermute x18, waiting for transfers between devices: 18.1 us -> 9.82 us  [shifted(): return lax.ppermute(value, 'z', [(i, (i + by) % RING) for i in range(RING)])]
    pallas_call x1 -> x2, Pallas kernels: 10.8 us -> 14.5 us  [weight_grad(): pl.pallas_call(weights_body, grid=(hidden // width,), in_specs=[block] *...]
    all_to_all x4, waiting for transfers between devices: 10.5 us -> 13.5 us  [over_plane(): return lax.all_to_all(value, PLANE, 0, 0, tiled=True)]
    ppermute x18, starting transfers between devices: 23.6 us -> 21.4 us  [shifted(): return lax.ppermute(value, 'z', [(i, (i + by) % RING) for i in range(RING)])]
    unnamed x24 -> x28, local copies, waits for them, and re-layouts: 3.27 us -> 4.62 us
  transfers between devices with their start and end apart: 31 -> 31, of which waited for: 16 -> 15; matrix products, arithmetic and copies ran while one was open for 2% -> 3% of each run, Pallas kernels for 25% -> 30%
where the time goes in v8:
time: 143 us; the launch traced here: 142 us
  starting transfers between devices  53.4 us (37%)
  Pallas kernels  50 us (35%)
  waiting for transfers between devices  28 us (20%)
  local copies, waits for them, and re-layouts  7.91 us (6%)
  other arithmetic  1.98 us (1%)
    all_to_all x4, starting transfers between devices, over_plane(): return lax.all_to_all(value, PLANE, 0, 0, tiled=True)  22 us
    ppermute x18, starting transfers between devices, shifted(): return lax.ppermute(value, 'z', [(i, (i + by) % RING) for i in range(RING)])  21.4 us
    pallas_call x2, Pallas kernels, weight_grad(): pl.pallas_call(weights_body, grid=(hidden // width,), in_specs=[block] *...  14.5 us
    pallas_call x2, Pallas kernels, project(): pl.pallas_call(functools.partial(project_body, pieces), in_specs=[SMEM, V...  13.6 us
    all_to_all x4, waiting for transfers between devices, over_plane(): return lax.all_to_all(value, PLANE, 0, 0, tiled=True)  13.5 us
    ppermute x9, starting transfers between devices, swapped(): return lax.ppermute(value, 'c', [(0, 1), (1, 0)])  10.1 us
    ppermute x18, waiting for transfers between devices, shifted(): return lax.ppermute(value, 'z', [(i, (i + by) % RING) for i in range(RING)])  9.82 us
    pallas_call x1, Pallas kernels, staged(): pl.pallas_call(stage_body, grid=(blocks,), in_specs=[pl.BlockSpec((2 * HD...  9.05 us
  transfers between devices with their start and end apart: 31, of which 15 were waited for; matrix products, arithmetic and copies ran while one was open for 3% of the time, Pallas kernels for 30%

profile of v8, /device:TPU:1, one launch (start us, length us, event | category | flops | bytes accessed | tf_op | source)
XLA Modules:
  0.0 142.3 jit_solution(16148486125215610945)
XLA Ops:
  5.0 6.8 %all-to-all-start = ((bf16[16,32,512]{2,1,0:T(8,128)(2,1)}), bf16[16,32,512]{2,1,0:T(8,128)(2,1)S(1)}, u32[]{:S(2)}, u32[]{:S(2)}) async-start(bf16[16,32,512]{2,1,0:T(8,128)(2,1)} %broadcast_in_dim.18), calls=%async_computation | async-start | bytes 1048576 | tf_op jit(solution)/shard_map/all_to_all | solution.py:411
  12.4 3.8 %collective-permute-start.9 = (bf16[32,512]{1,0:T(8,128)(2,1)S(1)}, bf16[32,512]{1,0:T(8,128)(2,1)S(1)}, u32[]{:S(2)}, u32[]{:S(2)}) collective-permute-start(bf16[32,512]{1,0:T(8,128)(2,1)S(1)} %get-tuple-element.92), channel_id=1, source_target_pairs={{0,6},{2,0},{4,2},{6,4},{1,7},{3,1},{5,3},{7,5},{8,14},{10,8},{12,... | collective-permute-start | bytes 98312 | tf_op jit(solution)/shard_map/ppermute | solution.py:407
  17.2 3.5 %collective-permute-done.10 = bf16[32,512]{1,0:T(8,128)(2,1)S(1)} collective-permute-done((bf16[32,512]{1,0:T(8,128)(2,1)S(1)}, bf16[32,512]{1,0:T(8,128)(2,1)S(1)}, u32[]{:S(2)}, u32[]{:S(2)}) %collective-permute-start.10) | collective-permute-done | bytes 32800 | tf_op jit(solution)/shard_map/ppermute | solution.py:407
  20.7 2.0 %all-to-all-done = bf16[16,32,512]{2,1,0:T(8,128)(2,1)S(1)} async-done(((bf16[16,32,512]{2,1,0:T(8,128)(2,1)}), bf16[16,32,512]{2,1,0:T(8,128)(2,1)S(1)}, u32[]{:S(2)}, u32[]{:S(2)}) %all-to-all-start) | async-done | bytes 524320 | tf_op jit(solution)/shard_map/all_to_all | solution.py:411
  24.4 4.6 %all-to-all-start.1 = ((bf16[16,4,32,512]{3,2,1,0:T(8,128)(2,1)}), bf16[16,4,32,512]{3,2,1,0:T(8,128)(2,1)S(1)}, u32[]{:S(2)}, u32[]{:S(2)}) async-start(bf16[16,4,32,512]{3,2,1,0:T(8,128)(2,1)} %broadcast_in_dim.19), calls=%async_computation.1 | async-start | bytes 4194304 | tf_op jit(solution)/shard_map/all_to_all | solution.py:411
  29.9 2.2 %collective-permute-start.4 = (bf16[8,32,512]{2,1,0:T(8,128)(2,1)S(1)}, bf16[8,32,512]{2,1,0:T(8,128)(2,1)S(1)}, u32[]{:S(2)}, u32[]{:S(2)}) collective-permute-start(bf16[8,32,512]{2,1,0:T(8,128)(2,1)S(1)} %get-tuple-element.89), channel_id=1, source_target_pairs={{0,6},{2,0},{4,2},{6,4},{1,7},{3,1},{5,3},{7,5},{8,14},{10,8},{12,... | collective-permute-start | bytes 786440 | tf_op jit(solution)/shard_map/ppermute | solution.py:407
  33.4 3.3 %collective-permute-done.1 = bf16[8,32,512]{2,1,0:T(8,128)(2,1)S(1)} collective-permute-done((bf16[8,32,512]{2,1,0:T(8,128)(2,1)S(1)}, bf16[8,32,512]{2,1,0:T(8,128)(2,1)S(1)}, u32[]{:S(2)}, u32[]{:S(2)}) %collective-permute-start.1) | collective-permute-done | bytes 262176 | tf_op jit(solution)/shard_map/ppermute | solution.py:407
  39.5 9.1 %stage.1 = (bf16[8,256,1024]{2,1,0:T(8,128)(2,1)}, bf16[8,256,1024]{2,1,0:T(8,128)(2,1)}) custom-call(bf16[4096,256]{1,0:T(8,128)(2,1)} %bitcast.48, bf16[4096,256]{1,0:T(8,128)(2,1)} %bitcast.50, bf16[4096,256]{1,0:T(8,128)(2,1)} %collective-permute-done.7.refs_2_, bf16[4096,256]{1,0:T(8,128)(2,1)} %collective-permute-done.8.refs_3_), custom_call_target="tpu_custom_call" | custom-call | bytes 16777216 | tf_op jit(solution)/shard_map/stage/pallas_call | solution.py:68
  49.0 6.7 %project_a.1 = (bf16[256,512]{1,0:T(8,128)(2,1)S(1)}, bf16[256,512]{1,0:T(8,128)(2,1)S(1)}, f32[256,1]{1,0:T(8,128)S(1)}, bf16[256,4096]{1,0:T(8,128)(2,1)}) custom-call(s32[1]{0:T(128)} %bitcast.2.z_ref, f32[8,1,512]{2,1,0:T(1,128)S(1)} %bitcast.37, bf16[8,2,32,512]{3,2,1,0:T(8,128)(2,1)} %bitcast.42, bf16[4,2,32,512]{3,2,1,0:T(8,128)(2,1)} %bitcast.51, ...), custom_call_target="tpu_custom_call" | custom-call | flops 2147483648 | bytes 12582912 | tf_op jit(solution)/shard_map/project_a/pallas_call | solution.py:126
  56.9 6.9 %project_b.1 = (bf16[256,512]{1,0:T(8,128)(2,1)S(1)}, bf16[256,512]{1,0:T(8,128)(2,1)S(1)}, f32[256,1]{1,0:T(8,128)S(1)}, bf16[256,4096]{1,0:T(8,128)(2,1)}) custom-call(s32[1]{0:T(128)} %bitcast.2.z_ref, f32[8,1,512]{2,1,0:T(1,128)S(1)} %bitcast.38, bf16[8,2,4,32,512]{4,3,2,1,0:T(8,128)(2,1)S(1)} %bitcast.33, bf16[8,2,4,32,512]{4,3,2,1,0:T(8,128)(2,1)S(1)} %bitcast.34, ...), custom_call_target="tpu_custom_call" | custom-call | flops 2147483648 | bytes 12582912 | tf_op jit(solution)/shard_map/project_b/pallas_call | solution.py:126
  64.4 4.4 %collective-permute-start.13 = (bf16[256,512]{1,0:T(8,128)(2,1)S(1)}, bf16[256,512]{1,0:T(8,128)(2,1)S(1)}, u32[]{:S(2)}, u32[]{:S(2)}) collective-permute-start(bf16[256,512]{1,0:T(8,128)(2,1)S(1)} %get-tuple-element.54), channel_id=1, source_target_pairs={{0,1},{1,0},{2,3},{3,2},{4,5},{5,4},{6,7},{7,6},{8,9},{9,8},{10,11... | collective-permute-start | bytes 786440 | tf_op jit(solution)/shard_map/ppermute | solution.py:403
  70.7 6.2 %attention.1 = (bf16[1024,256]{1,0:T(8,128)(2,1)}, bf16[1024,256]{1,0:T(8,128)(2,1)}, bf16[512,512]{1,0:T(8,128)(2,1)S(1)}, bf16[528,512]{1,0:T(8,128)(2,1)S(1)}, f32[1,512]{1,0:T(1,128)S(1)}) custom-call(bf16[1024,256]{1,0:T(8,128)(2,1)S(1)} %bitcast.40, bf16[1024,256]{1,0:T(8,128)(2,1)S(1)} %bitcast.41, bf16[256,512]{1,0:T(8,128)(2,1)S(1)} %copy-done.10, ...), custom_call_target="tpu_custom_call" | custom-call | flops 3221225472 | bytes 4194304 | tf_op jit(solution)/shard_map/attention/pallas_call | solution.py:207
  78.9 3.3 %back_b.1 = bf16[8,2,272,256]{3,2,1,0:T(8,128)(2,1)} custom-call(s32[1]{0:T(128)} %bitcast.2.z_ref, bf16[512,512]{1,0:T(8,128)(2,1)S(1)} %get-tuple-element.61.gnear_ref.own_ref, bf16[528,512]{1,0:T(8,128)(2,1)S(1)} %collective-permute-done.16.sib_ref, f32[1,512]{1,0:T(1,128)S(1)} %get-tuple-element.65.dots_ref, bf16[8,256,1024]{2,1,0:T(8,128)(2,1)S(1)} %copy-done.1), custom_call_target="tpu_custom_call" | custom-call | flops 2147483648 | bytes 4194304 | tf_op jit(solution)/shard_map/back_b/pallas_call | solution.py:255
  82.2 6.9 %all-to-all-start.2 = ((bf16[16,272,256]{2,1,0:T(8,128)(2,1)}), bf16[16,272,256]{2,1,0:T(8,128)(2,1)S(1)}, u32[]{:S(2)}, u32[]{:S(2)}) async-start(bf16[16,272,256]{2,1,0:T(8,128)(2,1)} %bitcast.45), calls=%async_computation.2 | async-start | bytes 4456448 | tf_op jit(solution)/shard_map/all_to_all | solution.py:411
  89.2 2.2 %copy-done = bf16[8,256,1024]{2,1,0:T(8,128)(2,1)S(1)} copy-done((bf16[8,256,1024]{2,1,0:T(8,128)(2,1)S(1)}, bf16[8,256,1024]{2,1,0:T(8,128)(2,1)}, u32[]{:S(2)}) %copy-start) | copy-done | bytes 4194328
  92.4 2.4 %back_a.1 = (bf16[4,2,64,256]{3,2,1,0:T(8,128)(2,1)S(1)}, bf16[4,2,64,256]{3,2,1,0:T(8,128)(2,1)S(1)}, bf16[4,2,64,256]{3,2,1,0:T(8,128)(2,1)S(1)}, bf16[4,2,64,...) custom-call(s32[1]{0:T(128)} %bitcast.2.z_ref, ...), custom_call_target="tpu_custom_call" | custom-call | flops 2147483648 | bytes 4194304 | tf_op jit(solution)/shard_map/back_a/pallas_call | solution.py:288
  94.8 2.7 %collective-permute-start.20 = (bf16[4,2,64,256]{3,2,1,0:T(8,128)(2,1)S(1)}, bf16[4,2,64,256]{3,2,1,0:T(8,128)(2,1)S(1)}, u32[]{:S(2)}, u32[]{:S(2)}) collective-permute-start(bf16[4,2,64,256]{3,2,1,0:T(8,128)(2,1)S(1)} %get-tuple-element.73), channel_id=1, source_target_pairs={{0,6},{2,0},{4,2},{6,4},{1,7},{3,1},{5,3},{7,5},{8,14},{10,8},{12,... | collective-permute-start | bytes 786440 | tf_op jit(solution)/shard_map/ppermute | solution.py:407
  99.0 7.2 %key_grad.1 = f32[4096,256]{1,0:T(8,128)} custom-call(bf16[256,4096]{1,0:T(8,128)(2,1)} %get-tuple-element.59.near_a, bf16[256,4096]{1,0:T(8,128)(2,1)} %get-tuple-element.60.near_b, bf16[256,4096]{1,0:T(8,128)(2,1)} %collective-permute-done.14.far_a, bf16[256,4096]{1,0:T(8,128)(2,1)} %collective-permute-done.15.far_b, ...), custom_call_target="tpu_custom_call" | custom-call | flops 2147483648 | bytes 13631488 | tf_op jit(solution)/shard_map/key_grad/pallas_call | solution.py:308
  108.2 7.3 %value_grad.1 = f32[4096,256]{1,0:T(8,128)} custom-call(bf16[256,4096]{1,0:T(8,128)(2,1)} %get-tuple-element.59.near_a, bf16[256,4096]{1,0:T(8,128)(2,1)} %get-tuple-element.60.near_b, bf16[256,4096]{1,0:T(8,128)(2,1)} %collective-permute-done.14.far_a, bf16[256,4096]{1,0:T(8,128)(2,1)} %collective-permute-done.15.far_b, ...), custom_call_target="tpu_custom_call" | custom-call | flops 2147483648 | bytes 13631488 | tf_op jit(solution)/shard_map/value_grad/pallas_call | solution.py:308
  116.6 7.3 %all-to-all-done.2.arrived_ref = bf16[16,272,256]{2,1,0:T(8,128)(2,1)S(1)} async-done(((bf16[16,272,256]{2,1,0:T(8,128)(2,1)}), bf16[16,272,256]{2,1,0:T(8,128)(2,1)S(1)}, u32[]{:S(2)}, u32[]{:S(2)}) %all-to-all-start.2) | async-done | bytes 2228256 | tf_op jit(solution)/shard_map/all_to_all | solution.py:411
  123.9 3.6 %all-to-all-start.3 = ((bf16[16,64,256]{2,1,0:T(8,128)(2,1)}), bf16[16,64,256]{2,1,0:T(8,128)(2,1)S(1)}, u32[]{:S(2)}, u32[]{:S(2)}) async-start(bf16[16,64,256]{2,1,0:T(8,128)(2,1)} %bitcast.46), calls=%async_computation.3 | async-start | bytes 1048576 | tf_op jit(solution)/shard_map/all_to_all | solution.py:411
  127.8 2.9 %collective-permute-start.24 = (bf16[80,256]{1,0:T(8,128)(2,1)S(1)}, bf16[80,256]{1,0:T(8,128)(2,1)S(1)}, u32[]{:S(2)}, u32[]{:S(2)}) collective-permute-start(bf16[80,256]{1,0:T(8,128)(2,1)S(1)} %get-tuple-element.83), channel_id=1, source_target_pairs={{0,4},{2,6},{4,0},{6,2},{1,5},{3,7},{5,1},{7,3},{8,12},{10,14},{12... | collective-permute-start | bytes 122888 | tf_op jit(solution)/shard_map/ppermute | solution.py:407
  133.9 3.7 %all-to-all-done.3.arrived_ref = bf16[16,64,256]{2,1,0:T(8,128)(2,1)S(1)} async-done(((bf16[16,64,256]{2,1,0:T(8,128)(2,1)}), bf16[16,64,256]{2,1,0:T(8,128)(2,1)S(1)}, u32[]{:S(2)}, u32[]{:S(2)}) %all-to-all-start.3) | async-done | bytes 524320 | tf_op jit(solution)/shard_map/all_to_all | solution.py:411
  138.3 2.4 %collective-permute-start.26 = (f32[64,256]{1,0:T(8,128)S(1)}, f32[64,256]{1,0:T(8,128)S(1)}, u32[]{:S(2)}, u32[]{:S(2)}) collective-permute-start(f32[64,256]{1,0:T(8,128)S(1)} %get-tuple-element.86), channel_id=1, source_target_pairs={{0,1},{1,0},{2,3},{3,2},{4,5},{5,4},{6,7},{7,6},{8,9},{9,8},{10,11... | collective-permute-start | bytes 196616 | tf_op jit(solution)/shard_map/ppermute | solution.py:403
  (89 shorter events, 30.0 us)
Async XLA Ops:
  3.7 34.0 %collective-permute-start.7 = (bf16[4096,256]{1,0:T(8,128)(2,1)}, bf16[4096,256]{1,0:T(8,128)(2,1)}, u32[]{:S(2)}, u32[]{:S(2)}) collective-permute-start(bf16[4096,256]{1,0:T(8,128)(2,1)} %bitcast.47), channel_id=1, source_target_pairs={{0,1},{1,0},{2,3},{3,2},{4,5},{5,4},{6,7},{7,6},{8,9},{9,8},{10,11... | collective-permute-start | bytes 6291464 | tf_op jit(solution)/shard_map/ppermute | solution.py:403
  5.0 17.8 %all-to-all-start = ((bf16[16,32,512]{2,1,0:T(8,128)(2,1)}), bf16[16,32,512]{2,1,0:T(8,128)(2,1)S(1)}, u32[]{:S(2)}, u32[]{:S(2)}) async-start(bf16[16,32,512]{2,1,0:T(8,128)(2,1)} %broadcast_in_dim.18), calls=%async_computation | async-start | bytes 1048576 | tf_op jit(solution)/shard_map/all_to_all | solution.py:411
  11.8 27.7 %collective-permute-start.8 = (bf16[4096,256]{1,0:T(8,128)(2,1)}, bf16[4096,256]{1,0:T(8,128)(2,1)}, u32[]{:S(2)}, u32[]{:S(2)}) collective-permute-start(bf16[4096,256]{1,0:T(8,128)(2,1)} %bitcast.49), channel_id=1, source_target_pairs={{0,1},{1,0},{2,3},{3,2},{4,5},{5,4},{6,7},{7,6},{8,9},{9,8},{10,11... | collective-permute-start | bytes 6291464 | tf_op jit(solution)/shard_map/ppermute | solution.py:403
  12.4 4.8 %collective-permute-start.9 = (bf16[32,512]{1,0:T(8,128)(2,1)S(1)}, bf16[32,512]{1,0:T(8,128)(2,1)S(1)}, u32[]{:S(2)}, u32[]{:S(2)}) collective-permute-start(bf16[32,512]{1,0:T(8,128)(2,1)S(1)} %get-tuple-element.92), channel_id=1, source_target_pairs={{0,6},{2,0},{4,2},{6,4},{1,7},{3,1},{5,3},{7,5},{8,14},{10,8},{12,... | collective-permute-start | bytes 98312 | tf_op jit(solution)/shard_map/ppermute | solution.py:407
  16.1 4.6 %collective-permute-start.10 = (bf16[32,512]{1,0:T(8,128)(2,1)S(1)}, bf16[32,512]{1,0:T(8,128)(2,1)S(1)}, u32[]{:S(2)}, u32[]{:S(2)}) collective-permute-start(bf16[32,512]{1,0:T(8,128)(2,1)S(1)} %get-tuple-element.92), channel_id=1, source_target_pairs={{0,4},{2,6},{4,0},{6,2},{1,5},{3,7},{5,1},{7,3},{8,12},{10,14},{12... | collective-permute-start | bytes 98312 | tf_op jit(solution)/shard_map/ppermute | solution.py:407
  24.4 32.5 %all-to-all-start.1 = ((bf16[16,4,32,512]{3,2,1,0:T(8,128)(2,1)}), bf16[16,4,32,512]{3,2,1,0:T(8,128)(2,1)S(1)}, u32[]{:S(2)}, u32[]{:S(2)}) async-start(bf16[16,4,32,512]{3,2,1,0:T(8,128)(2,1)} %broadcast_in_dim.19), calls=%async_computation.1 | async-start | bytes 4194304 | tf_op jit(solution)/shard_map/all_to_all | solution.py:411
  29.1 7.7 %collective-permute-start.1 = (bf16[8,32,512]{2,1,0:T(8,128)(2,1)S(1)}, bf16[8,32,512]{2,1,0:T(8,128)(2,1)S(1)}, u32[]{:S(2)}, u32[]{:S(2)}) collective-permute-start(bf16[8,32,512]{2,1,0:T(8,128)(2,1)S(1)} %get-tuple-element.90), channel_id=1, source_target_pairs={{0,2},{2,4},{4,6},{6,0},{1,3},{3,5},{5,7},{7,1},{8,10},{10,12},{12... | collective-permute-start | bytes 786440 | tf_op jit(solution)/shard_map/ppermute | solution.py:407
  29.9 6.9 %collective-permute-start.4 = (bf16[8,32,512]{2,1,0:T(8,128)(2,1)S(1)}, bf16[8,32,512]{2,1,0:T(8,128)(2,1)S(1)}, u32[]{:S(2)}, u32[]{:S(2)}) collective-permute-start(bf16[8,32,512]{2,1,0:T(8,128)(2,1)S(1)} %get-tuple-element.89), channel_id=1, source_target_pairs={{0,6},{2,0},{4,2},{6,4},{1,7},{3,1},{5,3},{7,5},{8,14},{10,8},{12,... | collective-permute-start | bytes 786440 | tf_op jit(solution)/shard_map/ppermute | solution.py:407
  32.1 16.5 %collective-permute-start.3 = (bf16[8,32,512]{2,1,0:T(8,128)(2,1)S(1)}, bf16[8,32,512]{2,1,0:T(8,128)(2,1)}, u32[]{:S(2)}, u32[]{:S(2)}) collective-permute-start(bf16[8,32,512]{2,1,0:T(8,128)(2,1)S(1)} %get-tuple-element.90), channel_id=1, source_target_pairs={{0,6},{2,0},{4,2},{6,4},{1,7},{3,1},{5,3},{7,5},{8,14},{10,8},{12,... | collective-permute-start | bytes 786440 | tf_op jit(solution)/shard_map/ppermute | solution.py:407
  36.7 11.9 %collective-permute-start.2 = (bf16[8,32,512]{2,1,0:T(8,128)(2,1)S(1)}, bf16[8,32,512]{2,1,0:T(8,128)(2,1)}, u32[]{:S(2)}, u32[]{:S(2)}) collective-permute-start(bf16[8,32,512]{2,1,0:T(8,128)(2,1)S(1)} %get-tuple-element.89), channel_id=1, source_target_pairs={{0,2},{2,4},{4,6},{6,0},{1,3},{3,5},{5,7},{7,1},{8,10},{10,12},{12... | collective-permute-start | bytes 786440 | tf_op jit(solution)/shard_map/ppermute | solution.py:407
  36.8 12.2 %collective-permute-start.5 = (bf16[8,32,512]{2,1,0:T(8,128)(2,1)S(1)}, bf16[8,32,512]{2,1,0:T(8,128)(2,1)}, u32[]{:S(2)}, u32[]{:S(2)}) collective-permute-start(bf16[8,32,512]{2,1,0:T(8,128)(2,1)S(1)} %collective-permute-done.1), channel_id=1, source_target_pairs={{0,2},{2,4},{4,6},{6,0},{1,3},{3,5},{5,7},{7,1},{8,10},{10,12},{12... | collective-permute-start | bytes 786440 | tf_op jit(solution)/shard_map/ppermute | solution.py:407
  37.7 11.2 %collective-permute-start.6 = (bf16[8,32,512]{2,1,0:T(8,128)(2,1)S(1)}, bf16[8,32,512]{2,1,0:T(8,128)(2,1)}, u32[]{:S(2)}, u32[]{:S(2)}) collective-permute-start(bf16[8,32,512]{2,1,0:T(8,128)(2,1)S(1)} %collective-permute-done.4), channel_id=1, source_target_pairs={{0,6},{2,0},{4,2},{6,4},{1,7},{3,1},{5,3},{7,5},{8,14},{10,8},{12,... | collective-permute-start | bytes 786440 | tf_op jit(solution)/shard_map/ppermute | solution.py:407
  64.4 5.6 %collective-permute-start.13 = (bf16[256,512]{1,0:T(8,128)(2,1)S(1)}, bf16[256,512]{1,0:T(8,128)(2,1)S(1)}, u32[]{:S(2)}, u32[]{:S(2)}) collective-permute-start(bf16[256,512]{1,0:T(8,128)(2,1)S(1)} %get-tuple-element.54), channel_id=1, source_target_pairs={{0,1},{1,0},{2,3},{3,2},{4,5},{5,4},{6,7},{7,6},{8,9},{9,8},{10,11... | collective-permute-start | bytes 786440 | tf_op jit(solution)/shard_map/ppermute | solution.py:403
  70.0 28.0 %collective-permute-start.15 = (bf16[256,4096]{1,0:T(8,128)(2,1)}, bf16[256,4096]{1,0:T(8,128)(2,1)}, u32[]{:S(2)}, u32[]{:S(2)}) collective-permute-start(bf16[256,4096]{1,0:T(8,128)(2,1)} %get-tuple-element.60.near_b), channel_id=1, source_target_pairs={{0,1},{1,0},{2,3},{3,2},{4,5},{5,4},{6,7},{7,6},{8,9},{9,8},{10,11... | collective-permute-start | bytes 6291464 | tf_op jit(solution)/shard_map/ppermute | solution.py:403
  70.4 28.6 %collective-permute-start.14 = (bf16[256,4096]{1,0:T(8,128)(2,1)}, bf16[256,4096]{1,0:T(8,128)(2,1)}, u32[]{:S(2)}, u32[]{:S(2)}) collective-permute-start(bf16[256,4096]{1,0:T(8,128)(2,1)} %get-tuple-element.59.near_a), channel_id=1, source_target_pairs={{0,1},{1,0},{2,3},{3,2},{4,5},{5,4},{6,7},{7,6},{8,9},{9,8},{10,11... | collective-permute-start | bytes 6291464 | tf_op jit(solution)/shard_map/ppermute | solution.py:403
  82.2 41.7 %all-to-all-start.2 = ((bf16[16,272,256]{2,1,0:T(8,128)(2,1)}), bf16[16,272,256]{2,1,0:T(8,128)(2,1)S(1)}, u32[]{:S(2)}, u32[]{:S(2)}) async-start(bf16[16,272,256]{2,1,0:T(8,128)(2,1)} %bitcast.45), calls=%async_computation.2 | async-start | bytes 4456448 | tf_op jit(solution)/shard_map/all_to_all | solution.py:411
  94.8 11.5 %collective-permute-start.19 = (bf16[4,2,64,256]{3,2,1,0:T(8,128)(2,1)S(1)}, bf16[4,2,64,256]{3,2,1,0:T(8,128)(2,1)S(1)}, u32[]{:S(2)}, u32[]{:S(2)}) collective-permute-start(bf16[4,2,64,256]{3,2,1,0:T(8,128)(2,1)S(1)} %get-tuple-element.72), channel_id=1, source_target_pairs={{0,2},{2,4},{4,6},{6,0},{1,3},{3,5},{5,7},{7,1},{8,10},{10,12},{12... | collective-permute-start | bytes 786440 | tf_op jit(solution)/shard_map/ppermute | solution.py:407
  94.8 11.4 %collective-permute-start.20 = (bf16[4,2,64,256]{3,2,1,0:T(8,128)(2,1)S(1)}, bf16[4,2,64,256]{3,2,1,0:T(8,128)(2,1)S(1)}, u32[]{:S(2)}, u32[]{:S(2)}) collective-permute-start(bf16[4,2,64,256]{3,2,1,0:T(8,128)(2,1)S(1)} %get-tuple-element.73), channel_id=1, source_target_pairs={{0,6},{2,0},{4,2},{6,4},{1,7},{3,1},{5,3},{7,5},{8,14},{10,8},{12,... | collective-permute-start | bytes 786440 | tf_op jit(solution)/shard_map/ppermute | solution.py:407
  97.5 17.9 %collective-permute-start.17 = (bf16[4,2,64,256]{3,2,1,0:T(8,128)(2,1)S(1)}, bf16[4,2,64,256]{3,2,1,0:T(8,128)(2,1)S(1)}, u32[]{:S(2)}, u32[]{:S(2)}) collective-permute-start(bf16[4,2,64,256]{3,2,1,0:T(8,128)(2,1)S(1)} %get-tuple-element.68), channel_id=1, source_target_pairs={{0,6},{2,0},{4,2},{6,4},{1,7},{3,1},{5,3},{7,5},{8,14},{10,8},{12,... | collective-permute-start | bytes 786440 | tf_op jit(solution)/shard_map/ppermute | solution.py:407
  98.0 17.5 %collective-permute-start.18 = (bf16[4,2,64,256]{3,2,1,0:T(8,128)(2,1)S(1)}, bf16[4,2,64,256]{3,2,1,0:T(8,128)(2,1)S(1)}, u32[]{:S(2)}, u32[]{:S(2)}) collective-permute-start(bf16[4,2,64,256]{3,2,1,0:T(8,128)(2,1)S(1)} %get-tuple-element.69), channel_id=1, source_target_pairs={{0,2},{2,4},{4,6},{6,0},{1,3},{3,5},{5,7},{7,1},{8,10},{10,12},{12... | collective-permute-start | bytes 786440 | tf_op jit(solution)/shard_map/ppermute | solution.py:407
  106.3 9.2 %collective-permute-start.22 = (bf16[4,2,64,256]{3,2,1,0:T(8,128)(2,1)S(1)}, bf16[4,2,64,256]{3,2,1,0:T(8,128)(2,1)S(1)}, u32[]{:S(2)}, u32[]{:S(2)}) collective-permute-start(bf16[4,2,64,256]{3,2,1,0:T(8,128)(2,1)S(1)} %add_convert_fusion.1), channel_id=1, source_target_pairs={{0,6},{2,0},{4,2},{6,4},{1,7},{3,1},{5,3},{7,5},{8,14},{10,8},{12,... | collective-permute-start | bytes 786440 | tf_op jit(solution)/shard_map/ppermute | solution.py:407
  108.1 7.4 %collective-permute-start.21 = (bf16[4,2,64,256]{3,2,1,0:T(8,128)(2,1)S(1)}, bf16[4,2,64,256]{3,2,1,0:T(8,128)(2,1)S(1)}, u32[]{:S(2)}, u32[]{:S(2)}) collective-permute-start(bf16[4,2,64,256]{3,2,1,0:T(8,128)(2,1)S(1)} %add_convert_fusion.3), channel_id=1, source_target_pairs={{0,2},{2,4},{4,6},{6,0},{1,3},{3,5},{5,7},{7,1},{8,10},{10,12},{12... | collective-permute-start | bytes 786440 | tf_op jit(solution)/shard_map/ppermute | solution.py:407
  123.9 13.7 %all-to-all-start.3 = ((bf16[16,64,256]{2,1,0:T(8,128)(2,1)}), bf16[16,64,256]{2,1,0:T(8,128)(2,1)S(1)}, u32[]{:S(2)}, u32[]{:S(2)}) async-start(bf16[16,64,256]{2,1,0:T(8,128)(2,1)} %bitcast.46), calls=%async_computation.3 | async-start | bytes 1048576 | tf_op jit(solution)/shard_map/all_to_all | solution.py:411
  127.8 4.7 %collective-permute-start.24 = (bf16[80,256]{1,0:T(8,128)(2,1)S(1)}, bf16[80,256]{1,0:T(8,128)(2,1)S(1)}, u32[]{:S(2)}, u32[]{:S(2)}) collective-permute-start(bf16[80,256]{1,0:T(8,128)(2,1)S(1)} %get-tuple-element.83), channel_id=1, source_target_pairs={{0,4},{2,6},{4,0},{6,2},{1,5},{3,7},{5,1},{7,3},{8,12},{10,14},{12... | collective-permute-start | bytes 122888 | tf_op jit(solution)/shard_map/ppermute | solution.py:407
  (21 other events, 139.8 us)

commit v9 on v8

--- a/solution.py
+++ b/solution.py
@@ -54,32 +54,9 @@
     return pl.CostEstimate(flops=flops, bytes_accessed=int(mib * MIB), transcendentals=transcendentals)
 
 
-def stage_body(*refs):
-    sources, (first_ref, second_ref) = refs[:-2], refs[-2:]
-    for i, source in enumerate(sources):
-        first_ref[0, :, i * HD : (i + 1) * HD] = source[:HD]
-        second_ref[0, :, i * HD : (i + 1) * HD] = source[HD:]
-
-
-def staged(weights):
-    count, blocks = len(weights), weights[0].shape[0] // (2 * HD)
-    block = pl.BlockSpec((1, HD, count * HD), lambda i: (i, 0, 0))
-    out = pltpu.HBM((blocks, HD, count * HD), BF16)
-    return pl.pallas_call(
-        stage_body,
-        grid=(blocks,),
-        in_specs=[pl.BlockSpec((2 * HD, HD), lambda i: (i, 0))] * count,
-        out_specs=[block] * 2,
-        out_shape=[out] * 2,
-        compiler_params=limits(8),
-        cost_estimate=cost(0, 16),
-        name="stage",
-    )(*[in_hbm(w) for w in weights])
-
-
 def project_body(pieces, z_ref, gain_ref, *refs):
     xs = refs[: len(pieces)]
-    w_refs, refs = refs[len(pieces) : len(pieces) + 2], refs[len(pieces) + 2 :]
+    w_refs, refs = refs[len(pieces) : len(pieces) + 4], refs[len(pieces) + 4 :]
     own_ref, sib_ref, scale_ref, normed_ref, held, rows_low, weights, x_sem, w_sem, out_sem = refs
     blocks, segs, part, width = held.shape
     rows = segs * part
@@ -109,13 +86,10 @@
         rows_low[:, p * width : (p + 1) * width] = (wide * scale * gain_ref[p]).astype(BF16)
     out = pltpu.make_async_copy(rows_low, normed_ref, out_sem)
     out.start()
-    total = 0.0
     for i, load in enumerate(loads):
         load.wait()
-        columns = beside(*[rows_low[:, (2 * p + i) * HD : (2 * p + i + 1) * HD] for p in range(blocks)])
-        total += nn(columns, weights[i].reshape(blocks * HD, 4 * HD))
-    own_ref[...] = total[:, : 2 * HD].astype(BF16)
-    sib_ref[...] = total[:, 2 * HD :].astype(BF16)
+        out_ref, at = (own_ref, sib_ref)[i // 2], (i % 2) * HD
+        out_ref[:, at : at + HD] = nn(rows_low[...], weights[i]).astype(BF16)
     out.wait()
 
 
@@ -125,7 +99,7 @@
     rows = segs * part
     return pl.pallas_call(
         functools.partial(project_body, pieces),
-        in_specs=[SMEM, VMEM] + [ANYWHERE] * (len(xs) + 2),
+        in_specs=[SMEM, VMEM] + [ANYWHERE] * (len(xs) + 4),
         out_specs=[VMEM, VMEM, VMEM, ANYWHERE],
         out_shape=[
             jax.ShapeDtypeStruct((rows, 2 * HD), BF16),
@@ -136,9 +110,9 @@
         scratch_shapes=[
             pltpu.VMEM((blocks, segs, part, width), BF16),
             pltpu.VMEM((rows, blocks * width), BF16),
-            pltpu.VMEM((2, blocks, HD, 4 * HD), BF16),
+            pltpu.VMEM((4, blocks * width, HD), BF16),
             pltpu.SemaphoreType.DMA((2 * len(xs),)),
-            pltpu.SemaphoreType.DMA((2,)),
+            pltpu.SemaphoreType.DMA((4,)),
             pltpu.SemaphoreType.DMA(()),
         ],
         compiler_params=limits(24),
@@ -221,11 +195,14 @@
     )(q, dc, near_a, near_b, far_a, far_b)
 
 
-def feature_block(z, rows, w_ref, distance, side):
-    return nt(rows, w_ref[side * RING + lax.rem(z + distance, RING)]).astype(BF16)
-
-
-def back_b_body(z_ref, own_ref, sib_ref, dots_ref, w_ref, out_ref, stage, out_sem):
+def feature_block(z, rows, weights, feature_half, distance, side):
+    block = side * RING + lax.rem(z + distance, RING)
+    at = pl.ds(pl.multiple_of((2 * block + feature_half) * HD, HD), HD)
+    return nt(rows, beside(*[w[at, :] for w in weights])).astype(BF16)
+
+
+def back_b_body(z_ref, own_ref, sib_ref, dots_ref, ko, vo, ks, vs, out_ref, stage, out_sem):
+    z, core = z_ref[0], z_ref[1]
     half = own_ref.shape[0]
     segs = out_ref.shape[0]
     part = half // segs // 2
@@ -234,7 +211,7 @@
     for distance in range(RING):
         at = distance * 2 * part
         for side in range(2):
-            value = feature_block(z_ref[0], rows, w_ref, distance, side).reshape(2, segs, part, HD)
+            value = feature_block(z, rows, (ko, vo, ks, vs), 1 - core, distance, side).reshape(2, segs, part, HD)
             for k in range(2):
                 stage[:, side, at + k * part : at + (k + 1) * part] = value[k]
         size = 2 * part
@@ -254,7 +231,7 @@
     shape = (segs, 2, RING * rows // segs + EXTRA, HD)
     return pl.pallas_call(
         back_b_body,
-        in_specs=[SMEM] + [VMEM] * 4,
+        in_specs=[SMEM] + [VMEM] * 7,
         out_specs=ANYWHERE,
         out_shape=pltpu.HBM(shape, BF16),
         scratch_shapes=[
@@ -264,17 +241,18 @@
         compiler_params=limits(16),
         cost_estimate=cost(2 * rows * 8 * HD * 4 * HD, 4),
         name="back_b",
-    )(z, own, sib, dots, in_vmem(weights))
-
-
-def back_a_body(z_ref, own_ref, sib_ref, w_ref, *outs):
+    )(z, own, sib, dots, *[in_vmem(w) for w in weights])
+
+
+def back_a_body(z_ref, own_ref, sib_ref, ko, vo, ks, vs, *outs):
+    z, core = z_ref[0], z_ref[1]
     rows = beside(own_ref[...], sib_ref[: own_ref.shape[0]])
     segs = outs[-1].shape[0]
     part = rows.shape[0] // segs // 2
     lands = {2: ((0, 0), (1, segs // 2)), 1: ((2, 0), (3, segs // 2)), 3: ((4, 0), (5, segs // 2)), 0: ((6, 0),)}
     for distance in (2, 1, 3, 0):
         for side in range(2):
-            value = feature_block(z_ref[0], rows, w_ref, distance, side).reshape(2, segs, part, HD)
+            value = feature_block(z, rows, (ko, vo, ks, vs), core, distance, side).reshape(2, segs, part, HD)
             for index, first in lands[distance]:
                 for k in range(2):
                     count = outs[index].shape[0]
@@ -287,13 +265,13 @@
     full = jax.ShapeDtypeStruct((segs, 2, rows // segs, HD), BF16)
     return pl.pallas_call(
         back_a_body,
-        in_specs=[SMEM] + [VMEM] * 3,
+        in_specs=[SMEM] + [VMEM] * 6,
         out_specs=[VMEM] * 7,
         out_shape=[half] * 6 + [full],
         compiler_params=limits(16),
         cost_estimate=cost(2 * rows * 8 * HD * 4 * HD, 4),
         name="back_a",
-    )(z, own, sib, in_vmem(weights))
+    )(z, own, sib, *[in_vmem(w) for w in weights])
 
 
 def weights_body(near_a, near_b, far_a, far_b, gnear_ref, gfar_ref, out_ref):
@@ -344,17 +322,14 @@
     )(arrived)
 
 
-def finish_body(hidden, place_ref, gain_ref, block_ref, scale_a, scale_b, arrived_ref, kept_ref, dots_ref, r1, r2, r3,
-                keep_ref, send_ref):
+def finish_b_body(hidden, place_ref, gain_ref, block_ref, scale_a, scale_b, kept_ref, dots_ref, r1, r2, r3,
+                  out_ref, scale_ref, mean_ref):
     core, segment, pair = place_ref[0], place_ref[1], place_ref[2]
     half = block_ref.shape[0]
     part = half // 2
-    left = arrived_ref[0].astype(F32)
-    for i in range(1, arrived_ref.shape[0]):
-        left += arrived_ref[i].astype(F32)
-    right, dots = kept_ref[...], dots_ref[...]
+    total, dots = kept_ref[...], dots_ref[...]
     for ref in (r1, r2, r3):
-        right += ref[:half].astype(F32)
+        total += ref[:half].astype(F32)
         dots += dots_of(ref[half:].astype(F32))
     lane = lax.broadcasted_iota(jnp.int32, (part, HD), 1)
     row = lax.broadcasted_iota(jnp.int32, (part, HD), 0)
@@ -363,32 +338,55 @@
     mean = above(pick(dots[:, :HD]), pick(dots[:, HD:])) / hidden
     rows = pl.ds(pl.multiple_of(segment * part, part), part)
     scale = above(scale_a[rows], scale_b[rows])
-    gain = gain_ref[pair]
-    for side, total in enumerate((left, right)):
-        at = slice(side * HD, (side + 1) * HD)
-        value = scale * (total * gain[:, at] - block_ref[:, at].astype(F32) * scale * mean)
-
-        @pl.when(core == side)
-        def _():
-            keep_ref[...] = value
-
-        @pl.when(core != side)
-        def _():
-            send_ref[...] = value
-
-
-def finish(place, gain, block, scale_a, scale_b, arrived, kept, dots, received):
+    out_ref[...] = finished(core == 1, total, gain_ref[pair], block_ref[...], scale, mean)
+    scale_ref[...] = scale
+    mean_ref[...] = mean
+
+
+def finished(first, total, gain, block, scale, mean):
+    gain = jnp.where(first, gain[:, :HD], gain[:, HD:])
+    centered = jnp.where(first, block[:, :HD].astype(F32), block[:, HD:].astype(F32)) * scale
+    return scale * (total * gain - centered * mean)
+
+
+def finish_b(place, gain, block, scale_a, scale_b, kept, dots, received):
     half, width = block.shape
     hidden = gain.shape[0]
-    return pl.pallas_call(
-        functools.partial(finish_body, hidden),
-        in_specs=[SMEM] + [VMEM] * 10,
-        out_specs=[VMEM] * 2,
-        out_shape=[jax.ShapeDtypeStruct((half, HD), F32)] * 2,
+    column = jax.ShapeDtypeStruct((half, 1), F32)
+    return pl.pallas_call(
+        functools.partial(finish_b_body, hidden),
+        in_specs=[SMEM] + [VMEM] * 9,
+        out_specs=[VMEM] * 3,
+        out_shape=[jax.ShapeDtypeStruct((half, HD), F32), column, column],
         compiler_params=limits(16),
         cost_estimate=cost(0, 1),
-        name="finish",
-    )(place, gain.reshape(hidden // width, 1, width), block, scale_a, scale_b, arrived, kept, dots, *received)
+        name="finish_b",
+    )(place, gain.reshape(hidden // width, 1, width), block, scale_a, scale_b, kept, dots, *received)
+
+
+def finish_a_body(place_ref, gain_ref, block_ref, scale_ref, mean_ref, came_ref, arrived_ref, out_ref):
+    core, pair = place_ref[0], place_ref[2]
+    half = block_ref.shape[0]
+    total = arrived_ref[0].astype(F32)
+    for i in range(1, arrived_ref.shape[0]):
+        total += arrived_ref[i].astype(F32)
+    kept = finished(core == 0, total, gain_ref[pair], block_ref[...], scale_ref[...], mean_ref[...])
+    out_ref[pl.ds(pl.multiple_of(core * half, half), half)] = kept
+    out_ref[pl.ds(pl.multiple_of((1 - core) * half, half), half)] = came_ref[...]
+
+
+def finish_a(place, gain, block, scale, mean, came, arrived):
+    half, width = block.shape
+    hidden = gain.shape[0]
+    return pl.pallas_call(
+        finish_a_body,
+        in_specs=[SMEM] + [VMEM] * 6,
+        out_specs=VMEM,
+        out_shape=jax.ShapeDtypeStruct((2 * half, HD), F32),
+        compiler_params=limits(16),
+        cost_estimate=cost(0, 1),
+        name="finish_a",
+    )(place, gain.reshape(hidden // width, 1, width), block, scale, mean, came, arrived)
 
 
 def in_vmem(value):
@@ -423,7 +421,7 @@
     segment = lax.axis_index(("y", "xh"))
     pair = lax.axis_index(("xl", "z"))
     segs, plane = lax.axis_size(("y", "xh")), lax.axis_size(PLANE)
-    z_array = z.astype(jnp.int32).reshape(1)
+    z_array = jnp.stack([z, core]).astype(jnp.int32)
     place = jnp.stack([core, segment, pair]).astype(jnp.int32)
     wide = lambda value: value.astype(F32)
 
@@ -443,7 +441,7 @@
     deep = lambda value: value.reshape(segs // 2, 2, part, width)
 
     key_own, value_own = after((key_weight[0], value_weight[0]), block)
-    weights = staged((key_own, value_own, swapped(key_own), swapped(value_own)))
+    weights = (key_own, value_own, swapped(key_own), swapped(value_own))
 
     top = segs // 2
     pieces_a = [(0, 0, None), (3, 0, None), (3, top, None), (1, 0, None), (1, top, None), (2, 0, None), (2, top, None)]
@@ -460,10 +458,10 @@
     context, query_grad, gnear, gfar, near_dots = attention(queries[0], context_grad[0], own_a, own_b, far_a, far_b)
     gsib = swapped(gfar)
 
-    parts_b = back_b(z_array, gnear, gsib, near_dots, weights[1], segs)
+    parts_b = back_b(z_array, gnear, gsib, near_dots, weights, segs)
     arrived_b = over_plane(parts_b.reshape(plane, RING * half + EXTRA, HD))
     z_later, = after((z_array,), parts_b)
-    opp_low, opp_high, up_low, up_high, down_low, down_high, kept = back_a(z_later, gnear, gsib, weights[0], segs)
+    opp_low, opp_high, up_low, up_high, down_low, down_high, kept = back_a(z_later, gnear, gsib, weights, segs)
     from_low, from_high = shifted(opp_low, 1), shifted(opp_high, -1)
     got_high, got_low = shifted(up_high, 1), shifted(down_low, -1)
     all_normed = (normed_a, normed_b, normed_far_a, normed_far_b)
@@ -481,9 +479,8 @@
     arrived_a = over_plane(summed_a)
     kept_b, dots, to_1, to_2, to_3 = merge_b(arrived_b, half)
     received = (shifted(to_1, 1), shifted(to_2, 2), shifted(to_3, -1))
-    keep, send = finish(place, norm_gain, block, scale_a, scale_b, arrived_a, kept_b, dots, received)
-    came = swapped(send)
-    result = jnp.where(core == 0, above(keep, came), above(came, keep))
+    value_b, own_scale, mean = finish_b(place, norm_gain, block, scale_a, scale_b, kept_b, dots, received)
+    result = finish_a(place, norm_gain, block, own_scale, mean, swapped(value_b), arrived_a)
     return context[None], query_grad[None], key_grad[None], value_grad[None], result
 
 

time: 143 us -> 148 us (1.035)
  waiting for transfers between devices: 28 us -> 32.9 us
  Pallas kernels: 50 us -> 51.8 us
    ppermute x18, waiting for transfers between devices: 9.82 us -> 21.5 us  [shifted(): return lax.ppermute(value, 'z', [(i, (i + by) % RING) for i in range(RING)])]
    all_to_all x4, waiting for transfers between devices: 13.5 us -> 7.58 us  [over_plane(): return lax.all_to_all(value, PLANE, 0, 0, tiled=True)]
    pallas_call x2, Pallas kernels: 13.6 us -> 16.9 us  [project(): pl.pallas_call(functools.partial(project_body, pieces), in_specs=[SMEM, V...]
    pallas_call x4, Pallas kernels: 15.5 us -> 12.2 us  [the longest x1 5.54 us: back_b(): pl.pallas_call(back_b_body, in_specs=[SMEM] + [VMEM] * 7, out_specs=ANYWH...]
    pallas_call x1, Pallas kernels: 0.29 us -> 1.92 us  [merge_b(): pl.pallas_call(merge_b_body, in_specs=[VMEM], out_specs=[VMEM] * 5, out_s...]
    unnamed x28 -> x30, local copies, waits for them, and re-layouts: 4.62 us -> 3.79 us
  transfers between devices with their start and end apart: 31 -> 31, of which waited for: 15 -> 15; matrix products, arithmetic and copies ran while one was open for 3% -> 2% of each run, Pallas kernels for 30% -> 29%
where the time goes in v9:
time: 148 us; the launch traced here: 147 us
  starting transfers between devices  53.2 us (36%)
  Pallas kernels  51.8 us (35%)
  waiting for transfers between devices  32.9 us (22%)
  local copies, waits for them, and re-layouts  7.04 us (5%)
    all_to_all x4, starting transfers between devices, over_plane(): return lax.all_to_all(value, PLANE, 0, 0, tiled=True)  22.5 us
    ppermute x18, waiting for transfers between devices, shifted(): return lax.ppermute(value, 'z', [(i, (i + by) % RING) for i in range(RING)])  21.5 us
    ppermute x18, starting transfers between devices, shifted(): return lax.ppermute(value, 'z', [(i, (i + by) % RING) for i in range(RING)])  20.5 us
    pallas_call x2, Pallas kernels, project(): pl.pallas_call(functools.partial(project_body, pieces), in_specs=[SMEM, V...  16.9 us
    pallas_call x2, Pallas kernels, weight_grad(): pl.pallas_call(weights_body, grid=(hidden // width,), in_specs=[block] *...  14.5 us
    ppermute x9, starting transfers between devices, swapped(): return lax.ppermute(value, 'c', [(0, 1), (1, 0)])  10.3 us
    all_to_all x4, waiting for transfers between devices, over_plane(): return lax.all_to_all(value, PLANE, 0, 0, tiled=True)  7.58 us
    pallas_call x1, Pallas kernels, attention(): pl.pallas_call(functools.partial(attend_body, tile), in_specs=[VMEM] * 6,...  6.26 us
  transfers between devices with their start and end apart: 31, of which 15 were waited for; matrix products, arithmetic and copies ran while one was open for 2% of the time, Pallas kernels for 29%

profile of v9, /device:TPU:1, one launch (start us, length us, event | category | flops | bytes accessed | tf_op | source)
XLA Modules:
  0.0 147.3 jit_solution(7520852238590858739)
XLA Ops:
  4.6 6.8 %all-to-all-start = ((bf16[16,32,512]{2,1,0:T(8,128)(2,1)}), bf16[16,32,512]{2,1,0:T(8,128)(2,1)S(1)}, u32[]{:S(2)}, u32[]{:S(2)}) async-start(bf16[16,32,512]{2,1,0:T(8,128)(2,1)} %broadcast_in_dim.18), calls=%async_computation | async-start | bytes 1048576 | tf_op jit(solution)/shard_map/all_to_all | solution.py:409
  12.2 3.8 %collective-permute-start.9 = (bf16[32,512]{1,0:T(8,128)(2,1)S(1)}, bf16[32,512]{1,0:T(8,128)(2,1)S(1)}, u32[]{:S(2)}, u32[]{:S(2)}) collective-permute-start(bf16[32,512]{1,0:T(8,128)(2,1)S(1)} %get-tuple-element.90), channel_id=1, source_target_pairs={{0,6},{2,0},{4,2},{6,4},{1,7},{3,1},{5,3},{7,5},{8,14},{10,8},{12,... | collective-permute-start | bytes 98312 | tf_op jit(solution)/shard_map/ppermute | solution.py:405
  17.0 3.5 %collective-permute-done.10 = bf16[32,512]{1,0:T(8,128)(2,1)S(1)} collective-permute-done((bf16[32,512]{1,0:T(8,128)(2,1)S(1)}, bf16[32,512]{1,0:T(8,128)(2,1)S(1)}, u32[]{:S(2)}, u32[]{:S(2)}) %collective-permute-start.10) | collective-permute-done | bytes 32800 | tf_op jit(solution)/shard_map/ppermute | solution.py:405
  23.7 5.2 %all-to-all-start.1 = ((bf16[16,4,32,512]{3,2,1,0:T(8,128)(2,1)}), bf16[16,4,32,512]{3,2,1,0:T(8,128)(2,1)S(1)}, u32[]{:S(2)}, u32[]{:S(2)}) async-start(bf16[16,4,32,512]{3,2,1,0:T(8,128)(2,1)} %broadcast_in_dim.19), calls=%async_computation.1 | async-start | bytes 4194304 | tf_op jit(solution)/shard_map/all_to_all | solution.py:409
  29.4 2.4 %collective-permute-start.4 = (bf16[8,32,512]{2,1,0:T(8,128)(2,1)S(1)}, bf16[8,32,512]{2,1,0:T(8,128)(2,1)S(1)}, u32[]{:S(2)}, u32[]{:S(2)}) collective-permute-start(bf16[8,32,512]{2,1,0:T(8,128)(2,1)S(1)} %get-tuple-element.87), channel_id=1, source_target_pairs={{0,6},{2,0},{4,2},{6,4},{1,7},{3,1},{5,3},{7,5},{8,14},{10,8},{12,... | collective-permute-start | bytes 786440 | tf_op jit(solution)/shard_map/ppermute | solution.py:405
  31.8 4.2 %collective-permute-done.1 = bf16[8,32,512]{2,1,0:T(8,128)(2,1)S(1)} collective-permute-done((bf16[8,32,512]{2,1,0:T(8,128)(2,1)S(1)}, bf16[8,32,512]{2,1,0:T(8,128)(2,1)S(1)}, u32[]{:S(2)}, u32[]{:S(2)}) %collective-permute-start.1) | collective-permute-done | bytes 262176 | tf_op jit(solution)/shard_map/ppermute | solution.py:405
  37.6 4.0 %collective-permute-done.2 = bf16[8,32,512]{2,1,0:T(8,128)(2,1)S(1)} collective-permute-done((bf16[8,32,512]{2,1,0:T(8,128)(2,1)S(1)}, bf16[8,32,512]{2,1,0:T(8,128)(2,1)S(1)}, u32[]{:S(2)}, u32[]{:S(2)}) %collective-permute-start.2) | collective-permute-done | bytes 262176 | tf_op jit(solution)/shard_map/ppermute | solution.py:405
  43.2 3.8 %collective-permute-done.5 = bf16[8,32,512]{2,1,0:T(8,128)(2,1)} collective-permute-done((bf16[8,32,512]{2,1,0:T(8,128)(2,1)S(1)}, bf16[8,32,512]{2,1,0:T(8,128)(2,1)}, u32[]{:S(2)}, u32[]{:S(2)}) %collective-permute-start.5) | collective-permute-done | bytes 262176 | tf_op jit(solution)/shard_map/ppermute | solution.py:405
  47.0 2.5 %collective-permute-done.6 = bf16[8,32,512]{2,1,0:T(8,128)(2,1)S(1)} collective-permute-done((bf16[8,32,512]{2,1,0:T(8,128)(2,1)S(1)}, bf16[8,32,512]{2,1,0:T(8,128)(2,1)S(1)}, u32[]{:S(2)}, u32[]{:S(2)}) %collective-permute-start.6) | collective-permute-done | bytes 262176 | tf_op jit(solution)/shard_map/ppermute | solution.py:405
  50.3 9.6 %project_a.1 = (bf16[256,512]{1,0:T(8,128)(2,1)S(1)}, bf16[256,512]{1,0:T(8,128)(2,1)S(1)}, f32[256,1]{1,0:T(8,128)S(1)}, bf16[256,4096]{1,0:T(8,128)(2,1)}) custom-call(s32[2]{0:T(128)S(1)} %pad_add_fusion.z_ref, f32[8,1,512]{2,1,0:T(1,128)S(1)} %bitcast.47, bf16[8,2,32,512]{3,2,1,0:T(8,128)(2,1)} %bitcast.54, bf16[4,2,32,512]{3,2,1,0:T(8,128)(2,1)} %bitcast.57, ...), custom_call_target="tpu_custom_call" | custom-call | flops 2147483648 | bytes 12582912 | tf_op jit(solution)/shard_map/project_a/pallas_call | solution.py:100
  60.5 7.3 %project_b.1 = (bf16[256,512]{1,0:T(8,128)(2,1)S(1)}, bf16[256,512]{1,0:T(8,128)(2,1)S(1)}, f32[256,1]{1,0:T(8,128)S(1)}, bf16[256,4096]{1,0:T(8,128)(2,1)}) custom-call(s32[2]{0:T(128)S(1)} %pad_add_fusion.z_ref, f32[8,1,512]{2,1,0:T(1,128)S(1)} %bitcast.48, bf16[8,2,4,32,512]{4,3,2,1,0:T(8,128)(2,1)S(1)} %bitcast.33, ...), custom_call_target="tpu_custom_call" | custom-call | flops 2147483648 | bytes 12582912 | tf_op jit(solution)/shard_map/project_b/pallas_call | solution.py:100
  67.9 4.2 %collective-permute-start.13 = (bf16[256,512]{1,0:T(8,128)(2,1)S(1)}, bf16[256,512]{1,0:T(8,128)(2,1)S(1)}, u32[]{:S(2)}, u32[]{:S(2)}) collective-permute-start(bf16[256,512]{1,0:T(8,128)(2,1)S(1)} %get-tuple-element.51), channel_id=1, source_target_pairs={{0,1},{1,0},{2,3},{3,2},{4,5},{5,4},{6,7},{7,6},{8,9},{9,8},{10,11... | collective-permute-start | bytes 786440 | tf_op jit(solution)/shard_map/ppermute | solution.py:401
  74.0 6.3 %attention.1 = (bf16[1024,256]{1,0:T(8,128)(2,1)}, bf16[1024,256]{1,0:T(8,128)(2,1)}, bf16[512,512]{1,0:T(8,128)(2,1)S(1)}, bf16[528,512]{1,0:T(8,128)(2,1)S(1)}, f32[1,512]{1,0:T(1,128)S(1)}) custom-call(bf16[1024,256]{1,0:T(8,128)(2,1)S(1)} %bitcast.51, bf16[1024,256]{1,0:T(8,128)(2,1)S(1)} %bitcast.52, bf16[256,512]{1,0:T(8,128)(2,1)S(1)} %copy-done.9, ...), custom_call_target="tpu_custom_call" | custom-call | flops 3221225472 | bytes 4194304 | tf_op jit(solution)/shard_map/attention/pallas_call | solution.py:181
  82.2 5.5 %back_b.1 = bf16[8,2,272,256]{3,2,1,0:T(8,128)(2,1)} custom-call(s32[2]{0:T(128)S(1)} %pad_add_fusion.z_ref, bf16[512,512]{1,0:T(8,128)(2,1)S(1)} %get-tuple-element.58.gnear_ref.own_ref, bf16[528,512]{1,0:T(8,128)(2,1)S(1)} %collective-permute-done.16.sib_ref, f32[1,512]{1,0:T(1,128)S(1)} %get-tuple-element.62.dots_ref, bf16[4096,256]{1,0:T(8,128)(2,1)S(1)} %bitcast.40, ...), custom_call_target="tpu_custom_call" | custom-call | flops 2147483648 | bytes 4194304 | tf_op jit(solution)/shard_map/back_b/pallas_call | solution.py:232
  87.7 6.9 %all-to-all-start.2 = ((bf16[16,272,256]{2,1,0:T(8,128)(2,1)}), bf16[16,272,256]{2,1,0:T(8,128)(2,1)}, u32[]{:S(2)}, u32[]{:S(2)}) async-start(bf16[16,272,256]{2,1,0:T(8,128)(2,1)} %bitcast.53), calls=%async_computation.2 | async-start | bytes 4456448 | tf_op jit(solution)/shard_map/all_to_all | solution.py:409
  96.2 4.7 %back_a.1 = (bf16[4,2,64,256]{3,2,1,0:T(8,128)(2,1)S(1)}, bf16[4,2,64,256]{3,2,1,0:T(8,128)(2,1)S(1)}, bf16[4,2,64,256]{3,2,1,0:T(8,128)(2,1)S(1)}, bf16[4,2,64,...) custom-call(s32[2]{0:T(128)S(1)} %pad_add_fusion.z_ref, ...), custom_call_target="tpu_custom_call" | custom-call | flops 2147483648 | bytes 4194304 | tf_op jit(solution)/shard_map/back_a/pallas_call | solution.py:266
  101.0 2.7 %collective-permute-start.20 = (bf16[4,2,64,256]{3,2,1,0:T(8,128)(2,1)S(1)}, bf16[4,2,64,256]{3,2,1,0:T(8,128)(2,1)S(1)}, u32[]{:S(2)}, u32[]{:S(2)}) collective-permute-start(bf16[4,2,64,256]{3,2,1,0:T(8,128)(2,1)S(1)} %get-tuple-element.70), channel_id=1, source_target_pairs={{0,6},{2,0},{4,2},{6,4},{1,7},{3,1},{5,3},{7,5},{8,14},{10,8},{12,... | collective-permute-start | bytes 786440 | tf_op jit(solution)/shard_map/ppermute | solution.py:405
  105.1 7.2 %key_grad.1 = f32[4096,256]{1,0:T(8,128)} custom-call(bf16[256,4096]{1,0:T(8,128)(2,1)} %get-tuple-element.56.near_a, bf16[256,4096]{1,0:T(8,128)(2,1)} %get-tuple-element.57.near_b, bf16[256,4096]{1,0:T(8,128)(2,1)} %collective-permute-done.14.far_a, bf16[256,4096]{1,0:T(8,128)(2,1)} %collective-permute-done.15.far_b, ...), custom_call_target="tpu_custom_call" | custom-call | flops 2147483648 | bytes 13631488 | tf_op jit(solution)/shard_map/key_grad/pallas_call | solution.py:286
  112.4 2.4 %collective-permute-start.22 = (bf16[4,2,64,256]{3,2,1,0:T(8,128)(2,1)S(1)}, bf16[4,2,64,256]{3,2,1,0:T(8,128)(2,1)S(1)}, u32[]{:S(2)}, u32[]{:S(2)}) collective-permute-start(bf16[4,2,64,256]{3,2,1,0:T(8,128)(2,1)S(1)} %add_convert_fusion.1), channel_id=1, source_target_pairs={{0,6},{2,0},{4,2},{6,4},{1,7},{3,1},{5,3},{7,5},{8,14},{10,8},{12,... | collective-permute-start | bytes 786440 | tf_op jit(solution)/shard_map/ppermute | solution.py:405
  115.0 7.3 %value_grad.1 = f32[4096,256]{1,0:T(8,128)} custom-call(bf16[256,4096]{1,0:T(8,128)(2,1)} %get-tuple-element.56.near_a, bf16[256,4096]{1,0:T(8,128)(2,1)} %get-tuple-element.57.near_b, bf16[256,4096]{1,0:T(8,128)(2,1)} %collective-permute-done.14.far_a, bf16[256,4096]{1,0:T(8,128)(2,1)} %collective-permute-done.15.far_b, ...), custom_call_target="tpu_custom_call" | custom-call | flops 2147483648 | bytes 13631488 | tf_op jit(solution)/shard_map/value_grad/pallas_call | solution.py:286
  123.4 6.0 %all-to-all-done.2.arrived_ref = bf16[16,272,256]{2,1,0:T(8,128)(2,1)} async-done(((bf16[16,272,256]{2,1,0:T(8,128)(2,1)}), bf16[16,272,256]{2,1,0:T(8,128)(2,1)}, u32[]{:S(2)}, u32[]{:S(2)}) %all-to-all-start.2) | async-done | bytes 2228256 | tf_op jit(solution)/shard_map/all_to_all | solution.py:409
  129.4 3.6 %all-to-all-start.3 = ((bf16[16,64,256]{2,1,0:T(8,128)(2,1)}), bf16[16,64,256]{2,1,0:T(8,128)(2,1)S(1)}, u32[]{:S(2)}, u32[]{:S(2)}) async-start(bf16[16,64,256]{2,1,0:T(8,128)(2,1)} %bitcast.29), calls=%async_computation.3 | async-start | bytes 1048576 | tf_op jit(solution)/shard_map/all_to_all | solution.py:409
  135.0 3.3 %collective-permute-start.24 = (bf16[80,256]{1,0:T(8,128)(2,1)S(1)}, bf16[80,256]{1,0:T(8,128)(2,1)S(1)}, u32[]{:S(2)}, u32[]{:S(2)}) collective-permute-start(bf16[80,256]{1,0:T(8,128)(2,1)S(1)} %get-tuple-element.79), channel_id=1, source_target_pairs={{0,4},{2,6},{4,0},{6,2},{1,5},{3,7},{5,1},{7,3},{8,12},{10,14},{12... | collective-permute-start | bytes 122888 | tf_op jit(solution)/shard_map/ppermute | solution.py:405
  142.1 2.9 %collective-permute-start.26 = (f32[64,256]{1,0:T(8,128)S(1)}, f32[64,256]{1,0:T(8,128)S(1)}, u32[]{:S(2)}, u32[]{:S(2)}) collective-permute-start(f32[64,256]{1,0:T(8,128)S(1)} %get-tuple-element.83), channel_id=1, source_target_pairs={{0,1},{1,0},{2,3},{3,2},{4,5},{5,4},{6,7},{7,6},{8,9},{9,8},{10,11... | collective-permute-start | bytes 196616 | tf_op jit(solution)/shard_map/ppermute | solution.py:401
  (91 shorter events, 30.4 us)
Async XLA Ops:
  4.6 17.6 %all-to-all-start = ((bf16[16,32,512]{2,1,0:T(8,128)(2,1)}), bf16[16,32,512]{2,1,0:T(8,128)(2,1)S(1)}, u32[]{:S(2)}, u32[]{:S(2)}) async-start(bf16[16,32,512]{2,1,0:T(8,128)(2,1)} %broadcast_in_dim.18), calls=%async_computation | async-start | bytes 1048576 | tf_op jit(solution)/shard_map/all_to_all | solution.py:409
  11.4 38.1 %collective-permute-start.7 = (bf16[4096,256]{1,0:T(8,128)(2,1)}, bf16[4096,256]{1,0:T(8,128)(2,1)}, u32[]{:S(2)}, u32[]{:S(2)}) collective-permute-start(bf16[4096,256]{1,0:T(8,128)(2,1)} %bitcast.37), channel_id=1, source_target_pairs={{0,1},{1,0},{2,3},{3,2},{4,5},{5,4},{6,7},{7,6},{8,9},{9,8},{10,11... | collective-permute-start | bytes 6291464 | tf_op jit(solution)/shard_map/ppermute | solution.py:401
  12.1 37.4 %collective-permute-start.8 = (bf16[4096,256]{1,0:T(8,128)(2,1)}, bf16[4096,256]{1,0:T(8,128)(2,1)}, u32[]{:S(2)}, u32[]{:S(2)}) collective-permute-start(bf16[4096,256]{1,0:T(8,128)(2,1)} %bitcast.42), channel_id=1, source_target_pairs={{0,1},{1,0},{2,3},{3,2},{4,5},{5,4},{6,7},{7,6},{8,9},{9,8},{10,11... | collective-permute-start | bytes 6291464 | tf_op jit(solution)/shard_map/ppermute | solution.py:401
  12.2 4.8 %collective-permute-start.9 = (bf16[32,512]{1,0:T(8,128)(2,1)S(1)}, bf16[32,512]{1,0:T(8,128)(2,1)S(1)}, u32[]{:S(2)}, u32[]{:S(2)}) collective-permute-start(bf16[32,512]{1,0:T(8,128)(2,1)S(1)} %get-tuple-element.90), channel_id=1, source_target_pairs={{0,6},{2,0},{4,2},{6,4},{1,7},{3,1},{5,3},{7,5},{8,14},{10,8},{12,... | collective-permute-start | bytes 98312 | tf_op jit(solution)/shard_map/ppermute | solution.py:405
  16.0 4.6 %collective-permute-start.11 = (bf16[32,512]{1,0:T(8,128)(2,1)S(1)}, bf16[32,512]{1,0:T(8,128)(2,1)S(1)}, u32[]{:S(2)}, u32[]{:S(2)}) collective-permute-start(bf16[32,512]{1,0:T(8,128)(2,1)S(1)} %get-tuple-element.90), channel_id=1, source_target_pairs={{0,2},{2,4},{4,6},{6,0},{1,3},{3,5},{5,7},{7,1},{8,10},{10,12},{12... | collective-permute-start | bytes 98312 | tf_op jit(solution)/shard_map/ppermute | solution.py:405
  23.7 36.8 %all-to-all-start.1 = ((bf16[16,4,32,512]{3,2,1,0:T(8,128)(2,1)}), bf16[16,4,32,512]{3,2,1,0:T(8,128)(2,1)S(1)}, u32[]{:S(2)}, u32[]{:S(2)}) async-start(bf16[16,4,32,512]{3,2,1,0:T(8,128)(2,1)} %broadcast_in_dim.19), calls=%async_computation.1 | async-start | bytes 4194304 | tf_op jit(solution)/shard_map/all_to_all | solution.py:409
  29.0 7.0 %collective-permute-start.1 = (bf16[8,32,512]{2,1,0:T(8,128)(2,1)S(1)}, bf16[8,32,512]{2,1,0:T(8,128)(2,1)S(1)}, u32[]{:S(2)}, u32[]{:S(2)}) collective-permute-start(bf16[8,32,512]{2,1,0:T(8,128)(2,1)S(1)} %get-tuple-element.88), channel_id=1, source_target_pairs={{0,2},{2,4},{4,6},{6,0},{1,3},{3,5},{5,7},{7,1},{8,10},{10,12},{12... | collective-permute-start | bytes 786440 | tf_op jit(solution)/shard_map/ppermute | solution.py:405
  29.4 8.2 %collective-permute-start.4 = (bf16[8,32,512]{2,1,0:T(8,128)(2,1)S(1)}, bf16[8,32,512]{2,1,0:T(8,128)(2,1)S(1)}, u32[]{:S(2)}, u32[]{:S(2)}) collective-permute-start(bf16[8,32,512]{2,1,0:T(8,128)(2,1)S(1)} %get-tuple-element.87), channel_id=1, source_target_pairs={{0,6},{2,0},{4,2},{6,4},{1,7},{3,1},{5,3},{7,5},{8,14},{10,8},{12,... | collective-permute-start | bytes 786440 | tf_op jit(solution)/shard_map/ppermute | solution.py:405
  31.7 9.8 %collective-permute-start.2 = (bf16[8,32,512]{2,1,0:T(8,128)(2,1)S(1)}, bf16[8,32,512]{2,1,0:T(8,128)(2,1)S(1)}, u32[]{:S(2)}, u32[]{:S(2)}) collective-permute-start(bf16[8,32,512]{2,1,0:T(8,128)(2,1)S(1)} %get-tuple-element.87), channel_id=1, source_target_pairs={{0,2},{2,4},{4,6},{6,0},{1,3},{3,5},{5,7},{7,1},{8,10},{10,12},{12... | collective-permute-start | bytes 786440 | tf_op jit(solution)/shard_map/ppermute | solution.py:405
  36.0 7.3 %collective-permute-start.3 = (bf16[8,32,512]{2,1,0:T(8,128)(2,1)S(1)}, bf16[8,32,512]{2,1,0:T(8,128)(2,1)}, u32[]{:S(2)}, u32[]{:S(2)}) collective-permute-start(bf16[8,32,512]{2,1,0:T(8,128)(2,1)S(1)} %get-tuple-element.88), channel_id=1, source_target_pairs={{0,6},{2,0},{4,2},{6,4},{1,7},{3,1},{5,3},{7,5},{8,14},{10,8},{12,... | collective-permute-start | bytes 786440 | tf_op jit(solution)/shard_map/ppermute | solution.py:405
  37.5 9.5 %collective-permute-start.5 = (bf16[8,32,512]{2,1,0:T(8,128)(2,1)S(1)}, bf16[8,32,512]{2,1,0:T(8,128)(2,1)}, u32[]{:S(2)}, u32[]{:S(2)}) collective-permute-start(bf16[8,32,512]{2,1,0:T(8,128)(2,1)S(1)} %collective-permute-done.1), channel_id=1, source_target_pairs={{0,2},{2,4},{4,6},{6,0},{1,3},{3,5},{5,7},{7,1},{8,10},{10,12},{12... | collective-permute-start | bytes 786440 | tf_op jit(solution)/shard_map/ppermute | solution.py:405
  41.6 8.0 %collective-permute-start.6 = (bf16[8,32,512]{2,1,0:T(8,128)(2,1)S(1)}, bf16[8,32,512]{2,1,0:T(8,128)(2,1)S(1)}, u32[]{:S(2)}, u32[]{:S(2)}) collective-permute-start(bf16[8,32,512]{2,1,0:T(8,128)(2,1)S(1)} %collective-permute-done.4), channel_id=1, source_target_pairs={{0,6},{2,0},{4,2},{6,4},{1,7},{3,1},{5,3},{7,5},{8,14},{10,8},{12,... | collective-permute-start | bytes 786440 | tf_op jit(solution)/shard_map/ppermute | solution.py:405
  67.9 5.3 %collective-permute-start.13 = (bf16[256,512]{1,0:T(8,128)(2,1)S(1)}, bf16[256,512]{1,0:T(8,128)(2,1)S(1)}, u32[]{:S(2)}, u32[]{:S(2)}) collective-permute-start(bf16[256,512]{1,0:T(8,128)(2,1)S(1)} %get-tuple-element.51), channel_id=1, source_target_pairs={{0,1},{1,0},{2,3},{3,2},{4,5},{5,4},{6,7},{7,6},{8,9},{9,8},{10,11... | collective-permute-start | bytes 786440 | tf_op jit(solution)/shard_map/ppermute | solution.py:401
  73.2 31.3 %collective-permute-start.15 = (bf16[256,4096]{1,0:T(8,128)(2,1)}, bf16[256,4096]{1,0:T(8,128)(2,1)}, u32[]{:S(2)}, u32[]{:S(2)}) collective-permute-start(bf16[256,4096]{1,0:T(8,128)(2,1)} %get-tuple-element.57.near_b), channel_id=1, source_target_pairs={{0,1},{1,0},{2,3},{3,2},{4,5},{5,4},{6,7},{7,6},{8,9},{9,8},{10,11... | collective-permute-start | bytes 6291464 | tf_op jit(solution)/shard_map/ppermute | solution.py:401
  73.6 31.5 %collective-permute-start.14 = (bf16[256,4096]{1,0:T(8,128)(2,1)}, bf16[256,4096]{1,0:T(8,128)(2,1)}, u32[]{:S(2)}, u32[]{:S(2)}) collective-permute-start(bf16[256,4096]{1,0:T(8,128)(2,1)} %get-tuple-element.56.near_a), channel_id=1, source_target_pairs={{0,1},{1,0},{2,3},{3,2},{4,5},{5,4},{6,7},{7,6},{8,9},{9,8},{10,11... | collective-permute-start | bytes 6291464 | tf_op jit(solution)/shard_map/ppermute | solution.py:401
  87.7 41.7 %all-to-all-start.2 = ((bf16[16,272,256]{2,1,0:T(8,128)(2,1)}), bf16[16,272,256]{2,1,0:T(8,128)(2,1)}, u32[]{:S(2)}, u32[]{:S(2)}) async-start(bf16[16,272,256]{2,1,0:T(8,128)(2,1)} %bitcast.53), calls=%async_computation.2 | async-start | bytes 4456448 | tf_op jit(solution)/shard_map/all_to_all | solution.py:409
  100.9 11.5 %collective-permute-start.19 = (bf16[4,2,64,256]{3,2,1,0:T(8,128)(2,1)S(1)}, bf16[4,2,64,256]{3,2,1,0:T(8,128)(2,1)S(1)}, u32[]{:S(2)}, u32[]{:S(2)}) collective-permute-start(bf16[4,2,64,256]{3,2,1,0:T(8,128)(2,1)S(1)} %get-tuple-element.69), channel_id=1, source_target_pairs={{0,2},{2,4},{4,6},{6,0},{1,3},{3,5},{5,7},{7,1},{8,10},{10,12},{12... | collective-permute-start | bytes 786440 | tf_op jit(solution)/shard_map/ppermute | solution.py:405
  101.0 11.4 %collective-permute-start.20 = (bf16[4,2,64,256]{3,2,1,0:T(8,128)(2,1)S(1)}, bf16[4,2,64,256]{3,2,1,0:T(8,128)(2,1)S(1)}, u32[]{:S(2)}, u32[]{:S(2)}) collective-permute-start(bf16[4,2,64,256]{3,2,1,0:T(8,128)(2,1)S(1)} %get-tuple-element.70), channel_id=1, source_target_pairs={{0,6},{2,0},{4,2},{6,4},{1,7},{3,1},{5,3},{7,5},{8,14},{10,8},{12,... | collective-permute-start | bytes 786440 | tf_op jit(solution)/shard_map/ppermute | solution.py:405
  103.6 18.6 %collective-permute-start.17 = (bf16[4,2,64,256]{3,2,1,0:T(8,128)(2,1)S(1)}, bf16[4,2,64,256]{3,2,1,0:T(8,128)(2,1)S(1)}, u32[]{:S(2)}, u32[]{:S(2)}) collective-permute-start(bf16[4,2,64,256]{3,2,1,0:T(8,128)(2,1)S(1)} %get-tuple-element.65), channel_id=1, source_target_pairs={{0,6},{2,0},{4,2},{6,4},{1,7},{3,1},{5,3},{7,5},{8,14},{10,8},{12,... | collective-permute-start | bytes 786440 | tf_op jit(solution)/shard_map/ppermute | solution.py:405
  104.5 17.7 %collective-permute-start.18 = (bf16[4,2,64,256]{3,2,1,0:T(8,128)(2,1)S(1)}, bf16[4,2,64,256]{3,2,1,0:T(8,128)(2,1)S(1)}, u32[]{:S(2)}, u32[]{:S(2)}) collective-permute-start(bf16[4,2,64,256]{3,2,1,0:T(8,128)(2,1)S(1)} %get-tuple-element.66), channel_id=1, source_target_pairs={{0,2},{2,4},{4,6},{6,0},{1,3},{3,5},{5,7},{7,1},{8,10},{10,12},{12... | collective-permute-start | bytes 786440 | tf_op jit(solution)/shard_map/ppermute | solution.py:405
  112.4 9.8 %collective-permute-start.22 = (bf16[4,2,64,256]{3,2,1,0:T(8,128)(2,1)S(1)}, bf16[4,2,64,256]{3,2,1,0:T(8,128)(2,1)S(1)}, u32[]{:S(2)}, u32[]{:S(2)}) collective-permute-start(bf16[4,2,64,256]{3,2,1,0:T(8,128)(2,1)S(1)} %add_convert_fusion.1), channel_id=1, source_target_pairs={{0,6},{2,0},{4,2},{6,4},{1,7},{3,1},{5,3},{7,5},{8,14},{10,8},{12,... | collective-permute-start | bytes 786440 | tf_op jit(solution)/shard_map/ppermute | solution.py:405
  114.9 7.4 %collective-permute-start.21 = (bf16[4,2,64,256]{3,2,1,0:T(8,128)(2,1)S(1)}, bf16[4,2,64,256]{3,2,1,0:T(8,128)(2,1)S(1)}, u32[]{:S(2)}, u32[]{:S(2)}) collective-permute-start(bf16[4,2,64,256]{3,2,1,0:T(8,128)(2,1)S(1)} %add_convert_fusion.3), channel_id=1, source_target_pairs={{0,2},{2,4},{4,6},{6,0},{1,3},{3,5},{5,7},{7,1},{8,10},{10,12},{12... | collective-permute-start | bytes 786440 | tf_op jit(solution)/shard_map/ppermute | solution.py:405
  129.4 16.6 %all-to-all-start.3 = ((bf16[16,64,256]{2,1,0:T(8,128)(2,1)}), bf16[16,64,256]{2,1,0:T(8,128)(2,1)S(1)}, u32[]{:S(2)}, u32[]{:S(2)}) async-start(bf16[16,64,256]{2,1,0:T(8,128)(2,1)} %bitcast.29), calls=%async_computation.3 | async-start | bytes 1048576 | tf_op jit(solution)/shard_map/all_to_all | solution.py:409
  135.0 5.1 %collective-permute-start.24 = (bf16[80,256]{1,0:T(8,128)(2,1)S(1)}, bf16[80,256]{1,0:T(8,128)(2,1)S(1)}, u32[]{:S(2)}, u32[]{:S(2)}) collective-permute-start(bf16[80,256]{1,0:T(8,128)(2,1)S(1)} %get-tuple-element.79), channel_id=1, source_target_pairs={{0,4},{2,6},{4,0},{6,2},{1,5},{3,7},{5,1},{7,3},{8,12},{10,14},{12... | collective-permute-start | bytes 122888 | tf_op jit(solution)/shard_map/ppermute | solution.py:405
  (22 other events, 158.1 us)

commit v10 on v9

--- a/solution.py
+++ b/solution.py
@@ -54,9 +54,59 @@
     return pl.CostEstimate(flops=flops, bytes_accessed=int(mib * MIB), transcendentals=transcendentals)
 
 
+def copies_body(count, *refs):
+    pieces, out_ref, held, sem = refs[:-3], refs[-3], refs[-2], refs[-1]
+    for i, piece in enumerate(pieces):
+        held[i] = piece[...]
+    copies = [pltpu.make_async_copy(held, out_ref.at[j], sem.at[j]) for j in range(count)]
+    for copy in copies:
+        copy.start()
+    for copy in copies:
+        copy.wait()
+
+
+def copies_of(pieces, count, name):
+    shape = (len(pieces), *pieces[0].shape)
+    return pl.pallas_call(
+        functools.partial(copies_body, count),
+        in_specs=[VMEM] * len(pieces),
+        out_specs=ANYWHERE,
+        out_shape=pltpu.HBM((count, *shape), BF16),
+        scratch_shapes=[pltpu.VMEM(shape, BF16), pltpu.SemaphoreType.DMA((count,))],
+        compiler_params=limits(4),
+        cost_estimate=cost(0, 2),
+        name=name,
+    )(*pieces)
+
+
+def stage_body(place_ref, *refs):
+    sources, outs = refs[:-2], refs[-2:]
+    for j, out in enumerate(outs):
+        half = place_ref[1] if j == 0 else 1 - place_ref[1]
+        at = pl.ds(pl.multiple_of(half * HD, HD), HD)
+        for i, source in enumerate(sources):
+            out[0, :, i * HD : (i + 1) * HD] = source[at, :]
+
+
+def staged(place, weights):
+    count, blocks = len(weights), weights[0].shape[0] // (2 * HD)
+    block = pl.BlockSpec((1, HD, count * HD), lambda i: (i, 0, 0))
+    out = pltpu.HBM((blocks, HD, count * HD), BF16)
+    return pl.pallas_call(
+        stage_body,
+        grid=(blocks,),
+        in_specs=[SMEM] + [pl.BlockSpec((2 * HD, HD), lambda i: (i, 0))] * count,
+        out_specs=[block] * 2,
+        out_shape=[out] * 2,
+        compiler_params=limits(8),
+        cost_estimate=cost(0, 16),
+        name="stage",
+    )(place, *[in_hbm(w) for w in weights])
+
+
 def project_body(pieces, z_ref, gain_ref, *refs):
     xs = refs[: len(pieces)]
-    w_refs, refs = refs[len(pieces) : len(pieces) + 4], refs[len(pieces) + 4 :]
+    w_refs, refs = refs[len(pieces) : len(pieces) + 2], refs[len(pieces) + 2 :]
     own_ref, sib_ref, scale_ref, normed_ref, held, rows_low, weights, x_sem, w_sem, out_sem = refs
     blocks, segs, part, width = held.shape
     rows = segs * part
@@ -86,10 +136,14 @@
         rows_low[:, p * width : (p + 1) * width] = (wide * scale * gain_ref[p]).astype(BF16)
     out = pltpu.make_async_copy(rows_low, normed_ref, out_sem)
     out.start()
+    total = 0.0
     for i, load in enumerate(loads):
         load.wait()
-        out_ref, at = (own_ref, sib_ref)[i // 2], (i % 2) * HD
-        out_ref[:, at : at + HD] = nn(rows_low[...], weights[i]).astype(BF16)
+        first = z_ref[1] if i == 0 else 1 - z_ref[1]
+        columns = beside(*[rows_low[:, pl.ds(pl.multiple_of((2 * p + first) * HD, HD), HD)] for p in range(blocks)])
+        total += nn(columns, weights[i].reshape(blocks * HD, 4 * HD))
+    own_ref[...] = total[:, : 2 * HD].astype(BF16)
+    sib_ref[...] = total[:, 2 * HD :].astype(BF16)
     out.wait()
 
 
@@ -99,7 +153,7 @@
     rows = segs * part
     return pl.pallas_call(
         functools.partial(project_body, pieces),
-        in_specs=[SMEM, VMEM] + [ANYWHERE] * (len(xs) + 4),
+        in_specs=[SMEM, VMEM] + [ANYWHERE] * (len(xs) + 2),
         out_specs=[VMEM, VMEM, VMEM, ANYWHERE],
         out_shape=[
             jax.ShapeDtypeStruct((rows, 2 * HD), BF16),
@@ -110,9 +164,9 @@
         scratch_shapes=[
             pltpu.VMEM((blocks, segs, part, width), BF16),
             pltpu.VMEM((rows, blocks * width), BF16),
-            pltpu.VMEM((4, blocks * width, HD), BF16),
+            pltpu.VMEM((2, blocks, HD, 4 * HD), BF16),
             pltpu.SemaphoreType.DMA((2 * len(xs),)),
-            pltpu.SemaphoreType.DMA((4,)),
+            pltpu.SemaphoreType.DMA((2,)),
             pltpu.SemaphoreType.DMA(()),
         ],
         compiler_params=limits(24),
@@ -195,14 +249,11 @@
     )(q, dc, near_a, near_b, far_a, far_b)
 
 
-def feature_block(z, rows, weights, feature_half, distance, side):
-    block = side * RING + lax.rem(z + distance, RING)
-    at = pl.ds(pl.multiple_of((2 * block + feature_half) * HD, HD), HD)
-    return nt(rows, beside(*[w[at, :] for w in weights])).astype(BF16)
-
-
-def back_b_body(z_ref, own_ref, sib_ref, dots_ref, ko, vo, ks, vs, out_ref, stage, out_sem):
-    z, core = z_ref[0], z_ref[1]
+def feature_block(z, rows, w_ref, distance, side):
+    return nt(rows, w_ref[side * RING + lax.rem(z + distance, RING)]).astype(BF16)
+
+
+def back_b_body(z_ref, own_ref, sib_ref, dots_ref, w_ref, out_ref, stage, out_sem):
     half = own_ref.shape[0]
     segs = out_ref.shape[0]
     part = half // segs // 2
@@ -211,7 +262,7 @@
     for distance in range(RING):
         at = distance * 2 * part
         for side in range(2):
-            value = feature_block(z, rows, (ko, vo, ks, vs), 1 - core, distance, side).reshape(2, segs, part, HD)
+            value = feature_block(z_ref[0], rows, w_ref, distance, side).reshape(2, segs, part, HD)
             for k in range(2):
                 stage[:, side, at + k * part : at + (k + 1) * part] = value[k]
         size = 2 * part
@@ -231,7 +282,7 @@
     shape = (segs, 2, RING * rows // segs + EXTRA, HD)
     return pl.pallas_call(
         back_b_body,
-        in_specs=[SMEM] + [VMEM] * 7,
+        in_specs=[SMEM] + [VMEM] * 4,
         out_specs=ANYWHERE,
         out_shape=pltpu.HBM(shape, BF16),
         scratch_shapes=[
@@ -241,18 +292,17 @@
         compiler_params=limits(16),
         cost_estimate=cost(2 * rows * 8 * HD * 4 * HD, 4),
         name="back_b",
-    )(z, own, sib, dots, *[in_vmem(w) for w in weights])
-
-
-def back_a_body(z_ref, own_ref, sib_ref, ko, vo, ks, vs, *outs):
-    z, core = z_ref[0], z_ref[1]
+    )(z, own, sib, dots, in_vmem(weights))
+
+
+def back_a_body(z_ref, own_ref, sib_ref, w_ref, *outs):
     rows = beside(own_ref[...], sib_ref[: own_ref.shape[0]])
     segs = outs[-1].shape[0]
     part = rows.shape[0] // segs // 2
     lands = {2: ((0, 0), (1, segs // 2)), 1: ((2, 0), (3, segs // 2)), 3: ((4, 0), (5, segs // 2)), 0: ((6, 0),)}
     for distance in (2, 1, 3, 0):
         for side in range(2):
-            value = feature_block(z, rows, (ko, vo, ks, vs), core, distance, side).reshape(2, segs, part, HD)
+            value = feature_block(z_ref[0], rows, w_ref, distance, side).reshape(2, segs, part, HD)
             for index, first in lands[distance]:
                 for k in range(2):
                     count = outs[index].shape[0]
@@ -265,13 +315,13 @@
     full = jax.ShapeDtypeStruct((segs, 2, rows // segs, HD), BF16)
     return pl.pallas_call(
         back_a_body,
-        in_specs=[SMEM] + [VMEM] * 6,
+        in_specs=[SMEM] + [VMEM] * 3,
         out_specs=[VMEM] * 7,
         out_shape=[half] * 6 + [full],
         compiler_params=limits(16),
         cost_estimate=cost(2 * rows * 8 * HD * 4 * HD, 4),
         name="back_a",
-    )(z, own, sib, *[in_vmem(w) for w in weights])
+    )(z, own, sib, in_vmem(weights))
 
 
 def weights_body(near_a, near_b, far_a, far_b, gnear_ref, gfar_ref, out_ref):
@@ -429,10 +479,10 @@
     mine = lax.dynamic_index_in_dim(halves, core, 0, keepdims=False)
     other = swapped(lax.dynamic_index_in_dim(halves, 1 - core, 0, keepdims=False))
     block = jnp.where(core == 0, beside(mine, other), beside(other, mine))
-    first_a = over_plane(jnp.broadcast_to(block[:part], (plane, part, width)))
+    first_a = over_plane(copies_of([block[:part]], plane, "copies_a").reshape(plane, part, width))
     high = block[part:]
-    near_z = jnp.stack([high, shifted(high, -1), shifted(high, 2), shifted(high, 1)])
-    all_b = over_plane(jnp.broadcast_to(near_z, (plane, RING, part, width)))
+    near_z = [high, shifted(high, -1), shifted(high, 2), shifted(high, 1)]
+    all_b = over_plane(copies_of(near_z, plane, "copies_b"))
     all_b = all_b.reshape(segs, 2, RING, part, width)
     low_0, high_0 = first_a[: plane // 2], first_a[plane // 2 :]
     low_3, high_1 = shifted(low_0, 1), shifted(high_0, -1)
@@ -441,7 +491,7 @@
     deep = lambda value: value.reshape(segs // 2, 2, part, width)
 
     key_own, value_own = after((key_weight[0], value_weight[0]), block)
-    weights = (key_own, value_own, swapped(key_own), swapped(value_own))
+    weights = staged(z_array, (key_own, value_own, swapped(key_own), swapped(value_own)))
 
     top = segs // 2
     pieces_a = [(0, 0, None), (3, 0, None), (3, top, None), (1, 0, None), (1, top, None), (2, 0, None), (2, top, None)]
@@ -458,10 +508,10 @@
     context, query_grad, gnear, gfar, near_dots = attention(queries[0], context_grad[0], own_a, own_b, far_a, far_b)
     gsib = swapped(gfar)
 
-    parts_b = back_b(z_array, gnear, gsib, near_dots, weights, segs)
+    parts_b = back_b(z_array, gnear, gsib, near_dots, weights[1], segs)
     arrived_b = over_plane(parts_b.reshape(plane, RING * half + EXTRA, HD))
     z_later, = after((z_array,), parts_b)
-    opp_low, opp_high, up_low, up_high, down_low, down_high, kept = back_a(z_later, gnear, gsib, weights, segs)
+    opp_low, opp_high, up_low, up_high, down_low, down_high, kept = back_a(z_later, gnear, gsib, weights[0], segs)
     from_low, from_high = shifted(opp_low, 1), shifted(opp_high, -1)
     got_high, got_low = shifted(up_high, 1), shifted(down_low, -1)
     all_normed = (normed_a, normed_b, normed_far_a, normed_far_b)

time: 148 us -> 144 us (0.973)
  waiting for transfers between devices: 32.9 us -> 21.6 us
  Pallas kernels: 51.8 us -> 56 us
  starting transfers between devices: 53.2 us -> 56.7 us
  local copies, waits for them, and re-layouts: 7.04 us -> 5.44 us
    ppermute x18, waiting for transfers between devices: 21.5 us -> 8.84 us  [shifted(): return lax.ppermute(value, 'z', [(i, (i + by) % RING) for i in range(RING)])]
    pallas_call x2 -> x5, Pallas kernels: 10.2 us -> 18.3 us  [the longest x1 9.05 us: staged(): pl.pallas_call(stage_body, grid=(blocks,), in_specs=[SMEM] + [pl.BlockSpe...]
    broadcast_in_dim x2 -> x0, local copies, waits for them, and re-layouts: 2.42 us -> none  [the longest x1 1.57 us: local(): all_b = over_plane(jnp.broadcast_to(near_z, (plane, RING, part, width)))]
    pallas_call x2, Pallas kernels: 16.9 us -> 14.7 us  [project(): pl.pallas_call(functools.partial(project_body, pieces), in_specs=[SMEM, V...]
    ppermute x9, starting transfers between devices: 10.3 us -> 12.1 us  [swapped(): return lax.ppermute(value, 'c', [(0, 1), (1, 0)])]
    pallas_call x1, Pallas kernels: 1.92 us -> 0.29 us  [merge_b(): pl.pallas_call(merge_b_body, in_specs=[VMEM], out_specs=[VMEM] * 5, out_s...]
    unnamed x30 -> x26, local copies, waits for them, and re-layouts: 3.79 us -> 4.61 us
  transfers between devices with their start and end apart: 31 -> 31, of which waited for: 15 -> 11; matrix products, arithmetic and copies ran while one was open for 2% -> 1% of each run, Pallas kernels for 29% -> 33%
where the time goes in v10:
time: 144 us; the launch traced here: 142 us
  starting transfers between devices  56.7 us (39%)
  Pallas kernels  56 us (39%)
  waiting for transfers between devices  21.6 us (15%)
  local copies, waits for them, and re-layouts  5.44 us (4%)
    all_to_all x4, starting transfers between devices, over_plane(): return lax.all_to_all(value, PLANE, 0, 0, tiled=True)  23 us
    ppermute x18, starting transfers between devices, shifted(): return lax.ppermute(value, 'z', [(i, (i + by) % RING) for i in range(RING)])  21.7 us
    pallas_call x2, Pallas kernels, project(): pl.pallas_call(functools.partial(project_body, pieces), in_specs=[SMEM, V...  14.7 us
    pallas_call x2, Pallas kernels, weight_grad(): pl.pallas_call(weights_body, grid=(hidden // width,), in_specs=[block] *...  14.5 us
    ppermute x9, starting transfers between devices, swapped(): return lax.ppermute(value, 'c', [(0, 1), (1, 0)])  12.1 us
    pallas_call x1, Pallas kernels, staged(): pl.pallas_call(stage_body, grid=(blocks,), in_specs=[SMEM] + [pl.BlockSpe...  9.05 us
    ppermute x18, waiting for transfers between devices, shifted(): return lax.ppermute(value, 'z', [(i, (i + by) % RING) for i in range(RING)])  8.84 us
    all_to_all x4, waiting for transfers between devices, over_plane(): return lax.all_to_all(value, PLANE, 0, 0, tiled=True)  8 us
  transfers between devices with their start and end apart: 31, of which 11 were waited for; matrix products, arithmetic and copies ran while one was open for 1% of the time, Pallas kernels for 33%

profile of v10, /device:TPU:1, one launch (start us, length us, event | category | flops | bytes accessed | tf_op | source)
XLA Modules:
  0.0 142.0 jit_solution(11921016508337299749)
XLA Ops:
  5.1 6.8 %all-to-all-start = ((bf16[16,32,512]{2,1,0:T(8,128)(2,1)}), bf16[16,32,512]{2,1,0:T(8,128)(2,1)S(1)}, u32[]{:S(2)}, u32[]{:S(2)}) async-start(bf16[16,32,512]{2,1,0:T(8,128)(2,1)} %bitcast.44), calls=%async_computation | async-start | bytes 1048576 | tf_op jit(solution)/shard_map/all_to_all | solution.py:459
  12.5 3.6 %collective-permute-start.10 = (bf16[32,512]{1,0:T(8,128)(2,1)S(1)}, bf16[32,512]{1,0:T(8,128)(2,1)S(1)}, u32[]{:S(2)}, u32[]{:S(2)}) collective-permute-start(bf16[32,512]{1,0:T(8,128)(2,1)S(1)} %get-tuple-element.93.refs_0_), channel_id=1, source_target_pairs={{0,4},{2,6},{4,0},{6,2},{1,5},{3,7},{5,1},{7,3},{8,12},{10,14},{12... | collective-permute-start | bytes 98312 | tf_op jit(solution)/shard_map/ppermute | solution.py:455
  16.8 1.9 %collective-permute-start.9 = (bf16[32,512]{1,0:T(8,128)(2,1)S(1)}, bf16[32,512]{1,0:T(8,128)(2,1)S(1)}, u32[]{:S(2)}, u32[]{:S(2)}) collective-permute-start(bf16[32,512]{1,0:T(8,128)(2,1)S(1)} %get-tuple-element.93.refs_0_), channel_id=1, source_target_pairs={{0,6},{2,0},{4,2},{6,4},{1,7},{3,1},{5,3},{7,5},{8,14},{10,8},{12,... | collective-permute-start | bytes 98312 | tf_op jit(solution)/shard_map/ppermute | solution.py:455
  22.9 5.6 %all-to-all-start.1 = ((bf16[16,4,32,512]{3,2,1,0:T(8,128)(2,1)}), bf16[16,4,32,512]{3,2,1,0:T(8,128)(2,1)S(1)}, u32[]{:S(2)}, u32[]{:S(2)}) async-start(bf16[16,4,32,512]{3,2,1,0:T(8,128)(2,1)} %copies_b.1), calls=%async_computation.1 | async-start | bytes 4194304 | tf_op jit(solution)/shard_map/all_to_all | solution.py:459
  28.6 2.9 %collective-permute-start.4 = (bf16[8,32,512]{2,1,0:T(8,128)(2,1)S(1)}, bf16[8,32,512]{2,1,0:T(8,128)(2,1)}, u32[]{:S(2)}, u32[]{:S(2)}) collective-permute-start(bf16[8,32,512]{2,1,0:T(8,128)(2,1)S(1)} %get-tuple-element.91), channel_id=1, source_target_pairs={{0,6},{2,0},{4,2},{6,4},{1,7},{3,1},{5,3},{7,5},{8,14},{10,8},{12,... | collective-permute-start | bytes 786440 | tf_op jit(solution)/shard_map/ppermute | solution.py:455
  31.5 4.6 %collective-permute-done.1 = bf16[8,32,512]{2,1,0:T(8,128)(2,1)S(1)} collective-permute-done((bf16[8,32,512]{2,1,0:T(8,128)(2,1)S(1)}, bf16[8,32,512]{2,1,0:T(8,128)(2,1)S(1)}, u32[]{:S(2)}, u32[]{:S(2)}) %collective-permute-start.1) | collective-permute-done | bytes 262176 | tf_op jit(solution)/shard_map/ppermute | solution.py:455
  37.6 2.4 %collective-permute-start.6 = (bf16[8,32,512]{2,1,0:T(8,128)(2,1)}, bf16[8,32,512]{2,1,0:T(8,128)(2,1)}, u32[]{:S(2)}, u32[]{:S(2)}) collective-permute-start(bf16[8,32,512]{2,1,0:T(8,128)(2,1)} %collective-permute-done.4), channel_id=1, source_target_pairs={{0,6},{2,0},{4,2},{6,4},{1,7},{3,1},{5,3},{7,5},{8,14},{10,8},{12,... | collective-permute-start | bytes 786440 | tf_op jit(solution)/shard_map/ppermute | solution.py:455
  40.0 9.0 %stage.1 = (bf16[8,256,1024]{2,1,0:T(8,128)(2,1)}, bf16[8,256,1024]{2,1,0:T(8,128)(2,1)}) custom-call(s32[2]{0:T(128)S(1)} %pad_add_fusion.place_ref.z_ref, bf16[4096,256]{1,0:T(8,128)(2,1)} %bitcast.46, bf16[4096,256]{1,0:T(8,128)(2,1)} %bitcast.48, bf16[4096,256]{1,0:T(8,128)(2,1)} %collective-permute-done.7.refs_2_, ...), custom_call_target="tpu_custom_call" | custom-call | bytes 16777216 | tf_op jit(solution)/shard_map/stage/pallas_call | solution.py:95
  49.1 7.4 %project_a.1 = (bf16[256,512]{1,0:T(8,128)(2,1)S(1)}, bf16[256,512]{1,0:T(8,128)(2,1)S(1)}, f32[256,1]{1,0:T(8,128)S(1)}, bf16[256,4096]{1,0:T(8,128)(2,1)}) custom-call(s32[2]{0:T(128)S(1)} %pad_add_fusion.place_ref.z_ref, f32[8,1,512]{2,1,0:T(1,128)S(1)} %bitcast.33, bf16[8,2,32,512]{3,2,1,0:T(8,128)(2,1)} %bitcast.39, bf16[4,2,32,512]{3,2,1,0:T(8,128)(2,1)} %bitcast.49, ...), custom_call_target="tpu_custom_call" | custom-call | flops 2147483648 | bytes 12582912 | tf_op jit(solution)/shard_map/project_a/pallas_call | solution.py:154
  57.2 7.4 %project_b.1 = (bf16[256,512]{1,0:T(8,128)(2,1)S(1)}, bf16[256,512]{1,0:T(8,128)(2,1)S(1)}, f32[256,1]{1,0:T(8,128)S(1)}, bf16[256,4096]{1,0:T(8,128)(2,1)}) custom-call(s32[2]{0:T(128)S(1)} %pad_add_fusion.place_ref.z_ref, f32[8,1,512]{2,1,0:T(1,128)S(1)} %bitcast.34, bf16[8,2,4,32,512]{4,3,2,1,0:T(8,128)(2,1)S(1)} %bitcast.29, ...), custom_call_target="tpu_custom_call" | custom-call | flops 2147483648 | bytes 12582912 | tf_op jit(solution)/shard_map/project_b/pallas_call | solution.py:154
  65.2 6.2 %collective-permute-start.13 = (bf16[256,512]{1,0:T(8,128)(2,1)S(1)}, bf16[256,512]{1,0:T(8,128)(2,1)S(1)}, u32[]{:S(2)}, u32[]{:S(2)}) collective-permute-start(bf16[256,512]{1,0:T(8,128)(2,1)S(1)} %get-tuple-element.55), channel_id=1, source_target_pairs={{0,1},{1,0},{2,3},{3,2},{4,5},{5,4},{6,7},{7,6},{8,9},{9,8},{10,11... | collective-permute-start | bytes 786440 | tf_op jit(solution)/shard_map/ppermute | solution.py:451
  73.3 6.2 %attention.1 = (bf16[1024,256]{1,0:T(8,128)(2,1)}, bf16[1024,256]{1,0:T(8,128)(2,1)}, bf16[512,512]{1,0:T(8,128)(2,1)S(1)}, bf16[528,512]{1,0:T(8,128)(2,1)S(1)}, f32[1,512]{1,0:T(1,128)S(1)}) custom-call(bf16[1024,256]{1,0:T(8,128)(2,1)S(1)} %bitcast.37, bf16[1024,256]{1,0:T(8,128)(2,1)S(1)} %bitcast.38, bf16[256,512]{1,0:T(8,128)(2,1)S(1)} %copy-done.10, ...), custom_call_target="tpu_custom_call" | custom-call | flops 3221225472 | bytes 4194304 | tf_op jit(solution)/shard_map/attention/pallas_call | solution.py:235
  79.7 1.8 %collective-permute-done.16.sib_ref = bf16[528,512]{1,0:T(8,128)(2,1)S(1)} collective-permute-done((bf16[528,512]{1,0:T(8,128)(2,1)S(1)}, bf16[528,512]{1,0:T(8,128)(2,1)S(1)}, u32[]{:S(2)}, u32[]{:S(2)}) %collective-permute-start.16) | collective-permute-done | bytes 540704 | tf_op jit(solution)/shard_map/ppermute | solution.py:451
  81.5 3.9 %back_b.1 = bf16[8,2,272,256]{3,2,1,0:T(8,128)(2,1)} custom-call(s32[2]{0:T(128)S(1)} %pad_add_fusion.place_ref.z_ref, bf16[512,512]{1,0:T(8,128)(2,1)S(1)} %get-tuple-element.62.gnear_ref.own_ref, bf16[528,512]{1,0:T(8,128)(2,1)S(1)} %collective-permute-done.16.sib_ref, f32[1,512]{1,0:T(1,128)S(1)} %get-tuple-element.66.dots_ref, ...), custom_call_target="tpu_custom_call" | custom-call | flops 2147483648 | bytes 4194304 | tf_op jit(solution)/shard_map/back_b/pallas_call | solution.py:283
  85.4 7.0 %all-to-all-start.2 = ((bf16[16,272,256]{2,1,0:T(8,128)(2,1)}), bf16[16,272,256]{2,1,0:T(8,128)(2,1)S(1)}, u32[]{:S(2)}, u32[]{:S(2)}) async-start(bf16[16,272,256]{2,1,0:T(8,128)(2,1)} %bitcast.42), calls=%async_computation.2 | async-start | bytes 4456448 | tf_op jit(solution)/shard_map/all_to_all | solution.py:459
  92.3 2.2 %copy-done = bf16[8,256,1024]{2,1,0:T(8,128)(2,1)S(1)} copy-done((bf16[8,256,1024]{2,1,0:T(8,128)(2,1)S(1)}, bf16[8,256,1024]{2,1,0:T(8,128)(2,1)}, u32[]{:S(2)}) %copy-start) | copy-done | bytes 4194328
  95.6 3.0 %back_a.1 = (bf16[4,2,64,256]{3,2,1,0:T(8,128)(2,1)S(1)}, bf16[4,2,64,256]{3,2,1,0:T(8,128)(2,1)S(1)}, bf16[4,2,64,256]{3,2,1,0:T(8,128)(2,1)S(1)}, bf16[4,2,64,...) custom-call(s32[2]{0:T(128)S(1)} %pad_add_fusion.place_ref.z_ref, ...), custom_call_target="tpu_custom_call" | custom-call | flops 2147483648 | bytes 4194304 | tf_op jit(solution)/shard_map/back_a/pallas_call | solution.py:316
  98.6 2.7 %collective-permute-start.20 = (bf16[4,2,64,256]{3,2,1,0:T(8,128)(2,1)S(1)}, bf16[4,2,64,256]{3,2,1,0:T(8,128)(2,1)S(1)}, u32[]{:S(2)}, u32[]{:S(2)}) collective-permute-start(bf16[4,2,64,256]{3,2,1,0:T(8,128)(2,1)S(1)} %get-tuple-element.74), channel_id=1, source_target_pairs={{0,6},{2,0},{4,2},{6,4},{1,7},{3,1},{5,3},{7,5},{8,14},{10,8},{12,... | collective-permute-start | bytes 786440 | tf_op jit(solution)/shard_map/ppermute | solution.py:455
  102.8 7.2 %key_grad.1 = f32[4096,256]{1,0:T(8,128)} custom-call(bf16[256,4096]{1,0:T(8,128)(2,1)} %get-tuple-element.60.near_a, bf16[256,4096]{1,0:T(8,128)(2,1)} %get-tuple-element.61.near_b, bf16[256,4096]{1,0:T(8,128)(2,1)} %collective-permute-done.14.far_a, bf16[256,4096]{1,0:T(8,128)(2,1)} %collective-permute-done.15.far_b, ...), custom_call_target="tpu_custom_call" | custom-call | flops 2147483648 | bytes 13631488 | tf_op jit(solution)/shard_map/key_grad/pallas_call | solution.py:336
  111.8 7.2 %value_grad.1 = f32[4096,256]{1,0:T(8,128)} custom-call(bf16[256,4096]{1,0:T(8,128)(2,1)} %get-tuple-element.60.near_a, bf16[256,4096]{1,0:T(8,128)(2,1)} %get-tuple-element.61.near_b, bf16[256,4096]{1,0:T(8,128)(2,1)} %collective-permute-done.14.far_a, bf16[256,4096]{1,0:T(8,128)(2,1)} %collective-permute-done.15.far_b, ...), custom_call_target="tpu_custom_call" | custom-call | flops 2147483648 | bytes 13631488 | tf_op jit(solution)/shard_map/value_grad/pallas_call | solution.py:336
  120.1 7.0 %all-to-all-done.2.arrived_ref = bf16[16,272,256]{2,1,0:T(8,128)(2,1)S(1)} async-done(((bf16[16,272,256]{2,1,0:T(8,128)(2,1)}), bf16[16,272,256]{2,1,0:T(8,128)(2,1)S(1)}, u32[]{:S(2)}, u32[]{:S(2)}) %all-to-all-start.2) | async-done | bytes 2228256 | tf_op jit(solution)/shard_map/all_to_all | solution.py:459
  127.1 3.6 %all-to-all-start.3 = ((bf16[16,64,256]{2,1,0:T(8,128)(2,1)}), bf16[16,64,256]{2,1,0:T(8,128)(2,1)S(1)}, u32[]{:S(2)}, u32[]{:S(2)}) async-start(bf16[16,64,256]{2,1,0:T(8,128)(2,1)} %bitcast.43), calls=%async_computation.3 | async-start | bytes 1048576 | tf_op jit(solution)/shard_map/all_to_all | solution.py:459
  131.9 1.8 %collective-permute-start.25 = (bf16[80,256]{1,0:T(8,128)(2,1)S(1)}, bf16[80,256]{1,0:T(8,128)(2,1)S(1)}, u32[]{:S(2)}, u32[]{:S(2)}) collective-permute-start(bf16[80,256]{1,0:T(8,128)(2,1)S(1)} %get-tuple-element.84), channel_id=1, source_target_pairs={{0,6},{2,0},{4,2},{6,4},{1,7},{3,1},{5,3},{7,5},{8,14},{10,8},{12,... | collective-permute-start | bytes 122888 | tf_op jit(solution)/shard_map/ppermute | solution.py:455
  137.1 2.7 %collective-permute-start.26 = (f32[64,256]{1,0:T(8,128)S(1)}, f32[64,256]{1,0:T(8,128)S(1)}, u32[]{:S(2)}, u32[]{:S(2)}) collective-permute-start(f32[64,256]{1,0:T(8,128)S(1)} %get-tuple-element.87), channel_id=1, source_target_pairs={{0,1},{1,0},{2,3},{3,2},{4,5},{5,4},{6,7},{7,6},{8,9},{9,8},{10,11... | collective-permute-start | bytes 196616 | tf_op jit(solution)/shard_map/ppermute | solution.py:451
  (87 shorter events, 27.2 us)
Async XLA Ops:
  3.7 33.8 %collective-permute-start.7 = (bf16[4096,256]{1,0:T(8,128)(2,1)}, bf16[4096,256]{1,0:T(8,128)(2,1)}, u32[]{:S(2)}, u32[]{:S(2)}) collective-permute-start(bf16[4096,256]{1,0:T(8,128)(2,1)} %bitcast.45), channel_id=1, source_target_pairs={{0,1},{1,0},{2,3},{3,2},{4,5},{5,4},{6,7},{7,6},{8,9},{9,8},{10,11... | collective-permute-start | bytes 6291464 | tf_op jit(solution)/shard_map/ppermute | solution.py:451
  5.1 17.8 %all-to-all-start = ((bf16[16,32,512]{2,1,0:T(8,128)(2,1)}), bf16[16,32,512]{2,1,0:T(8,128)(2,1)S(1)}, u32[]{:S(2)}, u32[]{:S(2)}) async-start(bf16[16,32,512]{2,1,0:T(8,128)(2,1)} %bitcast.44), calls=%async_computation | async-start | bytes 1048576 | tf_op jit(solution)/shard_map/all_to_all | solution.py:459
  11.9 28.1 %collective-permute-start.8 = (bf16[4096,256]{1,0:T(8,128)(2,1)}, bf16[4096,256]{1,0:T(8,128)(2,1)}, u32[]{:S(2)}, u32[]{:S(2)}) collective-permute-start(bf16[4096,256]{1,0:T(8,128)(2,1)} %bitcast.47), channel_id=1, source_target_pairs={{0,1},{1,0},{2,3},{3,2},{4,5},{5,4},{6,7},{7,6},{8,9},{9,8},{10,11... | collective-permute-start | bytes 6291464 | tf_op jit(solution)/shard_map/ppermute | solution.py:451
  12.5 6.3 %collective-permute-start.10 = (bf16[32,512]{1,0:T(8,128)(2,1)S(1)}, bf16[32,512]{1,0:T(8,128)(2,1)S(1)}, u32[]{:S(2)}, u32[]{:S(2)}) collective-permute-start(bf16[32,512]{1,0:T(8,128)(2,1)S(1)} %get-tuple-element.93.refs_0_), channel_id=1, source_target_pairs={{0,4},{2,6},{4,0},{6,2},{1,5},{3,7},{5,1},{7,3},{8,12},{10,14},{12... | collective-permute-start | bytes 98312 | tf_op jit(solution)/shard_map/ppermute | solution.py:455
  22.9 34.3 %all-to-all-start.1 = ((bf16[16,4,32,512]{3,2,1,0:T(8,128)(2,1)}), bf16[16,4,32,512]{3,2,1,0:T(8,128)(2,1)S(1)}, u32[]{:S(2)}, u32[]{:S(2)}) async-start(bf16[16,4,32,512]{3,2,1,0:T(8,128)(2,1)} %copies_b.1), calls=%async_computation.1 | async-start | bytes 4194304 | tf_op jit(solution)/shard_map/all_to_all | solution.py:459
  28.5 7.6 %collective-permute-start.1 = (bf16[8,32,512]{2,1,0:T(8,128)(2,1)S(1)}, bf16[8,32,512]{2,1,0:T(8,128)(2,1)S(1)}, u32[]{:S(2)}, u32[]{:S(2)}) collective-permute-start(bf16[8,32,512]{2,1,0:T(8,128)(2,1)S(1)} %get-tuple-element.92), channel_id=1, source_target_pairs={{0,2},{2,4},{4,6},{6,0},{1,3},{3,5},{5,7},{7,1},{8,10},{10,12},{12... | collective-permute-start | bytes 786440 | tf_op jit(solution)/shard_map/ppermute | solution.py:455
  28.6 8.7 %collective-permute-start.4 = (bf16[8,32,512]{2,1,0:T(8,128)(2,1)S(1)}, bf16[8,32,512]{2,1,0:T(8,128)(2,1)}, u32[]{:S(2)}, u32[]{:S(2)}) collective-permute-start(bf16[8,32,512]{2,1,0:T(8,128)(2,1)S(1)} %get-tuple-element.91), channel_id=1, source_target_pairs={{0,6},{2,0},{4,2},{6,4},{1,7},{3,1},{5,3},{7,5},{8,14},{10,8},{12,... | collective-permute-start | bytes 786440 | tf_op jit(solution)/shard_map/ppermute | solution.py:455
  31.5 17.6 %collective-permute-start.2 = (bf16[8,32,512]{2,1,0:T(8,128)(2,1)S(1)}, bf16[8,32,512]{2,1,0:T(8,128)(2,1)}, u32[]{:S(2)}, u32[]{:S(2)}) collective-permute-start(bf16[8,32,512]{2,1,0:T(8,128)(2,1)S(1)} %get-tuple-element.91), channel_id=1, source_target_pairs={{0,2},{2,4},{4,6},{6,0},{1,3},{3,5},{5,7},{7,1},{8,10},{10,12},{12... | collective-permute-start | bytes 786440 | tf_op jit(solution)/shard_map/ppermute | solution.py:455
  36.1 13.0 %collective-permute-start.3 = (bf16[8,32,512]{2,1,0:T(8,128)(2,1)S(1)}, bf16[8,32,512]{2,1,0:T(8,128)(2,1)}, u32[]{:S(2)}, u32[]{:S(2)}) collective-permute-start(bf16[8,32,512]{2,1,0:T(8,128)(2,1)S(1)} %get-tuple-element.92), channel_id=1, source_target_pairs={{0,6},{2,0},{4,2},{6,4},{1,7},{3,1},{5,3},{7,5},{8,14},{10,8},{12,... | collective-permute-start | bytes 786440 | tf_op jit(solution)/shard_map/ppermute | solution.py:455
  37.3 11.8 %collective-permute-start.5 = (bf16[8,32,512]{2,1,0:T(8,128)(2,1)S(1)}, bf16[8,32,512]{2,1,0:T(8,128)(2,1)}, u32[]{:S(2)}, u32[]{:S(2)}) collective-permute-start(bf16[8,32,512]{2,1,0:T(8,128)(2,1)S(1)} %collective-permute-done.1), channel_id=1, source_target_pairs={{0,2},{2,4},{4,6},{6,0},{1,3},{3,5},{5,7},{7,1},{8,10},{10,12},{12... | collective-permute-start | bytes 786440 | tf_op jit(solution)/shard_map/ppermute | solution.py:455
  37.6 11.6 %collective-permute-start.6 = (bf16[8,32,512]{2,1,0:T(8,128)(2,1)}, bf16[8,32,512]{2,1,0:T(8,128)(2,1)}, u32[]{:S(2)}, u32[]{:S(2)}) collective-permute-start(bf16[8,32,512]{2,1,0:T(8,128)(2,1)} %collective-permute-done.4), channel_id=1, source_target_pairs={{0,6},{2,0},{4,2},{6,4},{1,7},{3,1},{5,3},{7,5},{8,14},{10,8},{12,... | collective-permute-start | bytes 786440 | tf_op jit(solution)/shard_map/ppermute | solution.py:455
  65.2 7.3 %collective-permute-start.13 = (bf16[256,512]{1,0:T(8,128)(2,1)S(1)}, bf16[256,512]{1,0:T(8,128)(2,1)S(1)}, u32[]{:S(2)}, u32[]{:S(2)}) collective-permute-start(bf16[256,512]{1,0:T(8,128)(2,1)S(1)} %get-tuple-element.55), channel_id=1, source_target_pairs={{0,1},{1,0},{2,3},{3,2},{4,5},{5,4},{6,7},{7,6},{8,9},{9,8},{10,11... | collective-permute-start | bytes 786440 | tf_op jit(solution)/shard_map/ppermute | solution.py:451
  72.6 28.8 %collective-permute-start.15 = (bf16[256,4096]{1,0:T(8,128)(2,1)}, bf16[256,4096]{1,0:T(8,128)(2,1)}, u32[]{:S(2)}, u32[]{:S(2)}) collective-permute-start(bf16[256,4096]{1,0:T(8,128)(2,1)} %get-tuple-element.61.near_b), channel_id=1, source_target_pairs={{0,1},{1,0},{2,3},{3,2},{4,5},{5,4},{6,7},{7,6},{8,9},{9,8},{10,11... | collective-permute-start | bytes 6291464 | tf_op jit(solution)/shard_map/ppermute | solution.py:451
  72.9 29.8 %collective-permute-start.14 = (bf16[256,4096]{1,0:T(8,128)(2,1)}, bf16[256,4096]{1,0:T(8,128)(2,1)}, u32[]{:S(2)}, u32[]{:S(2)}) collective-permute-start(bf16[256,4096]{1,0:T(8,128)(2,1)} %get-tuple-element.60.near_a), channel_id=1, source_target_pairs={{0,1},{1,0},{2,3},{3,2},{4,5},{5,4},{6,7},{7,6},{8,9},{9,8},{10,11... | collective-permute-start | bytes 6291464 | tf_op jit(solution)/shard_map/ppermute | solution.py:451
  85.4 41.7 %all-to-all-start.2 = ((bf16[16,272,256]{2,1,0:T(8,128)(2,1)}), bf16[16,272,256]{2,1,0:T(8,128)(2,1)S(1)}, u32[]{:S(2)}, u32[]{:S(2)}) async-start(bf16[16,272,256]{2,1,0:T(8,128)(2,1)} %bitcast.42), calls=%async_computation.2 | async-start | bytes 4456448 | tf_op jit(solution)/shard_map/all_to_all | solution.py:459
  98.6 11.5 %collective-permute-start.19 = (bf16[4,2,64,256]{3,2,1,0:T(8,128)(2,1)S(1)}, bf16[4,2,64,256]{3,2,1,0:T(8,128)(2,1)S(1)}, u32[]{:S(2)}, u32[]{:S(2)}) collective-permute-start(bf16[4,2,64,256]{3,2,1,0:T(8,128)(2,1)S(1)} %get-tuple-element.73), channel_id=1, source_target_pairs={{0,2},{2,4},{4,6},{6,0},{1,3},{3,5},{5,7},{7,1},{8,10},{10,12},{12... | collective-permute-start | bytes 786440 | tf_op jit(solution)/shard_map/ppermute | solution.py:455
  98.6 11.4 %collective-permute-start.20 = (bf16[4,2,64,256]{3,2,1,0:T(8,128)(2,1)S(1)}, bf16[4,2,64,256]{3,2,1,0:T(8,128)(2,1)S(1)}, u32[]{:S(2)}, u32[]{:S(2)}) collective-permute-start(bf16[4,2,64,256]{3,2,1,0:T(8,128)(2,1)S(1)} %get-tuple-element.74), channel_id=1, source_target_pairs={{0,6},{2,0},{4,2},{6,4},{1,7},{3,1},{5,3},{7,5},{8,14},{10,8},{12,... | collective-permute-start | bytes 786440 | tf_op jit(solution)/shard_map/ppermute | solution.py:455
  101.3 17.7 %collective-permute-start.17 = (bf16[4,2,64,256]{3,2,1,0:T(8,128)(2,1)S(1)}, bf16[4,2,64,256]{3,2,1,0:T(8,128)(2,1)S(1)}, u32[]{:S(2)}, u32[]{:S(2)}) collective-permute-start(bf16[4,2,64,256]{3,2,1,0:T(8,128)(2,1)S(1)} %get-tuple-element.69), channel_id=1, source_target_pairs={{0,6},{2,0},{4,2},{6,4},{1,7},{3,1},{5,3},{7,5},{8,14},{10,8},{12,... | collective-permute-start | bytes 786440 | tf_op jit(solution)/shard_map/ppermute | solution.py:455
  101.3 17.7 %collective-permute-start.18 = (bf16[4,2,64,256]{3,2,1,0:T(8,128)(2,1)S(1)}, bf16[4,2,64,256]{3,2,1,0:T(8,128)(2,1)S(1)}, u32[]{:S(2)}, u32[]{:S(2)}) collective-permute-start(bf16[4,2,64,256]{3,2,1,0:T(8,128)(2,1)S(1)} %get-tuple-element.70), channel_id=1, source_target_pairs={{0,2},{2,4},{4,6},{6,0},{1,3},{3,5},{5,7},{7,1},{8,10},{10,12},{12... | collective-permute-start | bytes 786440 | tf_op jit(solution)/shard_map/ppermute | solution.py:455
  110.1 8.9 %collective-permute-start.22 = (bf16[4,2,64,256]{3,2,1,0:T(8,128)(2,1)S(1)}, bf16[4,2,64,256]{3,2,1,0:T(8,128)(2,1)S(1)}, u32[]{:S(2)}, u32[]{:S(2)}) collective-permute-start(bf16[4,2,64,256]{3,2,1,0:T(8,128)(2,1)S(1)} %add_convert_fusion.1), channel_id=1, source_target_pairs={{0,6},{2,0},{4,2},{6,4},{1,7},{3,1},{5,3},{7,5},{8,14},{10,8},{12,... | collective-permute-start | bytes 786440 | tf_op jit(solution)/shard_map/ppermute | solution.py:455
  111.5 7.5 %collective-permute-start.21 = (bf16[4,2,64,256]{3,2,1,0:T(8,128)(2,1)S(1)}, bf16[4,2,64,256]{3,2,1,0:T(8,128)(2,1)S(1)}, u32[]{:S(2)}, u32[]{:S(2)}) collective-permute-start(bf16[4,2,64,256]{3,2,1,0:T(8,128)(2,1)S(1)} %add_convert_fusion.3), channel_id=1, source_target_pairs={{0,2},{2,4},{4,6},{6,0},{1,3},{3,5},{5,7},{7,1},{8,10},{10,12},{12... | collective-permute-start | bytes 786440 | tf_op jit(solution)/shard_map/ppermute | solution.py:455
  127.1 13.7 %all-to-all-start.3 = ((bf16[16,64,256]{2,1,0:T(8,128)(2,1)}), bf16[16,64,256]{2,1,0:T(8,128)(2,1)S(1)}, u32[]{:S(2)}, u32[]{:S(2)}) async-start(bf16[16,64,256]{2,1,0:T(8,128)(2,1)} %bitcast.43), calls=%async_computation.3 | async-start | bytes 1048576 | tf_op jit(solution)/shard_map/all_to_all | solution.py:459
  131.1 4.6 %collective-permute-start.24 = (bf16[80,256]{1,0:T(8,128)(2,1)S(1)}, bf16[80,256]{1,0:T(8,128)(2,1)S(1)}, u32[]{:S(2)}, u32[]{:S(2)}) collective-permute-start(bf16[80,256]{1,0:T(8,128)(2,1)S(1)} %get-tuple-element.83), channel_id=1, source_target_pairs={{0,4},{2,6},{4,0},{6,2},{1,5},{3,7},{5,1},{7,3},{8,12},{10,14},{12... | collective-permute-start | bytes 122888 | tf_op jit(solution)/shard_map/ppermute | solution.py:455
  131.9 4.5 %collective-permute-start.25 = (bf16[80,256]{1,0:T(8,128)(2,1)S(1)}, bf16[80,256]{1,0:T(8,128)(2,1)S(1)}, u32[]{:S(2)}, u32[]{:S(2)}) collective-permute-start(bf16[80,256]{1,0:T(8,128)(2,1)S(1)} %get-tuple-element.84), channel_id=1, source_target_pairs={{0,6},{2,0},{4,2},{6,4},{1,7},{3,1},{5,3},{7,5},{8,14},{10,8},{12,... | collective-permute-start | bytes 122888 | tf_op jit(solution)/shard_map/ppermute | solution.py:455
  (20 other events, 131.2 us)

commit v11 on v10

--- a/solution.py
+++ b/solution.py
@@ -52,31 +52,6 @@
 
 def cost(flops, mib, transcendentals=0):
     return pl.CostEstimate(flops=flops, bytes_accessed=int(mib * MIB), transcendentals=transcendentals)
-
-
-def copies_body(count, *refs):
-    pieces, out_ref, held, sem = refs[:-3], refs[-3], refs[-2], refs[-1]
-    for i, piece in enumerate(pieces):
-        held[i] = piece[...]
-    copies = [pltpu.make_async_copy(held, out_ref.at[j], sem.at[j]) for j in range(count)]
-    for copy in copies:
-        copy.start()
-    for copy in copies:
-        copy.wait()
-
-
-def copies_of(pieces, count, name):
-    shape = (len(pieces), *pieces[0].shape)
-    return pl.pallas_call(
-        functools.partial(copies_body, count),
-        in_specs=[VMEM] * len(pieces),
-        out_specs=ANYWHERE,
-        out_shape=pltpu.HBM((count, *shape), BF16),
-        scratch_shapes=[pltpu.VMEM(shape, BF16), pltpu.SemaphoreType.DMA((count,))],
-        compiler_params=limits(4),
-        cost_estimate=cost(0, 2),
-        name=name,
-    )(*pieces)
 
 
 def stage_body(place_ref, *refs):
@@ -324,25 +299,29 @@
     )(z, own, sib, in_vmem(weights))
 
 
-def weights_body(near_a, near_b, far_a, far_b, gnear_ref, gfar_ref, out_ref):
+def weights_body(near_a, near_b, far_a, far_b, gnear_ref, gfar_ref, gk_ref, gv_ref):
     rows = above(near_a[...], near_b[...], far_a[...], far_b[...])
-    out_ref[...] = tn(rows, above(gnear_ref[...], gfar_ref[...]))
-
-
-def weight_grad(normed, gnear, gfar, which, width=1024):
-    rows, hidden = normed[0].shape
+    total = tn(rows, above(gnear_ref[...], gfar_ref[: gnear_ref.shape[0]]))
+    gk_ref[...] = total[:, :HD]
+    gv_ref[...] = total[:, HD:]
+
+
+def weight_grads(near_a, near_b, far_a, far_b, gnear, gfar, width=512):
+    rows, hidden = near_a.shape
     block = pl.BlockSpec((rows, width), lambda i: (0, i))
-    columns = pl.BlockSpec((2 * rows, HD), lambda i: (0, which))
+    near = pl.BlockSpec(gnear.shape, lambda i: (0, 0))
+    far = pl.BlockSpec(gfar.shape, lambda i: (0, 0))
+    out = pl.BlockSpec((width, HD), lambda i: (i, 0))
     return pl.pallas_call(
         weights_body,
         grid=(hidden // width,),
-        in_specs=[block] * 4 + [columns, columns],
-        out_specs=pl.BlockSpec((width, HD), lambda i: (i, 0)),
-        out_shape=jax.ShapeDtypeStruct((hidden, HD), F32),
-        compiler_params=limits(24),
-        cost_estimate=cost(8 * rows * hidden * HD, 13),
-        name=("key_grad", "value_grad")[which],
-    )(*normed, gnear, gfar)
+        in_specs=[block] * 4 + [near, far],
+        out_specs=[out, out],
+        out_shape=[jax.ShapeDtypeStruct((hidden, HD), F32)] * 2,
+        compiler_params=limits(16),
+        cost_estimate=cost(16 * rows * hidden * HD, 17),
+        name="weight_grads",
+    )(near_a, near_b, far_a, far_b, gnear, gfar)
 
 
 def merge_b_body(arrived_ref, kept_ref, dots_ref, *send_refs):
@@ -479,10 +458,10 @@
     mine = lax.dynamic_index_in_dim(halves, core, 0, keepdims=False)
     other = swapped(lax.dynamic_index_in_dim(halves, 1 - core, 0, keepdims=False))
     block = jnp.where(core == 0, beside(mine, other), beside(other, mine))
-    first_a = over_plane(copies_of([block[:part]], plane, "copies_a").reshape(plane, part, width))
+    first_a = over_plane(jnp.broadcast_to(block[:part], (plane, part, width)))
     high = block[part:]
-    near_z = [high, shifted(high, -1), shifted(high, 2), shifted(high, 1)]
-    all_b = over_plane(copies_of(near_z, plane, "copies_b"))
+    near_z = jnp.stack([high, shifted(high, -1), shifted(high, 2), shifted(high, 1)])
+    all_b = over_plane(jnp.broadcast_to(near_z, (plane, RING, part, width)))
     all_b = all_b.reshape(segs, 2, RING, part, width)
     low_0, high_0 = first_a[: plane // 2], first_a[plane // 2 :]
     low_3, high_1 = shifted(low_0, 1), shifted(high_0, -1)
@@ -515,12 +494,10 @@
     from_low, from_high = shifted(opp_low, 1), shifted(opp_high, -1)
     got_high, got_low = shifted(up_high, 1), shifted(down_low, -1)
     all_normed = (normed_a, normed_b, normed_far_a, normed_far_b)
-    key_grad = weight_grad(all_normed, gnear, gfar, 0)
-    from_low, from_high = after((from_low, from_high), key_grad)
+    key_grad, value_grad = weight_grads(*all_normed, gnear, gfar)
+    from_low, from_high = after((from_low, from_high), key_grad, value_grad)
     last_low = shifted((wide(up_low) + wide(from_low)).astype(BF16), 1)
     last_high = shifted((wide(down_high) + wide(from_high)).astype(BF16), -1)
-    value_grad = weight_grad(all_normed, gnear, gfar, 1)
-    got_low, got_high = after((got_low, got_high), value_grad)
     summed_low = wide(kept[: segs // 2]) + wide(got_low) + wide(last_low)
     summed_high = wide(kept[segs // 2 :]) + wide(got_high) + wide(last_high)
     summed_a = above(summed_low, summed_high).astype(BF16).reshape(plane, half, HD)

time: 144 us -> 144 us (level)
  Pallas kernels: 56 us -> 50 us
  waiting for transfers between devices: 21.6 us -> 25.7 us
  starting transfers between devices: 56.7 us -> 58.4 us
    ppermute x18, waiting for transfers between devices: 8.84 us -> 16.9 us  [shifted(): return lax.ppermute(value, 'z', [(i, (i + by) % RING) for i in range(RING)])]
    pallas_call x4 -> x1, Pallas kernels: 16.9 us -> 10.9 us  [weight_grads(): pl.pallas_call(weights_body, grid=(hidden // width,), in_specs=[block] *...]
    all_to_all x4, waiting for transfers between devices: 8 us -> 4.44 us  [over_plane(): return lax.all_to_all(value, PLANE, 0, 0, tiled=True)]
    broadcast_in_dim x0 -> x2, local copies, waits for them, and re-layouts: none -> 2.45 us  [the longest x1 1.6 us: local(): all_b = over_plane(jnp.broadcast_to(near_z, (plane, RING, part, width)))]
    ppermute x9, starting transfers between devices: 12.1 us -> 14.2 us  [swapped(): return lax.ppermute(value, 'c', [(0, 1), (1, 0)])]
    unnamed x26 -> x22, local copies, waits for them, and re-layouts: 4.61 us -> 3.27 us
  transfers between devices with their start and end apart: 31 -> 31, of which waited for: 11 -> 16; matrix products, arithmetic and copies ran while one was open for 1% -> 3% of each run, Pallas kernels for 33% -> 34%
where the time goes in v11:
time: 144 us; the launch traced here: 143 us
  starting transfers between devices  58.4 us (41%)
  Pallas kernels  50 us (35%)
  waiting for transfers between devices  25.7 us (18%)
  local copies, waits for them, and re-layouts  6.55 us (5%)
    ppermute x18, starting transfers between devices, shifted(): return lax.ppermute(value, 'z', [(i, (i + by) % RING) for i in range(RING)])  22.2 us
    all_to_all x4, starting transfers between devices, over_plane(): return lax.all_to_all(value, PLANE, 0, 0, tiled=True)  22 us
    ppermute x18, waiting for transfers between devices, shifted(): return lax.ppermute(value, 'z', [(i, (i + by) % RING) for i in range(RING)])  16.9 us
    pallas_call x2, Pallas kernels, project(): pl.pallas_call(functools.partial(project_body, pieces), in_specs=[SMEM, V...  14.7 us
    ppermute x9, starting transfers between devices, swapped(): return lax.ppermute(value, 'c', [(0, 1), (1, 0)])  14.2 us
    pallas_call x1, Pallas kernels, weight_grads(): pl.pallas_call(weights_body, grid=(hidden // width,), in_specs=[block] *...  10.9 us
    pallas_call x1, Pallas kernels, staged(): pl.pallas_call(stage_body, grid=(blocks,), in_specs=[SMEM] + [pl.BlockSpe...  9.05 us
    pallas_call x1, Pallas kernels, attention(): pl.pallas_call(functools.partial(attend_body, tile), in_specs=[VMEM] * 6,...  6.23 us
  transfers between devices with their start and end apart: 31, of which 16 were waited for; matrix products, arithmetic and copies ran while one was open for 3% of the time, Pallas kernels for 34%

profile of v11, /device:TPU:1, one launch (start us, length us, event | category | flops | bytes accessed | tf_op | source)
XLA Modules:
  0.0 143.0 jit_solution(13837600428081155278)
XLA Ops:
  5.0 6.8 %all-to-all-start = ((bf16[16,32,512]{2,1,0:T(8,128)(2,1)}), bf16[16,32,512]{2,1,0:T(8,128)(2,1)S(1)}, u32[]{:S(2)}, u32[]{:S(2)}) async-start(bf16[16,32,512]{2,1,0:T(8,128)(2,1)} %broadcast_in_dim.18), calls=%async_computation | async-start | bytes 1048576 | tf_op jit(solution)/shard_map/all_to_all | solution.py:438
  12.4 3.6 %collective-permute-start.10 = (bf16[32,512]{1,0:T(8,128)(2,1)S(1)}, bf16[32,512]{1,0:T(8,128)(2,1)S(1)}, u32[]{:S(2)}, u32[]{:S(2)}) collective-permute-start(bf16[32,512]{1,0:T(8,128)(2,1)S(1)} %get-tuple-element.94), channel_id=1, source_target_pairs={{0,4},{2,6},{4,0},{6,2},{1,5},{3,7},{5,1},{7,3},{8,12},{10,14},{12... | collective-permute-start | bytes 98312 | tf_op jit(solution)/shard_map/ppermute | solution.py:434
  20.7 2.0 %all-to-all-done = bf16[16,32,512]{2,1,0:T(8,128)(2,1)S(1)} async-done(((bf16[16,32,512]{2,1,0:T(8,128)(2,1)}), bf16[16,32,512]{2,1,0:T(8,128)(2,1)S(1)}, u32[]{:S(2)}, u32[]{:S(2)}) %all-to-all-start) | async-done | bytes 524320 | tf_op jit(solution)/shard_map/all_to_all | solution.py:438
  24.4 4.5 %all-to-all-start.1 = ((bf16[16,4,32,512]{3,2,1,0:T(8,128)(2,1)}), bf16[16,4,32,512]{3,2,1,0:T(8,128)(2,1)S(1)}, u32[]{:S(2)}, u32[]{:S(2)}) async-start(bf16[16,4,32,512]{3,2,1,0:T(8,128)(2,1)} %broadcast_in_dim.19), calls=%async_computation.1 | async-start | bytes 4194304 | tf_op jit(solution)/shard_map/all_to_all | solution.py:438
  29.0 3.0 %collective-permute-start.4 = (bf16[8,32,512]{2,1,0:T(8,128)(2,1)S(1)}, bf16[8,32,512]{2,1,0:T(8,128)(2,1)S(1)}, u32[]{:S(2)}, u32[]{:S(2)}) collective-permute-start(bf16[8,32,512]{2,1,0:T(8,128)(2,1)S(1)} %get-tuple-element.91), channel_id=1, source_target_pairs={{0,6},{2,0},{4,2},{6,4},{1,7},{3,1},{5,3},{7,5},{8,14},{10,8},{12,... | collective-permute-start | bytes 786440 | tf_op jit(solution)/shard_map/ppermute | solution.py:434
  32.0 4.0 %collective-permute-done.4 = bf16[8,32,512]{2,1,0:T(8,128)(2,1)S(1)} collective-permute-done((bf16[8,32,512]{2,1,0:T(8,128)(2,1)S(1)}, bf16[8,32,512]{2,1,0:T(8,128)(2,1)S(1)}, u32[]{:S(2)}, u32[]{:S(2)}) %collective-permute-start.4) | collective-permute-done | bytes 262176 | tf_op jit(solution)/shard_map/ppermute | solution.py:434
  36.0 3.4 %collective-permute-start.3 = (bf16[8,32,512]{2,1,0:T(8,128)(2,1)S(1)}, bf16[8,32,512]{2,1,0:T(8,128)(2,1)}, u32[]{:S(2)}, u32[]{:S(2)}) collective-permute-start(bf16[8,32,512]{2,1,0:T(8,128)(2,1)S(1)} %get-tuple-element.92), channel_id=1, source_target_pairs={{0,6},{2,0},{4,2},{6,4},{1,7},{3,1},{5,3},{7,5},{8,14},{10,8},{12,... | collective-permute-start | bytes 786440 | tf_op jit(solution)/shard_map/ppermute | solution.py:434
  41.0 9.0 %stage.1 = (bf16[8,256,1024]{2,1,0:T(8,128)(2,1)}, bf16[8,256,1024]{2,1,0:T(8,128)(2,1)}) custom-call(s32[2]{0:T(128)S(1)} %pad_add_fusion.place_ref.z_ref, bf16[4096,256]{1,0:T(8,128)(2,1)} %bitcast.47, bf16[4096,256]{1,0:T(8,128)(2,1)} %bitcast.49, bf16[4096,256]{1,0:T(8,128)(2,1)} %collective-permute-done.7.refs_2_, ...), custom_call_target="tpu_custom_call" | custom-call | bytes 16777216 | tf_op jit(solution)/shard_map/stage/pallas_call | solution.py:70
  50.5 7.3 %project_a.1 = (bf16[256,512]{1,0:T(8,128)(2,1)S(1)}, bf16[256,512]{1,0:T(8,128)(2,1)S(1)}, f32[256,1]{1,0:T(8,128)S(1)}, bf16[256,4096]{1,0:T(8,128)(2,1)}) custom-call(s32[2]{0:T(128)S(1)} %pad_add_fusion.place_ref.z_ref, f32[8,1,512]{2,1,0:T(1,128)S(1)} %bitcast.37, bf16[8,2,32,512]{3,2,1,0:T(8,128)(2,1)} %bitcast.43, ...), custom_call_target="tpu_custom_call" | custom-call | flops 2147483648 | bytes 12582912 | tf_op jit(solution)/shard_map/project_a/pallas_call | solution.py:129
  57.9 5.4 %collective-permute-start.12 = (bf16[256,512]{1,0:T(8,128)(2,1)S(1)}, bf16[256,512]{1,0:T(8,128)(2,1)S(1)}, u32[]{:S(2)}, u32[]{:S(2)}) collective-permute-start(bf16[256,512]{1,0:T(8,128)(2,1)S(1)} %get-tuple-element.54), channel_id=1, source_target_pairs={{0,1},{1,0},{2,3},{3,2},{4,5},{5,4},{6,7},{7,6},{8,9},{9,8},{10,11... | collective-permute-start | bytes 786440 | tf_op jit(solution)/shard_map/ppermute | solution.py:430
  63.3 7.4 %project_b.1 = (bf16[256,512]{1,0:T(8,128)(2,1)S(1)}, bf16[256,512]{1,0:T(8,128)(2,1)S(1)}, f32[256,1]{1,0:T(8,128)S(1)}, bf16[256,4096]{1,0:T(8,128)(2,1)}) custom-call(s32[2]{0:T(128)S(1)} %pad_add_fusion.place_ref.z_ref, f32[8,1,512]{2,1,0:T(1,128)S(1)} %bitcast.38, bf16[8,2,4,32,512]{4,3,2,1,0:T(8,128)(2,1)S(1)} %bitcast.33, ...), custom_call_target="tpu_custom_call" | custom-call | flops 2147483648 | bytes 12582912 | tf_op jit(solution)/shard_map/project_b/pallas_call | solution.py:129
  72.4 6.2 %attention.1 = (bf16[1024,256]{1,0:T(8,128)(2,1)}, bf16[1024,256]{1,0:T(8,128)(2,1)}, bf16[512,512]{1,0:T(8,128)(2,1)S(1)}, bf16[528,512]{1,0:T(8,128)(2,1)S(1)}, f32[1,512]{1,0:T(1,128)S(1)}) custom-call(bf16[1024,256]{1,0:T(8,128)(2,1)S(1)} %bitcast.41, bf16[1024,256]{1,0:T(8,128)(2,1)S(1)} %bitcast.42, bf16[256,512]{1,0:T(8,128)(2,1)S(1)} %get-tuple-element.51.near_a, ...), custom_call_target="tpu_custom_call" | custom-call | flops 3221225472 | bytes 4194304 | tf_op jit(solution)/shard_map/attention/pallas_call | solution.py:210
  80.6 3.9 %back_b.1 = bf16[8,2,272,256]{3,2,1,0:T(8,128)(2,1)} custom-call(s32[2]{0:T(128)S(1)} %pad_add_fusion.place_ref.z_ref, bf16[512,512]{1,0:T(8,128)(2,1)S(1)} %get-tuple-element.62.gnear_ref.own_ref, bf16[528,512]{1,0:T(8,128)(2,1)S(1)} %collective-permute-done.16.sib_ref, f32[1,512]{1,0:T(1,128)S(1)} %get-tuple-element.68.dots_ref, ...), custom_call_target="tpu_custom_call" | custom-call | flops 2147483648 | bytes 4194304 | tf_op jit(solution)/shard_map/back_b/pallas_call | solution.py:258
  84.5 6.9 %all-to-all-start.2 = ((bf16[16,272,256]{2,1,0:T(8,128)(2,1)}), bf16[16,272,256]{2,1,0:T(8,128)(2,1)S(1)}, u32[]{:S(2)}, u32[]{:S(2)}) async-start(bf16[16,272,256]{2,1,0:T(8,128)(2,1)} %bitcast.44), calls=%async_computation.2 | async-start | bytes 4456448 | tf_op jit(solution)/shard_map/all_to_all | solution.py:438
  91.4 2.2 %copy-done = bf16[8,256,1024]{2,1,0:T(8,128)(2,1)S(1)} copy-done((bf16[8,256,1024]{2,1,0:T(8,128)(2,1)S(1)}, bf16[8,256,1024]{2,1,0:T(8,128)(2,1)}, u32[]{:S(2)}) %copy-start) | copy-done | bytes 4194328
  94.6 3.0 %back_a.1 = (bf16[4,2,64,256]{3,2,1,0:T(8,128)(2,1)S(1)}, bf16[4,2,64,256]{3,2,1,0:T(8,128)(2,1)S(1)}, bf16[4,2,64,256]{3,2,1,0:T(8,128)(2,1)S(1)}, bf16[4,2,64,...) custom-call(s32[2]{0:T(128)S(1)} %pad_add_fusion.place_ref.z_ref, ...), custom_call_target="tpu_custom_call" | custom-call | flops 2147483648 | bytes 4194304 | tf_op jit(solution)/shard_map/back_a/pallas_call | solution.py:291
  99.1 2.1 %collective-permute-start.19 = (bf16[4,2,64,256]{3,2,1,0:T(8,128)(2,1)S(1)}, bf16[4,2,64,256]{3,2,1,0:T(8,128)(2,1)S(1)}, u32[]{:S(2)}, u32[]{:S(2)}) collective-permute-start(bf16[4,2,64,256]{3,2,1,0:T(8,128)(2,1)S(1)} %get-tuple-element.74), channel_id=1, source_target_pairs={{0,6},{2,0},{4,2},{6,4},{1,7},{3,1},{5,3},{7,5},{8,14},{10,8},{12,... | collective-permute-start | bytes 786440 | tf_op jit(solution)/shard_map/ppermute | solution.py:434
  101.3 10.9 %weight_grads.1 = (f32[4096,256]{1,0:T(8,128)}, f32[4096,256]{1,0:T(8,128)}) custom-call(bf16[256,4096]{1,0:T(8,128)(2,1)} %get-tuple-element.60.near_a, bf16[256,4096]{1,0:T(8,128)(2,1)} %get-tuple-element.61.near_b, bf16[256,4096]{1,0:T(8,128)(2,1)} %collective-permute-done.14.far_a, bf16[256,4096]{1,0:T(8,128)(2,1)} %collective-permute-done.15.far_b, ...), custom_call_target="tpu_custom_call" | custom-call | flops 4294967296 | bytes 17825792 | tf_op jit(solution)/shard_map/weight_grads/pallas_call | solution.py:315
  112.3 2.7 %collective-permute-start.22 = (bf16[4,2,64,256]{3,2,1,0:T(8,128)(2,1)S(1)}, bf16[4,2,64,256]{3,2,1,0:T(8,128)(2,1)S(1)}, u32[]{:S(2)}, u32[]{:S(2)}) collective-permute-start(bf16[4,2,64,256]{3,2,1,0:T(8,128)(2,1)S(1)} %add_convert_fusion.1), channel_id=1, source_target_pairs={{0,6},{2,0},{4,2},{6,4},{1,7},{3,1},{5,3},{7,5},{8,14},{10,8},{12,... | collective-permute-start | bytes 786440 | tf_op jit(solution)/shard_map/ppermute | solution.py:434
  115.2 3.7 %collective-permute-done.22 = bf16[4,2,64,256]{3,2,1,0:T(8,128)(2,1)S(1)} collective-permute-done((bf16[4,2,64,256]{3,2,1,0:T(8,128)(2,1)S(1)}, bf16[4,2,64,256]{3,2,1,0:T(8,128)(2,1)S(1)}, u32[]{:S(2)}, u32[]{:S(2)}) %collective-permute-start.22) | collective-permute-done | bytes 262176 | tf_op jit(solution)/shard_map/ppermute | solution.py:434
  118.8 3.3 %collective-permute-done.20 = bf16[4,2,64,256]{3,2,1,0:T(8,128)(2,1)S(1)} collective-permute-done((bf16[4,2,64,256]{3,2,1,0:T(8,128)(2,1)S(1)}, bf16[4,2,64,256]{3,2,1,0:T(8,128)(2,1)S(1)}, u32[]{:S(2)}, u32[]{:S(2)}) %collective-permute-start.20) | collective-permute-done | bytes 262176 | tf_op jit(solution)/shard_map/ppermute | solution.py:434
  123.2 2.4 %all-to-all-done.2.arrived_ref = bf16[16,272,256]{2,1,0:T(8,128)(2,1)S(1)} async-done(((bf16[16,272,256]{2,1,0:T(8,128)(2,1)}), bf16[16,272,256]{2,1,0:T(8,128)(2,1)S(1)}, u32[]{:S(2)}, u32[]{:S(2)}) %all-to-all-start.2) | async-done | bytes 2228256 | tf_op jit(solution)/shard_map/all_to_all | solution.py:438
  125.6 3.7 %all-to-all-start.3 = ((bf16[16,64,256]{2,1,0:T(8,128)(2,1)}), bf16[16,64,256]{2,1,0:T(8,128)(2,1)S(1)}, u32[]{:S(2)}, u32[]{:S(2)}) async-start(bf16[16,64,256]{2,1,0:T(8,128)(2,1)} %bitcast.45), calls=%async_computation.3 | async-start | bytes 1048576 | tf_op jit(solution)/shard_map/all_to_all | solution.py:438
  135.5 5.3 %collective-permute-start.26 = (f32[64,256]{1,0:T(8,128)S(1)}, f32[64,256]{1,0:T(8,128)S(1)}, u32[]{:S(2)}, u32[]{:S(2)}) collective-permute-start(f32[64,256]{1,0:T(8,128)S(1)} %get-tuple-element.87), channel_id=1, source_target_pairs={{0,1},{1,0},{2,3},{3,2},{4,5},{5,4},{6,7},{7,6},{8,9},{9,8},{10,11... | collective-permute-start | bytes 196616 | tf_op jit(solution)/shard_map/ppermute | solution.py:430
  (83 shorter events, 29.2 us)
Async XLA Ops:
  3.7 35.8 %collective-permute-start.7 = (bf16[4096,256]{1,0:T(8,128)(2,1)}, bf16[4096,256]{1,0:T(8,128)(2,1)}, u32[]{:S(2)}, u32[]{:S(2)}) collective-permute-start(bf16[4096,256]{1,0:T(8,128)(2,1)} %bitcast.46), channel_id=1, source_target_pairs={{0,1},{1,0},{2,3},{3,2},{4,5},{5,4},{6,7},{7,6},{8,9},{9,8},{10,11... | collective-permute-start | bytes 6291464 | tf_op jit(solution)/shard_map/ppermute | solution.py:430
  5.0 17.8 %all-to-all-start = ((bf16[16,32,512]{2,1,0:T(8,128)(2,1)}), bf16[16,32,512]{2,1,0:T(8,128)(2,1)S(1)}, u32[]{:S(2)}, u32[]{:S(2)}) async-start(bf16[16,32,512]{2,1,0:T(8,128)(2,1)} %broadcast_in_dim.18), calls=%async_computation | async-start | bytes 1048576 | tf_op jit(solution)/shard_map/all_to_all | solution.py:438
  11.8 29.1 %collective-permute-start.8 = (bf16[4096,256]{1,0:T(8,128)(2,1)}, bf16[4096,256]{1,0:T(8,128)(2,1)}, u32[]{:S(2)}, u32[]{:S(2)}) collective-permute-start(bf16[4096,256]{1,0:T(8,128)(2,1)} %bitcast.48), channel_id=1, source_target_pairs={{0,1},{1,0},{2,3},{3,2},{4,5},{5,4},{6,7},{7,6},{8,9},{9,8},{10,11... | collective-permute-start | bytes 6291464 | tf_op jit(solution)/shard_map/ppermute | solution.py:430
  12.4 5.3 %collective-permute-start.10 = (bf16[32,512]{1,0:T(8,128)(2,1)S(1)}, bf16[32,512]{1,0:T(8,128)(2,1)S(1)}, u32[]{:S(2)}, u32[]{:S(2)}) collective-permute-start(bf16[32,512]{1,0:T(8,128)(2,1)S(1)} %get-tuple-element.94), channel_id=1, source_target_pairs={{0,4},{2,6},{4,0},{6,2},{1,5},{3,7},{5,1},{7,3},{8,12},{10,14},{12... | collective-permute-start | bytes 98312 | tf_op jit(solution)/shard_map/ppermute | solution.py:434
  24.4 33.5 %all-to-all-start.1 = ((bf16[16,4,32,512]{3,2,1,0:T(8,128)(2,1)}), bf16[16,4,32,512]{3,2,1,0:T(8,128)(2,1)S(1)}, u32[]{:S(2)}, u32[]{:S(2)}) async-start(bf16[16,4,32,512]{3,2,1,0:T(8,128)(2,1)} %broadcast_in_dim.19), calls=%async_computation.1 | async-start | bytes 4194304 | tf_op jit(solution)/shard_map/all_to_all | solution.py:438
  29.0 7.0 %collective-permute-start.4 = (bf16[8,32,512]{2,1,0:T(8,128)(2,1)S(1)}, bf16[8,32,512]{2,1,0:T(8,128)(2,1)S(1)}, u32[]{:S(2)}, u32[]{:S(2)}) collective-permute-start(bf16[8,32,512]{2,1,0:T(8,128)(2,1)S(1)} %get-tuple-element.91), channel_id=1, source_target_pairs={{0,6},{2,0},{4,2},{6,4},{1,7},{3,1},{5,3},{7,5},{8,14},{10,8},{12,... | collective-permute-start | bytes 786440 | tf_op jit(solution)/shard_map/ppermute | solution.py:434
  32.0 7.4 %collective-permute-start.1 = (bf16[8,32,512]{2,1,0:T(8,128)(2,1)S(1)}, bf16[8,32,512]{2,1,0:T(8,128)(2,1)}, u32[]{:S(2)}, u32[]{:S(2)}) collective-permute-start(bf16[8,32,512]{2,1,0:T(8,128)(2,1)S(1)} %get-tuple-element.92), channel_id=1, source_target_pairs={{0,2},{2,4},{4,6},{6,0},{1,3},{3,5},{5,7},{7,1},{8,10},{10,12},{12... | collective-permute-start | bytes 786440 | tf_op jit(solution)/shard_map/ppermute | solution.py:434
  32.0 18.0 %collective-permute-start.2 = (bf16[8,32,512]{2,1,0:T(8,128)(2,1)S(1)}, bf16[8,32,512]{2,1,0:T(8,128)(2,1)}, u32[]{:S(2)}, u32[]{:S(2)}) collective-permute-start(bf16[8,32,512]{2,1,0:T(8,128)(2,1)S(1)} %get-tuple-element.91), channel_id=1, source_target_pairs={{0,2},{2,4},{4,6},{6,0},{1,3},{3,5},{5,7},{7,1},{8,10},{10,12},{12... | collective-permute-start | bytes 786440 | tf_op jit(solution)/shard_map/ppermute | solution.py:434
  36.0 14.0 %collective-permute-start.3 = (bf16[8,32,512]{2,1,0:T(8,128)(2,1)S(1)}, bf16[8,32,512]{2,1,0:T(8,128)(2,1)}, u32[]{:S(2)}, u32[]{:S(2)}) collective-permute-start(bf16[8,32,512]{2,1,0:T(8,128)(2,1)S(1)} %get-tuple-element.92), channel_id=1, source_target_pairs={{0,6},{2,0},{4,2},{6,4},{1,7},{3,1},{5,3},{7,5},{8,14},{10,8},{12,... | collective-permute-start | bytes 786440 | tf_op jit(solution)/shard_map/ppermute | solution.py:434
  39.4 10.6 %collective-permute-start.6 = (bf16[8,32,512]{2,1,0:T(8,128)(2,1)S(1)}, bf16[8,32,512]{2,1,0:T(8,128)(2,1)}, u32[]{:S(2)}, u32[]{:S(2)}) collective-permute-start(bf16[8,32,512]{2,1,0:T(8,128)(2,1)S(1)} %collective-permute-done.4), channel_id=1, source_target_pairs={{0,6},{2,0},{4,2},{6,4},{1,7},{3,1},{5,3},{7,5},{8,14},{10,8},{12,... | collective-permute-start | bytes 786440 | tf_op jit(solution)/shard_map/ppermute | solution.py:434
  39.5 11.0 %collective-permute-start.5 = (bf16[8,32,512]{2,1,0:T(8,128)(2,1)}, bf16[8,32,512]{2,1,0:T(8,128)(2,1)}, u32[]{:S(2)}, u32[]{:S(2)}) collective-permute-start(bf16[8,32,512]{2,1,0:T(8,128)(2,1)} %collective-permute-done.1), channel_id=1, source_target_pairs={{0,2},{2,4},{4,6},{6,0},{1,3},{3,5},{5,7},{7,1},{8,10},{10,12},{12... | collective-permute-start | bytes 786440 | tf_op jit(solution)/shard_map/ppermute | solution.py:434
  57.9 12.9 %collective-permute-start.12 = (bf16[256,512]{1,0:T(8,128)(2,1)S(1)}, bf16[256,512]{1,0:T(8,128)(2,1)S(1)}, u32[]{:S(2)}, u32[]{:S(2)}) collective-permute-start(bf16[256,512]{1,0:T(8,128)(2,1)S(1)} %get-tuple-element.54), channel_id=1, source_target_pairs={{0,1},{1,0},{2,3},{3,2},{4,5},{5,4},{6,7},{7,6},{8,9},{9,8},{10,11... | collective-permute-start | bytes 786440 | tf_op jit(solution)/shard_map/ppermute | solution.py:430
  70.8 30.5 %collective-permute-start.14 = (bf16[256,4096]{1,0:T(8,128)(2,1)}, bf16[256,4096]{1,0:T(8,128)(2,1)}, u32[]{:S(2)}, u32[]{:S(2)}) collective-permute-start(bf16[256,4096]{1,0:T(8,128)(2,1)} %get-tuple-element.60.near_a), channel_id=1, source_target_pairs={{0,1},{1,0},{2,3},{3,2},{4,5},{5,4},{6,7},{7,6},{8,9},{9,8},{10,11... | collective-permute-start | bytes 6291464 | tf_op jit(solution)/shard_map/ppermute | solution.py:430
  72.3 29.0 %collective-permute-start.15 = (bf16[256,4096]{1,0:T(8,128)(2,1)}, bf16[256,4096]{1,0:T(8,128)(2,1)}, u32[]{:S(2)}, u32[]{:S(2)}) collective-permute-start(bf16[256,4096]{1,0:T(8,128)(2,1)} %get-tuple-element.61.near_b), channel_id=1, source_target_pairs={{0,1},{1,0},{2,3},{3,2},{4,5},{5,4},{6,7},{7,6},{8,9},{9,8},{10,11... | collective-permute-start | bytes 6291464 | tf_op jit(solution)/shard_map/ppermute | solution.py:430
  84.5 41.1 %all-to-all-start.2 = ((bf16[16,272,256]{2,1,0:T(8,128)(2,1)}), bf16[16,272,256]{2,1,0:T(8,128)(2,1)S(1)}, u32[]{:S(2)}, u32[]{:S(2)}) async-start(bf16[16,272,256]{2,1,0:T(8,128)(2,1)} %bitcast.44), calls=%async_computation.2 | async-start | bytes 4456448 | tf_op jit(solution)/shard_map/all_to_all | solution.py:438
  97.6 17.6 %collective-permute-start.17 = (bf16[4,2,64,256]{3,2,1,0:T(8,128)(2,1)S(1)}, bf16[4,2,64,256]{3,2,1,0:T(8,128)(2,1)S(1)}, u32[]{:S(2)}, u32[]{:S(2)}) collective-permute-start(bf16[4,2,64,256]{3,2,1,0:T(8,128)(2,1)S(1)} %get-tuple-element.71), channel_id=1, source_target_pairs={{0,6},{2,0},{4,2},{6,4},{1,7},{3,1},{5,3},{7,5},{8,14},{10,8},{12,... | collective-permute-start | bytes 786440 | tf_op jit(solution)/shard_map/ppermute | solution.py:434
  98.6 13.6 %collective-permute-start.18 = (bf16[4,2,64,256]{3,2,1,0:T(8,128)(2,1)S(1)}, bf16[4,2,64,256]{3,2,1,0:T(8,128)(2,1)S(1)}, u32[]{:S(2)}, u32[]{:S(2)}) collective-permute-start(bf16[4,2,64,256]{3,2,1,0:T(8,128)(2,1)S(1)} %get-tuple-element.73), channel_id=1, source_target_pairs={{0,2},{2,4},{4,6},{6,0},{1,3},{3,5},{5,7},{7,1},{8,10},{10,12},{12... | collective-permute-start | bytes 786440 | tf_op jit(solution)/shard_map/ppermute | solution.py:434
  99.1 13.1 %collective-permute-start.19 = (bf16[4,2,64,256]{3,2,1,0:T(8,128)(2,1)S(1)}, bf16[4,2,64,256]{3,2,1,0:T(8,128)(2,1)S(1)}, u32[]{:S(2)}, u32[]{:S(2)}) collective-permute-start(bf16[4,2,64,256]{3,2,1,0:T(8,128)(2,1)S(1)} %get-tuple-element.74), channel_id=1, source_target_pairs={{0,6},{2,0},{4,2},{6,4},{1,7},{3,1},{5,3},{7,5},{8,14},{10,8},{12,... | collective-permute-start | bytes 786440 | tf_op jit(solution)/shard_map/ppermute | solution.py:434
  101.3 13.9 %collective-permute-start.21 = (bf16[4,2,64,256]{3,2,1,0:T(8,128)(2,1)S(1)}, bf16[4,2,64,256]{3,2,1,0:T(8,128)(2,1)S(1)}, u32[]{:S(2)}, u32[]{:S(2)}) collective-permute-start(bf16[4,2,64,256]{3,2,1,0:T(8,128)(2,1)S(1)} %get-tuple-element.76), channel_id=1, source_target_pairs={{0,2},{2,4},{4,6},{6,0},{1,3},{3,5},{5,7},{7,1},{8,10},{10,12},{12... | collective-permute-start | bytes 786440 | tf_op jit(solution)/shard_map/ppermute | solution.py:434
  112.3 6.6 %collective-permute-start.22 = (bf16[4,2,64,256]{3,2,1,0:T(8,128)(2,1)S(1)}, bf16[4,2,64,256]{3,2,1,0:T(8,128)(2,1)S(1)}, u32[]{:S(2)}, u32[]{:S(2)}) collective-permute-start(bf16[4,2,64,256]{3,2,1,0:T(8,128)(2,1)S(1)} %add_convert_fusion.1), channel_id=1, source_target_pairs={{0,6},{2,0},{4,2},{6,4},{1,7},{3,1},{5,3},{7,5},{8,14},{10,8},{12,... | collective-permute-start | bytes 786440 | tf_op jit(solution)/shard_map/ppermute | solution.py:434
  115.1 7.0 %collective-permute-start.20 = (bf16[4,2,64,256]{3,2,1,0:T(8,128)(2,1)S(1)}, bf16[4,2,64,256]{3,2,1,0:T(8,128)(2,1)S(1)}, u32[]{:S(2)}, u32[]{:S(2)}) collective-permute-start(bf16[4,2,64,256]{3,2,1,0:T(8,128)(2,1)S(1)} %add_convert_fusion.3), channel_id=1, source_target_pairs={{0,2},{2,4},{4,6},{6,0},{1,3},{3,5},{5,7},{7,1},{8,10},{10,12},{12... | collective-permute-start | bytes 786440 | tf_op jit(solution)/shard_map/ppermute | solution.py:434
  125.6 16.1 %all-to-all-start.3 = ((bf16[16,64,256]{2,1,0:T(8,128)(2,1)}), bf16[16,64,256]{2,1,0:T(8,128)(2,1)S(1)}, u32[]{:S(2)}, u32[]{:S(2)}) async-start(bf16[16,64,256]{2,1,0:T(8,128)(2,1)} %bitcast.45), calls=%async_computation.3 | async-start | bytes 1048576 | tf_op jit(solution)/shard_map/all_to_all | solution.py:438
  129.7 4.5 %collective-permute-start.24 = (bf16[80,256]{1,0:T(8,128)(2,1)S(1)}, bf16[80,256]{1,0:T(8,128)(2,1)S(1)}, u32[]{:S(2)}, u32[]{:S(2)}) collective-permute-start(bf16[80,256]{1,0:T(8,128)(2,1)S(1)} %get-tuple-element.83), channel_id=1, source_target_pairs={{0,4},{2,6},{4,0},{6,2},{1,5},{3,7},{5,1},{7,3},{8,12},{10,14},{12... | collective-permute-start | bytes 122888 | tf_op jit(solution)/shard_map/ppermute | solution.py:434
  135.5 6.2 %collective-permute-start.26 = (f32[64,256]{1,0:T(8,128)S(1)}, f32[64,256]{1,0:T(8,128)S(1)}, u32[]{:S(2)}, u32[]{:S(2)}) collective-permute-start(f32[64,256]{1,0:T(8,128)S(1)} %get-tuple-element.87), channel_id=1, source_target_pairs={{0,1},{1,0},{2,3},{3,2},{4,5},{5,4},{6,7},{7,6},{8,9},{9,8},{10,11... | collective-permute-start | bytes 196616 | tf_op jit(solution)/shard_map/ppermute | solution.py:430
  (18 other events, 107.2 us)

commit v12 on v11

--- a/solution.py
+++ b/solution.py
@@ -111,14 +111,18 @@
         rows_low[:, p * width : (p + 1) * width] = (wide * scale * gain_ref[p]).astype(BF16)
     out = pltpu.make_async_copy(rows_low, normed_ref, out_sem)
     out.start()
-    total = 0.0
-    for i, load in enumerate(loads):
-        load.wait()
-        first = z_ref[1] if i == 0 else 1 - z_ref[1]
-        columns = beside(*[rows_low[:, pl.ds(pl.multiple_of((2 * p + first) * HD, HD), HD)] for p in range(blocks)])
-        total += nn(columns, weights[i].reshape(blocks * HD, 4 * HD))
-    own_ref[...] = total[:, : 2 * HD].astype(BF16)
-    sib_ref[...] = total[:, 2 * HD :].astype(BF16)
+
+    def products(core):
+        total = 0.0
+        for i, load in enumerate(loads):
+            load.wait()
+            half = core if i == 0 else 1 - core
+            columns = beside(*[rows_low[:, (2 * p + half) * HD : (2 * p + half + 1) * HD] for p in range(blocks)])
+            total += nn(columns, weights[i].reshape(blocks * HD, 4 * HD))
+        own_ref[...] = total[:, : 2 * HD].astype(BF16)
+        sib_ref[...] = total[:, 2 * HD :].astype(BF16)
+
+    lax.cond(z_ref[1] == 0, lambda: products(0), lambda: products(1))
     out.wait()
 
 
@@ -465,6 +469,7 @@
     all_b = all_b.reshape(segs, 2, RING, part, width)
     low_0, high_0 = first_a[: plane // 2], first_a[plane // 2 :]
     low_3, high_1 = shifted(low_0, 1), shifted(high_0, -1)
+    high_0, low_0 = after((high_0, low_0), low_3, high_1)
     high_3, low_1 = shifted(high_0, 1), shifted(low_0, -1)
     low_2, high_2 = shifted(low_3, 1), shifted(high_1, -1)
     deep = lambda value: value.reshape(segs // 2, 2, part, width)

time: 144 us -> 145 us (level)
  waiting for transfers between devices: 25.7 us -> 28.5 us
  starting transfers between devices: 58.4 us -> 56.1 us
    ppermute x18, waiting for transfers between devices: 16.9 us -> 19.8 us  [shifted(): return lax.ppermute(value, 'z', [(i, (i + by) % RING) for i in range(RING)])]
where the time goes in v12:
time: 145 us; the launch traced here: 143 us
  starting transfers between devices  56.1 us (39%)
  Pallas kernels  50 us (34%)
  waiting for transfers between devices  28.5 us (20%)
  local copies, waits for them, and re-layouts  6.55 us (5%)
    all_to_all x4, starting transfers between devices, over_plane(): return lax.all_to_all(value, PLANE, 0, 0, tiled=True)  21.7 us
    ppermute x18, starting transfers between devices, shifted(): return lax.ppermute(value, 'z', [(i, (i + by) % RING) for i in range(RING)])  21.5 us
    ppermute x18, waiting for transfers between devices, shifted(): return lax.ppermute(value, 'z', [(i, (i + by) % RING) for i in range(RING)])  19.8 us
    pallas_call x2, Pallas kernels, project(): pl.pallas_call(functools.partial(project_body, pieces), in_specs=[SMEM, V...  14.7 us
    ppermute x9, starting transfers between devices, swapped(): return lax.ppermute(value, 'c', [(0, 1), (1, 0)])  12.9 us
    pallas_call x1, Pallas kernels, weight_grads(): pl.pallas_call(weights_body, grid=(hidden // width,), in_specs=[block] *...  10.9 us
    pallas_call x1, Pallas kernels, staged(): pl.pallas_call(stage_body, grid=(blocks,), in_specs=[SMEM] + [pl.BlockSpe...  9.05 us
    pallas_call x1, Pallas kernels, attention(): pl.pallas_call(functools.partial(attend_body, tile), in_specs=[VMEM] * 6,...  6.23 us
  transfers between devices with their start and end apart: 31, of which 16 were waited for; matrix products, arithmetic and copies ran while one was open for 3% of the time, Pallas kernels for 34%

profile of v12, /device:TPU:1, one launch (start us, length us, event | category | flops | bytes accessed | tf_op | source)
XLA Modules:
  0.0 143.5 jit_solution(9041583525467914610)
XLA Ops:
  5.0 6.8 %all-to-all-start = ((bf16[16,32,512]{2,1,0:T(8,128)(2,1)}), bf16[16,32,512]{2,1,0:T(8,128)(2,1)S(1)}, u32[]{:S(2)}, u32[]{:S(2)}) async-start(bf16[16,32,512]{2,1,0:T(8,128)(2,1)} %broadcast_in_dim.18), calls=%async_computation | async-start | bytes 1048576 | tf_op jit(solution)/shard_map/all_to_all | solution.py:442
  12.4 3.6 %collective-permute-start.10 = (bf16[32,512]{1,0:T(8,128)(2,1)S(1)}, bf16[32,512]{1,0:T(8,128)(2,1)S(1)}, u32[]{:S(2)}, u32[]{:S(2)}) collective-permute-start(bf16[32,512]{1,0:T(8,128)(2,1)S(1)} %get-tuple-element.98), channel_id=1, source_target_pairs={{0,4},{2,6},{4,0},{6,2},{1,5},{3,7},{5,1},{7,3},{8,12},{10,14},{12... | collective-permute-start | bytes 98312 | tf_op jit(solution)/shard_map/ppermute | solution.py:438
  24.4 4.5 %all-to-all-start.1 = ((bf16[16,4,32,512]{3,2,1,0:T(8,128)(2,1)}), bf16[16,4,32,512]{3,2,1,0:T(8,128)(2,1)S(1)}, u32[]{:S(2)}, u32[]{:S(2)}) async-start(bf16[16,4,32,512]{3,2,1,0:T(8,128)(2,1)} %broadcast_in_dim.19), calls=%async_computation.1 | async-start | bytes 4194304 | tf_op jit(solution)/shard_map/all_to_all | solution.py:442
  29.0 3.0 %collective-permute-start.2 = (bf16[8,32,512]{2,1,0:T(8,128)(2,1)S(1)}, bf16[8,32,512]{2,1,0:T(8,128)(2,1)S(1)}, u32[]{:S(2)}, u32[]{:S(2)}) collective-permute-start(bf16[8,32,512]{2,1,0:T(8,128)(2,1)S(1)} %get-tuple-element.49), channel_id=1, source_target_pairs={{0,6},{2,0},{4,2},{6,4},{1,7},{3,1},{5,3},{7,5},{8,14},{10,8},{12,... | collective-permute-start | bytes 786440 | tf_op jit(solution)/shard_map/ppermute | solution.py:438
  32.0 4.0 %collective-permute-done.2 = bf16[8,32,512]{2,1,0:T(8,128)(2,1)S(1)} collective-permute-done((bf16[8,32,512]{2,1,0:T(8,128)(2,1)S(1)}, bf16[8,32,512]{2,1,0:T(8,128)(2,1)S(1)}, u32[]{:S(2)}, u32[]{:S(2)}) %collective-permute-start.2) | collective-permute-done | bytes 262176 | tf_op jit(solution)/shard_map/ppermute | solution.py:438
  36.0 3.2 %collective-permute-done.1 = bf16[8,32,512]{2,1,0:T(8,128)(2,1)} collective-permute-done((bf16[8,32,512]{2,1,0:T(8,128)(2,1)S(1)}, bf16[8,32,512]{2,1,0:T(8,128)(2,1)}, u32[]{:S(2)}, u32[]{:S(2)}) %collective-permute-start.1) | collective-permute-done | bytes 262176 | tf_op jit(solution)/shard_map/ppermute | solution.py:438
  39.2 2.7 %collective-permute-start.6 = (bf16[8,32,512]{2,1,0:T(8,128)(2,1)S(1)}, bf16[8,32,512]{2,1,0:T(8,128)(2,1)}, u32[]{:S(2)}, u32[]{:S(2)}) collective-permute-start(bf16[8,32,512]{2,1,0:T(8,128)(2,1)S(1)} %collective-permute-done.2), channel_id=1, source_target_pairs={{0,6},{2,0},{4,2},{6,4},{1,7},{3,1},{5,3},{7,5},{8,14},{10,8},{12,... | collective-permute-start | bytes 786440 | tf_op jit(solution)/shard_map/ppermute | solution.py:438
  43.5 9.0 %stage.1 = (bf16[8,256,1024]{2,1,0:T(8,128)(2,1)}, bf16[8,256,1024]{2,1,0:T(8,128)(2,1)}) custom-call(s32[2]{0:T(128)S(1)} %pad_add_fusion.place_ref.z_ref, bf16[4096,256]{1,0:T(8,128)(2,1)} %bitcast.47, bf16[4096,256]{1,0:T(8,128)(2,1)} %bitcast.49, bf16[4096,256]{1,0:T(8,128)(2,1)} %collective-permute-done.7.refs_2_, ...), custom_call_target="tpu_custom_call" | custom-call | bytes 16777216 | tf_op jit(solution)/shard_map/stage/pallas_call | solution.py:70
  52.6 7.3 %project_a.1 = (bf16[256,512]{1,0:T(8,128)(2,1)S(1)}, bf16[256,512]{1,0:T(8,128)(2,1)S(1)}, f32[256,1]{1,0:T(8,128)S(1)}, bf16[256,4096]{1,0:T(8,128)(2,1)}) custom-call(s32[2]{0:T(128)S(1)} %pad_add_fusion.place_ref.z_ref, f32[8,1,512]{2,1,0:T(1,128)S(1)} %bitcast.37, bf16[8,2,32,512]{3,2,1,0:T(8,128)(2,1)} %bitcast.43, ...), custom_call_target="tpu_custom_call" | custom-call | flops 2147483648 | bytes 12582912 | tf_op jit(solution)/shard_map/project_a/pallas_call | solution.py:133
  59.9 4.1 %collective-permute-start.12 = (bf16[256,512]{1,0:T(8,128)(2,1)S(1)}, bf16[256,512]{1,0:T(8,128)(2,1)S(1)}, u32[]{:S(2)}, u32[]{:S(2)}) collective-permute-start(bf16[256,512]{1,0:T(8,128)(2,1)S(1)} %get-tuple-element.58), channel_id=1, source_target_pairs={{0,1},{1,0},{2,3},{3,2},{4,5},{5,4},{6,7},{7,6},{8,9},{9,8},{10,11... | collective-permute-start | bytes 786440 | tf_op jit(solution)/shard_map/ppermute | solution.py:434
  64.1 7.3 %project_b.1 = (bf16[256,512]{1,0:T(8,128)(2,1)S(1)}, bf16[256,512]{1,0:T(8,128)(2,1)S(1)}, f32[256,1]{1,0:T(8,128)S(1)}, bf16[256,4096]{1,0:T(8,128)(2,1)}) custom-call(s32[2]{0:T(128)S(1)} %pad_add_fusion.place_ref.z_ref, f32[8,1,512]{2,1,0:T(1,128)S(1)} %bitcast.38, bf16[8,2,4,32,512]{4,3,2,1,0:T(8,128)(2,1)S(1)} %bitcast.33, ...), custom_call_target="tpu_custom_call" | custom-call | flops 2147483648 | bytes 12582912 | tf_op jit(solution)/shard_map/project_b/pallas_call | solution.py:133
  73.2 6.2 %attention.1 = (bf16[1024,256]{1,0:T(8,128)(2,1)}, bf16[1024,256]{1,0:T(8,128)(2,1)}, bf16[512,512]{1,0:T(8,128)(2,1)S(1)}, bf16[528,512]{1,0:T(8,128)(2,1)S(1)}, f32[1,512]{1,0:T(1,128)S(1)}) custom-call(bf16[1024,256]{1,0:T(8,128)(2,1)S(1)} %bitcast.41, bf16[1024,256]{1,0:T(8,128)(2,1)S(1)} %bitcast.42, bf16[256,512]{1,0:T(8,128)(2,1)S(1)} %get-tuple-element.55.near_a, ...), custom_call_target="tpu_custom_call" | custom-call | flops 3221225472 | bytes 4194304 | tf_op jit(solution)/shard_map/attention/pallas_call | solution.py:214
  81.3 3.9 %back_b.1 = bf16[8,2,272,256]{3,2,1,0:T(8,128)(2,1)} custom-call(s32[2]{0:T(128)S(1)} %pad_add_fusion.place_ref.z_ref, bf16[512,512]{1,0:T(8,128)(2,1)S(1)} %get-tuple-element.66.gnear_ref.own_ref, bf16[528,512]{1,0:T(8,128)(2,1)S(1)} %collective-permute-done.16.sib_ref, f32[1,512]{1,0:T(1,128)S(1)} %get-tuple-element.72.dots_ref, ...), custom_call_target="tpu_custom_call" | custom-call | flops 2147483648 | bytes 4194304 | tf_op jit(solution)/shard_map/back_b/pallas_call | solution.py:262
  85.3 6.6 %all-to-all-start.2 = ((bf16[16,272,256]{2,1,0:T(8,128)(2,1)}), bf16[16,272,256]{2,1,0:T(8,128)(2,1)S(1)}, u32[]{:S(2)}, u32[]{:S(2)}) async-start(bf16[16,272,256]{2,1,0:T(8,128)(2,1)} %bitcast.44), calls=%async_computation.2 | async-start | bytes 4456448 | tf_op jit(solution)/shard_map/all_to_all | solution.py:442
  91.9 2.2 %copy-done = bf16[8,256,1024]{2,1,0:T(8,128)(2,1)S(1)} copy-done((bf16[8,256,1024]{2,1,0:T(8,128)(2,1)S(1)}, bf16[8,256,1024]{2,1,0:T(8,128)(2,1)}, u32[]{:S(2)}) %copy-start) | copy-done | bytes 4194328
  95.1 3.0 %back_a.1 = (bf16[4,2,64,256]{3,2,1,0:T(8,128)(2,1)S(1)}, bf16[4,2,64,256]{3,2,1,0:T(8,128)(2,1)S(1)}, bf16[4,2,64,256]{3,2,1,0:T(8,128)(2,1)S(1)}, bf16[4,2,64,...) custom-call(s32[2]{0:T(128)S(1)} %pad_add_fusion.place_ref.z_ref, ...), custom_call_target="tpu_custom_call" | custom-call | flops 2147483648 | bytes 4194304 | tf_op jit(solution)/shard_map/back_a/pallas_call | solution.py:295
  99.6 2.2 %collective-permute-start.19 = (bf16[4,2,64,256]{3,2,1,0:T(8,128)(2,1)S(1)}, bf16[4,2,64,256]{3,2,1,0:T(8,128)(2,1)S(1)}, u32[]{:S(2)}, u32[]{:S(2)}) collective-permute-start(bf16[4,2,64,256]{3,2,1,0:T(8,128)(2,1)S(1)} %get-tuple-element.78), channel_id=1, source_target_pairs={{0,6},{2,0},{4,2},{6,4},{1,7},{3,1},{5,3},{7,5},{8,14},{10,8},{12,... | collective-permute-start | bytes 786440 | tf_op jit(solution)/shard_map/ppermute | solution.py:438
  101.8 10.9 %weight_grads.1 = (f32[4096,256]{1,0:T(8,128)}, f32[4096,256]{1,0:T(8,128)}) custom-call(bf16[256,4096]{1,0:T(8,128)(2,1)} %get-tuple-element.64.near_a, bf16[256,4096]{1,0:T(8,128)(2,1)} %get-tuple-element.65.near_b, bf16[256,4096]{1,0:T(8,128)(2,1)} %collective-permute-done.14.far_a, bf16[256,4096]{1,0:T(8,128)(2,1)} %collective-permute-done.15.far_b, ...), custom_call_target="tpu_custom_call" | custom-call | flops 4294967296 | bytes 17825792 | tf_op jit(solution)/shard_map/weight_grads/pallas_call | solution.py:319
  112.8 2.7 %collective-permute-start.22 = (bf16[4,2,64,256]{3,2,1,0:T(8,128)(2,1)S(1)}, bf16[4,2,64,256]{3,2,1,0:T(8,128)(2,1)S(1)}, u32[]{:S(2)}, u32[]{:S(2)}) collective-permute-start(bf16[4,2,64,256]{3,2,1,0:T(8,128)(2,1)S(1)} %add_convert_fusion.1), channel_id=1, source_target_pairs={{0,6},{2,0},{4,2},{6,4},{1,7},{3,1},{5,3},{7,5},{8,14},{10,8},{12,... | collective-permute-start | bytes 786440 | tf_op jit(solution)/shard_map/ppermute | solution.py:438
  115.7 3.7 %collective-permute-done.22 = bf16[4,2,64,256]{3,2,1,0:T(8,128)(2,1)S(1)} collective-permute-done((bf16[4,2,64,256]{3,2,1,0:T(8,128)(2,1)S(1)}, bf16[4,2,64,256]{3,2,1,0:T(8,128)(2,1)S(1)}, u32[]{:S(2)}, u32[]{:S(2)}) %collective-permute-start.22) | collective-permute-done | bytes 262176 | tf_op jit(solution)/shard_map/ppermute | solution.py:438
  119.3 3.3 %collective-permute-done.20 = bf16[4,2,64,256]{3,2,1,0:T(8,128)(2,1)S(1)} collective-permute-done((bf16[4,2,64,256]{3,2,1,0:T(8,128)(2,1)S(1)}, bf16[4,2,64,256]{3,2,1,0:T(8,128)(2,1)S(1)}, u32[]{:S(2)}, u32[]{:S(2)}) %collective-permute-start.20) | collective-permute-done | bytes 262176 | tf_op jit(solution)/shard_map/ppermute | solution.py:438
  123.7 2.4 %all-to-all-done.2.arrived_ref = bf16[16,272,256]{2,1,0:T(8,128)(2,1)S(1)} async-done(((bf16[16,272,256]{2,1,0:T(8,128)(2,1)}), bf16[16,272,256]{2,1,0:T(8,128)(2,1)S(1)}, u32[]{:S(2)}, u32[]{:S(2)}) %all-to-all-start.2) | async-done | bytes 2228256 | tf_op jit(solution)/shard_map/all_to_all | solution.py:442
  126.1 3.8 %all-to-all-start.3 = ((bf16[16,64,256]{2,1,0:T(8,128)(2,1)}), bf16[16,64,256]{2,1,0:T(8,128)(2,1)S(1)}, u32[]{:S(2)}, u32[]{:S(2)}) async-start(bf16[16,64,256]{2,1,0:T(8,128)(2,1)} %bitcast.45), calls=%async_computation.3 | async-start | bytes 1048576 | tf_op jit(solution)/shard_map/all_to_all | solution.py:442
  136.0 5.3 %collective-permute-start.26 = (f32[64,256]{1,0:T(8,128)S(1)}, f32[64,256]{1,0:T(8,128)S(1)}, u32[]{:S(2)}, u32[]{:S(2)}) collective-permute-start(f32[64,256]{1,0:T(8,128)S(1)} %get-tuple-element.91), channel_id=1, source_target_pairs={{0,1},{1,0},{2,3},{3,2},{4,5},{5,4},{6,7},{7,6},{8,9},{9,8},{10,11... | collective-permute-start | bytes 196616 | tf_op jit(solution)/shard_map/ppermute | solution.py:434
  (83 shorter events, 30.8 us)
Async XLA Ops:
  3.7 38.2 %collective-permute-start.7 = (bf16[4096,256]{1,0:T(8,128)(2,1)}, bf16[4096,256]{1,0:T(8,128)(2,1)}, u32[]{:S(2)}, u32[]{:S(2)}) collective-permute-start(bf16[4096,256]{1,0:T(8,128)(2,1)} %bitcast.46), channel_id=1, source_target_pairs={{0,1},{1,0},{2,3},{3,2},{4,5},{5,4},{6,7},{7,6},{8,9},{9,8},{10,11... | collective-permute-start | bytes 6291464 | tf_op jit(solution)/shard_map/ppermute | solution.py:434
  5.0 17.8 %all-to-all-start = ((bf16[16,32,512]{2,1,0:T(8,128)(2,1)}), bf16[16,32,512]{2,1,0:T(8,128)(2,1)S(1)}, u32[]{:S(2)}, u32[]{:S(2)}) async-start(bf16[16,32,512]{2,1,0:T(8,128)(2,1)} %broadcast_in_dim.18), calls=%async_computation | async-start | bytes 1048576 | tf_op jit(solution)/shard_map/all_to_all | solution.py:442
  11.8 31.6 %collective-permute-start.8 = (bf16[4096,256]{1,0:T(8,128)(2,1)}, bf16[4096,256]{1,0:T(8,128)(2,1)}, u32[]{:S(2)}, u32[]{:S(2)}) collective-permute-start(bf16[4096,256]{1,0:T(8,128)(2,1)} %bitcast.48), channel_id=1, source_target_pairs={{0,1},{1,0},{2,3},{3,2},{4,5},{5,4},{6,7},{7,6},{8,9},{9,8},{10,11... | collective-permute-start | bytes 6291464 | tf_op jit(solution)/shard_map/ppermute | solution.py:434
  12.4 5.3 %collective-permute-start.10 = (bf16[32,512]{1,0:T(8,128)(2,1)S(1)}, bf16[32,512]{1,0:T(8,128)(2,1)S(1)}, u32[]{:S(2)}, u32[]{:S(2)}) collective-permute-start(bf16[32,512]{1,0:T(8,128)(2,1)S(1)} %get-tuple-element.98), channel_id=1, source_target_pairs={{0,4},{2,6},{4,0},{6,2},{1,5},{3,7},{5,1},{7,3},{8,12},{10,14},{12... | collective-permute-start | bytes 98312 | tf_op jit(solution)/shard_map/ppermute | solution.py:438
  24.4 35.5 %all-to-all-start.1 = ((bf16[16,4,32,512]{3,2,1,0:T(8,128)(2,1)}), bf16[16,4,32,512]{3,2,1,0:T(8,128)(2,1)S(1)}, u32[]{:S(2)}, u32[]{:S(2)}) async-start(bf16[16,4,32,512]{3,2,1,0:T(8,128)(2,1)} %broadcast_in_dim.19), calls=%async_computation.1 | async-start | bytes 4194304 | tf_op jit(solution)/shard_map/all_to_all | solution.py:442
  29.0 7.0 %collective-permute-start.2 = (bf16[8,32,512]{2,1,0:T(8,128)(2,1)S(1)}, bf16[8,32,512]{2,1,0:T(8,128)(2,1)S(1)}, u32[]{:S(2)}, u32[]{:S(2)}) collective-permute-start(bf16[8,32,512]{2,1,0:T(8,128)(2,1)S(1)} %get-tuple-element.49), channel_id=1, source_target_pairs={{0,6},{2,0},{4,2},{6,4},{1,7},{3,1},{5,3},{7,5},{8,14},{10,8},{12,... | collective-permute-start | bytes 786440 | tf_op jit(solution)/shard_map/ppermute | solution.py:438
  32.0 7.3 %collective-permute-start.1 = (bf16[8,32,512]{2,1,0:T(8,128)(2,1)S(1)}, bf16[8,32,512]{2,1,0:T(8,128)(2,1)}, u32[]{:S(2)}, u32[]{:S(2)}) collective-permute-start(bf16[8,32,512]{2,1,0:T(8,128)(2,1)S(1)} %get-tuple-element.50), channel_id=1, source_target_pairs={{0,2},{2,4},{4,6},{6,0},{1,3},{3,5},{5,7},{7,1},{8,10},{10,12},{12... | collective-permute-start | bytes 786440 | tf_op jit(solution)/shard_map/ppermute | solution.py:438
  39.2 13.3 %collective-permute-start.3 = (bf16[8,32,512]{2,1,0:T(8,128)(2,1)S(1)}, bf16[8,32,512]{2,1,0:T(8,128)(2,1)}, u32[]{:S(2)}, u32[]{:S(2)}) collective-permute-start(bf16[8,32,512]{2,1,0:T(8,128)(2,1)S(1)} %get-tuple-element.49), channel_id=1, source_target_pairs={{0,2},{2,4},{4,6},{6,0},{1,3},{3,5},{5,7},{7,1},{8,10},{10,12},{12... | collective-permute-start | bytes 786440 | tf_op jit(solution)/shard_map/ppermute | solution.py:438
  39.2 13.3 %collective-permute-start.6 = (bf16[8,32,512]{2,1,0:T(8,128)(2,1)S(1)}, bf16[8,32,512]{2,1,0:T(8,128)(2,1)}, u32[]{:S(2)}, u32[]{:S(2)}) collective-permute-start(bf16[8,32,512]{2,1,0:T(8,128)(2,1)S(1)} %collective-permute-done.2), channel_id=1, source_target_pairs={{0,6},{2,0},{4,2},{6,4},{1,7},{3,1},{5,3},{7,5},{8,14},{10,8},{12,... | collective-permute-start | bytes 786440 | tf_op jit(solution)/shard_map/ppermute | solution.py:438
  41.9 10.6 %collective-permute-start.4 = (bf16[8,32,512]{2,1,0:T(8,128)(2,1)S(1)}, bf16[8,32,512]{2,1,0:T(8,128)(2,1)}, u32[]{:S(2)}, u32[]{:S(2)}) collective-permute-start(bf16[8,32,512]{2,1,0:T(8,128)(2,1)S(1)} %get-tuple-element.50), channel_id=1, source_target_pairs={{0,6},{2,0},{4,2},{6,4},{1,7},{3,1},{5,3},{7,5},{8,14},{10,8},{12,... | collective-permute-start | bytes 786440 | tf_op jit(solution)/shard_map/ppermute | solution.py:438
  41.9 10.6 %collective-permute-start.5 = (bf16[8,32,512]{2,1,0:T(8,128)(2,1)}, bf16[8,32,512]{2,1,0:T(8,128)(2,1)}, u32[]{:S(2)}, u32[]{:S(2)}) collective-permute-start(bf16[8,32,512]{2,1,0:T(8,128)(2,1)} %collective-permute-done.1), channel_id=1, source_target_pairs={{0,2},{2,4},{4,6},{6,0},{1,3},{3,5},{5,7},{7,1},{8,10},{10,12},{12... | collective-permute-start | bytes 786440 | tf_op jit(solution)/shard_map/ppermute | solution.py:438
  59.9 11.6 %collective-permute-start.12 = (bf16[256,512]{1,0:T(8,128)(2,1)S(1)}, bf16[256,512]{1,0:T(8,128)(2,1)S(1)}, u32[]{:S(2)}, u32[]{:S(2)}) collective-permute-start(bf16[256,512]{1,0:T(8,128)(2,1)S(1)} %get-tuple-element.58), channel_id=1, source_target_pairs={{0,1},{1,0},{2,3},{3,2},{4,5},{5,4},{6,7},{7,6},{8,9},{9,8},{10,11... | collective-permute-start | bytes 786440 | tf_op jit(solution)/shard_map/ppermute | solution.py:434
  71.5 30.3 %collective-permute-start.14 = (bf16[256,4096]{1,0:T(8,128)(2,1)}, bf16[256,4096]{1,0:T(8,128)(2,1)}, u32[]{:S(2)}, u32[]{:S(2)}) collective-permute-start(bf16[256,4096]{1,0:T(8,128)(2,1)} %get-tuple-element.64.near_a), channel_id=1, source_target_pairs={{0,1},{1,0},{2,3},{3,2},{4,5},{5,4},{6,7},{7,6},{8,9},{9,8},{10,11... | collective-permute-start | bytes 6291464 | tf_op jit(solution)/shard_map/ppermute | solution.py:434
  73.0 28.8 %collective-permute-start.15 = (bf16[256,4096]{1,0:T(8,128)(2,1)}, bf16[256,4096]{1,0:T(8,128)(2,1)}, u32[]{:S(2)}, u32[]{:S(2)}) collective-permute-start(bf16[256,4096]{1,0:T(8,128)(2,1)} %get-tuple-element.65.near_b), channel_id=1, source_target_pairs={{0,1},{1,0},{2,3},{3,2},{4,5},{5,4},{6,7},{7,6},{8,9},{9,8},{10,11... | collective-permute-start | bytes 6291464 | tf_op jit(solution)/shard_map/ppermute | solution.py:434
  85.3 40.8 %all-to-all-start.2 = ((bf16[16,272,256]{2,1,0:T(8,128)(2,1)}), bf16[16,272,256]{2,1,0:T(8,128)(2,1)S(1)}, u32[]{:S(2)}, u32[]{:S(2)}) async-start(bf16[16,272,256]{2,1,0:T(8,128)(2,1)} %bitcast.44), calls=%async_computation.2 | async-start | bytes 4456448 | tf_op jit(solution)/shard_map/all_to_all | solution.py:442
  98.1 17.6 %collective-permute-start.17 = (bf16[4,2,64,256]{3,2,1,0:T(8,128)(2,1)S(1)}, bf16[4,2,64,256]{3,2,1,0:T(8,128)(2,1)S(1)}, u32[]{:S(2)}, u32[]{:S(2)}) collective-permute-start(bf16[4,2,64,256]{3,2,1,0:T(8,128)(2,1)S(1)} %get-tuple-element.75), channel_id=1, source_target_pairs={{0,6},{2,0},{4,2},{6,4},{1,7},{3,1},{5,3},{7,5},{8,14},{10,8},{12,... | collective-permute-start | bytes 786440 | tf_op jit(solution)/shard_map/ppermute | solution.py:438
  99.1 13.6 %collective-permute-start.18 = (bf16[4,2,64,256]{3,2,1,0:T(8,128)(2,1)S(1)}, bf16[4,2,64,256]{3,2,1,0:T(8,128)(2,1)S(1)}, u32[]{:S(2)}, u32[]{:S(2)}) collective-permute-start(bf16[4,2,64,256]{3,2,1,0:T(8,128)(2,1)S(1)} %get-tuple-element.77), channel_id=1, source_target_pairs={{0,2},{2,4},{4,6},{6,0},{1,3},{3,5},{5,7},{7,1},{8,10},{10,12},{12... | collective-permute-start | bytes 786440 | tf_op jit(solution)/shard_map/ppermute | solution.py:438
  99.6 13.1 %collective-permute-start.19 = (bf16[4,2,64,256]{3,2,1,0:T(8,128)(2,1)S(1)}, bf16[4,2,64,256]{3,2,1,0:T(8,128)(2,1)S(1)}, u32[]{:S(2)}, u32[]{:S(2)}) collective-permute-start(bf16[4,2,64,256]{3,2,1,0:T(8,128)(2,1)S(1)} %get-tuple-element.78), channel_id=1, source_target_pairs={{0,6},{2,0},{4,2},{6,4},{1,7},{3,1},{5,3},{7,5},{8,14},{10,8},{12,... | collective-permute-start | bytes 786440 | tf_op jit(solution)/shard_map/ppermute | solution.py:438
  101.8 13.9 %collective-permute-start.21 = (bf16[4,2,64,256]{3,2,1,0:T(8,128)(2,1)S(1)}, bf16[4,2,64,256]{3,2,1,0:T(8,128)(2,1)S(1)}, u32[]{:S(2)}, u32[]{:S(2)}) collective-permute-start(bf16[4,2,64,256]{3,2,1,0:T(8,128)(2,1)S(1)} %get-tuple-element.80), channel_id=1, source_target_pairs={{0,2},{2,4},{4,6},{6,0},{1,3},{3,5},{5,7},{7,1},{8,10},{10,12},{12... | collective-permute-start | bytes 786440 | tf_op jit(solution)/shard_map/ppermute | solution.py:438
  112.8 6.6 %collective-permute-start.22 = (bf16[4,2,64,256]{3,2,1,0:T(8,128)(2,1)S(1)}, bf16[4,2,64,256]{3,2,1,0:T(8,128)(2,1)S(1)}, u32[]{:S(2)}, u32[]{:S(2)}) collective-permute-start(bf16[4,2,64,256]{3,2,1,0:T(8,128)(2,1)S(1)} %add_convert_fusion.1), channel_id=1, source_target_pairs={{0,6},{2,0},{4,2},{6,4},{1,7},{3,1},{5,3},{7,5},{8,14},{10,8},{12,... | collective-permute-start | bytes 786440 | tf_op jit(solution)/shard_map/ppermute | solution.py:438
  115.6 7.0 %collective-permute-start.20 = (bf16[4,2,64,256]{3,2,1,0:T(8,128)(2,1)S(1)}, bf16[4,2,64,256]{3,2,1,0:T(8,128)(2,1)S(1)}, u32[]{:S(2)}, u32[]{:S(2)}) collective-permute-start(bf16[4,2,64,256]{3,2,1,0:T(8,128)(2,1)S(1)} %add_convert_fusion.3), channel_id=1, source_target_pairs={{0,2},{2,4},{4,6},{6,0},{1,3},{3,5},{5,7},{7,1},{8,10},{10,12},{12... | collective-permute-start | bytes 786440 | tf_op jit(solution)/shard_map/ppermute | solution.py:438
  126.1 16.1 %all-to-all-start.3 = ((bf16[16,64,256]{2,1,0:T(8,128)(2,1)}), bf16[16,64,256]{2,1,0:T(8,128)(2,1)S(1)}, u32[]{:S(2)}, u32[]{:S(2)}) async-start(bf16[16,64,256]{2,1,0:T(8,128)(2,1)} %bitcast.45), calls=%async_computation.3 | async-start | bytes 1048576 | tf_op jit(solution)/shard_map/all_to_all | solution.py:442
  130.2 4.5 %collective-permute-start.24 = (bf16[80,256]{1,0:T(8,128)(2,1)S(1)}, bf16[80,256]{1,0:T(8,128)(2,1)S(1)}, u32[]{:S(2)}, u32[]{:S(2)}) collective-permute-start(bf16[80,256]{1,0:T(8,128)(2,1)S(1)} %get-tuple-element.87), channel_id=1, source_target_pairs={{0,4},{2,6},{4,0},{6,2},{1,5},{3,7},{5,1},{7,3},{8,12},{10,14},{12... | collective-permute-start | bytes 122888 | tf_op jit(solution)/shard_map/ppermute | solution.py:438
  136.0 6.2 %collective-permute-start.26 = (f32[64,256]{1,0:T(8,128)S(1)}, f32[64,256]{1,0:T(8,128)S(1)}, u32[]{:S(2)}, u32[]{:S(2)}) collective-permute-start(f32[64,256]{1,0:T(8,128)S(1)} %get-tuple-element.91), channel_id=1, source_target_pairs={{0,1},{1,0},{2,3},{3,2},{4,5},{5,4},{6,7},{7,6},{8,9},{9,8},{10,11... | collective-permute-start | bytes 196616 | tf_op jit(solution)/shard_map/ppermute | solution.py:434
  (18 other events, 106.8 us)

commit v13 on v7

--- a/solution.py
+++ b/solution.py
@@ -446,7 +446,7 @@
     low_2, high_2 = shifted(low_3, 1), shifted(high_1, -1)
     deep = lambda value: value.reshape(segs // 2, 2, part, width)
 
-    key_own, value_own = after((key_weight[0], value_weight[0]), near_z, first_a)
+    key_own, value_own = after((key_weight[0], value_weight[0]), block)
     weights = staged((key_own, value_own, swapped(key_own), swapped(value_own)))
 
     top = segs // 2
@@ -456,9 +456,11 @@
     own_a, sib_a, scale_a, normed_a = project(pieces_a, xs_a, z_array, norm_gain, weights, segs, "project_a")
     far_a = swapped(sib_a)
     all_b, = after((all_b,), own_a)
+    normed_far_a = swapped(after((normed_a,), all_b, far_a)[0])
     pieces_b = [(d, 0, d) for d in range(RING)]
     own_b, sib_b, scale_b, normed_b = project(pieces_b, [all_b] * RING, z_array, norm_gain, weights, segs, "project_b")
     far_b = swapped(sib_b)
+    normed_far_b = swapped(after((normed_b,), far_b)[0])
     context, query_grad, gnear, gfar, near_dots = attention(queries[0], context_grad[0], own_a, own_b, far_a, far_b)
     gsib = swapped(gfar)
 
@@ -466,10 +468,10 @@
     arrived_b = over_plane(parts_b.reshape(plane, RING * half + EXTRA, HD))
     z_later, = after((z_array,), parts_b)
     opp_low, opp_high, up_low, up_high, down_low, down_high, kept = back_a(z_later, gnear, gsib, weights[0], segs)
-    normed_far = [swapped(v) for v in after((normed_a, normed_b), parts_b)]
     from_low, from_high = shifted(opp_low, 1), shifted(opp_high, -1)
     got_high, got_low = shifted(up_high, 1), shifted(down_low, -1)
-    key_grad, value_grad = weight_grads(normed_a, normed_b, *normed_far, gnear, gfar)
+    all_normed = (normed_a, normed_b, normed_far_a, normed_far_b)
+    key_grad, value_grad = weight_grads(*all_normed, gnear, gfar)
     from_low, from_high = after((from_low, from_high), key_grad, value_grad)
     last_low = shifted((wide(up_low) + wide(from_low)).astype(BF16), 1)
     last_high = shifted((wide(down_high) + wide(from_high)).astype(BF16), -1)

time: 145 us -> 144 us (level)
  waiting for transfers between devices: 33.7 us -> 29.9 us
  starting transfers between devices: 54.6 us -> 57.5 us
    ppermute x9, starting transfers between devices: 9.99 us -> 13.4 us  [swapped(): return lax.ppermute(value, 'c', [(0, 1), (1, 0)])]
    all_to_all x4, waiting for transfers between devices: 10.5 us -> 8.51 us  [over_plane(): return lax.all_to_all(value, PLANE, 0, 0, tiled=True)]
  transfers between devices with their start and end apart: 31 -> 31, of which waited for: 16 -> 17; matrix products, arithmetic and copies ran while one was open for 2% -> 3% of each run, Pallas kernels for 25% -> 32%
where the time goes in v13:
time: 144 us; the launch traced here: 143 us
  starting transfers between devices  57.5 us (40%)
  Pallas kernels  46.3 us (32%)
  waiting for transfers between devices  29.9 us (21%)
  local copies, waits for them, and re-layouts  6.55 us (5%)
  other arithmetic  1.98 us (1%)
    ppermute x18, starting transfers between devices, shifted(): return lax.ppermute(value, 'z', [(i, (i + by) % RING) for i in range(RING)])  22.3 us
    all_to_all x4, starting transfers between devices, over_plane(): return lax.all_to_all(value, PLANE, 0, 0, tiled=True)  21.8 us
    ppermute x18, waiting for transfers between devices, shifted(): return lax.ppermute(value, 'z', [(i, (i + by) % RING) for i in range(RING)])  17 us
    pallas_call x2, Pallas kernels, project(): pl.pallas_call(functools.partial(project_body, pieces), in_specs=[SMEM, V...  13.5 us
    ppermute x9, starting transfers between devices, swapped(): return lax.ppermute(value, 'c', [(0, 1), (1, 0)])  13.4 us
    pallas_call x1, Pallas kernels, weight_grads(): pl.pallas_call(weights_body, grid=(hidden // width,), in_specs=[block] *...  10.8 us
    pallas_call x1, Pallas kernels, staged(): pl.pallas_call(stage_body, grid=(blocks,), in_specs=[pl.BlockSpec((2 * HD...  9.05 us
    all_to_all x4, waiting for transfers between devices, over_plane(): return lax.all_to_all(value, PLANE, 0, 0, tiled=True)  8.51 us
  transfers between devices with their start and end apart: 31, of which 17 were waited for; matrix products, arithmetic and copies ran while one was open for 3% of the time, Pallas kernels for 32%

profile of v13, /device:TPU:1, one launch (start us, length us, event | category | flops | bytes accessed | tf_op | source)
XLA Modules:
  0.0 143.1 jit_solution(17834431643956162306)
XLA Ops:
  5.0 6.8 %all-to-all-start = ((bf16[16,32,512]{2,1,0:T(8,128)(2,1)}), bf16[16,32,512]{2,1,0:T(8,128)(2,1)S(1)}, u32[]{:S(2)}, u32[]{:S(2)}) async-start(bf16[16,32,512]{2,1,0:T(8,128)(2,1)} %broadcast_in_dim.18), calls=%async_computation | async-start | bytes 1048576 | tf_op jit(solution)/shard_map/all_to_all | solution.py:415
  12.4 3.6 %collective-permute-start.10 = (bf16[32,512]{1,0:T(8,128)(2,1)S(1)}, bf16[32,512]{1,0:T(8,128)(2,1)S(1)}, u32[]{:S(2)}, u32[]{:S(2)}) collective-permute-start(bf16[32,512]{1,0:T(8,128)(2,1)S(1)} %get-tuple-element.92), channel_id=1, source_target_pairs={{0,4},{2,6},{4,0},{6,2},{1,5},{3,7},{5,1},{7,3},{8,12},{10,14},{12... | collective-permute-start | bytes 98312 | tf_op jit(solution)/shard_map/ppermute | solution.py:411
  24.4 4.5 %all-to-all-start.1 = ((bf16[16,4,32,512]{3,2,1,0:T(8,128)(2,1)}), bf16[16,4,32,512]{3,2,1,0:T(8,128)(2,1)S(1)}, u32[]{:S(2)}, u32[]{:S(2)}) async-start(bf16[16,4,32,512]{3,2,1,0:T(8,128)(2,1)} %broadcast_in_dim.19), calls=%async_computation.1 | async-start | bytes 4194304 | tf_op jit(solution)/shard_map/all_to_all | solution.py:415
  29.0 3.0 %collective-permute-start.4 = (bf16[8,32,512]{2,1,0:T(8,128)(2,1)S(1)}, bf16[8,32,512]{2,1,0:T(8,128)(2,1)S(1)}, u32[]{:S(2)}, u32[]{:S(2)}) collective-permute-start(bf16[8,32,512]{2,1,0:T(8,128)(2,1)S(1)} %get-tuple-element.89), channel_id=1, source_target_pairs={{0,6},{2,0},{4,2},{6,4},{1,7},{3,1},{5,3},{7,5},{8,14},{10,8},{12,... | collective-permute-start | bytes 786440 | tf_op jit(solution)/shard_map/ppermute | solution.py:411
  32.0 4.0 %collective-permute-done.4 = bf16[8,32,512]{2,1,0:T(8,128)(2,1)S(1)} collective-permute-done((bf16[8,32,512]{2,1,0:T(8,128)(2,1)S(1)}, bf16[8,32,512]{2,1,0:T(8,128)(2,1)S(1)}, u32[]{:S(2)}, u32[]{:S(2)}) %collective-permute-start.4) | collective-permute-done | bytes 262176 | tf_op jit(solution)/shard_map/ppermute | solution.py:411
  36.0 3.4 %collective-permute-start.3 = (bf16[8,32,512]{2,1,0:T(8,128)(2,1)S(1)}, bf16[8,32,512]{2,1,0:T(8,128)(2,1)}, u32[]{:S(2)}, u32[]{:S(2)}) collective-permute-start(bf16[8,32,512]{2,1,0:T(8,128)(2,1)S(1)} %get-tuple-element.90), channel_id=1, source_target_pairs={{0,6},{2,0},{4,2},{6,4},{1,7},{3,1},{5,3},{7,5},{8,14},{10,8},{12,... | collective-permute-start | bytes 786440 | tf_op jit(solution)/shard_map/ppermute | solution.py:411
  40.9 9.1 %stage.1 = (bf16[8,256,1024]{2,1,0:T(8,128)(2,1)}, bf16[8,256,1024]{2,1,0:T(8,128)(2,1)}) custom-call(bf16[4096,256]{1,0:T(8,128)(2,1)} %bitcast.46, bf16[4096,256]{1,0:T(8,128)(2,1)} %bitcast.48, bf16[4096,256]{1,0:T(8,128)(2,1)} %collective-permute-done.7.refs_2_, bf16[4096,256]{1,0:T(8,128)(2,1)} %collective-permute-done.8.refs_3_), custom_call_target="tpu_custom_call" | custom-call | bytes 16777216 | tf_op jit(solution)/shard_map/stage/pallas_call | solution.py:68
  50.5 6.7 %project_a.1 = (bf16[256,512]{1,0:T(8,128)(2,1)S(1)}, bf16[256,512]{1,0:T(8,128)(2,1)S(1)}, f32[256,1]{1,0:T(8,128)S(1)}, bf16[256,4096]{1,0:T(8,128)(2,1)}) custom-call(s32[1]{0:T(128)} %bitcast.2.z_ref, f32[8,1,512]{2,1,0:T(1,128)S(1)} %bitcast.37, bf16[8,2,32,512]{3,2,1,0:T(8,128)(2,1)} %bitcast.42, bf16[4,2,32,512]{3,2,1,0:T(8,128)(2,1)} %bitcast.50, ...), custom_call_target="tpu_custom_call" | custom-call | flops 2147483648 | bytes 12582912 | tf_op jit(solution)/shard_map/project_a/pallas_call | solution.py:126
  57.2 5.2 %collective-permute-start.12 = (bf16[256,512]{1,0:T(8,128)(2,1)S(1)}, bf16[256,512]{1,0:T(8,128)(2,1)S(1)}, u32[]{:S(2)}, u32[]{:S(2)}) collective-permute-start(bf16[256,512]{1,0:T(8,128)(2,1)S(1)} %get-tuple-element.53), channel_id=1, source_target_pairs={{0,1},{1,0},{2,3},{3,2},{4,5},{5,4},{6,7},{7,6},{8,9},{9,8},{10,11... | collective-permute-start | bytes 786440 | tf_op jit(solution)/shard_map/ppermute | solution.py:407
  62.5 6.8 %project_b.1 = (bf16[256,512]{1,0:T(8,128)(2,1)S(1)}, bf16[256,512]{1,0:T(8,128)(2,1)S(1)}, f32[256,1]{1,0:T(8,128)S(1)}, bf16[256,4096]{1,0:T(8,128)(2,1)}) custom-call(s32[1]{0:T(128)} %bitcast.2.z_ref, f32[8,1,512]{2,1,0:T(1,128)S(1)} %bitcast.38, bf16[8,2,4,32,512]{4,3,2,1,0:T(8,128)(2,1)S(1)} %bitcast.33, bf16[8,2,4,32,512]{4,3,2,1,0:T(8,128)(2,1)S(1)} %bitcast.34, ...), custom_call_target="tpu_custom_call" | custom-call | flops 2147483648 | bytes 12582912 | tf_op jit(solution)/shard_map/project_b/pallas_call | solution.py:126
  71.1 6.2 %attention.1 = (bf16[1024,256]{1,0:T(8,128)(2,1)}, bf16[1024,256]{1,0:T(8,128)(2,1)}, bf16[512,512]{1,0:T(8,128)(2,1)S(1)}, bf16[528,512]{1,0:T(8,128)(2,1)S(1)}, f32[1,512]{1,0:T(1,128)S(1)}) custom-call(bf16[1024,256]{1,0:T(8,128)(2,1)S(1)} %bitcast.40, bf16[1024,256]{1,0:T(8,128)(2,1)S(1)} %bitcast.41, bf16[256,512]{1,0:T(8,128)(2,1)S(1)} %get-tuple-element.50.near_a, ...), custom_call_target="tpu_custom_call" | custom-call | flops 3221225472 | bytes 4194304 | tf_op jit(solution)/shard_map/attention/pallas_call | solution.py:207
  79.2 3.3 %back_b.1 = bf16[8,2,272,256]{3,2,1,0:T(8,128)(2,1)} custom-call(s32[1]{0:T(128)} %bitcast.2.z_ref, bf16[512,512]{1,0:T(8,128)(2,1)S(1)} %get-tuple-element.61.gnear_ref.own_ref, bf16[528,512]{1,0:T(8,128)(2,1)S(1)} %collective-permute-done.16.sib_ref, f32[1,512]{1,0:T(1,128)S(1)} %get-tuple-element.67.dots_ref, bf16[8,256,1024]{2,1,0:T(8,128)(2,1)S(1)} %copy-done.1), custom_call_target="tpu_custom_call" | custom-call | flops 2147483648 | bytes 4194304 | tf_op jit(solution)/shard_map/back_b/pallas_call | solution.py:255
  82.5 6.9 %all-to-all-start.2 = ((bf16[16,272,256]{2,1,0:T(8,128)(2,1)}), bf16[16,272,256]{2,1,0:T(8,128)(2,1)S(1)}, u32[]{:S(2)}, u32[]{:S(2)}) async-start(bf16[16,272,256]{2,1,0:T(8,128)(2,1)} %bitcast.43), calls=%async_computation.2 | async-start | bytes 4456448 | tf_op jit(solution)/shard_map/all_to_all | solution.py:415
  92.6 2.4 %back_a.1 = (bf16[4,2,64,256]{3,2,1,0:T(8,128)(2,1)S(1)}, bf16[4,2,64,256]{3,2,1,0:T(8,128)(2,1)S(1)}, bf16[4,2,64,256]{3,2,1,0:T(8,128)(2,1)S(1)}, bf16[4,2,64,...) custom-call(s32[1]{0:T(128)} %bitcast.2.z_ref, ...), custom_call_target="tpu_custom_call" | custom-call | flops 2147483648 | bytes 4194304 | tf_op jit(solution)/shard_map/back_a/pallas_call | solution.py:288
  96.6 2.2 %collective-permute-start.19 = (bf16[4,2,64,256]{3,2,1,0:T(8,128)(2,1)S(1)}, bf16[4,2,64,256]{3,2,1,0:T(8,128)(2,1)S(1)}, u32[]{:S(2)}, u32[]{:S(2)}) collective-permute-start(bf16[4,2,64,256]{3,2,1,0:T(8,128)(2,1)S(1)} %get-tuple-element.73), channel_id=1, source_target_pairs={{0,6},{2,0},{4,2},{6,4},{1,7},{3,1},{5,3},{7,5},{8,14},{10,8},{12,... | collective-permute-start | bytes 786440 | tf_op jit(solution)/shard_map/ppermute | solution.py:411
  98.8 10.8 %weight_grads.1 = (f32[4096,256]{1,0:T(8,128)}, f32[4096,256]{1,0:T(8,128)}) custom-call(bf16[256,4096]{1,0:T(8,128)(2,1)} %get-tuple-element.59.near_a, bf16[256,4096]{1,0:T(8,128)(2,1)} %get-tuple-element.60.near_b, bf16[256,4096]{1,0:T(8,128)(2,1)} %collective-permute-done.14.far_a, bf16[256,4096]{1,0:T(8,128)(2,1)} %collective-permute-done.15.far_b, ...), custom_call_target="tpu_custom_call" | custom-call | flops 4294967296 | bytes 17825792 | tf_op jit(solution)/shard_map/weight_grads/pallas_call | solution.py:312
  109.7 2.7 %collective-permute-start.22 = (bf16[4,2,64,256]{3,2,1,0:T(8,128)(2,1)S(1)}, bf16[4,2,64,256]{3,2,1,0:T(8,128)(2,1)S(1)}, u32[]{:S(2)}, u32[]{:S(2)}) collective-permute-start(bf16[4,2,64,256]{3,2,1,0:T(8,128)(2,1)S(1)} %add_convert_fusion.1), channel_id=1, source_target_pairs={{0,6},{2,0},{4,2},{6,4},{1,7},{3,1},{5,3},{7,5},{8,14},{10,8},{12,... | collective-permute-start | bytes 786440 | tf_op jit(solution)/shard_map/ppermute | solution.py:411
  112.6 3.6 %collective-permute-done.22 = bf16[4,2,64,256]{3,2,1,0:T(8,128)(2,1)S(1)} collective-permute-done((bf16[4,2,64,256]{3,2,1,0:T(8,128)(2,1)S(1)}, bf16[4,2,64,256]{3,2,1,0:T(8,128)(2,1)S(1)}, u32[]{:S(2)}, u32[]{:S(2)}) %collective-permute-start.22) | collective-permute-done | bytes 262176 | tf_op jit(solution)/shard_map/ppermute | solution.py:411
  116.3 3.3 %collective-permute-done.20 = bf16[4,2,64,256]{3,2,1,0:T(8,128)(2,1)S(1)} collective-permute-done((bf16[4,2,64,256]{3,2,1,0:T(8,128)(2,1)S(1)}, bf16[4,2,64,256]{3,2,1,0:T(8,128)(2,1)S(1)}, u32[]{:S(2)}, u32[]{:S(2)}) %collective-permute-start.20) | collective-permute-done | bytes 262176 | tf_op jit(solution)/shard_map/ppermute | solution.py:411
  120.6 3.0 %all-to-all-done.2.arrived_ref = bf16[16,272,256]{2,1,0:T(8,128)(2,1)S(1)} async-done(((bf16[16,272,256]{2,1,0:T(8,128)(2,1)}), bf16[16,272,256]{2,1,0:T(8,128)(2,1)S(1)}, u32[]{:S(2)}, u32[]{:S(2)}) %all-to-all-start.2) | async-done | bytes 2228256 | tf_op jit(solution)/shard_map/all_to_all | solution.py:415
  123.6 3.6 %all-to-all-start.3 = ((bf16[16,64,256]{2,1,0:T(8,128)(2,1)}), bf16[16,64,256]{2,1,0:T(8,128)(2,1)S(1)}, u32[]{:S(2)}, u32[]{:S(2)}) async-start(bf16[16,64,256]{2,1,0:T(8,128)(2,1)} %bitcast.44), calls=%async_computation.3 | async-start | bytes 1048576 | tf_op jit(solution)/shard_map/all_to_all | solution.py:415
  127.5 2.2 %collective-permute-start.24 = (bf16[80,256]{1,0:T(8,128)(2,1)S(1)}, bf16[80,256]{1,0:T(8,128)(2,1)S(1)}, u32[]{:S(2)}, u32[]{:S(2)}) collective-permute-start(bf16[80,256]{1,0:T(8,128)(2,1)S(1)} %get-tuple-element.83), channel_id=1, source_target_pairs={{0,4},{2,6},{4,0},{6,2},{1,5},{3,7},{5,1},{7,3},{8,12},{10,14},{12... | collective-permute-start | bytes 122888 | tf_op jit(solution)/shard_map/ppermute | solution.py:411
  132.6 3.5 %all-to-all-done.3.arrived_ref = bf16[16,64,256]{2,1,0:T(8,128)(2,1)S(1)} async-done(((bf16[16,64,256]{2,1,0:T(8,128)(2,1)}), bf16[16,64,256]{2,1,0:T(8,128)(2,1)S(1)}, u32[]{:S(2)}, u32[]{:S(2)}) %all-to-all-start.3) | async-done | bytes 524320 | tf_op jit(solution)/shard_map/all_to_all | solution.py:415
  136.9 4.7 %collective-permute-start.26 = (f32[64,256]{1,0:T(8,128)S(1)}, f32[64,256]{1,0:T(8,128)S(1)}, u32[]{:S(2)}, u32[]{:S(2)}) collective-permute-start(f32[64,256]{1,0:T(8,128)S(1)} %get-tuple-element.86), channel_id=1, source_target_pairs={{0,1},{1,0},{2,3},{3,2},{4,5},{5,4},{6,7},{7,6},{8,9},{9,8},{10,11... | collective-permute-start | bytes 196616 | tf_op jit(solution)/shard_map/ppermute | solution.py:407
  (84 shorter events, 30.6 us)
Async XLA Ops:
  3.7 35.8 %collective-permute-start.7 = (bf16[4096,256]{1,0:T(8,128)(2,1)}, bf16[4096,256]{1,0:T(8,128)(2,1)}, u32[]{:S(2)}, u32[]{:S(2)}) collective-permute-start(bf16[4096,256]{1,0:T(8,128)(2,1)} %bitcast.45), channel_id=1, source_target_pairs={{0,1},{1,0},{2,3},{3,2},{4,5},{5,4},{6,7},{7,6},{8,9},{9,8},{10,11... | collective-permute-start | bytes 6291464 | tf_op jit(solution)/shard_map/ppermute | solution.py:407
  5.0 17.8 %all-to-all-start = ((bf16[16,32,512]{2,1,0:T(8,128)(2,1)}), bf16[16,32,512]{2,1,0:T(8,128)(2,1)S(1)}, u32[]{:S(2)}, u32[]{:S(2)}) async-start(bf16[16,32,512]{2,1,0:T(8,128)(2,1)} %broadcast_in_dim.18), calls=%async_computation | async-start | bytes 1048576 | tf_op jit(solution)/shard_map/all_to_all | solution.py:415
  11.8 29.0 %collective-permute-start.8 = (bf16[4096,256]{1,0:T(8,128)(2,1)}, bf16[4096,256]{1,0:T(8,128)(2,1)}, u32[]{:S(2)}, u32[]{:S(2)}) collective-permute-start(bf16[4096,256]{1,0:T(8,128)(2,1)} %bitcast.47), channel_id=1, source_target_pairs={{0,1},{1,0},{2,3},{3,2},{4,5},{5,4},{6,7},{7,6},{8,9},{9,8},{10,11... | collective-permute-start | bytes 6291464 | tf_op jit(solution)/shard_map/ppermute | solution.py:407
  12.4 5.3 %collective-permute-start.10 = (bf16[32,512]{1,0:T(8,128)(2,1)S(1)}, bf16[32,512]{1,0:T(8,128)(2,1)S(1)}, u32[]{:S(2)}, u32[]{:S(2)}) collective-permute-start(bf16[32,512]{1,0:T(8,128)(2,1)S(1)} %get-tuple-element.92), channel_id=1, source_target_pairs={{0,4},{2,6},{4,0},{6,2},{1,5},{3,7},{5,1},{7,3},{8,12},{10,14},{12... | collective-permute-start | bytes 98312 | tf_op jit(solution)/shard_map/ppermute | solution.py:411
  24.4 32.9 %all-to-all-start.1 = ((bf16[16,4,32,512]{3,2,1,0:T(8,128)(2,1)}), bf16[16,4,32,512]{3,2,1,0:T(8,128)(2,1)S(1)}, u32[]{:S(2)}, u32[]{:S(2)}) async-start(bf16[16,4,32,512]{3,2,1,0:T(8,128)(2,1)} %broadcast_in_dim.19), calls=%async_computation.1 | async-start | bytes 4194304 | tf_op jit(solution)/shard_map/all_to_all | solution.py:415
  29.0 7.0 %collective-permute-start.4 = (bf16[8,32,512]{2,1,0:T(8,128)(2,1)S(1)}, bf16[8,32,512]{2,1,0:T(8,128)(2,1)S(1)}, u32[]{:S(2)}, u32[]{:S(2)}) collective-permute-start(bf16[8,32,512]{2,1,0:T(8,128)(2,1)S(1)} %get-tuple-element.89), channel_id=1, source_target_pairs={{0,6},{2,0},{4,2},{6,4},{1,7},{3,1},{5,3},{7,5},{8,14},{10,8},{12,... | collective-permute-start | bytes 786440 | tf_op jit(solution)/shard_map/ppermute | solution.py:411
  32.0 7.4 %collective-permute-start.1 = (bf16[8,32,512]{2,1,0:T(8,128)(2,1)S(1)}, bf16[8,32,512]{2,1,0:T(8,128)(2,1)S(1)}, u32[]{:S(2)}, u32[]{:S(2)}) collective-permute-start(bf16[8,32,512]{2,1,0:T(8,128)(2,1)S(1)} %get-tuple-element.90), channel_id=1, source_target_pairs={{0,2},{2,4},{4,6},{6,0},{1,3},{3,5},{5,7},{7,1},{8,10},{10,12},{12... | collective-permute-start | bytes 786440 | tf_op jit(solution)/shard_map/ppermute | solution.py:411
  32.0 18.0 %collective-permute-start.2 = (bf16[8,32,512]{2,1,0:T(8,128)(2,1)S(1)}, bf16[8,32,512]{2,1,0:T(8,128)(2,1)}, u32[]{:S(2)}, u32[]{:S(2)}) collective-permute-start(bf16[8,32,512]{2,1,0:T(8,128)(2,1)S(1)} %get-tuple-element.89), channel_id=1, source_target_pairs={{0,2},{2,4},{4,6},{6,0},{1,3},{3,5},{5,7},{7,1},{8,10},{10,12},{12... | collective-permute-start | bytes 786440 | tf_op jit(solution)/shard_map/ppermute | solution.py:411
  36.0 14.0 %collective-permute-start.3 = (bf16[8,32,512]{2,1,0:T(8,128)(2,1)S(1)}, bf16[8,32,512]{2,1,0:T(8,128)(2,1)}, u32[]{:S(2)}, u32[]{:S(2)}) collective-permute-start(bf16[8,32,512]{2,1,0:T(8,128)(2,1)S(1)} %get-tuple-element.90), channel_id=1, source_target_pairs={{0,6},{2,0},{4,2},{6,4},{1,7},{3,1},{5,3},{7,5},{8,14},{10,8},{12,... | collective-permute-start | bytes 786440 | tf_op jit(solution)/shard_map/ppermute | solution.py:411
  39.4 10.6 %collective-permute-start.6 = (bf16[8,32,512]{2,1,0:T(8,128)(2,1)S(1)}, bf16[8,32,512]{2,1,0:T(8,128)(2,1)}, u32[]{:S(2)}, u32[]{:S(2)}) collective-permute-start(bf16[8,32,512]{2,1,0:T(8,128)(2,1)S(1)} %collective-permute-done.4), channel_id=1, source_target_pairs={{0,6},{2,0},{4,2},{6,4},{1,7},{3,1},{5,3},{7,5},{8,14},{10,8},{12,... | collective-permute-start | bytes 786440 | tf_op jit(solution)/shard_map/ppermute | solution.py:411
  39.5 11.0 %collective-permute-start.5 = (bf16[8,32,512]{2,1,0:T(8,128)(2,1)S(1)}, bf16[8,32,512]{2,1,0:T(8,128)(2,1)}, u32[]{:S(2)}, u32[]{:S(2)}) collective-permute-start(bf16[8,32,512]{2,1,0:T(8,128)(2,1)S(1)} %collective-permute-done.1), channel_id=1, source_target_pairs={{0,2},{2,4},{4,6},{6,0},{1,3},{3,5},{5,7},{7,1},{8,10},{10,12},{12... | collective-permute-start | bytes 786440 | tf_op jit(solution)/shard_map/ppermute | solution.py:411
  57.2 12.2 %collective-permute-start.12 = (bf16[256,512]{1,0:T(8,128)(2,1)S(1)}, bf16[256,512]{1,0:T(8,128)(2,1)S(1)}, u32[]{:S(2)}, u32[]{:S(2)}) collective-permute-start(bf16[256,512]{1,0:T(8,128)(2,1)S(1)} %get-tuple-element.53), channel_id=1, source_target_pairs={{0,1},{1,0},{2,3},{3,2},{4,5},{5,4},{6,7},{7,6},{8,9},{9,8},{10,11... | collective-permute-start | bytes 786440 | tf_op jit(solution)/shard_map/ppermute | solution.py:407
  69.4 29.4 %collective-permute-start.14 = (bf16[256,4096]{1,0:T(8,128)(2,1)}, bf16[256,4096]{1,0:T(8,128)(2,1)}, u32[]{:S(2)}, u32[]{:S(2)}) collective-permute-start(bf16[256,4096]{1,0:T(8,128)(2,1)} %get-tuple-element.59.near_a), channel_id=1, source_target_pairs={{0,1},{1,0},{2,3},{3,2},{4,5},{5,4},{6,7},{7,6},{8,9},{9,8},{10,11... | collective-permute-start | bytes 6291464 | tf_op jit(solution)/shard_map/ppermute | solution.py:407
  70.9 27.9 %collective-permute-start.15 = (bf16[256,4096]{1,0:T(8,128)(2,1)}, bf16[256,4096]{1,0:T(8,128)(2,1)}, u32[]{:S(2)}, u32[]{:S(2)}) collective-permute-start(bf16[256,4096]{1,0:T(8,128)(2,1)} %get-tuple-element.60.near_b), channel_id=1, source_target_pairs={{0,1},{1,0},{2,3},{3,2},{4,5},{5,4},{6,7},{7,6},{8,9},{9,8},{10,11... | collective-permute-start | bytes 6291464 | tf_op jit(solution)/shard_map/ppermute | solution.py:407
  82.5 41.1 %all-to-all-start.2 = ((bf16[16,272,256]{2,1,0:T(8,128)(2,1)}), bf16[16,272,256]{2,1,0:T(8,128)(2,1)S(1)}, u32[]{:S(2)}, u32[]{:S(2)}) async-start(bf16[16,272,256]{2,1,0:T(8,128)(2,1)} %bitcast.43), calls=%async_computation.2 | async-start | bytes 4456448 | tf_op jit(solution)/shard_map/all_to_all | solution.py:415
  95.0 17.6 %collective-permute-start.17 = (bf16[4,2,64,256]{3,2,1,0:T(8,128)(2,1)S(1)}, bf16[4,2,64,256]{3,2,1,0:T(8,128)(2,1)S(1)}, u32[]{:S(2)}, u32[]{:S(2)}) collective-permute-start(bf16[4,2,64,256]{3,2,1,0:T(8,128)(2,1)S(1)} %get-tuple-element.70), channel_id=1, source_target_pairs={{0,6},{2,0},{4,2},{6,4},{1,7},{3,1},{5,3},{7,5},{8,14},{10,8},{12,... | collective-permute-start | bytes 786440 | tf_op jit(solution)/shard_map/ppermute | solution.py:411
  96.1 13.5 %collective-permute-start.18 = (bf16[4,2,64,256]{3,2,1,0:T(8,128)(2,1)S(1)}, bf16[4,2,64,256]{3,2,1,0:T(8,128)(2,1)S(1)}, u32[]{:S(2)}, u32[]{:S(2)}) collective-permute-start(bf16[4,2,64,256]{3,2,1,0:T(8,128)(2,1)S(1)} %get-tuple-element.72), channel_id=1, source_target_pairs={{0,2},{2,4},{4,6},{6,0},{1,3},{3,5},{5,7},{7,1},{8,10},{10,12},{12... | collective-permute-start | bytes 786440 | tf_op jit(solution)/shard_map/ppermute | solution.py:411
  96.6 13.1 %collective-permute-start.19 = (bf16[4,2,64,256]{3,2,1,0:T(8,128)(2,1)S(1)}, bf16[4,2,64,256]{3,2,1,0:T(8,128)(2,1)S(1)}, u32[]{:S(2)}, u32[]{:S(2)}) collective-permute-start(bf16[4,2,64,256]{3,2,1,0:T(8,128)(2,1)S(1)} %get-tuple-element.73), channel_id=1, source_target_pairs={{0,6},{2,0},{4,2},{6,4},{1,7},{3,1},{5,3},{7,5},{8,14},{10,8},{12,... | collective-permute-start | bytes 786440 | tf_op jit(solution)/shard_map/ppermute | solution.py:411
  98.8 13.8 %collective-permute-start.21 = (bf16[4,2,64,256]{3,2,1,0:T(8,128)(2,1)S(1)}, bf16[4,2,64,256]{3,2,1,0:T(8,128)(2,1)S(1)}, u32[]{:S(2)}, u32[]{:S(2)}) collective-permute-start(bf16[4,2,64,256]{3,2,1,0:T(8,128)(2,1)S(1)} %get-tuple-element.75), channel_id=1, source_target_pairs={{0,2},{2,4},{4,6},{6,0},{1,3},{3,5},{5,7},{7,1},{8,10},{10,12},{12... | collective-permute-start | bytes 786440 | tf_op jit(solution)/shard_map/ppermute | solution.py:411
  109.7 6.5 %collective-permute-start.22 = (bf16[4,2,64,256]{3,2,1,0:T(8,128)(2,1)S(1)}, bf16[4,2,64,256]{3,2,1,0:T(8,128)(2,1)S(1)}, u32[]{:S(2)}, u32[]{:S(2)}) collective-permute-start(bf16[4,2,64,256]{3,2,1,0:T(8,128)(2,1)S(1)} %add_convert_fusion.1), channel_id=1, source_target_pairs={{0,6},{2,0},{4,2},{6,4},{1,7},{3,1},{5,3},{7,5},{8,14},{10,8},{12,... | collective-permute-start | bytes 786440 | tf_op jit(solution)/shard_map/ppermute | solution.py:411
  112.5 7.0 %collective-permute-start.20 = (bf16[4,2,64,256]{3,2,1,0:T(8,128)(2,1)S(1)}, bf16[4,2,64,256]{3,2,1,0:T(8,128)(2,1)S(1)}, u32[]{:S(2)}, u32[]{:S(2)}) collective-permute-start(bf16[4,2,64,256]{3,2,1,0:T(8,128)(2,1)S(1)} %add_convert_fusion.3), channel_id=1, source_target_pairs={{0,2},{2,4},{4,6},{6,0},{1,3},{3,5},{5,7},{7,1},{8,10},{10,12},{12... | collective-permute-start | bytes 786440 | tf_op jit(solution)/shard_map/ppermute | solution.py:411
  123.6 12.5 %all-to-all-start.3 = ((bf16[16,64,256]{2,1,0:T(8,128)(2,1)}), bf16[16,64,256]{2,1,0:T(8,128)(2,1)S(1)}, u32[]{:S(2)}, u32[]{:S(2)}) async-start(bf16[16,64,256]{2,1,0:T(8,128)(2,1)} %bitcast.44), calls=%async_computation.3 | async-start | bytes 1048576 | tf_op jit(solution)/shard_map/all_to_all | solution.py:415
  127.5 4.5 %collective-permute-start.24 = (bf16[80,256]{1,0:T(8,128)(2,1)S(1)}, bf16[80,256]{1,0:T(8,128)(2,1)S(1)}, u32[]{:S(2)}, u32[]{:S(2)}) collective-permute-start(bf16[80,256]{1,0:T(8,128)(2,1)S(1)} %get-tuple-element.83), channel_id=1, source_target_pairs={{0,4},{2,6},{4,0},{6,2},{1,5},{3,7},{5,1},{7,3},{8,12},{10,14},{12... | collective-permute-start | bytes 122888 | tf_op jit(solution)/shard_map/ppermute | solution.py:411
  136.9 5.6 %collective-permute-start.26 = (f32[64,256]{1,0:T(8,128)S(1)}, f32[64,256]{1,0:T(8,128)S(1)}, u32[]{:S(2)}, u32[]{:S(2)}) collective-permute-start(f32[64,256]{1,0:T(8,128)S(1)} %get-tuple-element.86), channel_id=1, source_target_pairs={{0,1},{1,0},{2,3},{3,2},{4,5},{5,4},{6,7},{7,6},{8,9},{9,8},{10,11... | collective-permute-start | bytes 196616 | tf_op jit(solution)/shard_map/ppermute | solution.py:407
  (19 other events, 114.3 us)
